TPU v7x, 32 devices: a whole 2x2x4 slice. The times are simulated.
32 devices in a mesh: ctx: 8 (over y, x, core), wsh: 4 (over z).
Axes of the slice: x: 2, y: 2, z: 4, core: 2. Of those that a mesh axis runs over, the one named last changes fastest.
Arguments:
- layer_input: bfloat16 [12, 1024, 1472], P('wsh', 'ctx'), may hold values from -6 to 6
- segments: int32 [12, 1024], P('wsh', 'ctx'), may hold values from 0 to 3, never falling along the last dimension, each value on 1 to 512 neighbouring positions
- cotangent: bfloat16 [12, 1024, 1472], P('wsh', 'ctx'), may hold values from -6 to 6
- query_weight: bfloat16 [1472, 384], P('wsh'), may hold values from -0.15625 to 0.15625
- key_weight: bfloat16 [1472, 384], P('wsh'), may hold values from -0.0390625 to 0.0390625
- value_weight: bfloat16 [1472, 384], P('wsh'), may hold values from -0.15625 to 0.15625
- projection: bfloat16 [384, 1472], P('wsh'), may hold values from -1.25 to 1.25
- gate_weight: bfloat16 [1472, 3584], P('wsh'), may hold values from -0.15625 to 0.15625
- up_weight: bfloat16 [1472, 3584], P('wsh'), may hold values from -0.15625 to 0.15625
- down_weight: bfloat16 [3584, 1472], P('wsh'), may hold values from -0.09375 to 0.09375
- gain_early: bfloat16 [1472], P('wsh'), may hold values from 0.099609375 to 1.8984375
- gain_late: bfloat16 [1472], P('wsh'), may hold values from 0.099609375 to 1.8984375
- bias_table: bfloat16 [32, 6], P('wsh'), may hold values from -4 to 4
Outputs:
- layer_output: bfloat16 [12, 1024, 1472], P('wsh', 'ctx')
- input_grad: bfloat16 [12, 1024, 1472], P('wsh', 'ctx')
- query_grad: float32 [1472, 384], P('wsh')
- key_grad: float32 [1472, 384], P('wsh')
- value_grad: float32 [1472, 384], P('wsh')
- projection_grad: float32 [384, 1472], P('wsh')
- gate_grad: float32 [1472, 3584], P('wsh')
- up_grad: float32 [1472, 3584], P('wsh')
- down_grad: float32 [3584, 1472], P('wsh')
- early_grad: float32 [1472], P('wsh')
- late_grad: float32 [1472], P('wsh')
- table_grad: float32 [32, 6], P('wsh')
Inputs may be any that keep to these rules, and one draw needn't show every extreme that they name: `segments`: document numbers never fall along a sequence; no document has more than 512 tokens, and some document has exactly that many.
All inputs are finite; a program needn't handle non-finite values.
Results may differ from a plain program's by a relative error of at most 0.02.
Values may be sent and summed in bfloat16 or wider, within the bound.
No kernel may reach another device: no remote copies, remote signals or barrier semaphores. Data moves between devices by JAX's collectives and lax.ppermute only.
A program may use at most 256 MiB of HBM per device.

v0:
```python
import jax
import jax.numpy as jnp
from jax import lax
from jax.sharding import PartitionSpec as P

BUCKETS = 32
MB = 3


EPSILON = 1e-06
NEGATIVE = -1e30
PRECISE = lax.Precision.HIGHEST
BUCKET_EDGES = (12, 16, 23, 32, 46, 64, 91)
FLOAT = jnp.float32
BFLOAT = jnp.bfloat16


def shifted(value, axis, steps):
    count = lax.axis_size(axis)
    pairs = [(source, (source + steps) % count) for source in range(count)]
    return lax.ppermute(value, axis, pairs)


def bucket_of(offsets):
    distance = jnp.abs(offsets)
    coarse = 8 + sum(((distance >= boundary).astype(jnp.int32) for boundary in BUCKET_EDGES))
    bucket_level = jnp.where(distance < 8, distance, coarse)
    return bucket_level + jnp.where(offsets > 0, 16, 0)


def rms_scale(hidden, gain_vector):
    return (
        hidden
        * lax.rsqrt(jnp.mean(hidden * hidden, axis=-1, keepdims=True) + EPSILON)
        * gain_vector
    )


def gated(gate_values, up_values):
    return jax.nn.gelu(gate_values, approximate=True) * up_values


def bucket_onehot(query_places, key_places):
    buckets = bucket_of(key_places[None, :] - query_places[:, None])
    return (buckets.reshape(-1, 1) == jnp.arange(BUCKETS, dtype=jnp.int32)[None, :]).astype(FLOAT)


def block_scores(queries, key_rows, query_places, key_places, query_segs, key_segs, table_rows):
    onehot = bucket_onehot(query_places, key_places)
    flat_bias = jnp.dot(onehot, table_rows, precision=PRECISE)
    bias_terms = jnp.transpose(
        flat_bias.reshape(query_places.shape[0], key_places.shape[0], table_rows.shape[1]),
        (2, 0, 1),
    )
    raw_scores = jnp.einsum("sihd,sjhd->shij", queries, key_rows, preferred_element_type=FLOAT)
    allowed = query_segs[:, None, :, None] == key_segs[:, None, None, :]
    return (jnp.where(allowed, raw_scores + bias_terms[None], NEGATIVE), onehot)


def forward_step(soft_state, key_rows, value_rows, key_places, key_segs, context):
    queries, query_places, query_segs, table_rows = context
    running_max, running_sum, weighted = soft_state
    scores = block_scores(
        queries, key_rows, query_places, key_places, query_segs, key_segs, table_rows
    )[0]
    new_max = jnp.maximum(running_max, jnp.max(scores, axis=-1))
    factor = jnp.exp(running_max - new_max)
    weights_raw = jnp.exp(scores - new_max[..., None])
    running_sum = running_sum * factor + jnp.sum(weights_raw, axis=-1)
    update = jnp.einsum(
        "shij,sjhd->sihd", weights_raw.astype(BFLOAT), value_rows, preferred_element_type=FLOAT
    )
    weighted = weighted * jnp.transpose(factor, (0, 2, 1))[..., None] + update
    return (new_max, running_sum, weighted)


def backward_step(key_rows, value_rows, key_places, key_segs, context, grad_inputs):
    queries, query_places, query_segs, table_rows = context
    attn_grad, logsum, row_delta = grad_inputs
    scores, onehot = block_scores(
        queries, key_rows, query_places, key_places, query_segs, key_segs, table_rows
    )
    soft_probs = jnp.exp(scores - logsum[..., None])
    prob_back = jnp.einsum("sihd,sjhd->shij", attn_grad, value_rows, preferred_element_type=FLOAT)
    score_grad = soft_probs * (prob_back - row_delta[..., None])
    summed = jnp.transpose(jnp.sum(score_grad, axis=0), (1, 2, 0)).reshape(-1, table_rows.shape[1])
    table_part = jnp.einsum("pb,ph->bh", onehot, summed, precision=PRECISE)
    score_low = score_grad.astype(BFLOAT)
    query_part = jnp.einsum("shij,sjhd->sihd", score_low, key_rows, preferred_element_type=FLOAT)
    key_part = jnp.einsum("shij,sihd->sjhd", score_low, queries, preferred_element_type=FLOAT)
    value_part = jnp.einsum(
        "shij,sihd->sjhd", soft_probs.astype(BFLOAT), attn_grad, preferred_element_type=FLOAT
    )
    return (query_part, key_part, value_part, table_part)


def unpack(gathered):
    joined_qkv = jnp.concatenate((gathered[0], gathered[1], gathered[2]), axis=1)
    return (
        joined_qkv,
        gathered[3],
        gathered[4],
        gathered[5],
        gathered[6],
        gathered[7].astype(FLOAT),
        gathered[8].astype(FLOAT),
        gathered[9].astype(FLOAT),
    )


def on_device(
    layer_input,
    segments,
    cotangent,
    query_weight,
    key_weight,
    value_weight,
    projection,
    gate_weight,
    up_weight,
    down_weight,
    gain_early,
    gain_late,
    bias_table,
):
    cycle_size = lax.axis_size("ctx")
    cycle_index = lax.axis_index("ctx")
    seq_local, block_rows, model_width = layer_input.shape
    per_batch = seq_local // MB
    inner_width = query_weight.shape[1]
    head_count = bias_table.shape[1]
    head_size = inner_width // head_count
    all_segs = lax.all_gather(segments, "ctx", axis=1, tiled=True)
    block_range = jnp.arange(block_rows, dtype=jnp.int32)
    query_places = cycle_index * block_rows + block_range
    qkv_total = jnp.zeros((model_width, 3 * inner_width), FLOAT)
    proj_total = jnp.zeros((inner_width, model_width), FLOAT)
    gate_total = jnp.zeros((model_width, gate_weight.shape[1]), FLOAT)
    up_total = jnp.zeros((model_width, gate_weight.shape[1]), FLOAT)
    down_total = jnp.zeros((gate_weight.shape[1], model_width), FLOAT)
    early_total = jnp.zeros((model_width,), FLOAT)
    late_total = jnp.zeros((model_width,), FLOAT)
    table_total = jnp.zeros((BUCKETS, head_count), FLOAT)
    outputs = []
    input_grads = []
    for micro_batch in range(MB):
        row_start = micro_batch * per_batch
        row_stop = row_start + per_batch
        joined_qkv, proj_full, gate_full, up_full, down_full, early_gain, late_gain, table_rows = (
            unpack(
                (
                    lax.all_gather(query_weight, "wsh", axis=0, tiled=True),
                    lax.all_gather(key_weight, "wsh", axis=0, tiled=True),
                    lax.all_gather(value_weight, "wsh", axis=0, tiled=True),
                    lax.all_gather(projection, "wsh", axis=0, tiled=True),
                    lax.all_gather(gate_weight, "wsh", axis=0, tiled=True),
                    lax.all_gather(up_weight, "wsh", axis=0, tiled=True),
                    lax.all_gather(down_weight, "wsh", axis=0, tiled=True),
                    lax.all_gather(gain_early, "wsh", axis=0, tiled=True),
                    lax.all_gather(gain_late, "wsh", axis=0, tiled=True),
                    lax.all_gather(bias_table, "wsh", axis=0, tiled=True),
                )
            )
        )
        hidden_in = layer_input[row_start:row_stop].astype(FLOAT)
        seg_own = segments[row_start:row_stop]
        seg_whole = all_segs[row_start:row_stop]
        normed = rms_scale(hidden_in, early_gain).astype(BFLOAT)
        flat_normed = normed.reshape(-1, model_width)
        qkv_rows = (
            jnp.dot(flat_normed, joined_qkv, preferred_element_type=FLOAT)
            .astype(BFLOAT)
            .reshape(per_batch, block_rows, 3, head_count, head_size)
        )
        queries = qkv_rows[:, :, 0]
        key_rows = qkv_rows[:, :, 1]
        value_rows = qkv_rows[:, :, 2]
        context = (queries, query_places, seg_own, table_rows)
        start_state = (
            jnp.full((per_batch, head_count, block_rows), NEGATIVE, FLOAT),
            jnp.zeros((per_batch, head_count, block_rows), FLOAT),
            jnp.zeros((per_batch, block_rows, head_count, head_size), FLOAT),
        )
        own_state = forward_step(start_state, key_rows, value_rows, query_places, seg_own, context)

        def cycle_turn(cycle_step, cycle_carry):
            keys_now, values_now, soft_state = cycle_carry
            keys_now, values_now = shifted((keys_now, values_now), "ctx", 1)
            source = (cycle_index - cycle_step) % cycle_size
            key_places = source * block_rows + block_range
            key_segs = lax.dynamic_slice_in_dim(seg_whole, source * block_rows, block_rows, 1)
            return (
                keys_now,
                values_now,
                forward_step(soft_state, keys_now, values_now, key_places, key_segs, context),
            )

        cycle_final = lax.fori_loop(1, cycle_size, cycle_turn, (key_rows, value_rows, own_state))
        soft_state = cycle_final[2]
        running_max, running_sum, weighted = soft_state
        attention = weighted / jnp.transpose(running_sum, (0, 2, 1))[..., None]
        logsum = running_max + jnp.log(running_sum)
        attn_low = attention.astype(BFLOAT).reshape(-1, inner_width)
        after_attn = hidden_in + jnp.dot(attn_low, proj_full, preferred_element_type=FLOAT).reshape(
            per_batch, block_rows, model_width
        )
        normed_late = rms_scale(after_attn, late_gain).astype(BFLOAT).reshape(-1, model_width)
        gate_pre = jnp.dot(normed_late, gate_full, preferred_element_type=FLOAT)
        up_pre = jnp.dot(normed_late, up_full, preferred_element_type=FLOAT)
        activation = gated(gate_pre, up_pre).astype(BFLOAT)
        result = after_attn + jnp.dot(activation, down_full, preferred_element_type=FLOAT).reshape(
            per_batch, block_rows, model_width
        )
        outputs.append(result.astype(BFLOAT))
        joined_qkv, proj_full, gate_full, up_full, down_full, early_gain, late_gain, table_rows = (
            unpack(
                (
                    lax.all_gather(query_weight, "wsh", axis=0, tiled=True),
                    lax.all_gather(key_weight, "wsh", axis=0, tiled=True),
                    lax.all_gather(value_weight, "wsh", axis=0, tiled=True),
                    lax.all_gather(projection, "wsh", axis=0, tiled=True),
                    lax.all_gather(gate_weight, "wsh", axis=0, tiled=True),
                    lax.all_gather(up_weight, "wsh", axis=0, tiled=True),
                    lax.all_gather(down_weight, "wsh", axis=0, tiled=True),
                    lax.all_gather(gain_early, "wsh", axis=0, tiled=True),
                    lax.all_gather(gain_late, "wsh", axis=0, tiled=True),
                    lax.all_gather(bias_table, "wsh", axis=0, tiled=True),
                )
            )
        )
        context = (queries, query_places, seg_own, table_rows)
        out_grad = cotangent[row_start:row_stop].reshape(-1, model_width)
        down_total = down_total + jnp.einsum(
            "tf,td->fd", activation, out_grad, preferred_element_type=FLOAT
        )
        act_grad = jnp.einsum("td,fd->tf", out_grad, down_full, preferred_element_type=FLOAT)
        gate_pull = jax.vjp(gated, gate_pre, up_pre)[1]
        gate_back, up_back = gate_pull(act_grad)
        gate_low = gate_back.astype(BFLOAT)
        up_low = up_back.astype(BFLOAT)
        gate_total = gate_total + jnp.einsum(
            "td,tf->df", normed_late, gate_low, preferred_element_type=FLOAT
        )
        up_total = up_total + jnp.einsum(
            "td,tf->df", normed_late, up_low, preferred_element_type=FLOAT
        )
        late_back = jnp.einsum(
            "tf,df->td", gate_low, gate_full, preferred_element_type=FLOAT
        ) + jnp.einsum("tf,df->td", up_low, up_full, preferred_element_type=FLOAT)
        late_pull = jax.vjp(rms_scale, after_attn, late_gain)[1]
        norm_back, late_part = late_pull(late_back.reshape(per_batch, block_rows, model_width))
        residual_grad = cotangent[row_start:row_stop].astype(FLOAT) + norm_back
        late_total = late_total + late_part
        mix_low = residual_grad.astype(BFLOAT).reshape(-1, model_width)
        proj_total = proj_total + jnp.einsum(
            "ti,td->id", attn_low, mix_low, preferred_element_type=FLOAT
        )
        attn_grad = (
            jnp.einsum("td,id->ti", mix_low, proj_full, preferred_element_type=FLOAT)
            .astype(BFLOAT)
            .reshape(per_batch, block_rows, head_count, head_size)
        )
        row_delta = jnp.transpose(jnp.sum(attn_grad.astype(FLOAT) * attention, axis=-1), (0, 2, 1))
        grad_inputs = (attn_grad, logsum, row_delta)
        zero_heads = jnp.zeros((per_batch, block_rows, head_count, head_size), FLOAT)
        zero_table = jnp.zeros((BUCKETS, head_count), FLOAT)

        def back_turn(cycle_step, cycle_carry):
            keys_now, values_now, key_acc, value_acc, query_acc, table_acc = cycle_carry
            source = (cycle_index - cycle_step) % cycle_size
            key_places = source * block_rows + block_range
            key_segs = lax.dynamic_slice_in_dim(seg_whole, source * block_rows, block_rows, 1)
            step_parts = backward_step(
                keys_now, values_now, key_places, key_segs, context, grad_inputs
            )
            return (
                keys_now,
                values_now,
                key_acc + step_parts[1],
                value_acc + step_parts[2],
                query_acc + step_parts[0],
                table_acc + step_parts[3],
            )

        def send_grads(key_acc, value_acc):
            return (
                shifted(key_acc.astype(jnp.bfloat16), "ctx", 1).astype(key_acc.dtype),
                shifted(value_acc.astype(jnp.bfloat16), "ctx", 1).astype(value_acc.dtype),
            )

        def cycle_back(cycle_step, cycle_carry):
            turn_done = back_turn(cycle_step, cycle_carry)
            keys_now, values_now = shifted((turn_done[0], turn_done[1]), "ctx", 1)
            key_acc, value_acc = send_grads(turn_done[2], turn_done[3])
            return (keys_now, values_now, key_acc, value_acc, turn_done[4], turn_done[5])

        looped = lax.fori_loop(
            0,
            cycle_size - 1,
            cycle_back,
            (key_rows, value_rows, zero_heads, zero_heads, zero_heads, zero_table),
        )
        turn_done = back_turn(cycle_size - 1, looped)
        key_acc, value_acc = send_grads(turn_done[2], turn_done[3])
        query_acc = turn_done[4]
        table_acc = turn_done[5]
        qkv_low = (
            jnp.stack((query_acc, key_acc, value_acc), axis=2)
            .astype(BFLOAT)
            .reshape(-1, 3 * inner_width)
        )
        qkv_total = qkv_total + jnp.einsum(
            "td,tc->dc", flat_normed, qkv_low, preferred_element_type=FLOAT
        )
        early_back = jnp.einsum("tc,dc->td", qkv_low, joined_qkv, preferred_element_type=FLOAT)
        early_pull = jax.vjp(rms_scale, hidden_in, early_gain)[1]
        norm_first, early_part = early_pull(early_back.reshape(per_batch, block_rows, model_width))
        early_total = early_total + early_part
        table_total = table_total + table_acc
        input_grads.append((residual_grad + norm_first).astype(BFLOAT))
    owned_grads = (
        lax.psum_scatter(
            qkv_total[:, :inner_width].astype(jnp.bfloat16), "wsh", scatter_dimension=0, tiled=True
        ).astype(jnp.float32),
        lax.psum_scatter(
            qkv_total[:, inner_width : 2 * inner_width].astype(jnp.bfloat16),
            "wsh",
            scatter_dimension=0,
            tiled=True,
        ).astype(jnp.float32),
        lax.psum_scatter(
            qkv_total[:, 2 * inner_width :].astype(jnp.bfloat16),
            "wsh",
            scatter_dimension=0,
            tiled=True,
        ).astype(jnp.float32),
        lax.psum_scatter(
            proj_total.astype(jnp.bfloat16), "wsh", scatter_dimension=0, tiled=True
        ).astype(jnp.float32),
        lax.psum_scatter(
            gate_total.astype(jnp.bfloat16), "wsh", scatter_dimension=0, tiled=True
        ).astype(jnp.float32),
        lax.psum_scatter(
            up_total.astype(jnp.bfloat16), "wsh", scatter_dimension=0, tiled=True
        ).astype(jnp.float32),
        lax.psum_scatter(
            down_total.astype(jnp.bfloat16), "wsh", scatter_dimension=0, tiled=True
        ).astype(jnp.float32),
        lax.psum_scatter(
            early_total.astype(jnp.bfloat16), "wsh", scatter_dimension=0, tiled=True
        ).astype(jnp.float32),
        lax.psum_scatter(
            late_total.astype(jnp.bfloat16), "wsh", scatter_dimension=0, tiled=True
        ).astype(jnp.float32),
        lax.psum_scatter(
            table_total.astype(jnp.bfloat16), "wsh", scatter_dimension=0, tiled=True
        ).astype(jnp.float32),
    )
    summed = lax.psum(
        (
            owned_grads[0],
            owned_grads[1],
            owned_grads[2],
            owned_grads[3],
            owned_grads[4],
            owned_grads[5],
            owned_grads[6],
            owned_grads[7],
            owned_grads[8],
            owned_grads[9],
        ),
        "ctx",
    )
    return (
        jnp.concatenate(outputs, axis=0),
        jnp.concatenate(input_grads, axis=0),
        summed[0],
        summed[1],
        summed[2],
        summed[3],
        summed[4],
        summed[5],
        summed[6],
        summed[7],
        summed[8],
        summed[9],
    )


def solution(mesh):
    return jax.shard_map(
        on_device,
        mesh=mesh,
        in_specs=(
            P("wsh", "ctx", None),
            P("wsh", "ctx"),
            P("wsh", "ctx", None),
            P("wsh", None),
            P("wsh", None),
            P("wsh", None),
            P("wsh", None),
            P("wsh", None),
            P("wsh", None),
            P("wsh", None),
            P("wsh"),
            P("wsh"),
            P("wsh", None),
        ),
        out_specs=(
            P("wsh", "ctx", None),
            P("wsh", "ctx", None),
            P("wsh", None),
            P("wsh", None),
            P("wsh", None),
            P("wsh", None),
            P("wsh", None),
            P("wsh", None),
            P("wsh", None),
            P("wsh"),
            P("wsh"),
            P("wsh", None),
        ),
        check_vma=False,
    )
```

profile of v0, /device:TPU:0, one launch (start us, length us, event | category | flops | bytes accessed | tf_op | source)
XLA Modules:
  0.0 2214.2 jit_solution(11966628708460419476)
XLA Ops:
  12.6 10.3 all_gather.27
  25.2 12.6 all-reduce.7
  37.8 11.9 all_gather.26
  58.2 14.4 all-gather.10.cloned.1.call-done
  74.1 28.9 %all-gather.12.cloned.1.call-done = bf16[1472,384]{1,0:T(8,128)(2,1)} async-done(((bf16[368,384]{1,0:T(8,128)(2,1)}), bf16[1472,384]{1,0:T(8,128)(2,1)}) %all-gather.12.cloned.1.call-update) | async-done | bytes 1130512 | tf_op jit(solution)/shard_map/all_gather | solution.py:154
  104.4 2.9 convolution_convert_fusion
  118.4 2.6 convolution_convert_fusion.2
  132.1 115.2 %while.150 = (s32[]{:T(128)}, bf16[1,128,6,64]{1,3,2,0:T(8,128)(2,1)}, bf16[1,128,6,64]{1,3,2,0:T(8,128)(2,1)}, f32[1,6,128]{2,1,0:T(8,128)}, f32[1,6,128]{2,1,0...) while((s32[]{:T(128)}, ...), condition=%wide.region_6.7_spmd.clone, body=%wide.region_3.6_spmd.clone.sunk | while | flops 64702992 | bytes 7234868 | solution.py:198
  248.8 2.8 multiply_reduce_fusion.2
  251.7 2.6 convolution_convert_fusion.1
  260.7 73.8 %while.151 = (s32[]{:T(128)}, bf16[1,128,6,64]{1,3,2,0:T(8,128)(2,1)}, bf16[1,128,6,64]{1,3,2,0:T(8,128)(2,1)}, f32[1,6,128]{2,1,0:T(8,128)S(1)}, f32[1,6,128]{2...) while((s32[]{:T(128)}, ...), condition=%wide.region_14.15_spmd.clone, body=%wide.region_11.14_spmd.clone.sunk | while | flops 64702992 | bytes 5625000 | solution.py:198
  273.8 2.7 collective-permute-done.2
  284.3 2.7 collective-permute-done.2
  294.9 2.6 collective-permute-done.2
  305.4 2.7 collective-permute-done.2
  316.0 2.6 collective-permute-done.2
  326.5 2.7 collective-permute-done.2
  337.6 74.3 %while.152 = (s32[]{:T(128)}, bf16[1,128,6,64]{1,3,2,0:T(8,128)(2,1)}, bf16[1,128,6,64]{1,3,2,0:T(8,128)(2,1)}, f32[1,6,128]{2,1,0:T(8,128)S(1)}, f32[1,6,128]{2...) while((s32[]{:T(128)}, ...), condition=%wide.region_22.23_spmd.clone, body=%wide.region_19.22_spmd.clone.sunk | while | flops 64702992 | bytes 5625000 | solution.py:198
  350.8 2.6 collective-permute-done.4
  361.3 2.7 collective-permute-done.4
  371.9 2.6 collective-permute-done.4
  382.3 2.7 collective-permute-done.4
  392.9 2.6 collective-permute-done.4
  403.4 2.7 collective-permute-done.4
  415.5 7.1 fusion.513
  422.5 82.0 %all-gather.18.cloned.1.call-done = bf16[1472,3584]{1,0:T(8,128)(2,1)} async-done(((bf16[368,3584]{1,0:T(8,128)(2,1)}), bf16[1472,3584]{1,0:T(8,128)(2,1)}) %all-gather.18.cloned.1.call-update) | async-done | bytes 10551312 | tf_op jit(solution)/shard_map/all_gather | solution.py:157
  504.5 7.0 fusion.514
  512.5 2.9 fusion.511
  517.5 3.0 fusion.512
  520.4 168.9 %all-gather.20.cloned.1.call-done = bf16[3584,1472]{0,1:T(8,128)(2,1)} async-done(((bf16[896,1472]{0,1:T(8,128)(2,1)}), bf16[3584,1472]{0,1:T(8,128)(2,1)}) %all-gather.20.cloned.1.call-update) | async-done | bytes 10551312 | tf_op jit(solution)/shard_map/all_gather | solution.py:158
  689.4 9.5 multiply_convert_fusion.4
  698.8 6.8 fusion.518
  705.8 6.1 multiply_convert_fusion.5
  711.9 5.2 fusion.517
  717.1 2.9 convolution_add_fusion.8
  720.1 5.6 convolution_add_fusion.9
  725.7 2.6 fusion.321
  728.3 2.9 fusion.515
  731.2 2.9 fusion.516
  734.0 5.9 multiply_convert_fusion.3
  739.9 4.5 fusion.519
  744.5 3.6 fusion.320
  754.1 147.3 %while.153 = (s32[]{:T(128)}, bf16[1,128,6,64]{1,3,2,0:T(8,128)(2,1)}, bf16[1,128,6,64]{1,3,2,0:T(8,128)(2,1)}, f32[1,128,6,64]{1,3,2,0:T(8,128)}, f32[1,128,6,6...) while((s32[]{:T(128)}, ...), condition=%wide.region_27.28_spmd.clone, body=%wide.region_26.27_spmd.clone.sunk | while | flops 141902480 | bytes 12179321 | solution.py:297
  916.5 144.7 %while.154 = (s32[]{:T(128)}, bf16[1,128,6,64]{1,3,2,0:T(8,128)(2,1)}, bf16[1,128,6,64]{1,3,2,0:T(8,128)(2,1)}, f32[1,128,6,64]{1,3,2,0:T(8,128)}, f32[1,128,6,6...) while((s32[]{:T(128)}, ...), condition=%wide.region_32.33_spmd.clone, body=%wide.region_31.32_spmd.clone.sunk | while | flops 141902480 | bytes 12179321 | solution.py:297
  1068.1 95.6 %while.155 = (s32[]{:T(128)}, bf16[1,128,6,64]{1,3,2,0:T(8,128)(2,1)}, bf16[1,128,6,64]{1,3,2,0:T(8,128)(2,1)}, f32[1,128,6,64]{1,3,2,0:T(8,128)}, f32[1,128,6,6...) while((s32[]{:T(128)}, ...), condition=%wide.region_37.38_spmd.clone, body=%wide.region_36.37_spmd.clone.sunk | while | flops 141902480 | bytes 12965781 | solution.py:297
  1198.2 8.6 fusion.376
  1206.9 8.6 fusion.369
  1215.5 19.0 add_convert_fusion
  1234.5 14.6 copy.557
  1250.3 8.8 fusion.520
  1259.2 8.7 fusion.521
  1267.9 18.9 add_convert_fusion.2
  1288.0 8.8 fusion.522
  1296.9 8.6 fusion.523
  1305.5 20.2 add_convert_fusion.1
  1332.7 7.1 fusion.227
  1339.8 2.9 fusion.228
  1342.8 3.1 fusion.229
  1351.9 20.7 all-reduce.6
  1376.2 111.4 %reduce-scatter.22.cloned.1.call-done = bf16[896,1472]{1,0:T(8,128)(2,1)} async-done(((bf16[3584,1472]{1,0:T(8,128)(2,1)}), bf16[896,1472]{1,0:T(8,128)(2,1)}) %reduce-scatter.22.cloned.1.call-update) | async-done | bytes 2637840
  1487.6 3.6 copy.558
  1491.2 178.8 %reduce-scatter.18.cloned.1.call-done = bf16[368,3584]{1,0:T(8,128)(2,1)} async-done(((bf16[1472,3584]{1,0:T(8,128)(2,1)}), bf16[368,3584]{1,0:T(8,128)(2,1)}) %reduce-scatter.18.cloned.1.call-update) | async-done | bytes 2637840 | tf_op jit(solution)/shard_map/reduce_scatter | solution.py:340
  1670.1 182.4 %reduce-scatter.20.cloned.1.call-done = bf16[368,3584]{1,0:T(8,128)(2,1)} async-done(((bf16[1472,3584]{1,0:T(8,128)(2,1)}), bf16[368,3584]{1,0:T(8,128)(2,1)}) %reduce-scatter.20.cloned.1.call-update) | async-done | bytes 2637840 | tf_op jit(solution)/shard_map/reduce_scatter | solution.py:343
  1852.4 355.0 %all-reduce.9 = (f32[368,384]{1,0:T(8,128)}, f32[368,384]{1,0:T(8,128)}, f32[368,384]{1,0:T(8,128)}, f32[96,1472]{1,0:T(8,128)}, f32[368,3584]{1,0:T(8,128)}, /*...) all-reduce(bf16[368,384]{1,0:T(8,128)(2,1)S(1)} %copy-done.138, ...), channel_id=1, replica_groups=mesh['ctx'=8,'wsh'=4] {'ctx'}, use_global_device_ids=true, to_apply=%region_40.41 | all-reduce | flops 4522768 | bytes 27138176 | tf_op jit(solution)/shard_map/psum | solution.py:359
  (1727 shorter events, 749.6 us)
Async XLA Ops:
  7.2 49.6 %all-gather.8.cloned.1.call-start = ((), (), s32[]{:S(2)}) async-start(), calls=%async_computation.7 | async-start | bytes 1413120 | tf_op jit(solution)/shard_map/all_gather | solution.py:152
  7.9 64.7 %all-gather.10.cloned.1.call-start = ((), (), s32[]{:S(2)}) async-start(), calls=%async_computation.8 | async-start | bytes 1413120 | tf_op jit(solution)/shard_map/all_gather | solution.py:153
  8.7 94.3 %all-gather.12.cloned.1.call-start = ((), (), s32[]{:S(2)}) async-start(), calls=%async_computation.9 | async-start | bytes 1413120 | tf_op jit(solution)/shard_map/all_gather | solution.py:154
  9.4 239.5 %all-gather.14.cloned.1.call-start = ((), (), s32[]{:S(2)}) async-start(), calls=%async_computation.10 | async-start | bytes 1474560 | tf_op jit(solution)/shard_map/all_gather | solution.py:155
  10.0 405.5 %all-gather.16.cloned.1.call-start = ((), (), s32[]{:S(2)}) async-start(), calls=%async_computation.11 | async-start | bytes 13189120 | tf_op jit(solution)/shard_map/all_gather | solution.py:156
  10.6 494.0 %all-gather.18.cloned.1.call-start = ((), (), s32[]{:S(2)}) async-start(), calls=%async_computation.12 | async-start | bytes 13189120 | tf_op jit(solution)/shard_map/all_gather | solution.py:157
  11.2 678.1 %all-gather.20.cloned.1.call-start = ((), (), s32[]{:S(2)}) async-start(), calls=%async_computation.13 | async-start | bytes 13189120 | tf_op jit(solution)/shard_map/all_gather | solution.py:158
  12.0 1364.2 %reduce-scatter.16.cloned.1.call-start = ((), (), s32[]{:S(2)}) async-start(), calls=%async_computation.17 | async-start | bytes 1474560 | tf_op jit(solution)/shard_map/reduce_scatter | solution.py:337
  132.4 13.3 collective-permute-start.1
  149.2 13.1 collective-permute-start.1
  165.6 13.1 collective-permute-start.1
  182.2 12.2 collective-permute-start.1
  197.8 13.1 collective-permute-start.1
  214.4 13.0 collective-permute-start.1
  230.8 13.2 collective-permute-start.1
  755.6 19.7 collective-permute-start.6
  757.2 18.2 collective-permute-start.7
  776.9 19.0 collective-permute-start.6
  778.4 17.4 collective-permute-start.7
  797.4 19.9 collective-permute-start.6
  799.0 18.3 collective-permute-start.7
  818.8 18.9 collective-permute-start.6
  820.3 17.4 collective-permute-start.7
  839.3 19.8 collective-permute-start.6
  840.9 18.2 collective-permute-start.7
  860.6 19.0 collective-permute-start.6
  862.2 17.4 collective-permute-start.7
  881.1 19.8 collective-permute-start.6
  882.7 18.2 collective-permute-start.7
  913.0 273.3 %collective-permute-start.19 = (bf16[1,128,6,64]{1,3,2,0:T(8,128)(2,1)}, bf16[1,128,6,64]{1,3,2,0:T(8,128)(2,1)}, u32[]{:S(2)}, u32[]{:S(2)}) collective-permute-start(bf16[1,128,6,64]{1,3,2,0:T(8,128)(2,1)} %fusion.277), channel_id=1, source_target_pairs={{0,4},{4,8},{8,12},{12,16},{16,20},{20,24},{24,28},{28,0},{1,5},{5... | collective-permute-start | bytes 294920 | tf_op jit(solution)/shard_map/ppermute | solution.py:21
  918.0 18.2 collective-permute-start.10
  921.1 15.2 collective-permute-start.11
  937.8 19.6 collective-permute-start.10
  940.4 16.9 collective-permute-start.11
  958.9 19.0 collective-permute-start.10
  961.7 16.2 collective-permute-start.11
  979.4 19.5 collective-permute-start.10
  982.0 16.9 collective-permute-start.11
  1000.5 19.0 collective-permute-start.10
  1003.3 16.1 collective-permute-start.11
  1021.0 19.6 collective-permute-start.10
  1023.6 17.0 collective-permute-start.11
  1042.2 19.0 collective-permute-start.10
  1044.9 16.2 collective-permute-start.11
  1069.1 13.4 collective-permute-start.14
  1071.1 11.4 collective-permute-start.15
  1083.5 12.4 collective-permute-start.14
  1084.4 11.5 collective-permute-start.15
  1096.8 12.7 collective-permute-start.14
  1097.8 11.8 collective-permute-start.15
  1110.5 11.9 collective-permute-start.14
  1123.4 13.4 collective-permute-start.14
  1124.3 12.4 collective-permute-start.15
  1137.7 12.3 collective-permute-start.14
  1151.0 12.8 collective-permute-start.14
  1151.9 11.8 collective-permute-start.15
  1172.1 14.9 collective-permute-start.18
  1175.2 12.7 collective-permute-start.21
  1184.0 192.1 %reduce-scatter.10.cloned.1.call-start = ((), (), s32[]{:S(2)}) async-start(), calls=%async_computation.14 | async-start | bytes 1413120 | tf_op jit(solution)/shard_map/reduce_scatter | solution.py:322
  1196.7 179.4 %reduce-scatter.12.cloned.1.call-start = ((), (), s32[]{:S(2)}) async-start(), calls=%async_computation.15 | async-start | bytes 1413120 | tf_op jit(solution)/shard_map/reduce_scatter | solution.py:325
  1197.3 178.9 %reduce-scatter.14.cloned.1.call-start = ((), (), s32[]{:S(2)}) async-start(), calls=%async_computation.16 | async-start | bytes 1413120 | tf_op jit(solution)/shard_map/reduce_scatter | solution.py:331
  1206.8 280.8 %reduce-scatter.22.cloned.1.call-start = ((), (), s32[]{:S(2)}) async-start(), calls=%async_computation.20 | async-start | bytes 13762560
  1249.1 421.0 %reduce-scatter.18.cloned.1.call-start = ((), (), s32[]{:S(2)}) async-start(), calls=%async_computation.18 | async-start | bytes 13189120 | tf_op jit(solution)/shard_map/reduce_scatter | solution.py:340
  1286.9 565.5 %reduce-scatter.20.cloned.1.call-start = ((), (), s32[]{:S(2)}) async-start(), calls=%async_computation.19 | async-start | bytes 13189120 | tf_op jit(solution)/shard_map/reduce_scatter | solution.py:343
  (378 other events, 4272.5 us)
Sparse Core Ops, SparseCore 0:
  9.6 32.5 all-gather.7
  43.7 28.8 all-gather.9
  74.2 28.7 all-gather.11
  104.4 29.9 all-gather.13
  135.7 184.0 all-gather.15
  321.3 183.2 all-gather.17
  506.1 183.1 all-gather.19
  1184.1 26.1 reduce-scatter.15
  1212.7 27.2 reduce-scatter.9
  1242.1 27.2 reduce-scatter.11
  1272.3 27.2 reduce-scatter.13
  1301.9 185.6 reduce-scatter.21
  1489.9 180.0 reduce-scatter.17
  1672.3 180.1 reduce-scatter.19
where the time goes:
time: 2230 us; the launch traced here: 2210 us
  waiting for transfers between devices  823 us (37%)
  matrix products  521 us (23%)
  blocking collectives  411 us (18%)
  local copies, waits for them, and re-layouts  243 us (11%)
  other arithmetic  119 us (5%)
  starting transfers between devices  72.3 us (3%)
    psum x1, blocking collectives, on_device(): lax.psum((owned_grads[0], owned_grads[1], owned_grads[2], owned_grads[3],...  355 us
    reduce_scatter x1, waiting for transfers between devices, on_device(): lax.psum_scatter(up_total.astype(jnp.bfloat16), 'wsh', scatter_dimension=...  182 us
    reduce_scatter x1, waiting for transfers between devices, on_device(): lax.psum_scatter(gate_total.astype(jnp.bfloat16), 'wsh', scatter_dimensio...  179 us
    all_gather x1, waiting for transfers between devices, on_device(): lax.all_gather(down_weight, 'wsh', axis=0, tiled=True)  169 us
    while x336, local copies, waits for them, and re-layouts  134 us
    unnamed x15, waiting for transfers between devices  116 us
    all_gather x1, waiting for transfers between devices, on_device(): lax.all_gather(up_weight, 'wsh', axis=0, tiled=True)  82 us
    ppermute x132, starting transfers between devices, shifted(): return lax.ppermute(value, axis, pairs)  71.7 us
  transfers between devices with their start and end apart: 146, of which 37 were waited for; matrix products, arithmetic and copies ran while one was open for 35% of the time, Pallas kernels for 0%

commit v1 on v0

v1 whole, which is shorter than its diff:
```python
import functools

import jax
import jax.numpy as jnp
import numpy as np
from jax import lax
from jax.experimental import pallas as pl
from jax.experimental.pallas import tpu as pltpu
from jax.sharding import PartitionSpec as P

BUCKETS = 32
GROUP = 8
EPSILON = 1e-06
NEGATIVE = -1e30
PRECISE = lax.Precision.HIGHEST
BUCKET_EDGES = (12, 16, 23, 32, 46, 64, 91)
FLOAT = jnp.float32
BFLOAT = jnp.bfloat16


def bucket_number(offset):
    distance = abs(offset)
    level = distance if distance < 8 else 8 + sum(distance >= edge for edge in BUCKET_EDGES)
    return level + (16 if offset > 0 else 0)


def bucket_of(offsets):
    distance = jnp.abs(offsets)
    coarse = 8 + sum(((distance >= boundary).astype(jnp.int32) for boundary in BUCKET_EDGES))
    level = jnp.where(distance < 8, distance, coarse)
    return level + jnp.where(offsets > 0, 16, 0)


def near_radius(rows):
    return -(-(BUCKET_EDGES[-1] - 1) // rows)


def tile_offsets(block_gap, rows):
    keys = lax.broadcasted_iota(jnp.int32, (rows, rows), 0)
    queries = lax.broadcasted_iota(jnp.int32, (rows, rows), 1)
    return block_gap * rows + keys - queries


def tile_buckets(block_gap, rows):
    low, high = block_gap * rows - (rows - 1), block_gap * rows + (rows - 1)
    return sorted({bucket_number(offset) for offset in range(low, high + 1)})


def nt(left, right):
    return lax.dot_general(left, right, (((1,), (1,)), ((), ())), preferred_element_type=FLOAT)


def tn(left, right):
    return lax.dot_general(left, right, (((0,), (0,)), ((), ())), preferred_element_type=FLOAT)


def block_number(meta, half, position):
    low = lax.rem(meta, GROUP)
    return (position // 4) * GROUP + lax.bitwise_xor(low, jnp.int32(2 * (position % 4) + half))


def tile_index(meta, half, position, radius):
    gap = block_number(meta, half, position) - meta
    return jnp.clip(gap, -(radius + 1), radius + 1) + radius + 1


def build_bias(bias_ref, table_ref, pair, rows, radius):
    for side, bucket in ((0, 15), (2 * radius + 2, 31)):
        for head in range(2):
            bias_ref[head, side] = jnp.full((rows, rows), table_ref[bucket, 2 * pair + head], FLOAT)
    for gap in range(-radius, radius + 1):
        buckets = bucket_of(tile_offsets(gap, rows))
        present = tile_buckets(gap, rows)
        tiles = [jnp.full((rows, rows), table_ref[present[0], 2 * pair + head], FLOAT) for head in range(2)]
        for bucket in present[1:]:
            hit = buckets == bucket
            tiles = [jnp.where(hit, table_ref[bucket, 2 * pair + head], tiles[head]) for head in range(2)]
        for head in range(2):
            bias_ref[head, gap + radius + 1] = tiles[head]


def build_mask(mask_ref, segs_ref, meta, seq, rows, count):
    own = segs_ref[seq, pl.ds(meta, 1), :]
    for half in range(2):
        for position in range(count):
            row = segs_ref[seq, pl.ds(block_number(meta, half, position), 1), :]
            keys = jnp.transpose(jnp.broadcast_to(row, (rows, rows)))
            mask_ref[seq, half * count + position] = jnp.where(keys == own, 0.0, NEGATIVE)


def half_scores(keys, query, meta, head, half, seq, bias_ref, mask_ref, rows, count, radius):
    raw = nt(keys, query)
    parts = []
    for position in range(count):
        extra = bias_ref[head, tile_index(meta, half, position, radius)]
        masked = mask_ref[seq, half * count + position]
        parts.append(raw[position * rows : (position + 1) * rows] + (extra + masked))
    return jnp.concatenate(parts, axis=0)


def head_rows(value, head, lane):
    return jnp.where((lane < 64) == (head == 0), value, jnp.zeros_like(value))


def forward_kernel(
    meta_ref, table_ref, segs_ref, q_ref, ko_ref, ks_ref, vo_ref, vs_ref, out_ref, lse_ref, bias_ref, mask_ref,
    *, rows, count, radius,
):
    pair, seq = pl.program_id(0), pl.program_id(1)
    meta = meta_ref[0]

    @pl.when(seq == 0)
    def _():
        build_bias(bias_ref, table_ref, pair, rows, radius)

    @pl.when(pair == 0)
    def _():
        build_mask(mask_ref, segs_ref, meta, seq, rows, count)

    query = q_ref[0]
    lane = lax.broadcasted_iota(jnp.int32, query.shape, 1)
    keys = [ref[...].reshape(count * rows, 128) for ref in (ko_ref, ks_ref)]
    values = [ref[...].reshape(count * rows, 128) for ref in (vo_ref, vs_ref)]
    pieces = []
    for head in range(2):
        one = head_rows(query, head, lane)
        scores = [
            half_scores(keys[half], one, meta, head, half, seq, bias_ref, mask_ref, rows, count, radius)
            for half in range(2)
        ]
        top = jnp.maximum(jnp.max(scores[0], axis=0, keepdims=True), jnp.max(scores[1], axis=0, keepdims=True))
        raised = [jnp.exp(part - top) for part in scores]
        total = jnp.sum(raised[0], axis=0, keepdims=True) + jnp.sum(raised[1], axis=0, keepdims=True)
        scale = 1.0 / total
        mixed = sum(tn(values[half], (raised[half] * scale).astype(BFLOAT)) for half in range(2))
        pieces.append(mixed[64 * head : 64 * head + 64])
        lse_ref[0, 0, head : head + 1] = top + jnp.log(total)
    out_ref[0] = jnp.transpose(jnp.concatenate(pieces, axis=0))


def backward_kernel(
    meta_ref, table_ref, segs_ref, q_ref, ko_ref, ks_ref, vo_ref, vs_ref, do_ref, out_ref, lse_ref,
    dq_ref, dko_ref, dks_ref, dvo_ref, dvs_ref, tab_ref, bias_ref, mask_ref, sum_ref,
    *, rows, count, radius,
):
    pair, seq = pl.program_id(0), pl.program_id(1)
    meta = meta_ref[0]

    @pl.when(seq == 0)
    def _():
        build_bias(bias_ref, table_ref, pair, rows, radius)
        sum_ref[...] = jnp.zeros_like(sum_ref)

    @pl.when(pair == 0)
    def _():
        build_mask(mask_ref, segs_ref, meta, seq, rows, count)

    query, grad = q_ref[0], do_ref[0]
    lane = lax.broadcasted_iota(jnp.int32, query.shape, 1)
    keys = [ref[...].reshape(count * rows, 128) for ref in (ko_ref, ks_ref)]
    values = [ref[...].reshape(count * rows, 128) for ref in (vo_ref, vs_ref)]
    picks = (
        lax.broadcasted_iota(jnp.int32, (8, 128), 1) // 64 == lax.broadcasted_iota(jnp.int32, (8, 128), 0)
    ).astype(FLOAT)
    deltas = lax.dot_general(
        picks, grad.astype(FLOAT) * out_ref[0], (((1,), (1,)), ((), ())), precision=PRECISE, preferred_element_type=FLOAT
    )
    query_heads = [head_rows(query, head, lane) for head in range(2)]
    grad_heads = [head_rows(grad, head, lane) for head in range(2)]
    probs, slopes = [[], []], [[], []]
    pieces = []
    for head in range(2):
        logsum = lse_ref[0, 0, head : head + 1]
        delta = deltas[head : head + 1]
        flow = None
        for half in range(2):
            scores = half_scores(
                keys[half], query_heads[head], meta, head, half, seq, bias_ref, mask_ref, rows, count, radius
            )
            prob = jnp.exp(scores - logsum)
            slope = prob * (nt(values[half], grad_heads[head]) - delta)
            for position in range(count):
                index = tile_index(meta, half, position, radius)
                sum_ref[head, index] = sum_ref[head, index] + slope[position * rows : (position + 1) * rows]
            slope_low = slope.astype(BFLOAT)
            probs[half].append(prob.astype(BFLOAT))
            slopes[half].append(slope_low)
            term = tn(keys[half], slope_low)
            flow = term if flow is None else flow + term
        pieces.append(flow[64 * head : 64 * head + 64])
    dq_ref[0] = jnp.transpose(jnp.concatenate(pieces, axis=0)).astype(BFLOAT)
    query_stack = jnp.concatenate(query_heads, axis=0)
    grad_stack = jnp.concatenate(grad_heads, axis=0)
    for half, (dk_ref, dv_ref) in enumerate(((dko_ref, dvo_ref), (dks_ref, dvs_ref))):
        dk = jnp.dot(jnp.concatenate(slopes[half], axis=1), query_stack, preferred_element_type=FLOAT)
        dv = jnp.dot(jnp.concatenate(probs[half], axis=1), grad_stack, preferred_element_type=FLOAT)
        dk_ref[...] = dk.astype(BFLOAT).reshape(dk_ref.shape)
        dv_ref[...] = dv.astype(BFLOAT).reshape(dv_ref.shape)

    @pl.when(seq == pl.num_programs(1) - 1)
    def _():
        for head in range(2):
            sums = {}
            for side, bucket in ((0, 15), (2 * radius + 2, 31)):
                sums[bucket] = jnp.sum(sum_ref[head, side], axis=0, keepdims=True)
            for gap in range(-radius, radius + 1):
                buckets = bucket_of(tile_offsets(gap, rows))
                tile = sum_ref[head, gap + radius + 1]
                for bucket in tile_buckets(gap, rows):
                    part = jnp.sum(jnp.where(buckets == bucket, tile, 0.0), axis=0, keepdims=True)
                    sums[bucket] = sums[bucket] + part if bucket in sums else part
            for bucket in range(BUCKETS):
                tab_ref[0, head, bucket : bucket + 1] = sums.get(bucket, jnp.zeros((1, rows), FLOAT))


def attention_specs(seqs, rows, count, blocks, pairs):
    small = [
        pl.BlockSpec(memory_space=pltpu.SMEM),
        pl.BlockSpec(memory_space=pltpu.SMEM),
        pl.BlockSpec((seqs, blocks, rows), lambda p, s: (0, 0, 0)),
    ]
    query = pl.BlockSpec((1, rows, 128), lambda p, s: (s, 0, p))
    key = pl.BlockSpec((count, 1, rows, 128), lambda p, s: (0, s, 0, p))
    value = pl.BlockSpec((count, 1, rows, 128), lambda p, s: (0, s, 0, pairs + p))
    stat = pl.BlockSpec((1, 1, 8, rows), lambda p, s: (p, s, 0, 0))
    return small, query, key, value, stat


def attention_scratch(seqs, rows, count, radius):
    return [
        pltpu.VMEM((2, 2 * radius + 3, rows, rows), FLOAT),
        pltpu.VMEM((seqs, 2 * count, rows, rows), FLOAT),
    ]


def attention_cost(seqs, rows, keys, width, products):
    return pl.CostEstimate(
        flops=2 * products * seqs * rows * keys * width,
        bytes_accessed=4 * seqs * keys * width * products,
        transcendentals=seqs * rows * keys * width // 64,
    )


def attention_forward(meta, table, segs, queries, kv_own, kv_sib):
    seqs, rows, inner = queries.shape
    count, blocks, pairs = kv_own.shape[0], segs.shape[1], inner // 128
    radius = near_radius(rows)
    small, query, key, value, stat = attention_specs(seqs, rows, count, blocks, pairs)
    return pl.pallas_call(
        functools.partial(forward_kernel, rows=rows, count=count, radius=radius),
        grid=(pairs, seqs),
        in_specs=[*small, query, key, key, value, value],
        out_specs=[query, stat],
        out_shape=[
            jax.ShapeDtypeStruct((seqs, rows, inner), FLOAT),
            jax.ShapeDtypeStruct((pairs, seqs, 8, rows), FLOAT),
        ],
        scratch_shapes=attention_scratch(seqs, rows, count, radius),
        cost_estimate=attention_cost(seqs, rows, blocks * rows, inner, 2),
        name="attention_forward",
    )(meta, table, segs, queries, kv_own, kv_sib, kv_own, kv_sib)


def attention_backward(meta, table, segs, queries, kv_own, kv_sib, grad, out, lse):
    seqs, rows, inner = queries.shape
    count, blocks, pairs = kv_own.shape[0], segs.shape[1], inner // 128
    radius = near_radius(rows)
    small, query, key, value, stat = attention_specs(seqs, rows, count, blocks, pairs)
    side = jax.ShapeDtypeStruct((count, seqs, rows, inner), BFLOAT)
    return pl.pallas_call(
        functools.partial(backward_kernel, rows=rows, count=count, radius=radius),
        grid=(pairs, seqs),
        in_specs=[*small, query, key, key, value, value, query, query, stat],
        out_specs=[query, key, key, key, key, pl.BlockSpec((1, 2, BUCKETS, rows), lambda p, s: (p, 0, 0, 0))],
        out_shape=[
            jax.ShapeDtypeStruct((seqs, rows, inner), BFLOAT), side, side, side, side,
            jax.ShapeDtypeStruct((pairs, 2, BUCKETS, rows), FLOAT),
        ],
        scratch_shapes=[
            *attention_scratch(seqs, rows, count, radius),
            pltpu.VMEM((2, 2 * radius + 3, rows, rows), FLOAT),
        ],
        cost_estimate=attention_cost(seqs, rows, blocks * rows, inner, 5),
        name="attention_backward",
    )(meta, table, segs, queries, kv_own, kv_sib, kv_own, kv_sib, grad, out, lse)


def swap(value, bit):
    count = lax.axis_size("ctx")
    return lax.ppermute(value, "ctx", [(source, source ^ bit) for source in range(count)])


def gather_four(own):
    cut = own.shape[0] // 2
    first, second = swap(own, 2), swap(own, 4)
    last = jnp.concatenate((swap(first[:cut], 4), swap(second[cut:], 2)), axis=0)
    return [own, first, second, last]


def scatter_four(blocks):
    own, first, second, last = blocks
    cut = own.shape[0] // 2
    low, high = swap(last[:cut], 4), swap(last[cut:], 2)
    first = jnp.concatenate(((first[:cut].astype(FLOAT) + low.astype(FLOAT)).astype(BFLOAT), first[cut:]), axis=0)
    second = jnp.concatenate((second[:cut], (second[cut:].astype(FLOAT) + high.astype(FLOAT)).astype(BFLOAT)), axis=0)
    got_first, got_second = swap(first, 2), swap(second, 4)
    return own.astype(FLOAT) + got_first.astype(FLOAT) + got_second.astype(FLOAT)


def rms_rows(hidden, gain):
    return hidden * lax.rsqrt(jnp.mean(hidden * hidden, axis=-1, keepdims=True) + EPSILON) * gain


def rms_back(hidden, gain, back):
    scale = lax.rsqrt(jnp.mean(hidden * hidden, axis=-1, keepdims=True) + EPSILON)
    lifted = back * gain
    return scale * lifted - hidden * (scale * scale * scale) * jnp.mean(lifted * hidden, axis=-1, keepdims=True)


def ordered(blocks, low):
    stacked = jnp.stack(blocks)
    return [lax.dynamic_index_in_dim(stacked, lax.bitwise_xor(low, jnp.int32(index)), 0, keepdims=False) for index in range(GROUP)]


def gather_eight(own, low):
    four = gather_four(own)
    other = swap(jnp.stack(four), 1)
    listed = [four[index // 2] if index % 2 == 0 else other[index // 2] for index in range(GROUP)]
    return ordered(listed, low)


def slice_rows(weight, low):
    total = weight.shape[0]
    size = -(-total // (GROUP * 16)) * 16
    start = jnp.minimum(low * size, total - size)
    return lax.dynamic_slice_in_dim(weight, start, size, 0)


def join_rows(pieces, depth, total):
    size = pieces[0].shape[0] // depth
    cut = [piece.reshape(depth, size, -1) for piece in pieces]
    rows = []
    covered = 0
    for index, piece in enumerate(cut):
        start = min(index * size, total - size)
        if start + size > covered:
            rows.append(piece[:, covered - start :])
            covered = start + size
    return jnp.concatenate(rows, axis=1).reshape(depth * total, -1)


def on_device(
    layer_input,
    segments,
    cotangent,
    query_weight,
    key_weight,
    value_weight,
    projection,
    gate_weight,
    up_weight,
    down_weight,
    gain_early,
    gain_late,
    bias_table,
):
    ring = lax.axis_size("ctx")
    depth = lax.axis_size("wsh")
    groups = ring // GROUP
    mine = lax.axis_index("ctx")
    low = lax.rem(mine, GROUP)
    chip, core = low // 2, lax.rem(low, 2)
    zed = lax.axis_index("wsh")
    seqs, rows, width = layer_input.shape
    inner = query_weight.shape[1]
    heads = bias_table.shape[1]
    hidden = gate_weight.shape[1]
    shard = width // depth
    slab = hidden // depth
    part = slab // 4
    piece = part // 2
    upper = [[group * GROUP + index for group in range(groups)] for index in range(GROUP)]
    is_zero = core == 0

    qkv_shard = jnp.concatenate((query_weight, key_weight, value_weight), axis=1)
    qkv_z = lax.all_gather(slice_rows(qkv_shard, low), "wsh", axis=0, tiled=True)
    proj_z = lax.all_gather(slice_rows(projection, low), "wsh", axis=0, tiled=True)
    qkv_full = join_rows(gather_eight(qkv_z, low), depth, shard)
    proj_full = join_rows(gather_eight(proj_z, low), depth, inner // depth)
    vectors = jnp.stack((gain_early, gain_late))
    vectors = lax.all_gather(vectors, "wsh", axis=1, tiled=True).astype(FLOAT)
    early_gain, late_gain = vectors[0], vectors[1]
    table = lax.all_gather(bias_table, "wsh", axis=0, tiled=True).astype(FLOAT)
    segs = lax.all_gather(segments, "ctx", axis=1, tiled=True).reshape(seqs, ring, rows).astype(FLOAT)
    meta = mine.astype(jnp.int32).reshape(1)

    def columns(weight):
        return jnp.concatenate(
            [lax.dynamic_slice_in_dim(weight, index * slab + chip * part, part, 1) for index in range(depth)], axis=1
        )

    pair_mine = lax.all_gather(jnp.where(is_zero, columns(gate_weight), columns(up_weight)), "wsh", axis=0, tiled=True)
    pair_other = swap(pair_mine, 1)
    down_slice = lax.dynamic_slice_in_dim(down_weight, chip * part + core * piece, piece, 0)
    down_mine = lax.all_gather(down_slice, "wsh", axis=0, tiled=True).reshape(depth, piece, width)
    down_other = swap(down_mine, 1)
    down_full = jnp.where(
        is_zero, jnp.stack((down_mine, down_other), axis=1), jnp.stack((down_other, down_mine), axis=1)
    ).reshape(depth * part, width)

    four_inputs = jnp.stack(gather_four(layer_input.reshape(seqs * rows, width)))
    four_cots = jnp.stack(gather_four(cotangent.reshape(seqs * rows, width)))
    hidden_in = layer_input.reshape(seqs * rows, width).astype(FLOAT)
    four_normed = rms_rows(four_inputs.astype(FLOAT), early_gain).astype(BFLOAT).reshape(-1, width)
    kv_own = jnp.dot(four_normed, qkv_full[:, inner:], preferred_element_type=FLOAT).astype(BFLOAT)
    own_normed = four_normed[: seqs * rows]
    queries = jnp.dot(own_normed, qkv_full[:, :inner], preferred_element_type=FLOAT).astype(BFLOAT)
    queries = queries.reshape(seqs, rows, inner)
    kv_own = kv_own.reshape(4, seqs, rows, 2 * inner)
    kv_sib = swap(kv_own, 1)

    def whole(value):
        if groups == 1:
            return value
        return lax.all_gather(value, "ctx", axis=0, tiled=True, axis_index_groups=upper)

    kv_all, kv_sib_all = whole(kv_own), whole(kv_sib)
    attention, lse = attention_forward(meta, table, segs, queries, kv_all, kv_sib_all)
    attn_low = attention.astype(BFLOAT).reshape(seqs * rows, inner)
    four_attn = jnp.stack(gather_four(attn_low)).reshape(-1, inner)
    four_after = four_inputs.reshape(-1, width).astype(FLOAT) + jnp.dot(
        four_attn, proj_full, preferred_element_type=FLOAT
    )
    after_attn = four_after[: seqs * rows]
    normed_late = rms_rows(four_after, late_gain).astype(BFLOAT)

    pre_mine = jnp.dot(normed_late, pair_mine, preferred_element_type=FLOAT)
    pre_other = jnp.dot(normed_late, pair_other, preferred_element_type=FLOAT)
    gate_pre = jnp.where(is_zero, pre_mine, pre_other)
    up_pre = jnp.where(is_zero, pre_other, pre_mine)

    def gated(gate_values, up_values):
        return jax.nn.gelu(gate_values, approximate=True) * up_values

    activation = gated(gate_pre, up_pre).astype(BFLOAT)
    cots = four_cots.reshape(-1, width)
    act_grad = lax.dot_general(cots, down_full, (((1,), (1,)), ((), ())), preferred_element_type=FLOAT)
    gate_back, up_back = jax.vjp(gated, gate_pre, up_pre)[1](act_grad)
    back_mine = jnp.where(is_zero, gate_back, up_back).astype(BFLOAT)
    back_other = jnp.where(is_zero, up_back, gate_back).astype(BFLOAT)
    late_part = lax.dot_general(
        back_mine, pair_mine, (((1,), (1,)), ((), ())), preferred_element_type=FLOAT
    ) + lax.dot_general(back_other, pair_other, (((1,), (1,)), ((), ())), preferred_element_type=FLOAT)
    late_part = late_part.astype(BFLOAT).reshape(4, seqs * rows, width)
    late_back = scatter_four([late_part[index] for index in range(4)])
    out_part = jnp.dot(activation, down_full, preferred_element_type=FLOAT).astype(BFLOAT)
    out_part = out_part.reshape(4, seqs * rows, width)
    result = (after_attn + scatter_four([out_part[index] for index in range(4)])).astype(BFLOAT)

    down_grad = tn(activation, cots).astype(BFLOAT).reshape(depth, 2, piece, width)
    mine_grad = tn(normed_late, back_mine).astype(BFLOAT)
    other_grad = tn(normed_late, back_other).astype(BFLOAT)

    def join(kept, sent):
        return (kept.astype(FLOAT) + swap(sent, 1).astype(FLOAT)).astype(BFLOAT)

    down_keep = jnp.where(is_zero, down_grad[:, 0], down_grad[:, 1]).reshape(depth * piece, width)
    down_send = jnp.where(is_zero, down_grad[:, 1], down_grad[:, 0]).reshape(depth * piece, width)
    down_sum = join(down_keep, down_send)
    pair_sum = join(mine_grad, other_grad)

    def over_groups(value):
        return lax.psum(value, "ctx", axis_index_groups=upper) if groups > 1 else value

    down_own = over_groups(lax.psum_scatter(down_sum, "wsh", scatter_dimension=0, tiled=True))
    pair_own = over_groups(lax.psum_scatter(pair_sum, "wsh", scatter_dimension=0, tiled=True))
    down_out = jnp.concatenate(gather_eight(down_own, low), axis=0).astype(FLOAT)
    four_pair = gather_four(pair_own)
    stacked_pair = jnp.stack(four_pair)
    stacked_other = swap(stacked_pair, 1)

    def spread(stack):
        chips = [
            lax.dynamic_index_in_dim(stack, lax.bitwise_xor(chip, jnp.int32(index)), 0, keepdims=False) for index in range(4)
        ]
        return jnp.concatenate(
            [chips[index][:, level * part : (level + 1) * part] for level in range(depth) for index in range(4)], axis=1
        )

    gate_out = spread(jnp.where(is_zero, stacked_pair, stacked_other)).astype(FLOAT)
    up_out = spread(jnp.where(is_zero, stacked_other, stacked_pair)).astype(FLOAT)

    cot_own = cotangent.reshape(seqs * rows, width).astype(FLOAT)
    residual_grad = cot_own + rms_back(after_attn, late_gain, late_back)
    mix_low = residual_grad.astype(BFLOAT)
    proj_grad = tn(attn_low, mix_low).astype(BFLOAT)
    attn_grad = lax.dot_general(mix_low, proj_full, (((1,), (1,)), ((), ())), preferred_element_type=FLOAT)
    attn_grad = attn_grad.astype(BFLOAT).reshape(seqs, rows, inner)
    dq, dk_own, dk_sib, dv_own, dv_sib, table_part = attention_backward(
        meta, table, segs, queries, kv_all, kv_sib_all, attn_grad, attention, lse
    )

    def owned(value):
        if groups == 1:
            return value
        return lax.psum_scatter(value, "ctx", scatter_dimension=0, tiled=True, axis_index_groups=upper)

    dkv_own = owned(jnp.concatenate((dk_own, dv_own), axis=-1))
    dkv_sib = owned(jnp.concatenate((dk_sib, dv_sib), axis=-1))
    dkv_four = (dkv_own.astype(FLOAT) + swap(dkv_sib, 1).astype(FLOAT)).astype(BFLOAT)
    dkv_four = dkv_four.reshape(4, seqs * rows, 2 * inner)
    dkv = scatter_four([dkv_four[index] for index in range(4)]).astype(BFLOAT)
    dq = dq.reshape(seqs * rows, inner)
    kv_grad = tn(four_normed, dkv_four.reshape(-1, 2 * inner)).astype(BFLOAT)
    q_grad = tn(own_normed, dq).astype(BFLOAT)
    dqkv = jnp.concatenate((dq, dkv), axis=1)
    early_back = lax.dot_general(dqkv, qkv_full, (((1,), (1,)), ((), ())), preferred_element_type=FLOAT)
    input_grad = (residual_grad + rms_back(hidden_in, early_gain, early_back)).astype(BFLOAT)

    qkv_grad = jnp.concatenate((q_grad, kv_grad), axis=1)
    qkv_out = lax.psum(lax.psum_scatter(qkv_grad, "wsh", scatter_dimension=0, tiled=True), "ctx").astype(FLOAT)
    proj_out = lax.psum(lax.psum_scatter(proj_grad, "wsh", scatter_dimension=0, tiled=True), "ctx").astype(FLOAT)
    table_sum = jnp.sum(table_part, axis=-1).reshape(heads, BUCKETS)
    table_sum = lax.psum(table_sum, ("ctx", "wsh"))
    table_rows = BUCKETS // depth
    table_out = jnp.transpose(lax.dynamic_slice_in_dim(table_sum, zed * table_rows, table_rows, 1))
    early_out = jnp.sum(qkv_out * qkv_shard.astype(FLOAT), axis=1) / gain_early.astype(FLOAT)
    late_out = (
        jnp.sum(gate_out * gate_weight.astype(FLOAT), axis=1) + jnp.sum(up_out * up_weight.astype(FLOAT), axis=1)
    ) / gain_late.astype(FLOAT)
    return (
        result.reshape(seqs, rows, width),
        input_grad.reshape(seqs, rows, width),
        qkv_out[:, :inner],
        qkv_out[:, inner : 2 * inner],
        qkv_out[:, 2 * inner :],
        proj_out,
        gate_out,
        up_out,
        down_out,
        early_out,
        late_out,
        table_out,
    )


def solution(mesh):
    rows = P("wsh", "ctx", None)
    split = P("wsh", None)
    vector = P("wsh")
    return jax.shard_map(
        on_device,
        mesh=mesh,
        in_specs=(rows, P("wsh", "ctx"), rows, split, split, split, split, split, split, split, vector, vector, split),
        out_specs=(rows, rows, split, split, split, split, split, split, split, vector, vector, split),
        check_vma=False,
    )
```

time: 2230 us -> 686 us (0.31)
  waiting for transfers between devices: 823 us -> 125 us
  matrix products: 521 us -> 104 us
  blocking collectives: 411 us -> 106 us
  local copies, waits for them, and re-layouts: 243 us -> 150 us
  Pallas kernels: 0 us -> 35.1 us
  starting transfers between devices: 72.3 us -> 46 us
    dot_general x281 -> x17, matrix products: 521 us -> 104 us  [the longest x6 36.1 us: tn(): lax.dot_general(left, right, (((0,), (0,)), ((), ())), preferred_element_...]
    reduce_scatter x6 -> x4, waiting for transfers between devices: 361 us -> 6.45 us  [the longest x1 6.45 us: on_device(): lax.psum_scatter(qkv_grad, 'wsh', scatter_dimension=0, tiled=True)]
    psum x1, blocking collectives: 355 us -> 37.8 us  [on_device(): table_sum = lax.psum(table_sum, ('ctx', 'wsh'))]
    all_gather x7 -> x2, waiting for transfers between devices: 294 us -> 0.01 us  [the longest x1 0.01 us: on_device(): lax.all_gather(down_slice, 'wsh', axis=0, tiled=True)]
    while x339 -> x0, local copies, waits for them, and re-layouts: 134 us -> none
    unnamed x15 -> x7, waiting for transfers between devices: 116 us -> 0.11 us
    psum x0 -> x1, waiting for transfers between devices: none -> 50.8 us  [on_device(): lax.psum(lax.psum_scatter(qkv_grad, 'wsh', scatter_dimension=0, tiled=Tru...]
    all_gather x2 -> x5, blocking collectives: 22.2 us -> 68.6 us  [the longest x1 20.5 us: on_device(): lax.all_gather(slice_rows(qkv_shard, low), 'wsh', axis=0, tiled=True)]
  transfers between devices with their start and end apart: 146 -> 57, of which waited for: 37 -> 16; matrix products, arithmetic and copies ran while one was open for 35% -> 39% of each run, Pallas kernels for 0% -> 5%
where the time goes in v1:
time: 686 us; the launch traced here: 679 us
  local copies, waits for them, and re-layouts  150 us (22%)
  waiting for transfers between devices  125 us (18%)
  blocking collectives  106 us (15%)
  matrix products  104 us (15%)
  other arithmetic  96.9 us (14%)
  starting transfers between devices  46 us (7%)
  Pallas kernels  35.1 us (5%)
  between operations  15.6 us (2%)
    ppermute x50, waiting for transfers between devices, swap(): lax.ppermute(value, 'ctx', [(source, source ^ bit) for source in range(co...  67.4 us
    unnamed x201, local copies, waits for them, and re-layouts  58.1 us
    psum x1, waiting for transfers between devices, on_device(): lax.psum(lax.psum_scatter(qkv_grad, 'wsh', scatter_dimension=0, tiled=Tru...  50.8 us
    ppermute x50, starting transfers between devices, swap(): lax.ppermute(value, 'ctx', [(source, source ^ bit) for source in range(co...  45.1 us
    psum x1, blocking collectives, on_device(): table_sum = lax.psum(table_sum, ('ctx', 'wsh'))  37.8 us
    dot_general x6, matrix products, tn(): lax.dot_general(left, right, (((0,), (0,)), ((), ())), preferred_element_...  36.1 us
    all_gather x1, blocking collectives, on_device(): lax.all_gather(slice_rows(qkv_shard, low), 'wsh', axis=0, tiled=True)  20.5 us
    pallas_call x1, Pallas kernels, attention_backward(): pl.pallas_call(functools.partial(backward_kernel, rows=rows, count=count,...  20.3 us
  transfers between devices with their start and end apart: 57, of which 16 were waited for; matrix products, arithmetic and copies ran while one was open for 39% of the time, Pallas kernels for 5%

profile of v1, /device:TPU:0, one launch (start us, length us, event | category | flops | bytes accessed | tf_op | source)
XLA Modules:
  0.0 678.9 jit_solution(9022512809795028708)
XLA Ops:
  13.2 3.0 collective-permute-start.1
  18.6 15.1 %all_gather.25 = bf16[64,1472]{1,0:T(8,128)(2,1)S(1)} all-gather(bf16[16,1472]{1,0:T(8,128)(2,1)S(1)} %constant_dynamic-slice_fusion.16), channel_id=1, replica_groups=mesh['ctx'=8,'wsh'=4] {'wsh'}, dimensions={0}, use_global_device_ids=true | all-gather | bytes 235520 | tf_op jit(solution)/shard_map/all_gather | solution.py:387
  34.7 20.5 %all_gather.24 = bf16[192,1152]{1,0:T(8,128)(2,1)S(1)} all-gather(bf16[48,1152]{1,0:T(8,128)(2,1)S(1)} %constant_dynamic-slice_fusion.25), channel_id=1, replica_groups=mesh['ctx'=8,'wsh'=4] {'wsh'}, dimensions={0}, use_global_device_ids=true | all-gather | bytes 552960 | tf_op jit(solution)/shard_map/all_gather | solution.py:386
  62.6 8.8 %all_gather.22 = s32[3,1024]{1,0:T(4,128)S(1)} all-gather(s32[3,128]{1,0:T(4,128)S(1)} %copy-done.64), channel_id=1, replica_groups=mesh['ctx'=8,'wsh'=4] {'ctx'}, dimensions={1}, use_global_device_ids=true | all-gather | bytes 13824 | tf_op jit(solution)/shard_map/all_gather | solution.py:394
  74.5 12.1 %all-gather = bf16[4,368,2]{1,2,0:T(2,128)(2,1)S(1)} all-gather(bf16[1,368,2]{1,2,0:T(2,128)(2,1)S(1)} %maximum_bitcast_fusion.7), channel_id=1, replica_groups=mesh['ctx'=8,'wsh'=4] {'wsh'}, dimensions={0}, use_global_device_ids=true | all-gather | bytes 7360 | tf_op jit(solution)/shard_map/all_gather | solution.py:391
  91.3 7.3 %collective-permute-done.4 = bf16[192,1152]{1,0:T(8,128)(2,1)S(1)} collective-permute-done((bf16[192,1152]{1,0:T(8,128)(2,1)S(1)}, bf16[192,1152]{1,0:T(8,128)(2,1)S(1)}, u32[]{:S(2)}, u32[]{:S(2)}) %collective-permute-start.4) | collective-permute-done | bytes 442400 | tf_op jit(solution)/shard_map/ppermute | solution.py:290
  102.9 12.2 %all_gather.21 = bf16[32,6]{1,0:T(8,128)(2,1)S(1)} all-gather(bf16[8,6]{1,0:T(8,128)(2,1)S(1)} %copy-done.65), channel_id=1, replica_groups=mesh['ctx'=8,'wsh'=4] {'wsh'}, dimensions={0}, use_global_device_ids=true | all-gather | bytes 480 | tf_op jit(solution)/shard_map/all_gather | solution.py:393
  119.7 2.5 pad_maximum_fusion.4
  134.2 2.4 copy.103
  142.8 6.8 collective-permute-done.3
  149.5 3.7 collective-permute-done.2
  155.9 3.1 maximum_convert_fusion
  166.3 4.4 fusion.10
  174.4 2.4 copy.123
  178.5 2.4 copy.121
  184.4 5.9 multiply_convert_fusion.1
  190.2 9.5 %copy.109 = f32[1536,1472]{0,1:T(8,128)} copy(f32[1536,1472]{1,0:T(8,128)} %bitcast.177) | data formatting | bytes 18087936 | tf_op jit(solution)/shard_map/convert_element_type | solution.py:431
  202.1 3.1 convolution_convert_fusion.8
  205.2 14.7 %attention_forward.1 = (f32[3,128,384]{2,1,0:T(8,128)}, f32[3,3,8,128]{3,2,1,0:T(8,128)}) custom-call(s32[1]{0:T(128)} %bitcast.6.meta_ref, f32[32,6]{1,0:T(8,128)} %convert_element_type.258.table_ref, f32[3,8,128]{2,1,0:T(8,128)} %bitcast.254, bf16[3,128,384]{2,1,0:T(8,128)(2,1)} %bitcast.244, bf16[4,3,128,768]{3,2,1,0:T(8,128)(2,1)} %bitcast.179, ...), custom_call_target="tpu_custom_call" | custom-call | flops 603979776 | bytes 9437184 | tf_op jit(solution)/shard_map/attention_forward/pallas_call | solution.py:249
  223.2 3.8 pad_maximum_fusion
  227.0 3.5 collective-permute-done.11
  237.1 6.9 %multiply_reduce_fusion.1 = (f32[1536]{0:T(1024)S(1)}, f32[1536,1472]{0,1:T(8,128)S(1)}) fusion(f32[1536,1472]{0,1:T(8,128)} %copy.109, bf16[1536,384]{1,0:T(8,128)(2,1)S(1)} %bitcast.197, bf16[384,1472]{1,0:T(8,128)(2,1)} %bitcast.42), kind=kOutput, calls=%fused_computation.6 | convolution fusion | flops 1743223296 | bytes 20404224 | tf_op jit(solution)/shard_map/dot_general | solution.py:431
  244.8 3.1 copy-done.2
  248.0 7.0 %fusion.42 = f32[1536,896]{1,0:T(8,128)} fusion(bf16[1536,1472]{0,1:T(8,128)(2,1)S(1)} %multiply_convert_fusion.2, bf16[1472,896]{1,0:T(8,128)(2,1)S(1)} %copy-done.66), kind=kOutput, calls=%fused_computation.216 | convolution fusion | flops 4051697664 | bytes 12664832 | tf_op jit(solution)/shard_map/dot_general | solution.py:437
  254.9 8.8 %fusion.43 = f32[1536,896]{1,0:T(8,128)} fusion(bf16[1536,1472]{0,1:T(8,128)(2,1)S(1)} %multiply_convert_fusion.2, bf16[1472,896]{1,0:T(8,128)(2,1)} %collective-permute-done.19), kind=kOutput, calls=%fused_computation.217 | convolution fusion | flops 4051697664 | bytes 12664832 | tf_op jit(solution)/shard_map/dot_general | solution.py:438
  263.8 14.1 %select_convert_fusion = (bf16[1536,896]{1,0:T(8,128)(2,1)}, bf16[1536,896]{1,0:T(8,128)(2,1)}, bf16[1536,896]{1,0:T(8,128)(2,1)}) fusion(pred[]{:T(512)S(6)} %eq.3, f32[1536,896]{1,0:T(8,128)} %fusion.42, f32[1536,896]{1,0:T(8,128)} %fusion.43, bf16[1536,1472]{1,0:T(8,128)(2,1)S(1)} %bitcast.203, bf16[896,1472]{1,0:T(8,128)(2,1)} %bitcast.216), kind=kOutput, calls=%fused_computation.17 | convolution fusion | flops 4092985344 | bytes 26427392 | tf_op jit(solution)/shard_map/dot_general | solution.py:447
  277.9 8.7 %convolution_convert_fusion.2 = bf16[1472,896]{1,0:T(8,128)(2,1)} fusion(bf16[1536,1472]{0,1:T(8,128)(2,1)S(1)} %multiply_convert_fusion.2, bf16[1536,896]{1,0:T(8,128)(2,1)} %get-tuple-element.98), kind=kOutput, calls=%fused_computation.31 | convolution fusion | flops 4053016576 | bytes 9912320 | tf_op jit(solution)/shard_map/dot_general | solution.py:54
  286.6 5.1 fusion.44
  291.6 7.2 %fusion = bf16[1536,1472]{0,1:T(8,128)(2,1)S(1)} fusion(f32[1536,1472]{0,1:T(8,128)S(1)} %fusion.44, bf16[1536,896]{1,0:T(8,128)(2,1)S(1)} %copy-done.71, bf16[1472,896]{1,0:T(8,128)(2,1)} %collective-permute-done.19), kind=kOutput, calls=%fused_computation.9 | convolution fusion | flops 4056219648 | bytes 18956288 | tf_op jit(solution)/shard_map/dot_general | solution.py:453
  305.4 9.6 %convolution_convert_fusion.1 = bf16[896,1472]{0,1:T(8,128)(2,1)} fusion(bf16[1536,896]{1,0:T(8,128)(2,1)} %get-tuple-element.100, bf16[1536,1472]{1,0:T(8,128)(2,1)} %bitcast.200), kind=kOutput, calls=%fused_computation.30 | convolution fusion | flops 4053016576 | bytes 9912320 | tf_op jit(solution)/shard_map/dot_general | solution.py:54
  314.9 4.4 copy.132
  319.4 3.2 broadcast_select_fusion.5
  323.3 5.1 convolution_convert_fusion
  328.4 2.6 fusion.30
  342.1 2.7 fusion.11
  345.4 2.6 add_convert_fusion.4
  357.4 3.7 add_convert_fusion.6
  361.1 9.0 %add_convert_fusion = bf16[1472,896]{1,0:T(8,128)(2,1)} fusion(bf16[1472,896]{1,0:T(8,128)(2,1)} %collective-permute-done.38, bf16[1536,1472]{0,1:T(8,128)(2,1)} %copy-done.18, bf16[1536,896]{1,0:T(8,128)(2,1)S(1)} %copy-done.70), kind=kOutput, calls=%fused_computation.22 | convolution fusion | flops 4058292224 | bytes 12550144 | tf_op jit(solution)/shard_map/dot_general | solution.py:54
  374.6 2.8 collective-permute-done.32
  377.4 2.6 collective-permute-done.30
  380.1 3.5 multiply_reduce_fusion.6
  383.6 17.0 %collective-permute-done.24 = bf16[384,1472]{0,1:T(8,128)(2,1)S(1)} collective-permute-done((bf16[384,1472]{0,1:T(8,128)(2,1)S(1)}, bf16[384,1472]{0,1:T(8,128)(2,1)S(1)}, u32[]{:S(2)}, u32[]{:S(2)}) %collective-permute-start.24) | collective-permute-done | bytes 1130528 | tf_op jit(solution)/shard_map/ppermute | solution.py:290
  403.0 4.7 subtract_add_fusion
  407.6 2.8 convolution_convert_fusion.7
  410.5 20.3 %attention_backward.1 = (bf16[3,128,384]{2,1,0:T(8,128)(2,1)}, bf16[4,3,128,384]{3,2,1,0:T(8,128)(2,1)}, bf16[4,3,128,384]{3,2,1,0:T(8,128)(2,1)}, bf16[4,3,128,...) custom-call(s32[1]{0:T(128)} %bitcast.6.meta_ref, ...), custom_call_target="tpu_custom_call" | custom-call | flops 1509949440 | bytes 23592960 | tf_op jit(solution)/shard_map/attention_backward/pallas_call | solution.py:270
  430.8 3.3 pad_maximum_fusion.3
  435.6 2.4 copy.116
  438.0 2.4 copy.133
  440.5 37.8 %psum.23 = f32[6,32]{1,0:T(8,128)S(1)} all-reduce(f32[6,32]{1,0:T(8,128)S(1)} %reshape.355), channel_id=1, replica_groups=mesh['ctx'=8,'wsh'=4] {'ctx','wsh'}, use_global_device_ids=true, to_apply=%region_16.17 | all-reduce | flops 192 | bytes 1536 | tf_op jit(solution)/shard_map/psum | solution.py:524
  481.2 3.2 convolution_convert_fusion.6
  487.7 3.1 add_convert_fusion.1
  494.8 3.8 convolution_convert_fusion.4
  511.5 2.4 pad_maximum_fusion.5
  513.9 7.1 %collective-permute-done.37 = bf16[384,768]{1,0:T(8,128)(2,1)S(1)} collective-permute-done((bf16[384,768]{1,0:T(8,128)(2,1)S(1)}, bf16[384,768]{1,0:T(8,128)(2,1)S(1)}, u32[]{:S(2)}, u32[]{:S(2)}) %collective-permute-start.37) | collective-permute-done | bytes 589856 | tf_op jit(solution)/shard_map/ppermute | solution.py:290
  521.3 3.4 fusion.17
  524.8 2.8 fusion.16
  538.5 10.3 %collective-permute-done.40 = bf16[368,896]{1,0:T(8,128)(2,1)S(1)} collective-permute-done((bf16[368,896]{1,0:T(8,128)(2,1)}, bf16[368,896]{1,0:T(8,128)(2,1)S(1)}, u32[]{:S(2)}, u32[]{:S(2)}) %collective-permute-start.40) | collective-permute-done | bytes 659488 | tf_op jit(solution)/shard_map/ppermute | solution.py:290
  569.9 6.4 reduce-scatter.5.cloned.1.call-done
  581.5 5.0 copy.135
  586.6 50.8 %all-reduce.3.cloned.1.call-done = (bf16[368,1152]{1,0:T(8,128)(2,1)}, bf16[96,1472]{1,0:T(8,128)(2,1)}) async-done(((bf16[368,1152]{1,0:T(8,128)(2,1)}, bf16[96,1472]{1,0:T(8,128)(2,1)}), (bf16[368,1152]{1,0:T(8,128)(2,1)}, bf16[96,1472]{1,0:T(8,128)(2,1)})) %all-reduce.3.cloned.1.call-update) | async-done | bytes 1130512 | tf_op jit(solution)/shard_map/psum | solution.py:521
  648.6 5.4 concatenate.96
  654.0 5.6 multiply_reduce_fusion.3
  660.9 4.6 concatenate.97
  665.5 5.7 multiply_reduce_fusion.2
  (419 shorter events, 193.2 us)
Async XLA Ops:
  7.2 177.2 %all-gather.6.cloned.1.call-start = ((), (), s32[]{:S(2)}) async-start(), calls=%async_computation.5 | async-start | bytes 1720320 | tf_op jit(solution)/shard_map/all_gather | solution.py:405
  10.1 226.8 %all-gather.4.cloned.1.call-start = ((), (), s32[]{:S(2)}) async-start(), calls=%async_computation.4 | async-start | bytes 3297280 | tf_op jit(solution)/shard_map/all_gather | solution.py:402
  11.8 144.1 %copy-start.5 = (bf16[3,128,1472]{2,1,0:T(8,128)(2,1)}, bf16[3,128,1472]{2,1,0:T(8,128)(2,1)S(1)}, u32[]{:S(2)}) copy-start(bf16[3,128,1472]{2,1,0:T(8,128)(2,1)S(1)} %copy.100) | copy-start | bytes 3391492
  13.2 116.9 %collective-permute-start.1 = (bf16[384,1472]{0,1:T(8,128)(2,1)}, bf16[384,1472]{0,1:T(8,128)(2,1)}, u32[]{:S(2)}, u32[]{:S(2)}) collective-permute-start(bf16[384,1472]{0,1:T(8,128)(2,1)} %copy.102), channel_id=1, source_target_pairs={{0,16},{4,20},{8,24},{12,28},{16,0},{20,4},{24,8},{28,12},{1,17},{... | collective-permute-start | bytes 3391496 | tf_op jit(solution)/shard_map/ppermute | solution.py:290
  16.2 118.0 %collective-permute-start = (bf16[384,1472]{0,1:T(8,128)(2,1)}, bf16[384,1472]{0,1:T(8,128)(2,1)}, u32[]{:S(2)}, u32[]{:S(2)}) collective-permute-start(bf16[384,1472]{0,1:T(8,128)(2,1)} %copy.102), channel_id=1, source_target_pairs={{0,8},{4,12},{8,0},{12,4},{16,24},{20,28},{24,16},{28,20},{1,9},{5... | collective-permute-start | bytes 3391496 | tf_op jit(solution)/shard_map/ppermute | solution.py:290
  33.6 37.8 %collective-permute-start.15 = (bf16[64,1472]{1,0:T(8,128)(2,1)S(1)}, bf16[64,1472]{1,0:T(8,128)(2,1)S(1)}, u32[]{:S(2)}, u32[]{:S(2)}) collective-permute-start(bf16[64,1472]{1,0:T(8,128)(2,1)S(1)} %all_gather.25), channel_id=1, source_target_pairs={{0,16},{4,20},{8,24},{12,28},{16,0},{20,4},{24,8},{28,12},{1,17},{... | collective-permute-start | bytes 565256 | tf_op jit(solution)/shard_map/ppermute | solution.py:290
  34.1 38.0 %collective-permute-start.14 = (bf16[64,1472]{1,0:T(8,128)(2,1)S(1)}, bf16[64,1472]{1,0:T(8,128)(2,1)}, u32[]{:S(2)}, u32[]{:S(2)}) collective-permute-start(bf16[64,1472]{1,0:T(8,128)(2,1)S(1)} %all_gather.25), channel_id=1, source_target_pairs={{0,8},{4,12},{8,0},{12,4},{16,24},{20,28},{24,16},{28,20},{1,9},{5... | collective-permute-start | bytes 565256 | tf_op jit(solution)/shard_map/ppermute | solution.py:290
  55.2 34.1 %collective-permute-start.5 = (bf16[192,1152]{1,0:T(8,128)(2,1)S(1)}, bf16[192,1152]{1,0:T(8,128)(2,1)S(1)}, u32[]{:S(2)}, u32[]{:S(2)}) collective-permute-start(bf16[192,1152]{1,0:T(8,128)(2,1)S(1)} %all_gather.24), channel_id=1, source_target_pairs={{0,16},{4,20},{8,24},{12,28},{16,0},{20,4},{24,8},{28,12},{1,17},{... | collective-permute-start | bytes 1327112 | tf_op jit(solution)/shard_map/ppermute | solution.py:290
  61.1 423.4 %reduce-scatter.11.cloned.1.call-start = ((), (), s32[]{:S(2)}) async-start(), calls=%async_computation.9 | async-start | bytes 1720320 | tf_op jit(solution)/shard_map/reduce_scatter | solution.py:475
  71.4 15.1 %collective-permute-start.17 = (bf16[32,1472]{1,0:T(8,128)(2,1)S(1)}, bf16[32,1472]{1,0:T(8,128)(2,1)S(1)}, u32[]{:S(2)}, u32[]{:S(2)}) collective-permute-start(bf16[32,1472]{1,0:T(8,128)(2,1)S(1)} %slice.434), channel_id=1, source_target_pairs={{0,8},{4,12},{8,0},{12,4},{16,24},{20,28},{24,16},{28,20},{1,9},{5... | collective-permute-start | bytes 282632 | tf_op jit(solution)/shard_map/ppermute | solution.py:290
  73.0 14.3 %collective-permute-start.16 = (bf16[32,1472]{1,0:T(8,128)(2,1)S(1)}, bf16[32,1472]{1,0:T(8,128)(2,1)S(1)}, u32[]{:S(2)}, u32[]{:S(2)}) collective-permute-start(bf16[32,1472]{1,0:T(8,128)(2,1)S(1)} %slice.433), channel_id=1, source_target_pairs={{0,16},{4,20},{8,24},{12,28},{16,0},{20,4},{24,8},{28,12},{1,17},{... | collective-permute-start | bytes 282632 | tf_op jit(solution)/shard_map/ppermute | solution.py:290
  86.5 12.1 %collective-permute-start.4 = (bf16[192,1152]{1,0:T(8,128)(2,1)S(1)}, bf16[192,1152]{1,0:T(8,128)(2,1)S(1)}, u32[]{:S(2)}, u32[]{:S(2)}) collective-permute-start(bf16[192,1152]{1,0:T(8,128)(2,1)S(1)} %all_gather.24), channel_id=1, source_target_pairs={{0,8},{4,12},{8,0},{12,4},{16,24},{20,28},{24,16},{28,20},{1,9},{5... | collective-permute-start | bytes 1327112 | tf_op jit(solution)/shard_map/ppermute | solution.py:290
  89.3 32.9 %collective-permute-start.18 = (bf16[4,64,1472]{2,1,0:T(8,128)(2,1)}, bf16[4,64,1472]{2,1,0:T(8,128)(2,1)}, u32[]{:S(2)}, u32[]{:S(2)}) collective-permute-start(bf16[4,64,1472]{2,1,0:T(8,128)(2,1)} %pad_maximum_fusion.11), channel_id=1, source_target_pairs={{0,4},{4,0},{8,12},{12,8},{16,20},{20,16},{24,28},{28,24},{1,5},{5... | collective-permute-start | bytes 2261000 | tf_op jit(solution)/shard_map/ppermute | solution.py:290
  90.0 26.4 %collective-permute-start.7 = (bf16[96,1152]{1,0:T(8,128)(2,1)}, bf16[96,1152]{1,0:T(8,128)(2,1)}, u32[]{:S(2)}, u32[]{:S(2)}) collective-permute-start(bf16[96,1152]{1,0:T(8,128)(2,1)} %slice.423), channel_id=1, source_target_pairs={{0,8},{4,12},{8,0},{12,4},{16,24},{20,28},{24,16},{28,20},{1,9},{5... | collective-permute-start | bytes 663560 | tf_op jit(solution)/shard_map/ppermute | solution.py:290
  99.3 18.8 %collective-permute-start.6 = (bf16[96,1152]{1,0:T(8,128)(2,1)}, bf16[96,1152]{1,0:T(8,128)(2,1)}, u32[]{:S(2)}, u32[]{:S(2)}) collective-permute-start(bf16[96,1152]{1,0:T(8,128)(2,1)} %slice.422), channel_id=1, source_target_pairs={{0,16},{4,20},{8,24},{12,28},{16,0},{20,4},{24,8},{28,12},{1,17},{... | collective-permute-start | bytes 663560 | tf_op jit(solution)/shard_map/ppermute | solution.py:290
  116.4 68.0 %copy-start.58 = (f32[1472]{0:T(1024)}, f32[1472]{0:T(1024)S(1)}, u32[]{:S(2)}) copy-start(f32[1472]{0:T(1024)S(1)} %get-tuple-element.91) | copy-start | bytes 17668
  116.4 58.0 %collective-permute-start.26 = (bf16[384,1472]{0,1:T(8,128)(2,1)}, bf16[384,1472]{0,1:T(8,128)(2,1)}, u32[]{:S(2)}, u32[]{:S(2)}) collective-permute-start(bf16[384,1472]{0,1:T(8,128)(2,1)} %copy.118), channel_id=1, source_target_pairs={{0,16},{4,20},{8,24},{12,28},{16,0},{20,4},{24,8},{28,12},{1,17},{... | collective-permute-start | bytes 3391496 | tf_op jit(solution)/shard_map/ppermute | solution.py:290
  118.1 60.4 %collective-permute-start.25 = (bf16[384,1472]{0,1:T(8,128)(2,1)}, bf16[384,1472]{0,1:T(8,128)(2,1)}, u32[]{:S(2)}, u32[]{:S(2)}) collective-permute-start(bf16[384,1472]{0,1:T(8,128)(2,1)} %copy.118), channel_id=1, source_target_pairs={{0,8},{4,12},{8,0},{12,4},{16,24},{20,28},{24,16},{28,20},{1,9},{5... | collective-permute-start | bytes 3391496 | tf_op jit(solution)/shard_map/ppermute | solution.py:290
  122.2 36.8 %collective-permute-start.8 = (bf16[4,192,1152]{2,1,0:T(8,128)(2,1)}, bf16[4,192,1152]{2,1,0:T(8,128)(2,1)}, u32[]{:S(2)}, u32[]{:S(2)}) collective-permute-start(bf16[4,192,1152]{2,1,0:T(8,128)(2,1)} %pad_maximum_fusion.4), channel_id=1, source_target_pairs={{0,4},{4,0},{8,12},{12,8},{16,20},{20,16},{24,28},{28,24},{1,5},{5... | collective-permute-start | bytes 5308424 | tf_op jit(solution)/shard_map/ppermute | solution.py:290
  132.6 16.9 %collective-permute-start.3 = (bf16[192,1472]{1,0:T(8,128)(2,1)}, bf16[192,1472]{1,0:T(8,128)(2,1)}, u32[]{:S(2)}, u32[]{:S(2)}) collective-permute-start(bf16[192,1472]{1,0:T(8,128)(2,1)} %slice.419), channel_id=1, source_target_pairs={{0,8},{4,12},{8,0},{12,4},{16,24},{20,28},{24,16},{28,20},{1,9},{5... | collective-permute-start | bytes 1695752 | tf_op jit(solution)/shard_map/ppermute | solution.py:290
  137.7 15.5 %collective-permute-start.2 = (bf16[192,1472]{1,0:T(8,128)(2,1)S(1)}, bf16[192,1472]{1,0:T(8,128)(2,1)S(1)}, u32[]{:S(2)}, u32[]{:S(2)}) collective-permute-start(bf16[192,1472]{1,0:T(8,128)(2,1)S(1)} %slice.418), channel_id=1, source_target_pairs={{0,16},{4,20},{8,24},{12,28},{16,0},{20,4},{24,8},{28,12},{1,17},{... | collective-permute-start | bytes 1695752 | tf_op jit(solution)/shard_map/ppermute | solution.py:290
  170.8 34.4 %collective-permute-start.9 = (bf16[4,3,128,768]{3,2,1,0:T(8,128)(2,1)S(1)}, bf16[4,3,128,768]{3,2,1,0:T(8,128)(2,1)}, u32[]{:S(2)}, u32[]{:S(2)}) collective-permute-start(bf16[4,3,128,768]{3,2,1,0:T(8,128)(2,1)S(1)} %bitcast.178), channel_id=1, source_target_pairs={{0,4},{4,0},{8,12},{12,8},{16,20},{20,16},{24,28},{28,24},{1,5},{5... | collective-permute-start | bytes 7077896 | tf_op jit(solution)/shard_map/ppermute | solution.py:290
  177.9 21.8 %collective-permute-start.28 = (bf16[192,1472]{1,0:T(8,128)(2,1)S(1)}, bf16[192,1472]{1,0:T(8,128)(2,1)}, u32[]{:S(2)}, u32[]{:S(2)}) collective-permute-start(bf16[192,1472]{1,0:T(8,128)(2,1)S(1)} %slice.449), channel_id=1, source_target_pairs={{0,8},{4,12},{8,0},{12,4},{16,24},{20,28},{24,16},{28,20},{1,9},{5... | collective-permute-start | bytes 1695752 | tf_op jit(solution)/shard_map/ppermute | solution.py:290
  182.8 16.9 %collective-permute-start.27 = (bf16[192,1472]{1,0:T(8,128)(2,1)}, bf16[192,1472]{1,0:T(8,128)(2,1)}, u32[]{:S(2)}, u32[]{:S(2)}) collective-permute-start(bf16[192,1472]{1,0:T(8,128)(2,1)} %slice.448), channel_id=1, source_target_pairs={{0,16},{4,20},{8,24},{12,28},{16,0},{20,4},{24,8},{28,12},{1,17},{... | collective-permute-start | bytes 1695752 | tf_op jit(solution)/shard_map/ppermute | solution.py:290
  184.4 48.4 %collective-permute-start.20 = (bf16[4,112,1472]{2,1,0:T(8,128)(2,1)}, bf16[4,112,1472]{2,1,0:T(8,128)(2,1)}, u32[]{:S(2)}, u32[]{:S(2)}) collective-permute-start(bf16[4,112,1472]{2,1,0:T(8,128)(2,1)} %bitcast.238), channel_id=1, source_target_pairs={{0,4},{4,0},{8,12},{12,8},{16,20},{20,16},{24,28},{28,24},{1,5},{5... | collective-permute-start | bytes 3956744 | tf_op jit(solution)/shard_map/ppermute | solution.py:290
  221.1 9.5 %collective-permute-start.11 = (bf16[384,384]{1,0:T(8,128)(2,1)S(1)}, bf16[384,384]{1,0:T(8,128)(2,1)S(1)}, u32[]{:S(2)}, u32[]{:S(2)}) collective-permute-start(bf16[384,384]{1,0:T(8,128)(2,1)S(1)} %bitcast.218), channel_id=1, source_target_pairs={{0,16},{4,20},{8,24},{12,28},{16,0},{20,4},{24,8},{28,12},{1,17},{... | collective-permute-start | bytes 884744 | tf_op jit(solution)/shard_map/ppermute | solution.py:290
  221.6 9.4 %collective-permute-start.10 = (bf16[384,384]{1,0:T(8,128)(2,1)S(1)}, bf16[384,384]{1,0:T(8,128)(2,1)S(1)}, u32[]{:S(2)}, u32[]{:S(2)}) collective-permute-start(bf16[384,384]{1,0:T(8,128)(2,1)S(1)} %bitcast.219), channel_id=1, source_target_pairs={{0,8},{4,12},{8,0},{12,4},{16,24},{20,28},{24,16},{28,20},{1,9},{5... | collective-permute-start | bytes 884744 | tf_op jit(solution)/shard_map/ppermute | solution.py:290
  230.6 6.3 collective-permute-start.13
  231.1 5.8 collective-permute-start.12
  236.8 18.1 %collective-permute-start.19 = (bf16[1472,896]{1,0:T(8,128)(2,1)}, bf16[1472,896]{1,0:T(8,128)(2,1)}, u32[]{:S(2)}, u32[]{:S(2)}) collective-permute-start(bf16[1472,896]{1,0:T(8,128)(2,1)} %all-gather.4.cloned.1.call-done), channel_id=1, source_target_pairs={{0,4},{4,0},{8,12},{12,8},{16,20},{20,16},{24,28},{28,24},{1,5},{5... | collective-permute-start | bytes 7913480 | tf_op jit(solution)/shard_map/ppermute | solution.py:290
  248.0 29.9 %copy-start.18 = (bf16[1536,1472]{0,1:T(8,128)(2,1)}, bf16[1536,1472]{0,1:T(8,128)(2,1)S(1)}, u32[]{:S(2)}) copy-start(bf16[1536,1472]{0,1:T(8,128)(2,1)S(1)} %multiply_convert_fusion.2) | copy-start | bytes 13565956
  302.3 34.5 %collective-permute-start.29 = (bf16[192,1472]{1,0:T(8,128)(2,1)}, bf16[192,1472]{1,0:T(8,128)(2,1)}, u32[]{:S(2)}, u32[]{:S(2)}) collective-permute-start(bf16[192,1472]{1,0:T(8,128)(2,1)} %copy.126), channel_id=1, source_target_pairs={{0,16},{4,20},{8,24},{12,28},{16,0},{20,4},{24,8},{28,12},{1,17},{... | collective-permute-start | bytes 1695752 | tf_op jit(solution)/shard_map/ppermute | solution.py:290
  304.4 35.5 %collective-permute-start.31 = (bf16[192,1472]{1,0:T(8,128)(2,1)}, bf16[192,1472]{1,0:T(8,128)(2,1)}, u32[]{:S(2)}, u32[]{:S(2)}) collective-permute-start(bf16[192,1472]{1,0:T(8,128)(2,1)} %copy.128), channel_id=1, source_target_pairs={{0,8},{4,12},{8,0},{12,4},{16,24},{20,28},{24,16},{28,20},{1,9},{5... | collective-permute-start | bytes 1695752 | tf_op jit(solution)/shard_map/ppermute | solution.py:290
  305.4 55.7 %collective-permute-start.38 = (bf16[1472,896]{1,0:T(8,128)(2,1)}, bf16[1472,896]{1,0:T(8,128)(2,1)}, u32[]{:S(2)}, u32[]{:S(2)}) collective-permute-start(bf16[1472,896]{1,0:T(8,128)(2,1)} %convolution_convert_fusion.2), channel_id=1, source_target_pairs={{0,4},{4,0},{8,12},{12,8},{16,20},{20,16},{24,28},{28,24},{1,5},{5... | collective-permute-start | bytes 7913480 | tf_op jit(solution)/shard_map/ppermute | solution.py:290
  322.5 19.6 %collective-permute-start.44 = (bf16[448,1472]{1,0:T(8,128)(2,1)}, bf16[448,1472]{1,0:T(8,128)(2,1)}, u32[]{:S(2)}, u32[]{:S(2)}) collective-permute-start(bf16[448,1472]{1,0:T(8,128)(2,1)} %bitcast.78), channel_id=1, source_target_pairs={{0,4},{4,0},{8,12},{12,8},{16,20},{20,16},{24,28},{28,24},{1,5},{5... | collective-permute-start | bytes 3956744 | tf_op jit(solution)/shard_map/ppermute | solution.py:290
  333.4 19.5 %collective-permute-start.21 = (bf16[192,1472]{1,0:T(8,128)(2,1)}, bf16[192,1472]{1,0:T(8,128)(2,1)}, u32[]{:S(2)}, u32[]{:S(2)}) collective-permute-start(bf16[192,1472]{1,0:T(8,128)(2,1)} %copy.112), channel_id=1, source_target_pairs={{0,16},{4,20},{8,24},{12,28},{16,0},{20,4},{24,8},{28,12},{1,17},{... | collective-permute-start | bytes 1695752 | tf_op jit(solution)/shard_map/ppermute | solution.py:290
  336.7 18.4 %collective-permute-start.23 = (bf16[192,1472]{1,0:T(8,128)(2,1)}, bf16[192,1472]{1,0:T(8,128)(2,1)}, u32[]{:S(2)}, u32[]{:S(2)}) collective-permute-start(bf16[192,1472]{1,0:T(8,128)(2,1)} %copy.114), channel_id=1, source_target_pairs={{0,8},{4,12},{8,0},{12,4},{16,24},{20,28},{24,16},{28,20},{1,9},{5... | collective-permute-start | bytes 1695752 | tf_op jit(solution)/shard_map/ppermute | solution.py:290
  344.9 189.3 %reduce-scatter.9.cloned.1.call-start = ((), (), s32[]{:S(2)}) async-start(), calls=%async_computation.8 | async-start | bytes 3297280 | tf_op jit(solution)/shard_map/reduce_scatter | solution.py:476
  349.4 28.0 %collective-permute-start.32 = (bf16[384,1472]{0,1:T(8,128)(2,1)}, bf16[384,1472]{0,1:T(8,128)(2,1)S(1)}, u32[]{:S(2)}, u32[]{:S(2)}) collective-permute-start(bf16[384,1472]{0,1:T(8,128)(2,1)} %pad_maximum_fusion.10), channel_id=1, source_target_pairs={{0,16},{4,20},{8,24},{12,28},{16,0},{20,4},{24,8},{28,12},{1,17},{... | collective-permute-start | bytes 3391496 | tf_op jit(solution)/shard_map/ppermute | solution.py:290
  352.0 28.0 %collective-permute-start.30 = (bf16[384,1472]{0,1:T(8,128)(2,1)}, bf16[384,1472]{0,1:T(8,128)(2,1)S(1)}, u32[]{:S(2)}, u32[]{:S(2)}) collective-permute-start(bf16[384,1472]{0,1:T(8,128)(2,1)} %pad_maximum_fusion.9), channel_id=1, source_target_pairs={{0,8},{4,12},{8,0},{12,4},{16,24},{20,28},{24,16},{28,20},{1,9},{5... | collective-permute-start | bytes 3391496 | tf_op jit(solution)/shard_map/ppermute | solution.py:290
  370.1 199.8 %reduce-scatter.7.cloned.1.call-start = ((), (), s32[]{:S(2)}) async-start(), calls=%async_computation.7 | async-start | bytes 1474560 | tf_op jit(solution)/shard_map/reduce_scatter | solution.py:522
  372.0 28.6 %collective-permute-start.24 = (bf16[384,1472]{0,1:T(8,128)(2,1)S(1)}, bf16[384,1472]{0,1:T(8,128)(2,1)S(1)}, u32[]{:S(2)}, u32[]{:S(2)}) collective-permute-start(bf16[384,1472]{0,1:T(8,128)(2,1)S(1)} %pad_maximum_fusion.8), channel_id=1, source_target_pairs={{0,16},{4,20},{8,24},{12,28},{16,0},{20,4},{24,8},{28,12},{1,17},{... | collective-permute-start | bytes 3391496 | tf_op jit(solution)/shard_map/ppermute | solution.py:290
  373.6 29.3 %collective-permute-start.22 = (bf16[384,1472]{0,1:T(8,128)(2,1)S(1)}, bf16[384,1472]{0,1:T(8,128)(2,1)S(1)}, u32[]{:S(2)}, u32[]{:S(2)}) collective-permute-start(bf16[384,1472]{0,1:T(8,128)(2,1)S(1)} %pad_maximum_fusion.7), channel_id=1, source_target_pairs={{0,8},{4,12},{8,0},{12,4},{16,24},{20,28},{24,16},{28,20},{1,9},{5... | collective-permute-start | bytes 3391496 | tf_op jit(solution)/shard_map/ppermute | solution.py:290
  434.1 53.6 %collective-permute-start.33 = (bf16[4,3,128,768]{3,2,1,0:T(8,128)(2,1)}, bf16[4,3,128,768]{3,2,1,0:T(8,128)(2,1)}, u32[]{:S(2)}, u32[]{:S(2)}) collective-permute-start(bf16[4,3,128,768]{3,2,1,0:T(8,128)(2,1)} %pad_maximum_fusion.3), channel_id=1, source_target_pairs={{0,4},{4,0},{8,12},{12,8},{16,20},{20,16},{24,28},{28,24},{1,5},{5... | collective-permute-start | bytes 7077896 | tf_op jit(solution)/shard_map/ppermute | solution.py:290
  435.6 43.5 %copy-start.30 = (bf16[3,128,384]{2,1,0:T(8,128)(2,1)S(1)}, bf16[3,128,384]{2,1,0:T(8,128)(2,1)}, u32[]{:S(2)}) copy-start(bf16[3,128,384]{2,1,0:T(8,128)(2,1)} %copy-done.29) | copy-start | bytes 884740
  440.4 40.8 %copy-start.67 = (bf16[3,128,384]{2,1,0:T(8,128)(2,1)S(1)}, bf16[3,128,384]{2,1,0:T(8,128)(2,1)}, u32[]{:S(2)}) copy-start(bf16[3,128,384]{2,1,0:T(8,128)(2,1)} %get-tuple-element.22) | copy-start | bytes 884740
  481.0 95.3 %reduce-scatter.5.cloned.1.call-start = ((), (), s32[]{:S(2)}) async-start(), calls=%async_computation.6 | async-start | bytes 4239360 | tf_op jit(solution)/shard_map/reduce_scatter | solution.py:521
  484.4 16.3 %collective-permute-start.46 = (bf16[112,1472]{1,0:T(8,128)(2,1)}, bf16[112,1472]{1,0:T(8,128)(2,1)S(1)}, u32[]{:S(2)}, u32[]{:S(2)}) collective-permute-start(bf16[112,1472]{1,0:T(8,128)(2,1)} %reduce-scatter.11.cloned.1.call-done), channel_id=1, source_target_pairs={{0,16},{4,20},{8,24},{12,28},{16,0},{20,4},{24,8},{28,12},{1,17},{... | collective-permute-start | bytes 989192 | tf_op jit(solution)/shard_map/ppermute | solution.py:290
  486.7 15.9 %collective-permute-start.45 = (bf16[112,1472]{1,0:T(8,128)(2,1)}, bf16[112,1472]{1,0:T(8,128)(2,1)}, u32[]{:S(2)}, u32[]{:S(2)}) collective-permute-start(bf16[112,1472]{1,0:T(8,128)(2,1)} %reduce-scatter.11.cloned.1.call-done), channel_id=1, source_target_pairs={{0,8},{4,12},{8,0},{12,4},{16,24},{20,28},{24,16},{28,20},{1,9},{5... | collective-permute-start | bytes 989192 | tf_op jit(solution)/shard_map/ppermute | solution.py:290
  492.7 11.9 %collective-permute-start.36 = (bf16[192,768]{1,0:T(8,128)(2,1)}, bf16[192,768]{1,0:T(8,128)(2,1)}, u32[]{:S(2)}, u32[]{:S(2)}) collective-permute-start(bf16[192,768]{1,0:T(8,128)(2,1)} %get-tuple-element.189), channel_id=1, source_target_pairs={{0,8},{4,12},{8,0},{12,4},{16,24},{20,28},{24,16},{28,20},{1,9},{5... | collective-permute-start | bytes 884744 | tf_op jit(solution)/shard_map/ppermute | solution.py:290
  494.5 13.3 %collective-permute-start.34 = (bf16[192,768]{1,0:T(8,128)(2,1)}, bf16[192,768]{1,0:T(8,128)(2,1)}, u32[]{:S(2)}, u32[]{:S(2)}) collective-permute-start(bf16[192,768]{1,0:T(8,128)(2,1)} %get-tuple-element.188), channel_id=1, source_target_pairs={{0,16},{4,20},{8,24},{12,28},{16,0},{20,4},{24,8},{28,12},{1,17},{... | collective-permute-start | bytes 884744 | tf_op jit(solution)/shard_map/ppermute | solution.py:290
  500.6 136.8 %all-reduce.3.cloned.1.call-start = ((), (), s32[]{:S(2)}) async-start(), calls=%async_computation.10 | async-start | bytes 2285568 | tf_op jit(solution)/shard_map/psum | solution.py:521
  500.7 9.2 %collective-permute-start.48 = (bf16[56,1472]{1,0:T(8,128)(2,1)S(1)}, bf16[56,1472]{1,0:T(8,128)(2,1)S(1)}, u32[]{:S(2)}, u32[]{:S(2)}) collective-permute-start(bf16[56,1472]{1,0:T(8,128)(2,1)S(1)} %slice.507), channel_id=1, source_target_pairs={{0,8},{4,12},{8,0},{12,4},{16,24},{20,28},{24,16},{28,20},{1,9},{5... | collective-permute-start | bytes 494600 | tf_op jit(solution)/shard_map/ppermute | solution.py:290
  503.6 7.3 %collective-permute-start.47 = (bf16[56,1472]{1,0:T(8,128)(2,1)S(1)}, bf16[56,1472]{1,0:T(8,128)(2,1)S(1)}, u32[]{:S(2)}, u32[]{:S(2)}) collective-permute-start(bf16[56,1472]{1,0:T(8,128)(2,1)S(1)} %slice.506), channel_id=1, source_target_pairs={{0,16},{4,20},{8,24},{12,28},{16,0},{20,4},{24,8},{28,12},{1,17},{... | collective-permute-start | bytes 494600 | tf_op jit(solution)/shard_map/ppermute | solution.py:290
  506.7 14.3 %collective-permute-start.37 = (bf16[384,768]{1,0:T(8,128)(2,1)S(1)}, bf16[384,768]{1,0:T(8,128)(2,1)S(1)}, u32[]{:S(2)}, u32[]{:S(2)}) collective-permute-start(bf16[384,768]{1,0:T(8,128)(2,1)S(1)} %pad_maximum_fusion.13), channel_id=1, source_target_pairs={{0,16},{4,20},{8,24},{12,28},{16,0},{20,4},{24,8},{28,12},{1,17},{... | collective-permute-start | bytes 1769480 | tf_op jit(solution)/shard_map/ppermute | solution.py:290
  509.0 12.0 %collective-permute-start.35 = (bf16[384,768]{1,0:T(8,128)(2,1)S(1)}, bf16[384,768]{1,0:T(8,128)(2,1)S(1)}, u32[]{:S(2)}, u32[]{:S(2)}) collective-permute-start(bf16[384,768]{1,0:T(8,128)(2,1)S(1)} %pad_maximum_fusion.12), channel_id=1, source_target_pairs={{0,8},{4,12},{8,0},{12,4},{16,24},{20,28},{24,16},{28,20},{1,9},{5... | collective-permute-start | bytes 1769480 | tf_op jit(solution)/shard_map/ppermute | solution.py:290
  513.9 16.8 %collective-permute-start.49 = (bf16[4,112,1472]{2,1,0:T(8,128)(2,1)}, bf16[4,112,1472]{2,1,0:T(8,128)(2,1)}, u32[]{:S(2)}, u32[]{:S(2)}) collective-permute-start(bf16[4,112,1472]{2,1,0:T(8,128)(2,1)} %pad_maximum_fusion.5), channel_id=1, source_target_pairs={{0,4},{4,0},{8,12},{12,8},{16,20},{20,16},{24,28},{28,24},{1,5},{5... | collective-permute-start | bytes 3956744 | tf_op jit(solution)/shard_map/ppermute | solution.py:290
  534.2 14.6 %collective-permute-start.40 = (bf16[368,896]{1,0:T(8,128)(2,1)}, bf16[368,896]{1,0:T(8,128)(2,1)S(1)}, u32[]{:S(2)}, u32[]{:S(2)}) collective-permute-start(bf16[368,896]{1,0:T(8,128)(2,1)} %reduce-scatter.9.cloned.1.call-done), channel_id=1, source_target_pairs={{0,16},{4,20},{8,24},{12,28},{16,0},{20,4},{24,8},{28,12},{1,17},{... | collective-permute-start | bytes 1978376 | tf_op jit(solution)/shard_map/ppermute | solution.py:290
  535.3 15.0 %collective-permute-start.39 = (bf16[368,896]{1,0:T(8,128)(2,1)}, bf16[368,896]{1,0:T(8,128)(2,1)S(1)}, u32[]{:S(2)}, u32[]{:S(2)}) collective-permute-start(bf16[368,896]{1,0:T(8,128)(2,1)} %reduce-scatter.9.cloned.1.call-done), channel_id=1, source_target_pairs={{0,8},{4,12},{8,0},{12,4},{16,24},{20,28},{24,16},{28,20},{1,9},{5... | collective-permute-start | bytes 1978376 | tf_op jit(solution)/shard_map/ppermute | solution.py:290
  548.9 7.6 %collective-permute-start.42 = (bf16[184,896]{1,0:T(8,128)(2,1)S(1)}, bf16[184,896]{1,0:T(8,128)(2,1)S(1)}, u32[]{:S(2)}, u32[]{:S(2)}) collective-permute-start(bf16[184,896]{1,0:T(8,128)(2,1)S(1)} %slice.471), channel_id=1, source_target_pairs={{0,8},{4,12},{8,0},{12,4},{16,24},{20,28},{24,16},{28,20},{1,9},{5... | collective-permute-start | bytes 989192 | tf_op jit(solution)/shard_map/ppermute | solution.py:290
  550.3 7.2 %collective-permute-start.41 = (bf16[184,896]{1,0:T(8,128)(2,1)S(1)}, bf16[184,896]{1,0:T(8,128)(2,1)S(1)}, u32[]{:S(2)}, u32[]{:S(2)}) collective-permute-start(bf16[184,896]{1,0:T(8,128)(2,1)S(1)} %slice.470), channel_id=1, source_target_pairs={{0,16},{4,20},{8,24},{12,28},{16,0},{20,4},{24,8},{28,12},{1,17},{... | collective-permute-start | bytes 989192 | tf_op jit(solution)/shard_map/ppermute | solution.py:290
  559.5 83.3 %collective-permute-start.43 = (bf16[4,368,896]{2,1,0:T(8,128)(2,1)}, bf16[4,368,896]{2,1,0:T(8,128)(2,1)}, u32[]{:S(2)}, u32[]{:S(2)}) collective-permute-start(bf16[4,368,896]{2,1,0:T(8,128)(2,1)} %pad_maximum_fusion.2), channel_id=1, source_target_pairs={{0,4},{4,0},{8,12},{12,8},{16,20},{20,16},{24,28},{28,24},{1,5},{5... | collective-permute-start | bytes 7913480 | tf_op jit(solution)/shard_map/ppermute | solution.py:290
  581.5 57.8 %copy-start.38 = (bf16[368,1152]{1,0:T(8,128)(2,1)S(1)}, bf16[368,1152]{1,0:T(8,128)(2,1)}, u32[]{:S(2)}) copy-start(bf16[368,1152]{1,0:T(8,128)(2,1)} %copy-done.37) | copy-start | bytes 2543620
  581.5 59.4 %copy-start.61 = (bf16[368]{0:T(512)(128)(2,1)S(1)}, bf16[368]{0:T(512)(128)(2,1)}, u32[]{:S(2)}) copy-start(bf16[368]{0:T(512)(128)(2,1)} %param.23) | copy-start | bytes 2212
  (70 other events, 668.1 us)
Sparse Core Ops, SparseCore 0:
  10.2 46.2 all-gather.5
  61.2 53.7 all-gather.3
  345.0 29.8 reduce-scatter.10
  377.2 51.3 reduce-scatter.8
  481.1 29.3 reduce-scatter.6
  513.3 62.9 reduce-scatter.4
  580.0 57.4 all-reduce.2

commit v2 on v1

--- a/solution.py
+++ b/solution.py
@@ -290,16 +290,23 @@
     return lax.ppermute(value, "ctx", [(source, source ^ bit) for source in range(count)])
 
 
-def gather_four(own):
-    cut = own.shape[0] // 2
+def swap_depth(value, bit):
+    count = lax.axis_size("wsh")
+    return lax.ppermute(value, "wsh", [(source, source ^ bit) for source in range(count)])
+
+
+def halves_four(own, cut):
     first, second = swap(own, 2), swap(own, 4)
-    last = jnp.concatenate((swap(first[:cut], 4), swap(second[cut:], 2)), axis=0)
-    return [own, first, second, last]
-
-
-def scatter_four(blocks):
-    own, first, second, last = blocks
-    cut = own.shape[0] // 2
+    return own, first, second, swap(first[:cut], 4), swap(second[cut:], 2)
+
+
+def gather_four(own, cut):
+    own, first, second, upper, lower = halves_four(own, cut)
+    return jnp.stack((own, first, second, jnp.concatenate((upper, lower), axis=0)))
+
+
+def scatter_four(blocks, cut):
+    own, first, second, last = (blocks[index] for index in range(4))
     low, high = swap(last[:cut], 4), swap(last[cut:], 2)
     first = jnp.concatenate(((first[:cut].astype(FLOAT) + low.astype(FLOAT)).astype(BFLOAT), first[cut:]), axis=0)
     second = jnp.concatenate((second[:cut], (second[cut:].astype(FLOAT) + high.astype(FLOAT)).astype(BFLOAT)), axis=0)
@@ -307,62 +314,298 @@
     return own.astype(FLOAT) + got_first.astype(FLOAT) + got_second.astype(FLOAT)
 
 
-def rms_rows(hidden, gain):
-    return hidden * lax.rsqrt(jnp.mean(hidden * hidden, axis=-1, keepdims=True) + EPSILON) * gain
-
-
 def rms_back(hidden, gain, back):
     scale = lax.rsqrt(jnp.mean(hidden * hidden, axis=-1, keepdims=True) + EPSILON)
     lifted = back * gain
     return scale * lifted - hidden * (scale * scale * scale) * jnp.mean(lifted * hidden, axis=-1, keepdims=True)
 
 
-def ordered(blocks, low):
-    stacked = jnp.stack(blocks)
-    return [lax.dynamic_index_in_dim(stacked, lax.bitwise_xor(low, jnp.int32(index)), 0, keepdims=False) for index in range(GROUP)]
-
-
-def gather_eight(own, low):
-    four = gather_four(own)
-    other = swap(jnp.stack(four), 1)
-    listed = [four[index // 2] if index % 2 == 0 else other[index // 2] for index in range(GROUP)]
-    return ordered(listed, low)
-
-
-def slice_rows(weight, low):
-    total = weight.shape[0]
-    size = -(-total // (GROUP * 16)) * 16
-    start = jnp.minimum(low * size, total - size)
-    return lax.dynamic_slice_in_dim(weight, start, size, 0)
-
-
-def join_rows(pieces, depth, total):
-    size = pieces[0].shape[0] // depth
-    cut = [piece.reshape(depth, size, -1) for piece in pieces]
-    rows = []
-    covered = 0
-    for index, piece in enumerate(cut):
-        start = min(index * size, total - size)
-        if start + size > covered:
-            rows.append(piece[:, covered - start :])
-            covered = start + size
-    return jnp.concatenate(rows, axis=1).reshape(depth * total, -1)
+VMEM_WHOLE = pl.BlockSpec(memory_space=pltpu.VMEM)
+SMEM_WHOLE = pl.BlockSpec(memory_space=pltpu.SMEM)
+BIG = pltpu.CompilerParams(vmem_limit_bytes=60 * 1024 * 1024)
+
+
+def slice_size(total):
+    return -(-total // (GROUP * 16)) * 16
+
+
+def slice_start(index, total, size):
+    return jnp.minimum(index * size, total - size)
+
+
+def join_kernel(place_ref, near_ref, far_ref, *out_refs, depth, total, size):
+    low, zed = place_ref[0], place_ref[1]
+    for index in range(GROUP):
+        gap = lax.bitwise_xor(low, jnp.int32(index))
+        slot, odd = gap // 2, lax.rem(gap, 2)
+        for level in range(depth):
+            step = lax.bitwise_xor(zed, jnp.int32(level)) if depth > 1 else 0
+            start = pl.multiple_of(step * size, 16)
+            near = near_ref[slot, pl.ds(start, size), :]
+            far = far_ref[slot, pl.ds(start, size), :]
+            rows = jnp.where(odd == 0, near, far)
+            base = level * total + min(index * size, total - size)
+            column = 0
+            for out_ref in out_refs:
+                wide = out_ref.shape[1]
+                out_ref[base : base + size, :] = rows[:, column : column + wide].astype(out_ref.dtype)
+                column += wide
+
+
+def join(place, near, far, depth, total, size, widths, dtype):
+    return pl.pallas_call(
+        functools.partial(join_kernel, depth=depth, total=total, size=size),
+        in_specs=[SMEM_WHOLE, VMEM_WHOLE, VMEM_WHOLE],
+        out_specs=[VMEM_WHOLE] * len(widths),
+        out_shape=[jax.ShapeDtypeStruct((depth * total, wide), dtype) for wide in widths],
+        compiler_params=BIG,
+        cost_estimate=pl.CostEstimate(flops=0, bytes_accessed=6 * depth * total * sum(widths), transcendentals=0),
+        name="join_rows",
+    )(place, near, far)
+
+
+def deal_kernel(place_ref, *refs, depth, total, size):
+    in_refs, (keep_ref, send_ref) = refs[:-2], refs[-2:]
+    low, zed = place_ref[0], place_ref[1]
+    for index in range(GROUP):
+        target = lax.bitwise_xor(low, jnp.int32(index))
+        out_ref = keep_ref if index % 2 == 0 else send_ref
+        for step in range(depth):
+            level = lax.bitwise_xor(zed, jnp.int32(step))
+            start = pl.multiple_of(level * total + slice_start(target, total, size), 16)
+            column = 0
+            for in_ref in in_refs:
+                wide = in_ref.shape[1]
+                out_ref[index // 2, step, :, column : column + wide] = in_ref[pl.ds(start, size), :]
+                column += wide
+
+
+def deal(place, parts, depth, total, size):
+    width = sum(part.shape[1] for part in parts)
+    shape = jax.ShapeDtypeStruct((4, depth, size, width), BFLOAT)
+    return pl.pallas_call(
+        functools.partial(deal_kernel, depth=depth, total=total, size=size),
+        in_specs=[SMEM_WHOLE] + [VMEM_WHOLE] * len(parts),
+        out_specs=[VMEM_WHOLE] * 2,
+        out_shape=[shape, shape],
+        compiler_params=BIG,
+        cost_estimate=pl.CostEstimate(flops=0, bytes_accessed=4 * depth * total * width, transcendentals=0),
+        name="deal_rows",
+    )(place, *parts)
+
+
+def misc_kernel(place_ref, misc_ref, near_ref, far_ref, gains_ref, table_ref, segs_ref, *, depth, shard, buckets, base):
+    low, zed = place_ref[0], place_ref[1]
+    for level in range(depth):
+        rows = misc_ref[lax.bitwise_xor(zed, jnp.int32(level))].astype(FLOAT)
+        gains_ref[:, level * shard : (level + 1) * shard] = rows[:8, :shard]
+        table_ref[level * buckets : (level + 1) * buckets, :] = rows[8 : 8 + buckets, :128]
+    seqs, _, rows = segs_ref.shape
+    for index in range(GROUP):
+        gap = lax.bitwise_xor(low, jnp.int32(index))
+        slot, odd = gap // 2, lax.rem(gap, 2)
+        own = jnp.where(odd == 0, near_ref[slot, base : base + 16, :128], far_ref[slot, base : base + 16, :128])
+        own = own.astype(FLOAT)
+        for seq in range(seqs):
+            segs_ref[seq, index : index + 1, :] = own[seq : seq + 1, :rows]
+
+
+def unpack_misc(place, misc, near, far, depth, shard, buckets, base, seqs, rows):
+    return pl.pallas_call(
+        functools.partial(misc_kernel, depth=depth, shard=shard, buckets=buckets, base=base),
+        in_specs=[SMEM_WHOLE, VMEM_WHOLE, VMEM_WHOLE, VMEM_WHOLE],
+        out_specs=[VMEM_WHOLE] * 3,
+        out_shape=[
+            jax.ShapeDtypeStruct((8, depth * shard), FLOAT),
+            jax.ShapeDtypeStruct((depth * buckets, 128), FLOAT),
+            jax.ShapeDtypeStruct((seqs, GROUP, rows), FLOAT),
+        ],
+        name="unpack_misc",
+    )(place, misc, near, far)
+
+
+def pick_block(refs, step, scratch_ref, cut):
+    for index in range(3):
+
+        @pl.when(step == index)
+        def _(index=index):
+            scratch_ref[...] = refs[index][...]
+
+    @pl.when(step == 3)
+    def _():
+        scratch_ref[:cut] = refs[3][...]
+        scratch_ref[cut:] = refs[4][...]
+
+
+def once(shape):
+    return pl.BlockSpec(shape, lambda g: (0,) * len(shape), pipeline_mode=pl.Buffered(1))
+
+
+def norm_kernel(x0, x1, x2, x3, x4, gain_ref, weight_ref, normed_ref, kv_ref, q_ref, x_scr, *, inner):
+    step = pl.program_id(0)
+    pick_block((x0, x1, x2, x3, x4), step, x_scr, x3.shape[0])
+    hidden = x_scr[...].astype(FLOAT)
+    scale = lax.rsqrt(jnp.mean(hidden * hidden, axis=-1, keepdims=True) + EPSILON)
+    normed = (hidden * scale * gain_ref[...]).astype(BFLOAT)
+    normed_ref[0] = normed
+    kv_ref[0] = jnp.dot(normed, weight_ref[:, inner:], preferred_element_type=FLOAT).astype(BFLOAT)
+
+    @pl.when(step == 0)
+    def _():
+        q_ref[...] = jnp.dot(normed, weight_ref[:, :inner], preferred_element_type=FLOAT).astype(BFLOAT)
+
+
+def norm_project(pieces, gain, weight, inner):
+    tokens, width = pieces[0].shape
+    return pl.pallas_call(
+        functools.partial(norm_kernel, inner=inner),
+        grid=(4,),
+        in_specs=[*[once(piece.shape) for piece in pieces], once(gain.shape), once(weight.shape)],
+        out_specs=[
+            pl.BlockSpec((1, tokens, width), lambda g: (g, 0, 0)),
+            pl.BlockSpec((1, tokens, 2 * inner), lambda g: (g, 0, 0)),
+            pl.BlockSpec((tokens, inner), lambda g: (0, 0)),
+        ],
+        out_shape=[
+            jax.ShapeDtypeStruct((4, tokens, width), BFLOAT),
+            jax.ShapeDtypeStruct((4, tokens, 2 * inner), BFLOAT),
+            jax.ShapeDtypeStruct((tokens, inner), BFLOAT),
+        ],
+        scratch_shapes=[pltpu.VMEM((tokens, width), BFLOAT)],
+        compiler_params=BIG,
+        cost_estimate=pl.CostEstimate(
+            flops=18 * tokens * width * inner, bytes_accessed=18 * tokens * width, transcendentals=0
+        ),
+        name="norm_project",
+    )(*pieces, gain, weight)
+
+
+GELU_SCALE = float(np.sqrt(2.0 / np.pi))
+
+
+def feed_kernel(
+    core_ref, a0, a1, a2, a3, a4, x0, x1, x2, x3, x4, c0, c1, c2, c3, c4, proj_ref, gain_ref, mine_ref, other_ref, down_ref,
+    after_ref, normed_ref, act_ref, dmine_ref, dother_ref, out_ref, late_ref, a_scr, x_scr, c_scr,
+):
+    step = pl.program_id(0)
+    cut = x3.shape[0]
+    pick_block((a0, a1, a2, a3, a4), step, a_scr, cut)
+    pick_block((x0, x1, x2, x3, x4), step, x_scr, cut)
+    pick_block((c0, c1, c2, c3, c4), step, c_scr, cut)
+    is_zero = core_ref[0] == 0
+    after = x_scr[...].astype(FLOAT) + jnp.dot(a_scr[...], proj_ref[...], preferred_element_type=FLOAT)
+
+    @pl.when(step == 0)
+    def _():
+        after_ref[...] = after
+
+    scale = lax.rsqrt(jnp.mean(after * after, axis=-1, keepdims=True) + EPSILON)
+    normed = (after * scale * gain_ref[...]).astype(BFLOAT)
+    normed_ref[0] = normed
+    pre_mine = jnp.dot(normed, mine_ref[...], preferred_element_type=FLOAT)
+    pre_other = jnp.dot(normed, other_ref[...], preferred_element_type=FLOAT)
+    gate = jnp.where(is_zero, pre_mine, pre_other)
+    up = jnp.where(is_zero, pre_other, pre_mine)
+    square = gate * gate
+    lifted = jnp.tanh(GELU_SCALE * (gate + 0.044715 * gate * square))
+    half = 0.5 * (1.0 + lifted)
+    smooth = gate * half
+    act = (smooth * up).astype(BFLOAT)
+    act_ref[0] = act
+    out_ref[0] = jnp.dot(act, down_ref[...], preferred_element_type=FLOAT).astype(BFLOAT)
+    act_back = nt(c_scr[...], down_ref[...])
+    slope = half + 0.5 * gate * (1.0 - lifted * lifted) * (GELU_SCALE * (1.0 + 3 * 0.044715 * square))
+    gate_back = act_back * up * slope
+    up_back = act_back * smooth
+    dmine = jnp.where(is_zero, gate_back, up_back).astype(BFLOAT)
+    dother = jnp.where(is_zero, up_back, gate_back).astype(BFLOAT)
+    dmine_ref[0] = dmine
+    dother_ref[0] = dother
+    late_ref[0] = (nt(dmine, mine_ref[...]) + nt(dother, other_ref[...])).astype(BFLOAT)
+
+
+def feed_forward(core, attn, inputs, cots, proj, gain, mine, other, down):
+    tokens, width = inputs[0].shape
+    inner, wide = attn[0].shape[1], mine.shape[1]
+
+    def block(size):
+        return pl.BlockSpec((1, tokens, size), lambda g: (g, 0, 0))
+
+    def shape(size):
+        return jax.ShapeDtypeStruct((4, tokens, size), BFLOAT)
+
+    return pl.pallas_call(
+        feed_kernel,
+        grid=(4,),
+        in_specs=[
+            SMEM_WHOLE,
+            *[once(piece.shape) for piece in (*attn, *inputs, *cots)],
+            *[once(value.shape) for value in (proj, gain, mine, other, down)],
+        ],
+        out_specs=[
+            pl.BlockSpec((tokens, width), lambda g: (0, 0)),
+            block(width), block(wide), block(wide), block(wide), block(width), block(width),
+        ],
+        out_shape=[
+            jax.ShapeDtypeStruct((tokens, width), FLOAT),
+            shape(width), shape(wide), shape(wide), shape(wide), shape(width), shape(width),
+        ],
+        scratch_shapes=[
+            pltpu.VMEM((tokens, inner), BFLOAT), pltpu.VMEM((tokens, width), BFLOAT), pltpu.VMEM((tokens, width), BFLOAT),
+        ],
+        compiler_params=BIG,
+        cost_estimate=pl.CostEstimate(
+            flops=8 * tokens * width * (6 * wide + inner), bytes_accessed=30 * tokens * width, transcendentals=4 * tokens * wide
+        ),
+        name="feed_forward",
+    )(core, *attn, *inputs, *cots, proj, gain, mine, other, down)
+
+
+def spread_kernel(place_ref, near_ref, far_ref, gate_ref, up_ref, gate_out, up_out, late_ref, *, depth, part):
+    low = place_ref[0]
+    chip, core = low // 2, lax.rem(low, 2)
+    for index in range(4):
+        slot = lax.bitwise_xor(chip, jnp.int32(index))
+        near, far = near_ref[slot].astype(FLOAT), far_ref[slot].astype(FLOAT)
+        gate = jnp.where(core == 0, near, far)
+        up = jnp.where(core == 0, far, near)
+        for level in range(depth):
+            base = (level * 4 + index) * part
+            gate_out[:, base : base + part] = gate[:, level * part : (level + 1) * part]
+            up_out[:, base : base + part] = up[:, level * part : (level + 1) * part]
+    total = gate_out[...] * gate_ref[...].astype(FLOAT) + up_out[...] * up_ref[...].astype(FLOAT)
+    late_ref[...] = jnp.broadcast_to(jnp.sum(total, axis=1, keepdims=True), late_ref.shape)
+
+
+def spread(place, near, far, gate, up, depth, part):
+    shard, hidden = gate.shape
+    tile = shard // 2 if shard % 32 == 0 else shard
+    tile = 184 if shard % 184 == 0 else shard
+    pieces = pl.BlockSpec((4, tile, near.shape[2]), lambda g: (0, g, 0))
+    rows = pl.BlockSpec((tile, hidden), lambda g: (g, 0))
+    return pl.pallas_call(
+        functools.partial(spread_kernel, depth=depth, part=part),
+        grid=(shard // tile,),
+        in_specs=[SMEM_WHOLE, pieces, pieces, rows, rows],
+        out_specs=[rows, rows, pl.BlockSpec((tile, 128), lambda g: (g, 0))],
+        out_shape=[
+            jax.ShapeDtypeStruct((shard, hidden), FLOAT),
+            jax.ShapeDtypeStruct((shard, hidden), FLOAT),
+            jax.ShapeDtypeStruct((shard, 128), FLOAT),
+        ],
+        compiler_params=BIG,
+        cost_estimate=pl.CostEstimate(flops=4 * shard * hidden, bytes_accessed=16 * shard * hidden, transcendentals=0),
+        name="spread_columns",
+    )(place, near, far, gate, up)
+
+
+def after(value, *others):
+    return lax.optimization_barrier((value, *others))[0]
 
 
 def on_device(
-    layer_input,
-    segments,
-    cotangent,
-    query_weight,
-    key_weight,
-    value_weight,
-    projection,
-    gate_weight,
-    up_weight,
-    down_weight,
-    gain_early,
-    gain_late,
-    bias_table,
+    layer_input, segments, cotangent, query_weight, key_weight, value_weight, projection, gate_weight, up_weight,
+    down_weight, gain_early, gain_late, bias_table,
 ):
     ring = lax.axis_size("ctx")
     depth = lax.axis_size("wsh")
@@ -374,25 +617,18 @@
     seqs, rows, width = layer_input.shape
     inner = query_weight.shape[1]
     heads = bias_table.shape[1]
-    hidden = gate_weight.shape[1]
     shard = width // depth
-    slab = hidden // depth
+    slab = gate_weight.shape[1] // depth
     part = slab // 4
     piece = part // 2
+    tokens = seqs * rows
+    cut = tokens // 2
+    buckets = BUCKETS // depth
     upper = [[group * GROUP + index for group in range(groups)] for index in range(GROUP)]
     is_zero = core == 0
-
-    qkv_shard = jnp.concatenate((query_weight, key_weight, value_weight), axis=1)
-    qkv_z = lax.all_gather(slice_rows(qkv_shard, low), "wsh", axis=0, tiled=True)
-    proj_z = lax.all_gather(slice_rows(projection, low), "wsh", axis=0, tiled=True)
-    qkv_full = join_rows(gather_eight(qkv_z, low), depth, shard)
-    proj_full = join_rows(gather_eight(proj_z, low), depth, inner // depth)
-    vectors = jnp.stack((gain_early, gain_late))
-    vectors = lax.all_gather(vectors, "wsh", axis=1, tiled=True).astype(FLOAT)
-    early_gain, late_gain = vectors[0], vectors[1]
-    table = lax.all_gather(bias_table, "wsh", axis=0, tiled=True).astype(FLOAT)
-    segs = lax.all_gather(segments, "ctx", axis=1, tiled=True).reshape(seqs, ring, rows).astype(FLOAT)
+    place = jnp.stack((low, zed)).astype(jnp.int32)
     meta = mine.astype(jnp.int32).reshape(1)
+    core_flag = core.astype(jnp.int32).reshape(1)
 
     def columns(weight):
         return jnp.concatenate(
@@ -400,102 +636,94 @@
         )
 
     pair_mine = lax.all_gather(jnp.where(is_zero, columns(gate_weight), columns(up_weight)), "wsh", axis=0, tiled=True)
-    pair_other = swap(pair_mine, 1)
     down_slice = lax.dynamic_slice_in_dim(down_weight, chip * part + core * piece, piece, 0)
     down_mine = lax.all_gather(down_slice, "wsh", axis=0, tiled=True).reshape(depth, piece, width)
+
+    own_x = layer_input.reshape(tokens, width)
+    own_cot = cotangent.reshape(tokens, width)
+    inputs = halves_four(own_x, cut)
+
+    size, proj_rows = slice_size(shard), inner // depth
+    proj_size = slice_size(proj_rows)
+    start = slice_start(low, shard, size)
+    qkv_slice = jnp.concatenate(
+        [lax.dynamic_slice_in_dim(weight, start, size, 0) for weight in (query_weight, key_weight, value_weight)], axis=1
+    )
+    proj_slice = lax.dynamic_slice_in_dim(projection, slice_start(low, proj_rows, proj_size), proj_size, 0)
+    vectors = jnp.pad(jnp.stack((gain_early, gain_late)), ((0, 6), (0, width - shard)))
+    table_rows = jnp.pad(bias_table, ((0, 8 - buckets), (0, width - heads)))
+    proj_slice = jnp.concatenate((proj_slice, vectors, table_rows), axis=0)
+    qkv_levels = [qkv_slice] + [swap_depth(qkv_slice, step) for step in range(1, depth)]
+    proj_levels = jnp.stack([proj_slice] + [swap_depth(proj_slice, step) for step in range(1, depth)])
+    seg_rows = jnp.pad(segments.astype(BFLOAT), ((0, 16 - seqs), (0, 3 * inner - rows)))
+    qkv_near = gather_four(jnp.concatenate((*qkv_levels, seg_rows), axis=0), (depth * size + 16) // 32 * 16)
+    qkv_far = swap(qkv_near, 1)
+    proj_near = gather_four(proj_levels[:, :proj_size].reshape(depth * proj_size, width), depth * proj_size // 2)
+    proj_far = swap(proj_near, 1)
+    qkv_full = join(place, qkv_near, qkv_far, depth, shard, size, (3 * inner,), BFLOAT)[0]
+    proj_full = join(place, proj_near, proj_far, depth, proj_rows, proj_size, (width,), BFLOAT)[0]
+    gains, table, segs = unpack_misc(
+        place, proj_levels[:, proj_size:], qkv_near, qkv_far, depth, shard, buckets, depth * size, seqs, rows
+    )
+
+    def whole(value, axis=0):
+        if groups == 1:
+            return value
+        return lax.all_gather(value, "ctx", axis=axis, tiled=True, axis_index_groups=upper)
+
+    segs = whole(segs, 1)
+
+    normed, kv_own, queries = norm_project(inputs, gains[0:1], qkv_full, inner)
+    kv_own = kv_own.reshape(4, seqs, rows, 2 * inner)
+    queries = queries.reshape(seqs, rows, inner)
+    kv_sib = swap(kv_own, 1)
+    kv_all, kv_sib_all = whole(kv_own), whole(kv_sib)
+    attention, lse = attention_forward(meta, table, segs, queries, kv_all, kv_sib_all)
+    attn_low = attention.astype(BFLOAT).reshape(tokens, inner)
+    attn = halves_four(attn_low, cut)
+    cots = halves_four(own_cot, cut)
+
+    pair_other = swap(pair_mine, 1)
     down_other = swap(down_mine, 1)
     down_full = jnp.where(
         is_zero, jnp.stack((down_mine, down_other), axis=1), jnp.stack((down_other, down_mine), axis=1)
     ).reshape(depth * part, width)
-
-    four_inputs = jnp.stack(gather_four(layer_input.reshape(seqs * rows, width)))
-    four_cots = jnp.stack(gather_four(cotangent.reshape(seqs * rows, width)))
-    hidden_in = layer_input.reshape(seqs * rows, width).astype(FLOAT)
-    four_normed = rms_rows(four_inputs.astype(FLOAT), early_gain).astype(BFLOAT).reshape(-1, width)
-    kv_own = jnp.dot(four_normed, qkv_full[:, inner:], preferred_element_type=FLOAT).astype(BFLOAT)
-    own_normed = four_normed[: seqs * rows]
-    queries = jnp.dot(own_normed, qkv_full[:, :inner], preferred_element_type=FLOAT).astype(BFLOAT)
-    queries = queries.reshape(seqs, rows, inner)
-    kv_own = kv_own.reshape(4, seqs, rows, 2 * inner)
-    kv_sib = swap(kv_own, 1)
-
-    def whole(value):
-        if groups == 1:
-            return value
-        return lax.all_gather(value, "ctx", axis=0, tiled=True, axis_index_groups=upper)
-
-    kv_all, kv_sib_all = whole(kv_own), whole(kv_sib)
-    attention, lse = attention_forward(meta, table, segs, queries, kv_all, kv_sib_all)
-    attn_low = attention.astype(BFLOAT).reshape(seqs * rows, inner)
-    four_attn = jnp.stack(gather_four(attn_low)).reshape(-1, inner)
-    four_after = four_inputs.reshape(-1, width).astype(FLOAT) + jnp.dot(
-        four_attn, proj_full, preferred_element_type=FLOAT
+    after_attn, normed_late, activation, back_mine, back_other, out_part, late_part = feed_forward(
+        core_flag, attn, inputs, cots, proj_full, gains[1:2], pair_mine, pair_other, down_full
     )
-    after_attn = four_after[: seqs * rows]
-    normed_late = rms_rows(four_after, late_gain).astype(BFLOAT)
-
-    pre_mine = jnp.dot(normed_late, pair_mine, preferred_element_type=FLOAT)
-    pre_other = jnp.dot(normed_late, pair_other, preferred_element_type=FLOAT)
-    gate_pre = jnp.where(is_zero, pre_mine, pre_other)
-    up_pre = jnp.where(is_zero, pre_other, pre_mine)
-
-    def gated(gate_values, up_values):
-        return jax.nn.gelu(gate_values, approximate=True) * up_values
-
-    activation = gated(gate_pre, up_pre).astype(BFLOAT)
-    cots = four_cots.reshape(-1, width)
-    act_grad = lax.dot_general(cots, down_full, (((1,), (1,)), ((), ())), preferred_element_type=FLOAT)
-    gate_back, up_back = jax.vjp(gated, gate_pre, up_pre)[1](act_grad)
-    back_mine = jnp.where(is_zero, gate_back, up_back).astype(BFLOAT)
-    back_other = jnp.where(is_zero, up_back, gate_back).astype(BFLOAT)
-    late_part = lax.dot_general(
-        back_mine, pair_mine, (((1,), (1,)), ((), ())), preferred_element_type=FLOAT
-    ) + lax.dot_general(back_other, pair_other, (((1,), (1,)), ((), ())), preferred_element_type=FLOAT)
-    late_part = late_part.astype(BFLOAT).reshape(4, seqs * rows, width)
-    late_back = scatter_four([late_part[index] for index in range(4)])
-    out_part = jnp.dot(activation, down_full, preferred_element_type=FLOAT).astype(BFLOAT)
-    out_part = out_part.reshape(4, seqs * rows, width)
-    result = (after_attn + scatter_four([out_part[index] for index in range(4)])).astype(BFLOAT)
-
-    down_grad = tn(activation, cots).astype(BFLOAT).reshape(depth, 2, piece, width)
-    mine_grad = tn(normed_late, back_mine).astype(BFLOAT)
-    other_grad = tn(normed_late, back_other).astype(BFLOAT)
-
-    def join(kept, sent):
-        return (kept.astype(FLOAT) + swap(sent, 1).astype(FLOAT)).astype(BFLOAT)
+    late_back = scatter_four(late_part, cut)
+    out_sum = scatter_four(out_part, cut)
+    result = (after_attn + out_sum).astype(BFLOAT)
+
+    def flat(value):
+        return value.reshape(4 * tokens, value.shape[2])
+
+    all_cots = jnp.concatenate(cots, axis=0)
+    down_grad = tn(flat(activation), all_cots).astype(BFLOAT).reshape(depth, 2, piece, width)
+    mine_grad = tn(flat(normed_late), flat(back_mine)).astype(BFLOAT)
+    other_grad = tn(flat(normed_late), flat(back_other)).astype(BFLOAT)
+
+    def add(kept, got):
+        return (kept.astype(FLOAT) + got.astype(FLOAT)).astype(BFLOAT)
+
+    def over_groups(value):
+        return lax.psum(value, "ctx", axis_index_groups=upper) if groups > 1 else value
 
     down_keep = jnp.where(is_zero, down_grad[:, 0], down_grad[:, 1]).reshape(depth * piece, width)
     down_send = jnp.where(is_zero, down_grad[:, 1], down_grad[:, 0]).reshape(depth * piece, width)
-    down_sum = join(down_keep, down_send)
-    pair_sum = join(mine_grad, other_grad)
-
-    def over_groups(value):
-        return lax.psum(value, "ctx", axis_index_groups=upper) if groups > 1 else value
-
+    down_sum = add(down_keep, swap(down_send, 1))
+    pair_sum = add(mine_grad, swap(other_grad, 1))
     down_own = over_groups(lax.psum_scatter(down_sum, "wsh", scatter_dimension=0, tiled=True))
     pair_own = over_groups(lax.psum_scatter(pair_sum, "wsh", scatter_dimension=0, tiled=True))
-    down_out = jnp.concatenate(gather_eight(down_own, low), axis=0).astype(FLOAT)
-    four_pair = gather_four(pair_own)
-    stacked_pair = jnp.stack(four_pair)
-    stacked_other = swap(stacked_pair, 1)
-
-    def spread(stack):
-        chips = [
-            lax.dynamic_index_in_dim(stack, lax.bitwise_xor(chip, jnp.int32(index)), 0, keepdims=False) for index in range(4)
-        ]
-        return jnp.concatenate(
-            [chips[index][:, level * part : (level + 1) * part] for level in range(depth) for index in range(4)], axis=1
-        )
-
-    gate_out = spread(jnp.where(is_zero, stacked_pair, stacked_other)).astype(FLOAT)
-    up_out = spread(jnp.where(is_zero, stacked_other, stacked_pair)).astype(FLOAT)
-
-    cot_own = cotangent.reshape(seqs * rows, width).astype(FLOAT)
-    residual_grad = cot_own + rms_back(after_attn, late_gain, late_back)
+    down_near = gather_four(down_own, piece // 32 * 16)
+    pair_near = gather_four(pair_own, shard // 32 * 16)
+    down_out = join(place, down_near, swap(down_near, 1), 1, slab, piece, (width,), FLOAT)[0]
+    gate_out, up_out, late_sum = spread(place, pair_near, swap(pair_near, 1), gate_weight, up_weight, depth, part)
+
+    residual_grad = own_cot.astype(FLOAT) + rms_back(after_attn, gains[1:2], late_back)
     mix_low = residual_grad.astype(BFLOAT)
     proj_grad = tn(attn_low, mix_low).astype(BFLOAT)
-    attn_grad = lax.dot_general(mix_low, proj_full, (((1,), (1,)), ((), ())), preferred_element_type=FLOAT)
-    attn_grad = attn_grad.astype(BFLOAT).reshape(seqs, rows, inner)
+    attn_grad = nt(mix_low, proj_full).astype(BFLOAT).reshape(seqs, rows, inner)
     dq, dk_own, dk_sib, dv_own, dv_sib, table_part = attention_backward(
         meta, table, segs, queries, kv_all, kv_sib_all, attn_grad, attention, lse
     )
@@ -505,35 +733,48 @@
             return value
         return lax.psum_scatter(value, "ctx", scatter_dimension=0, tiled=True, axis_index_groups=upper)
 
-    dkv_own = owned(jnp.concatenate((dk_own, dv_own), axis=-1))
-    dkv_sib = owned(jnp.concatenate((dk_sib, dv_sib), axis=-1))
-    dkv_four = (dkv_own.astype(FLOAT) + swap(dkv_sib, 1).astype(FLOAT)).astype(BFLOAT)
-    dkv_four = dkv_four.reshape(4, seqs * rows, 2 * inner)
-    dkv = scatter_four([dkv_four[index] for index in range(4)]).astype(BFLOAT)
-    dq = dq.reshape(seqs * rows, inner)
-    kv_grad = tn(four_normed, dkv_four.reshape(-1, 2 * inner)).astype(BFLOAT)
-    q_grad = tn(own_normed, dq).astype(BFLOAT)
+    def both(key_part, value_part):
+        return owned(jnp.concatenate((key_part, value_part), axis=-1)).reshape(4, tokens, 2 * inner)
+
+    dkv_four = add(both(dk_own, dv_own), swap(both(dk_sib, dv_sib), 1))
+    dkv = scatter_four(dkv_four, cut).astype(BFLOAT)
+    dq = dq.reshape(tokens, inner)
+    kv_grad = tn(flat(normed), flat(dkv_four)).astype(BFLOAT)
+    q_grad = tn(normed[0], dq).astype(BFLOAT)
     dqkv = jnp.concatenate((dq, dkv), axis=1)
-    early_back = lax.dot_general(dqkv, qkv_full, (((1,), (1,)), ((), ())), preferred_element_type=FLOAT)
-    input_grad = (residual_grad + rms_back(hidden_in, early_gain, early_back)).astype(BFLOAT)
-
-    qkv_grad = jnp.concatenate((q_grad, kv_grad), axis=1)
-    qkv_out = lax.psum(lax.psum_scatter(qkv_grad, "wsh", scatter_dimension=0, tiled=True), "ctx").astype(FLOAT)
-    proj_out = lax.psum(lax.psum_scatter(proj_grad, "wsh", scatter_dimension=0, tiled=True), "ctx").astype(FLOAT)
-    table_sum = jnp.sum(table_part, axis=-1).reshape(heads, BUCKETS)
-    table_sum = lax.psum(table_sum, ("ctx", "wsh"))
-    table_rows = BUCKETS // depth
-    table_out = jnp.transpose(lax.dynamic_slice_in_dim(table_sum, zed * table_rows, table_rows, 1))
-    early_out = jnp.sum(qkv_out * qkv_shard.astype(FLOAT), axis=1) / gain_early.astype(FLOAT)
-    late_out = (
-        jnp.sum(gate_out * gate_weight.astype(FLOAT), axis=1) + jnp.sum(up_out * up_weight.astype(FLOAT), axis=1)
-    ) / gain_late.astype(FLOAT)
+    early_back = nt(dqkv, qkv_full)
+    input_grad = (residual_grad + rms_back(own_x.astype(FLOAT), gains[0:1], early_back)).astype(BFLOAT)
+
+    def reduce_small(parts, total, rows_each, widths):
+        keep, send = deal(place, parts, depth, total, rows_each)
+        levels = scatter_four(add(keep, swap(send, 1)), depth // 2).astype(BFLOAT)
+        summed = levels[0].astype(FLOAT)
+        for step in range(1, depth):
+            summed = summed + swap_depth(levels[step], step).astype(FLOAT)
+        near = gather_four(over_groups(summed.astype(BFLOAT)), rows_each // 32 * 16 or rows_each // 2)
+        return join(place, near, swap(near, 1), 1, total, rows_each, widths, FLOAT)
+
+    proj_out = reduce_small((proj_grad,), proj_rows, proj_size, (width,))[0]
+    query_out, key_out, value_out = reduce_small((q_grad, kv_grad), shard, size, (inner,) * 3)
+    table_sum = jnp.pad(jnp.sum(table_part, axis=-1).reshape(heads, BUCKETS), ((0, 8 - heads), (0, 128 - BUCKETS)))
+    for bit in (1, 2, 4):
+        table_sum = table_sum + swap(table_sum, bit)
+    for bit in (1, 2):
+        table_sum = table_sum + swap_depth(table_sum, bit)
+    table_sum = over_groups(table_sum)
+    table_out = jnp.transpose(lax.dynamic_slice(table_sum, (0, zed * buckets), (heads, buckets)))
+    early_out = (
+        jnp.sum(query_out * query_weight.astype(FLOAT), axis=1)
+        + jnp.sum(key_out * key_weight.astype(FLOAT), axis=1)
+        + jnp.sum(value_out * value_weight.astype(FLOAT), axis=1)
+    ) / gain_early.astype(FLOAT)
+    late_out = late_sum[:, 0] / gain_late.astype(FLOAT)
     return (
         result.reshape(seqs, rows, width),
         input_grad.reshape(seqs, rows, width),
-        qkv_out[:, :inner],
-        qkv_out[:, inner : 2 * inner],
-        qkv_out[:, 2 * inner :],
+        query_out,
+        key_out,
+        value_out,
         proj_out,
         gate_out,
         up_out,

time: 686 us -> 591 us (0.86)
  blocking collectives: 106 us -> 0 us
  Pallas kernels: 35.1 us -> 126 us
  local copies, waits for them, and re-layouts: 150 us -> 88.9 us
  matrix products: 104 us -> 43 us
  starting transfers between devices: 46 us -> 103 us
  other arithmetic: 96.9 us -> 65.6 us
  waiting for transfers between devices: 125 us -> 144 us
    pallas_call x0 -> x11, Pallas kernels: none -> 90.9 us  [the longest x1 46.1 us: feed_forward(): pl.pallas_call(feed_kernel, grid=(4,), in_specs=[SMEM_WHOLE, *[once(piece...]
    all_gather x5 -> x0, blocking collectives: 68.6 us -> none  [the longest x1 20.5 us: on_device(): lax.all_gather(slice_rows(qkv_shard, low), 'wsh', axis=0, tiled=True)]
    dot_general x11 -> x2, matrix products: 67.9 us -> 4.6 us  [nt(): lax.dot_general(left, right, (((1,), (1,)), ((), ())), preferred_element_...]
    ppermute x50 -> x73, waiting for transfers between devices: 67.4 us -> 121 us  [swap(): lax.ppermute(value, 'ctx', [(source, source ^ bit) for source in range(co...]
    psum x1 -> x0, waiting for transfers between devices: 50.8 us -> none  [on_device(): lax.psum(lax.psum_scatter(qkv_grad, 'wsh', scatter_dimension=0, tiled=Tru...]
    ppermute x0 -> x14, starting transfers between devices: none -> 39 us  [swap_depth(): lax.ppermute(value, 'wsh', [(source, source ^ bit) for source in range(co...]
    psum x1 -> x0, blocking collectives: 37.8 us -> none  [on_device(): table_sum = lax.psum(table_sum, ('ctx', 'wsh'))]
    unnamed x201 -> x104, local copies, waits for them, and re-layouts: 58.1 us -> 29.7 us
  transfers between devices with their start and end apart: 57 -> 91, of which waited for: 16 -> 28; matrix products, arithmetic and copies ran while one was open for 39% -> 32% of each run, Pallas kernels for 5% -> 12%
where the time goes in v2:
time: 591 us; the launch traced here: 585 us
  waiting for transfers between devices  144 us (24%)
  Pallas kernels  126 us (21%)
  starting transfers between devices  103 us (17%)
  local copies, waits for them, and re-layouts  88.9 us (15%)
  other arithmetic  65.6 us (11%)
  matrix products  43 us (7%)
  between operations  14.9 us (3%)
    ppermute x73, waiting for transfers between devices, swap(): lax.ppermute(value, 'ctx', [(source, source ^ bit) for source in range(co...  121 us
    ppermute x73, starting transfers between devices, swap(): lax.ppermute(value, 'ctx', [(source, source ^ bit) for source in range(co...  63.9 us
    pallas_call x1, Pallas kernels, feed_forward(): pl.pallas_call(feed_kernel, grid=(4,), in_specs=[SMEM_WHOLE, *[once(piece...  46.1 us
    ppermute x14, starting transfers between devices, swap_depth(): lax.ppermute(value, 'wsh', [(source, source ^ bit) for source in range(co...  39 us
    dot_general x6, matrix products, tn(): lax.dot_general(left, right, (((0,), (0,)), ((), ())), preferred_element_...  38.4 us
    unnamed x104, local copies, waits for them, and re-layouts  29.7 us
    ppermute x14, waiting for transfers between devices, swap_depth(): lax.ppermute(value, 'wsh', [(source, source ^ bit) for source in range(co...  22.7 us
    pallas_call x1, Pallas kernels, attention_backward(): pl.pallas_call(functools.partial(backward_kernel, rows=rows, count=count,...  20.4 us
  transfers between devices with their start and end apart: 91, of which 28 were waited for; matrix products, arithmetic and copies ran while one was open for 32% of the time, Pallas kernels for 12%

profile of v2, /device:TPU:0, one launch (start us, length us, event | category | flops | bytes accessed | tf_op | source)
XLA Modules:
  0.0 585.1 jit_solution(8840864844569189499)
XLA Ops:
  7.3 2.5 constant_dynamic-slice_fusion.4
  13.0 3.1 collective-permute-start.3
  16.1 2.6 collective-permute-start.4
  19.1 13.1 %collective-permute-done.4 = bf16[48,1152]{1,0:T(8,128)(2,1)S(1)} collective-permute-done((bf16[48,1152]{1,0:T(8,128)(2,1)S(1)}, bf16[48,1152]{1,0:T(8,128)(2,1)S(1)}, u32[]{:S(2)}, u32[]{:S(2)}) %collective-permute-start.4) | collective-permute-done | bytes 110624 | tf_op jit(solution)/shard_map/ppermute | solution.py:295
  35.4 8.0 %collective-permute-done.7 = bf16[208,1152]{1,0:T(8,128)(2,1)S(1)} collective-permute-done((bf16[208,1152]{1,0:T(8,128)(2,1)S(1)}, bf16[208,1152]{1,0:T(8,128)(2,1)S(1)}, u32[]{:S(2)}, u32[]{:S(2)}) %collective-permute-start.7) | collective-permute-done | bytes 479264 | tf_op jit(solution)/shard_map/ppermute | solution.py:290
  46.7 4.4 collective-permute-done.8
  52.7 2.4 copy.92
  60.6 9.6 %collective-permute-start = (bf16[32,1472]{1,0:T(8,128)(2,1)S(1)}, bf16[32,1472]{1,0:T(8,128)(2,1)S(1)}, u32[]{:S(2)}, u32[]{:S(2)}) collective-permute-start(bf16[32,1472]{1,0:T(8,128)(2,1)S(1)} %get-tuple-element.179), channel_id=1, source_target_pairs={{0,1},{1,0},{2,3},{3,2},{4,5},{5,4},{6,7},{7,6},{8,9},{9,8},{10,11... | collective-permute-start | bytes 282632 | tf_op jit(solution)/shard_map/ppermute | solution.py:295
  73.6 3.1 collective-permute-start.2
  77.3 3.1 collective-permute-done.2
  80.4 4.7 collective-permute-done.11
  92.9 2.9 unpack_misc.1
  97.3 4.4 join_rows.5.weight_ref
  102.9 3.8 collective-permute-done.14.x4
  106.6 11.2 %norm_project.1 = (bf16[4,384,1472]{2,1,0:T(8,128)(2,1)}, bf16[4,384,768]{2,1,0:T(8,128)(2,1)}, bf16[384,384]{1,0:T(8,128)(2,1)}) custom-call(bf16[384,1472]{1,0:T(8,128)(2,1)} %bitcast.229, bf16[384,1472]{1,0:T(8,128)(2,1)} %copy-done.11, bf16[384,1472]{1,0:T(8,128)(2,1)} %copy-done.12, bf16[192,1472]{1,0:T(8,128)(2,1)} %collective-permute-done.13.x3, ...), custom_call_target="tpu_custom_call" | custom-call | flops 3906994176 | bytes 10174464 | tf_op jit(solution)/shard_map/norm_project/pallas_call | solution.py:460
  119.0 2.4 copy.99
  128.0 2.7 collective-permute-done.26
  130.7 22.1 %collective-permute-done.27 = bf16[32,1472]{1,0:T(8,128)(2,1)S(1)} collective-permute-done((bf16[32,1472]{1,0:T(8,128)(2,1)S(1)}, bf16[32,1472]{1,0:T(8,128)(2,1)S(1)}, u32[]{:S(2)}, u32[]{:S(2)}) %collective-permute-start.27) | collective-permute-done | bytes 94240 | tf_op jit(solution)/shard_map/ppermute | solution.py:290
  155.9 2.4 constant_dynamic-update-slice_fusion.8
  158.3 2.4 copy.108.c1
  164.1 2.4 copy.109.c2
  169.9 2.4 constant_dynamic-update-slice_fusion.7
  172.4 2.6 join_rows.6.proj_ref
  177.4 14.6 %attention_forward.1 = (f32[3,128,384]{2,1,0:T(8,128)}, f32[3,3,8,128]{3,2,1,0:T(8,128)}) custom-call(s32[1]{0:T(128)} %bitcast.1.meta_ref, f32[32,128]{1,0:T(8,128)} %get-tuple-element.43.table_ref, f32[3,8,128]{2,1,0:T(8,128)} %get-tuple-element.44.segs_ref, bf16[3,128,384]{2,1,0:T(8,128)(2,1)} %bitcast.243, bf16[4,3,128,768]{3,2,1,0:T(8,128)(2,1)} %bitcast.220, ...), custom_call_target="tpu_custom_call" | custom-call | flops 603979776 | bytes 9437184 | tf_op jit(solution)/shard_map/attention_forward/pallas_call | solution.py:249
  198.1 3.5 collective-permute-done.16.a1
  208.3 46.1 %feed_forward.1 = (f32[384,1472]{1,0:T(8,128)}, bf16[4,384,1472]{2,1,0:T(8,128)(2,1)}, bf16[4,384,896]{2,1,0:T(8,128)(2,1)}, bf16[4,384,896]{2,1,0:T(8,128)(2,1)...) custom-call(s32[1]{0:T(128)} %bitcast.core_ref, ...), custom_call_target="tpu_custom_call" | custom-call | flops 26046627840 | bytes 16957440 | tf_op jit(solution)/shard_map/feed_forward/pallas_call | solution.py:537
  254.5 3.0 slice_bitcast_fusion.8
  263.0 7.5 %convolution_convert_fusion = bf16[896,1472]{0,1:T(8,128)(2,1)S(1)} fusion(bf16[1536,896]{1,0:T(8,128)(2,1)S(1)} %bitcast.266, bf16[1536,1472]{1,0:T(8,128)(2,1)} %constant_dynamic-update-slice_fusion.4), kind=kOutput, calls=%fused_computation.6 | convolution fusion | flops 4053016576 | bytes 9912320 | tf_op jit(solution)/shard_map/dot_general | solution.py:54
  270.5 3.3 copy.125
  273.8 3.7 broadcast_select_fusion.1
  277.4 8.7 %bitcast_convert_fusion = bf16[1472,896]{1,0:T(8,128)(2,1)} fusion(bf16[4,384,1472]{2,1,0:T(8,128)(2,1)} %get-tuple-element.66, bf16[4,384,896]{2,1,0:T(8,128)(2,1)S(1)} %copy-done.44), kind=kOutput, calls=%fused_computation | convolution fusion | flops 4053016576 | bytes 9912320 | tf_op jit(solution)/shard_map/dot_general | solution.py:54
  286.1 2.8 fusion.17
  291.4 2.7 fusion.15
  302.8 9.6 %bitcast_convert_fusion.1 = bf16[1472,896]{1,0:T(8,128)(2,1)} fusion(bf16[4,384,1472]{2,1,0:T(8,128)(2,1)} %get-tuple-element.66, bf16[4,384,896]{2,1,0:T(8,128)(2,1)} %get-tuple-element.67), kind=kOutput, calls=%fused_computation.1 | convolution fusion | flops 4053016576 | bytes 9912320 | tf_op jit(solution)/shard_map/dot_general | solution.py:54
  312.4 30.0 %collective-permute-done.36 = bf16[384,1472]{0,1:T(8,128)(2,1)} collective-permute-done((bf16[384,1472]{0,1:T(8,128)(2,1)}, bf16[384,1472]{0,1:T(8,128)(2,1)}, u32[]{:S(2)}, u32[]{:S(2)}) %collective-permute-start.36) | collective-permute-done | bytes 1130528 | tf_op jit(solution)/shard_map/ppermute | solution.py:290
  345.9 3.3 multiply_reduce_fusion.1
  349.3 2.5 copy.111
  351.7 2.5 copy.113
  354.2 6.0 %subtract_add_fusion = (f32[384,1472]{1,0:T(8,128)S(1)}, bf16[384,1472]{1,0:T(8,128)(2,1)}) fusion(f32[384,1472]{1,0:T(8,128)} %get-tuple-element.49, bf16[384,1472]{1,0:T(8,128)(2,1)} %copy-done.5, bf16[384,1472]{1,0:T(8,128)(2,1)} %copy-done.4, f32[384]{0:T(512)S(1)} %broadcast_multiply_fusion.1, f32[384]{0:T(512)S(1)} %get-tuple-element.183, ...), kind=kLoop, calls=%fused_computation.31 | loop fusion | flops 10739712 | bytes 13576448 | tf_op jit(solution)/shard_map/add | solution.py:723
  362.2 2.4 copy.120.refs_0_
  364.5 2.5 deal_rows.3
  367.6 3.2 fusion.1
  370.8 2.8 convolution_convert_fusion.3
  373.6 20.4 %attention_backward.1 = (bf16[3,128,384]{2,1,0:T(8,128)(2,1)}, bf16[4,3,128,384]{3,2,1,0:T(8,128)(2,1)}, bf16[4,3,128,384]{3,2,1,0:T(8,128)(2,1)}, bf16[4,3,128,...) custom-call(s32[1]{0:T(128)} %bitcast.1.meta_ref, ...), custom_call_target="tpu_custom_call" | custom-call | flops 1509949440 | bytes 23592960 | tf_op jit(solution)/shard_map/attention_backward/pallas_call | solution.py:270
  395.1 3.3 pad_maximum_fusion.2
  407.1 3.2 convolution_convert_fusion.2.refs_0_
  412.4 9.5 %collective-permute-start.62 = (bf16[16,1472]{1,0:T(8,128)(2,1)S(1)}, bf16[16,1472]{1,0:T(8,128)(2,1)S(1)}, u32[]{:S(2)}, u32[]{:S(2)}) collective-permute-start(bf16[16,1472]{1,0:T(8,128)(2,1)S(1)} %get-tuple-element.173), channel_id=1, source_target_pairs={{0,1},{1,0},{2,3},{3,2},{4,5},{5,4},{6,7},{7,6},{8,9},{9,8},{10,11... | collective-permute-start | bytes 141320 | tf_op jit(solution)/shard_map/ppermute | solution.py:295
  431.6 4.0 add_convert_fusion
  438.1 3.2 fusion
  442.8 7.5 %bitcast_convert_fusion.2.refs_1_ = bf16[1472,768]{1,0:T(8,128)(2,1)} fusion(bf16[4,384,1472]{2,1,0:T(8,128)(2,1)} %get-tuple-element.58, bf16[4,384,768]{2,1,0:T(8,128)(2,1)S(1)} %fusion), kind=kOutput, calls=%fused_computation.5 | convolution fusion | flops 3474014208 | bytes 9142272 | tf_op jit(solution)/shard_map/dot_general | solution.py:54
  450.2 4.1 deal_rows.2
  461.2 2.5 copy.126
  481.6 12.8 %collective-permute-done.45 = bf16[2,48,1152]{2,1,0:T(8,128)(2,1)S(1)} collective-permute-done((bf16[2,48,1152]{2,1,0:T(8,128)(2,1)S(1)}, bf16[2,48,1152]{2,1,0:T(8,128)(2,1)S(1)}, u32[]{:S(2)}, u32[]{:S(2)}) %collective-permute-start.45) | collective-permute-done | bytes 221216 | tf_op jit(solution)/shard_map/ppermute | solution.py:290
  498.2 2.4 pad_maximum_fusion.4.near_ref
  504.4 2.5 collective-permute-done.46
  506.8 3.8 collective-permute-done.48
  512.1 9.4 %collective-permute-done.72 = bf16[368,896]{1,0:T(8,128)(2,1)S(1)} collective-permute-done((bf16[368,896]{1,0:T(8,128)(2,1)}, bf16[368,896]{1,0:T(8,128)(2,1)S(1)}, u32[]{:S(2)}, u32[]{:S(2)}) %collective-permute-start.72) | collective-permute-done | bytes 659488 | tf_op jit(solution)/shard_map/ppermute | solution.py:290
  526.5 3.1 collective-permute-done.73
  533.4 2.7 collective-permute-done.51
  543.7 2.6 collective-permute-done.54
  550.5 4.5 join_rows.9
  555.0 6.1 %copy.128 = f32[896,1472]{0,1:T(8,128)} copy(f32[896,1472]{1,0:T(8,128)} %join_rows.9) | data formatting | bytes 10551296
  561.8 2.4 join_rows.7
  568.5 8.2 %spread_columns.1 = (f32[368,3584]{1,0:T(8,128)}, f32[368,3584]{1,0:T(8,128)}, f32[368,128]{1,0:T(8,128)}) custom-call(s32[2]{0:T(128)} %pad_add_fusion.place_ref, bf16[4,368,896]{2,1,0:T(8,128)(2,1)} %pad_maximum_fusion.near_ref, bf16[4,368,896]{2,1,0:T(8,128)(2,1)} %collective-permute-done.75.far_ref, bf16[368,3584]{1,0:T(8,128)(2,1)} %gate_ref.1, ...), custom_call_target="tpu_custom_call" | custom-call | flops 5275648 | bytes 21102592 | tf_op jit(solution)/shard_map/spread_columns/pallas_call | solution.py:586
  (373 shorter events, 173.2 us)
Async XLA Ops:
  7.2 123.5 %all-gather.3.cloned.1.call-start = ((), (), s32[]{:S(2)}) async-start(), calls=%async_computation.2 | async-start | bytes 3297280 | tf_op jit(solution)/shard_map/all_gather | solution.py:638
  11.2 144.1 %all-gather.5.cloned.1.call-start = ((), (), s32[]{:S(2)}) async-start(), calls=%async_computation.3 | async-start | bytes 1720320 | tf_op jit(solution)/shard_map/all_gather | solution.py:640
  16.1 16.2 %collective-permute-start.4 = (bf16[48,1152]{1,0:T(8,128)(2,1)S(1)}, bf16[48,1152]{1,0:T(8,128)(2,1)S(1)}, u32[]{:S(2)}, u32[]{:S(2)}) collective-permute-start(bf16[48,1152]{1,0:T(8,128)(2,1)S(1)} %get-tuple-element.176), channel_id=1, source_target_pairs={{0,2},{1,3},{2,0},{3,1},{4,6},{5,7},{6,4},{7,5},{8,10},{9,11},{10,... | collective-permute-start | bytes 331784 | tf_op jit(solution)/shard_map/ppermute | solution.py:295
  18.6 13.6 %collective-permute-start.5 = (bf16[48,1152]{1,0:T(8,128)(2,1)S(1)}, bf16[48,1152]{1,0:T(8,128)(2,1)S(1)}, u32[]{:S(2)}, u32[]{:S(2)}) collective-permute-start(bf16[48,1152]{1,0:T(8,128)(2,1)S(1)} %get-tuple-element.176), channel_id=1, source_target_pairs={{0,3},{1,2},{2,1},{3,0},{4,7},{5,6},{6,5},{7,4},{8,11},{9,10},{10,... | collective-permute-start | bytes 331784 | tf_op jit(solution)/shard_map/ppermute | solution.py:295
  32.3 11.1 %collective-permute-start.7 = (bf16[208,1152]{1,0:T(8,128)(2,1)S(1)}, bf16[208,1152]{1,0:T(8,128)(2,1)S(1)}, u32[]{:S(2)}, u32[]{:S(2)}) collective-permute-start(bf16[208,1152]{1,0:T(8,128)(2,1)S(1)} %pad_dynamic-update-slice_fusion), channel_id=1, source_target_pairs={{0,16},{4,20},{8,24},{12,28},{16,0},{20,4},{24,8},{28,12},{1,17},{... | collective-permute-start | bytes 1437704 | tf_op jit(solution)/shard_map/ppermute | solution.py:290
  33.9 11.1 %collective-permute-start.6 = (bf16[208,1152]{1,0:T(8,128)(2,1)S(1)}, bf16[208,1152]{1,0:T(8,128)(2,1)S(1)}, u32[]{:S(2)}, u32[]{:S(2)}) collective-permute-start(bf16[208,1152]{1,0:T(8,128)(2,1)S(1)} %pad_dynamic-update-slice_fusion), channel_id=1, source_target_pairs={{0,8},{4,12},{8,0},{12,4},{16,24},{20,28},{24,16},{28,20},{1,9},{5... | collective-permute-start | bytes 1437704 | tf_op jit(solution)/shard_map/ppermute | solution.py:290
  52.7 40.2 %collective-permute-start.10 = (bf16[4,208,1152]{2,1,0:T(8,128)(2,1)}, bf16[4,208,1152]{2,1,0:T(8,128)(2,1)}, u32[]{:S(2)}, u32[]{:S(2)}) collective-permute-start(bf16[4,208,1152]{2,1,0:T(8,128)(2,1)} %pad_maximum_fusion.3.near_ref), channel_id=1, source_target_pairs={{0,4},{4,0},{8,12},{12,8},{16,20},{20,16},{24,28},{28,24},{1,5},{5... | collective-permute-start | bytes 5750792 | tf_op jit(solution)/shard_map/ppermute | solution.py:290
  57.5 27.6 %collective-permute-start.11 = (bf16[384,1472]{0,1:T(8,128)(2,1)}, bf16[384,1472]{0,1:T(8,128)(2,1)}, u32[]{:S(2)}, u32[]{:S(2)}) collective-permute-start(bf16[384,1472]{0,1:T(8,128)(2,1)} %copy.93), channel_id=1, source_target_pairs={{0,8},{4,12},{8,0},{12,4},{16,24},{20,28},{24,16},{28,20},{1,9},{5... | collective-permute-start | bytes 3391496 | tf_op jit(solution)/shard_map/ppermute | solution.py:290
  58.0 31.1 %collective-permute-start.12 = (bf16[384,1472]{0,1:T(8,128)(2,1)}, bf16[384,1472]{0,1:T(8,128)(2,1)}, u32[]{:S(2)}, u32[]{:S(2)}) collective-permute-start(bf16[384,1472]{0,1:T(8,128)(2,1)} %copy.93), channel_id=1, source_target_pairs={{0,16},{4,20},{8,24},{12,28},{16,0},{20,4},{24,8},{28,12},{1,17},{... | collective-permute-start | bytes 3391496 | tf_op jit(solution)/shard_map/ppermute | solution.py:290
  60.6 13.0 %collective-permute-start = (bf16[32,1472]{1,0:T(8,128)(2,1)S(1)}, bf16[32,1472]{1,0:T(8,128)(2,1)S(1)}, u32[]{:S(2)}, u32[]{:S(2)}) collective-permute-start(bf16[32,1472]{1,0:T(8,128)(2,1)S(1)} %get-tuple-element.179), channel_id=1, source_target_pairs={{0,1},{1,0},{2,3},{3,2},{4,5},{5,4},{6,7},{7,6},{8,9},{9,8},{10,11... | collective-permute-start | bytes 282632 | tf_op jit(solution)/shard_map/ppermute | solution.py:295
  73.2 381.9 %reduce-scatter.5.cloned.1.call-start = ((), (), s32[]{:S(2)}) async-start(), calls=%async_computation.5 | async-start | bytes 1720320 | tf_op jit(solution)/shard_map/reduce_scatter | solution.py:716
  87.6 15.2 %collective-permute-start.13 = (bf16[192,1472]{1,0:T(8,128)(2,1)}, bf16[192,1472]{1,0:T(8,128)(2,1)}, u32[]{:S(2)}, u32[]{:S(2)}) collective-permute-start(bf16[192,1472]{1,0:T(8,128)(2,1)} %slice.418), channel_id=1, source_target_pairs={{0,16},{4,20},{8,24},{12,28},{16,0},{20,4},{24,8},{28,12},{1,17},{... | collective-permute-start | bytes 1695752 | tf_op jit(solution)/shard_map/ppermute | solution.py:290
  91.7 15.0 %collective-permute-start.14 = (bf16[192,1472]{1,0:T(8,128)(2,1)}, bf16[192,1472]{1,0:T(8,128)(2,1)}, u32[]{:S(2)}, u32[]{:S(2)}) collective-permute-start(bf16[192,1472]{1,0:T(8,128)(2,1)} %slice.419), channel_id=1, source_target_pairs={{0,8},{4,12},{8,0},{12,4},{16,24},{20,28},{24,16},{28,20},{1,9},{5... | collective-permute-start | bytes 1695752 | tf_op jit(solution)/shard_map/ppermute | solution.py:290
  117.8 58.2 %collective-permute-start.15 = (bf16[4,3,128,768]{3,2,1,0:T(8,128)(2,1)}, bf16[4,3,128,768]{3,2,1,0:T(8,128)(2,1)S(1)}, u32[]{:S(2)}, u32[]{:S(2)}) collective-permute-start(bf16[4,3,128,768]{3,2,1,0:T(8,128)(2,1)} %bitcast.219), channel_id=1, source_target_pairs={{0,4},{4,0},{8,12},{12,8},{16,20},{20,16},{24,28},{28,24},{1,5},{5... | collective-permute-start | bytes 7077896 | tf_op jit(solution)/shard_map/ppermute | solution.py:290
  123.8 31.5 %collective-permute-start.20 = (bf16[384,1472]{0,1:T(8,128)(2,1)}, bf16[384,1472]{0,1:T(8,128)(2,1)}, u32[]{:S(2)}, u32[]{:S(2)}) collective-permute-start(bf16[384,1472]{0,1:T(8,128)(2,1)} %copy.100), channel_id=1, source_target_pairs={{0,8},{4,12},{8,0},{12,4},{16,24},{20,28},{24,16},{28,20},{1,9},{5... | collective-permute-start | bytes 3391496 | tf_op jit(solution)/shard_map/ppermute | solution.py:290
  126.9 25.9 %collective-permute-start.27 = (bf16[32,1472]{1,0:T(8,128)(2,1)S(1)}, bf16[32,1472]{1,0:T(8,128)(2,1)S(1)}, u32[]{:S(2)}, u32[]{:S(2)}) collective-permute-start(bf16[32,1472]{1,0:T(8,128)(2,1)S(1)} %slice.426), channel_id=1, source_target_pairs={{0,8},{4,12},{8,0},{12,4},{16,24},{20,28},{24,16},{28,20},{1,9},{5... | collective-permute-start | bytes 282632 | tf_op jit(solution)/shard_map/ppermute | solution.py:290
  127.5 35.1 %collective-permute-start.21 = (bf16[384,1472]{0,1:T(8,128)(2,1)}, bf16[384,1472]{0,1:T(8,128)(2,1)}, u32[]{:S(2)}, u32[]{:S(2)}) collective-permute-start(bf16[384,1472]{0,1:T(8,128)(2,1)} %copy.100), channel_id=1, source_target_pairs={{0,16},{4,20},{8,24},{12,28},{16,0},{20,4},{24,8},{28,12},{1,17},{... | collective-permute-start | bytes 3391496 | tf_op jit(solution)/shard_map/ppermute | solution.py:290
  130.7 77.0 %collective-permute-start.29 = (bf16[1472,896]{1,0:T(8,128)(2,1)}, bf16[1472,896]{1,0:T(8,128)(2,1)}, u32[]{:S(2)}, u32[]{:S(2)}) collective-permute-start(bf16[1472,896]{1,0:T(8,128)(2,1)} %all-gather.3.cloned.1.call-done.mine_ref), channel_id=1, source_target_pairs={{0,4},{4,0},{8,12},{12,8},{16,20},{20,16},{24,28},{28,24},{1,5},{5... | collective-permute-start | bytes 7913480 | tf_op jit(solution)/shard_map/ppermute | solution.py:290
  153.8 14.7 %collective-permute-start.28 = (bf16[4,64,1472]{2,1,0:T(8,128)(2,1)}, bf16[4,64,1472]{2,1,0:T(8,128)(2,1)}, u32[]{:S(2)}, u32[]{:S(2)}) collective-permute-start(bf16[4,64,1472]{2,1,0:T(8,128)(2,1)} %pad_maximum_fusion.9.near_ref), channel_id=1, source_target_pairs={{0,4},{4,0},{8,12},{12,8},{16,20},{20,16},{24,28},{28,24},{1,5},{5... | collective-permute-start | bytes 2261000 | tf_op jit(solution)/shard_map/ppermute | solution.py:290
  155.3 48.1 %collective-permute-start.30 = (bf16[4,112,1472]{2,1,0:T(8,128)(2,1)}, bf16[4,112,1472]{2,1,0:T(8,128)(2,1)}, u32[]{:S(2)}, u32[]{:S(2)}) collective-permute-start(bf16[4,112,1472]{2,1,0:T(8,128)(2,1)} %bitcast.236), channel_id=1, source_target_pairs={{0,4},{4,0},{8,12},{12,8},{16,20},{20,16},{24,28},{28,24},{1,5},{5... | collective-permute-start | bytes 3956744 | tf_op jit(solution)/shard_map/ppermute | solution.py:290
  162.6 31.2 %collective-permute-start.22 = (bf16[192,1472]{1,0:T(8,128)(2,1)}, bf16[192,1472]{1,0:T(8,128)(2,1)}, u32[]{:S(2)}, u32[]{:S(2)}) collective-permute-start(bf16[192,1472]{1,0:T(8,128)(2,1)} %slice.422), channel_id=1, source_target_pairs={{0,16},{4,20},{8,24},{12,28},{16,0},{20,4},{24,8},{28,12},{1,17},{... | collective-permute-start | bytes 1695752 | tf_op jit(solution)/shard_map/ppermute | solution.py:290
  168.4 27.8 %collective-permute-start.23 = (bf16[192,1472]{1,0:T(8,128)(2,1)}, bf16[192,1472]{1,0:T(8,128)(2,1)}, u32[]{:S(2)}, u32[]{:S(2)}) collective-permute-start(bf16[192,1472]{1,0:T(8,128)(2,1)} %slice.423), channel_id=1, source_target_pairs={{0,8},{4,12},{8,0},{12,4},{16,24},{20,28},{24,16},{28,20},{1,9},{5... | collective-permute-start | bytes 1695752 | tf_op jit(solution)/shard_map/ppermute | solution.py:290
  193.2 8.4 %collective-permute-start.16 = (bf16[384,384]{1,0:T(8,128)(2,1)S(1)}, bf16[384,384]{1,0:T(8,128)(2,1)S(1)}, u32[]{:S(2)}, u32[]{:S(2)}) collective-permute-start(bf16[384,384]{1,0:T(8,128)(2,1)S(1)} %bitcast.239), channel_id=1, source_target_pairs={{0,8},{4,12},{8,0},{12,4},{16,24},{20,28},{24,16},{28,20},{1,9},{5... | collective-permute-start | bytes 884744 | tf_op jit(solution)/shard_map/ppermute | solution.py:290
  193.8 8.4 %collective-permute-start.17 = (bf16[384,384]{1,0:T(8,128)(2,1)S(1)}, bf16[384,384]{1,0:T(8,128)(2,1)S(1)}, u32[]{:S(2)}, u32[]{:S(2)}) collective-permute-start(bf16[384,384]{1,0:T(8,128)(2,1)S(1)} %bitcast.240), channel_id=1, source_target_pairs={{0,16},{4,20},{8,24},{12,28},{16,0},{20,4},{24,8},{28,12},{1,17},{... | collective-permute-start | bytes 884744 | tf_op jit(solution)/shard_map/ppermute | solution.py:290
  257.5 28.6 %collective-permute-start.31 = (bf16[192,1472]{1,0:T(8,128)(2,1)}, bf16[192,1472]{1,0:T(8,128)(2,1)}, u32[]{:S(2)}, u32[]{:S(2)}) collective-permute-start(bf16[192,1472]{1,0:T(8,128)(2,1)} %get-tuple-element.134), channel_id=1, source_target_pairs={{0,16},{4,20},{8,24},{12,28},{16,0},{20,4},{24,8},{28,12},{1,17},{... | collective-permute-start | bytes 1695752 | tf_op jit(solution)/shard_map/ppermute | solution.py:290
  258.8 27.3 %collective-permute-start.33 = (bf16[192,1472]{1,0:T(8,128)(2,1)}, bf16[192,1472]{1,0:T(8,128)(2,1)}, u32[]{:S(2)}, u32[]{:S(2)}) collective-permute-start(bf16[192,1472]{1,0:T(8,128)(2,1)} %get-tuple-element.135), channel_id=1, source_target_pairs={{0,8},{4,12},{8,0},{12,4},{16,24},{20,28},{24,16},{28,20},{1,9},{5... | collective-permute-start | bytes 1695752 | tf_op jit(solution)/shard_map/ppermute | solution.py:290
  261.3 30.1 %collective-permute-start.35 = (bf16[192,1472]{1,0:T(8,128)(2,1)}, bf16[192,1472]{1,0:T(8,128)(2,1)}, u32[]{:S(2)}, u32[]{:S(2)}) collective-permute-start(bf16[192,1472]{1,0:T(8,128)(2,1)} %get-tuple-element.128), channel_id=1, source_target_pairs={{0,16},{4,20},{8,24},{12,28},{16,0},{20,4},{24,8},{28,12},{1,17},{... | collective-permute-start | bytes 1695752 | tf_op jit(solution)/shard_map/ppermute | solution.py:290
  261.9 29.5 %collective-permute-start.37 = (bf16[192,1472]{1,0:T(8,128)(2,1)}, bf16[192,1472]{1,0:T(8,128)(2,1)}, u32[]{:S(2)}, u32[]{:S(2)}) collective-permute-start(bf16[192,1472]{1,0:T(8,128)(2,1)} %get-tuple-element.129), channel_id=1, source_target_pairs={{0,8},{4,12},{8,0},{12,4},{16,24},{20,28},{24,16},{28,20},{1,9},{5... | collective-permute-start | bytes 1695752 | tf_op jit(solution)/shard_map/ppermute | solution.py:290
  277.4 90.1 %collective-permute-start.76 = (bf16[448,1472]{1,0:T(8,128)(2,1)}, bf16[448,1472]{1,0:T(8,128)(2,1)}, u32[]{:S(2)}, u32[]{:S(2)}) collective-permute-start(bf16[448,1472]{1,0:T(8,128)(2,1)} %bitcast.95), channel_id=1, source_target_pairs={{0,4},{4,0},{8,12},{12,8},{16,20},{20,16},{24,28},{28,24},{1,5},{5... | collective-permute-start | bytes 3956744 | tf_op jit(solution)/shard_map/ppermute | solution.py:290
  290.5 58.8 %collective-permute-start.32 = (bf16[384,1472]{0,1:T(8,128)(2,1)}, bf16[384,1472]{0,1:T(8,128)(2,1)}, u32[]{:S(2)}, u32[]{:S(2)}) collective-permute-start(bf16[384,1472]{0,1:T(8,128)(2,1)} %copy.110), channel_id=1, source_target_pairs={{0,8},{4,12},{8,0},{12,4},{16,24},{20,28},{24,16},{28,20},{1,9},{5... | collective-permute-start | bytes 3391496 | tf_op jit(solution)/shard_map/ppermute | solution.py:290
  295.6 46.7 %collective-permute-start.36 = (bf16[384,1472]{0,1:T(8,128)(2,1)}, bf16[384,1472]{0,1:T(8,128)(2,1)}, u32[]{:S(2)}, u32[]{:S(2)}) collective-permute-start(bf16[384,1472]{0,1:T(8,128)(2,1)} %copy.114), channel_id=1, source_target_pairs={{0,8},{4,12},{8,0},{12,4},{16,24},{20,28},{24,16},{28,20},{1,9},{5... | collective-permute-start | bytes 3391496 | tf_op jit(solution)/shard_map/ppermute | solution.py:290
  299.3 44.7 %collective-permute-start.38 = (bf16[384,1472]{0,1:T(8,128)(2,1)}, bf16[384,1472]{0,1:T(8,128)(2,1)}, u32[]{:S(2)}, u32[]{:S(2)}) collective-permute-start(bf16[384,1472]{0,1:T(8,128)(2,1)} %copy.116), channel_id=1, source_target_pairs={{0,16},{4,20},{8,24},{12,28},{16,0},{20,4},{24,8},{28,12},{1,17},{... | collective-permute-start | bytes 3391496 | tf_op jit(solution)/shard_map/ppermute | solution.py:290
  302.1 49.7 %collective-permute-start.34 = (bf16[384,1472]{0,1:T(8,128)(2,1)}, bf16[384,1472]{0,1:T(8,128)(2,1)}, u32[]{:S(2)}, u32[]{:S(2)}) collective-permute-start(bf16[384,1472]{0,1:T(8,128)(2,1)} %copy.112), channel_id=1, source_target_pairs={{0,16},{4,20},{8,24},{12,28},{16,0},{20,4},{24,8},{28,12},{1,17},{... | collective-permute-start | bytes 3391496 | tf_op jit(solution)/shard_map/ppermute | solution.py:290
  342.3 89.3 %collective-permute-start.70 = (bf16[1472,896]{1,0:T(8,128)(2,1)}, bf16[1472,896]{1,0:T(8,128)(2,1)}, u32[]{:S(2)}, u32[]{:S(2)}) collective-permute-start(bf16[1472,896]{1,0:T(8,128)(2,1)} %bitcast_convert_fusion), channel_id=1, source_target_pairs={{0,4},{4,0},{8,12},{12,8},{16,20},{20,16},{24,28},{28,24},{1,5},{5... | collective-permute-start | bytes 7913480 | tf_op jit(solution)/shard_map/ppermute | solution.py:290
  367.1 31.9 %collective-permute-start.57 = (bf16[4,4,16,1472]{3,2,1,0:T(8,128)(2,1)}, bf16[4,4,16,1472]{3,2,1,0:T(8,128)(2,1)S(1)}, u32[]{:S(2)}, u32[]{:S(2)}) collective-permute-start(bf16[4,4,16,1472]{3,2,1,0:T(8,128)(2,1)} %get-tuple-element.65), channel_id=1, source_target_pairs={{0,4},{4,0},{8,12},{12,8},{16,20},{20,16},{24,28},{28,24},{1,5},{5... | collective-permute-start | bytes 2261000 | tf_op jit(solution)/shard_map/ppermute | solution.py:290
  370.8 129.8 %reduce-scatter.3.cloned.1.call-start = ((), (), s32[]{:S(2)}) async-start(), calls=%async_computation.4 | async-start | bytes 3297280 | tf_op jit(solution)/shard_map/reduce_scatter | solution.py:717
  398.4 39.7 %collective-permute-start.39 = (bf16[4,384,768]{2,1,0:T(8,128)(2,1)}, bf16[4,384,768]{2,1,0:T(8,128)(2,1)}, u32[]{:S(2)}, u32[]{:S(2)}) collective-permute-start(bf16[4,384,768]{2,1,0:T(8,128)(2,1)} %bitcast.45), channel_id=1, source_target_pairs={{0,4},{4,0},{8,12},{12,8},{16,20},{20,16},{24,28},{28,24},{1,5},{5... | collective-permute-start | bytes 7077896 | tf_op jit(solution)/shard_map/ppermute | solution.py:290
  401.7 8.7 %collective-permute-start.83 = (f32[8,128]{1,0:T(8,128)S(1)}, f32[8,128]{1,0:T(8,128)S(1)}, u32[]{:S(2)}, u32[]{:S(2)}) collective-permute-start(f32[8,128]{1,0:T(8,128)S(1)} %pad_add_fusion.1), channel_id=1, source_target_pairs={{0,8},{4,12},{8,0},{12,4},{16,24},{20,28},{24,16},{28,20},{1,9},{5... | collective-permute-start | bytes 12296 | tf_op jit(solution)/shard_map/ppermute | solution.py:290
  410.4 13.5 %collective-permute-start.84 = (f32[8,128]{1,0:T(8,128)S(1)}, f32[8,128]{1,0:T(8,128)S(1)}, u32[]{:S(2)}, u32[]{:S(2)}) collective-permute-start(f32[8,128]{1,0:T(8,128)S(1)} %add.260), channel_id=1, source_target_pairs={{0,16},{4,20},{8,24},{12,28},{16,0},{20,4},{24,8},{28,12},{1,17},{... | collective-permute-start | bytes 12296 | tf_op jit(solution)/shard_map/ppermute | solution.py:290
  412.4 14.6 %collective-permute-start.62 = (bf16[16,1472]{1,0:T(8,128)(2,1)S(1)}, bf16[16,1472]{1,0:T(8,128)(2,1)S(1)}, u32[]{:S(2)}, u32[]{:S(2)}) collective-permute-start(bf16[16,1472]{1,0:T(8,128)(2,1)S(1)} %get-tuple-element.173), channel_id=1, source_target_pairs={{0,1},{1,0},{2,3},{3,2},{4,5},{5,4},{6,7},{7,6},{8,9},{9,8},{10,11... | collective-permute-start | bytes 141320 | tf_op jit(solution)/shard_map/ppermute | solution.py:295
  427.0 27.4 %collective-permute-start.85 = (f32[8,128]{1,0:T(8,128)S(1)}, f32[8,128]{1,0:T(8,128)S(1)}, u32[]{:S(2)}, u32[]{:S(2)}) collective-permute-start(f32[8,128]{1,0:T(8,128)S(1)} %add.261), channel_id=1, source_target_pairs={{0,1},{1,0},{2,3},{3,2},{4,5},{5,4},{6,7},{7,6},{8,9},{9,8},{10,11... | collective-permute-start | bytes 12296 | tf_op jit(solution)/shard_map/ppermute | solution.py:295
  435.7 19.1 %collective-permute-start.67 = (bf16[8,1472]{1,0:T(8,128)(2,1)S(1)}, bf16[8,1472]{1,0:T(8,128)(2,1)S(1)}, u32[]{:S(2)}, u32[]{:S(2)}) collective-permute-start(bf16[8,1472]{1,0:T(8,128)(2,1)S(1)} %slice.458), channel_id=1, source_target_pairs={{0,16},{4,20},{8,24},{12,28},{16,0},{20,4},{24,8},{28,12},{1,17},{... | collective-permute-start | bytes 70664 | tf_op jit(solution)/shard_map/ppermute | solution.py:290
  437.0 17.7 %collective-permute-start.68 = (bf16[8,1472]{1,0:T(8,128)(2,1)S(1)}, bf16[8,1472]{1,0:T(8,128)(2,1)S(1)}, u32[]{:S(2)}, u32[]{:S(2)}) collective-permute-start(bf16[8,1472]{1,0:T(8,128)(2,1)S(1)} %slice.459), channel_id=1, source_target_pairs={{0,8},{4,12},{8,0},{12,4},{16,24},{20,28},{24,16},{28,20},{1,9},{5... | collective-permute-start | bytes 70664 | tf_op jit(solution)/shard_map/ppermute | solution.py:290
  454.3 23.1 %collective-permute-start.44 = (bf16[4,4,48,1152]{3,2,1,0:T(8,128)(2,1)}, bf16[4,4,48,1152]{3,2,1,0:T(8,128)(2,1)}, u32[]{:S(2)}, u32[]{:S(2)}) collective-permute-start(bf16[4,4,48,1152]{3,2,1,0:T(8,128)(2,1)} %get-tuple-element.60), channel_id=1, source_target_pairs={{0,4},{4,0},{8,12},{12,8},{16,20},{20,16},{24,28},{28,24},{1,5},{5... | collective-permute-start | bytes 5308424 | tf_op jit(solution)/shard_map/ppermute | solution.py:290
  455.1 11.3 %collective-permute-start.78 = (bf16[112,1472]{1,0:T(8,128)(2,1)}, bf16[112,1472]{1,0:T(8,128)(2,1)}, u32[]{:S(2)}, u32[]{:S(2)}) collective-permute-start(bf16[112,1472]{1,0:T(8,128)(2,1)} %reduce-scatter.5.cloned.1.call-done), channel_id=1, source_target_pairs={{0,16},{4,20},{8,24},{12,28},{16,0},{20,4},{24,8},{28,12},{1,17},{... | collective-permute-start | bytes 989192 | tf_op jit(solution)/shard_map/ppermute | solution.py:290
  456.2 12.6 %collective-permute-start.77 = (bf16[112,1472]{1,0:T(8,128)(2,1)}, bf16[112,1472]{1,0:T(8,128)(2,1)}, u32[]{:S(2)}, u32[]{:S(2)}) collective-permute-start(bf16[112,1472]{1,0:T(8,128)(2,1)} %reduce-scatter.5.cloned.1.call-done), channel_id=1, source_target_pairs={{0,8},{4,12},{8,0},{12,4},{16,24},{20,28},{24,16},{28,20},{1,9},{5... | collective-permute-start | bytes 989192 | tf_op jit(solution)/shard_map/ppermute | solution.py:290
  460.5 11.6 %collective-permute-start.40 = (bf16[192,768]{1,0:T(8,128)(2,1)}, bf16[192,768]{1,0:T(8,128)(2,1)}, u32[]{:S(2)}, u32[]{:S(2)}) collective-permute-start(bf16[192,768]{1,0:T(8,128)(2,1)} %get-tuple-element.150), channel_id=1, source_target_pairs={{0,16},{4,20},{8,24},{12,28},{16,0},{20,4},{24,8},{28,12},{1,17},{... | collective-permute-start | bytes 884744 | tf_op jit(solution)/shard_map/ppermute | solution.py:290
  460.5 13.3 %collective-permute-start.42 = (bf16[192,768]{1,0:T(8,128)(2,1)S(1)}, bf16[192,768]{1,0:T(8,128)(2,1)}, u32[]{:S(2)}, u32[]{:S(2)}) collective-permute-start(bf16[192,768]{1,0:T(8,128)(2,1)S(1)} %get-tuple-element.151), channel_id=1, source_target_pairs={{0,8},{4,12},{8,0},{12,4},{16,24},{20,28},{24,16},{28,20},{1,9},{5... | collective-permute-start | bytes 884744 | tf_op jit(solution)/shard_map/ppermute | solution.py:290
  467.5 14.1 %collective-permute-start.80 = (bf16[64,1472]{1,0:T(8,128)(2,1)S(1)}, bf16[64,1472]{1,0:T(8,128)(2,1)S(1)}, u32[]{:S(2)}, u32[]{:S(2)}) collective-permute-start(bf16[64,1472]{1,0:T(8,128)(2,1)S(1)} %slice.465), channel_id=1, source_target_pairs={{0,8},{4,12},{8,0},{12,4},{16,24},{20,28},{24,16},{28,20},{1,9},{5... | collective-permute-start | bytes 565256 | tf_op jit(solution)/shard_map/ppermute | solution.py:290
  469.8 10.9 %collective-permute-start.79 = (bf16[48,1472]{1,0:T(8,128)(2,1)S(1)}, bf16[48,1472]{1,0:T(8,128)(2,1)S(1)}, u32[]{:S(2)}, u32[]{:S(2)}) collective-permute-start(bf16[48,1472]{1,0:T(8,128)(2,1)S(1)} %slice.464), channel_id=1, source_target_pairs={{0,16},{4,20},{8,24},{12,28},{16,0},{20,4},{24,8},{28,12},{1,17},{... | collective-permute-start | bytes 423944 | tf_op jit(solution)/shard_map/ppermute | solution.py:290
  475.2 25.3 %collective-permute-start.41 = (bf16[384,768]{1,0:T(8,128)(2,1)S(1)}, bf16[384,768]{1,0:T(8,128)(2,1)}, u32[]{:S(2)}, u32[]{:S(2)}) collective-permute-start(bf16[384,768]{1,0:T(8,128)(2,1)S(1)} %pad_maximum_fusion.10), channel_id=1, source_target_pairs={{0,8},{4,12},{8,0},{12,4},{16,24},{20,28},{24,16},{28,20},{1,9},{5... | collective-permute-start | bytes 1769480 | tf_op jit(solution)/shard_map/ppermute | solution.py:290
  476.5 25.3 %collective-permute-start.43 = (bf16[384,768]{1,0:T(8,128)(2,1)S(1)}, bf16[384,768]{1,0:T(8,128)(2,1)}, u32[]{:S(2)}, u32[]{:S(2)}) collective-permute-start(bf16[384,768]{1,0:T(8,128)(2,1)S(1)} %pad_maximum_fusion.11), channel_id=1, source_target_pairs={{0,16},{4,20},{8,24},{12,28},{16,0},{20,4},{24,8},{28,12},{1,17},{... | collective-permute-start | bytes 1769480 | tf_op jit(solution)/shard_map/ppermute | solution.py:290
  479.5 14.9 %collective-permute-start.45 = (bf16[2,48,1152]{2,1,0:T(8,128)(2,1)S(1)}, bf16[2,48,1152]{2,1,0:T(8,128)(2,1)S(1)}, u32[]{:S(2)}, u32[]{:S(2)}) collective-permute-start(bf16[2,48,1152]{2,1,0:T(8,128)(2,1)S(1)} %get-tuple-element.158), channel_id=1, source_target_pairs={{0,16},{4,20},{8,24},{12,28},{16,0},{20,4},{24,8},{28,12},{1,17},{... | collective-permute-start | bytes 663560 | tf_op jit(solution)/shard_map/ppermute | solution.py:290
  480.7 13.8 %collective-permute-start.47 = (bf16[2,48,1152]{2,1,0:T(8,128)(2,1)S(1)}, bf16[2,48,1152]{2,1,0:T(8,128)(2,1)S(1)}, u32[]{:S(2)}, u32[]{:S(2)}) collective-permute-start(bf16[2,48,1152]{2,1,0:T(8,128)(2,1)S(1)} %get-tuple-element.159), channel_id=1, source_target_pairs={{0,8},{4,12},{8,0},{12,4},{16,24},{20,28},{24,16},{28,20},{1,9},{5... | collective-permute-start | bytes 663560 | tf_op jit(solution)/shard_map/ppermute | solution.py:290
  495.4 11.4 %collective-permute-start.46 = (bf16[4,48,1152]{2,1,0:T(8,128)(2,1)}, bf16[4,48,1152]{2,1,0:T(8,128)(2,1)}, u32[]{:S(2)}, u32[]{:S(2)}) collective-permute-start(bf16[4,48,1152]{2,1,0:T(8,128)(2,1)} %pad_maximum_fusion.12), channel_id=1, source_target_pairs={{0,8},{4,12},{8,0},{12,4},{16,24},{20,28},{24,16},{28,20},{1,9},{5... | collective-permute-start | bytes 1327112 | tf_op jit(solution)/shard_map/ppermute | solution.py:290
  497.2 13.4 %collective-permute-start.48 = (bf16[4,48,1152]{2,1,0:T(8,128)(2,1)}, bf16[4,48,1152]{2,1,0:T(8,128)(2,1)}, u32[]{:S(2)}, u32[]{:S(2)}) collective-permute-start(bf16[4,48,1152]{2,1,0:T(8,128)(2,1)} %pad_maximum_fusion.13), channel_id=1, source_target_pairs={{0,16},{4,20},{8,24},{12,28},{16,0},{20,4},{24,8},{28,12},{1,17},{... | collective-permute-start | bytes 1327112 | tf_op jit(solution)/shard_map/ppermute | solution.py:290
  500.5 49.9 %collective-permute-start.81 = (bf16[4,112,1472]{2,1,0:T(8,128)(2,1)}, bf16[4,112,1472]{2,1,0:T(8,128)(2,1)}, u32[]{:S(2)}, u32[]{:S(2)}) collective-permute-start(bf16[4,112,1472]{2,1,0:T(8,128)(2,1)} %pad_maximum_fusion.4.near_ref), channel_id=1, source_target_pairs={{0,4},{4,0},{8,12},{12,8},{16,20},{20,16},{24,28},{28,24},{1,5},{5... | collective-permute-start | bytes 3956744 | tf_op jit(solution)/shard_map/ppermute | solution.py:290
  500.6 21.0 %collective-permute-start.72 = (bf16[368,896]{1,0:T(8,128)(2,1)}, bf16[368,896]{1,0:T(8,128)(2,1)S(1)}, u32[]{:S(2)}, u32[]{:S(2)}) collective-permute-start(bf16[368,896]{1,0:T(8,128)(2,1)} %reduce-scatter.3.cloned.1.call-done), channel_id=1, source_target_pairs={{0,16},{4,20},{8,24},{12,28},{16,0},{20,4},{24,8},{28,12},{1,17},{... | collective-permute-start | bytes 1978376 | tf_op jit(solution)/shard_map/ppermute | solution.py:290
  501.7 20.8 %collective-permute-start.71 = (bf16[368,896]{1,0:T(8,128)(2,1)}, bf16[368,896]{1,0:T(8,128)(2,1)S(1)}, u32[]{:S(2)}, u32[]{:S(2)}) collective-permute-start(bf16[368,896]{1,0:T(8,128)(2,1)} %reduce-scatter.3.cloned.1.call-done), channel_id=1, source_target_pairs={{0,8},{4,12},{8,0},{12,4},{16,24},{20,28},{24,16},{28,20},{1,9},{5... | collective-permute-start | bytes 1978376 | tf_op jit(solution)/shard_map/ppermute | solution.py:290
  521.6 9.8 %collective-permute-start.74 = (bf16[192,896]{1,0:T(8,128)(2,1)S(1)}, bf16[192,896]{1,0:T(8,128)(2,1)S(1)}, u32[]{:S(2)}, u32[]{:S(2)}) collective-permute-start(bf16[192,896]{1,0:T(8,128)(2,1)S(1)} %slice.461), channel_id=1, source_target_pairs={{0,8},{4,12},{8,0},{12,4},{16,24},{20,28},{24,16},{28,20},{1,9},{5... | collective-permute-start | bytes 1032200 | tf_op jit(solution)/shard_map/ppermute | solution.py:290
  523.6 9.8 %collective-permute-start.49 = (bf16[48,1152]{1,0:T(8,128)(2,1)S(1)}, bf16[48,1152]{1,0:T(8,128)(2,1)S(1)}, u32[]{:S(2)}, u32[]{:S(2)}) collective-permute-start(bf16[48,1152]{1,0:T(8,128)(2,1)S(1)} %get-tuple-element.168), channel_id=1, source_target_pairs={{0,1},{1,0},{2,3},{3,2},{4,5},{5,4},{6,7},{7,6},{8,9},{9,8},{10,11... | collective-permute-start | bytes 331784 | tf_op jit(solution)/shard_map/ppermute | solution.py:295
  525.0 8.4 %collective-permute-start.50 = (bf16[48,1152]{1,0:T(8,128)(2,1)S(1)}, bf16[48,1152]{1,0:T(8,128)(2,1)S(1)}, u32[]{:S(2)}, u32[]{:S(2)}) collective-permute-start(bf16[48,1152]{1,0:T(8,128)(2,1)S(1)} %get-tuple-element.170), channel_id=1, source_target_pairs={{0,2},{1,3},{2,0},{3,1},{4,6},{5,7},{6,4},{7,5},{8,10},{9,11},{10,... | collective-permute-start | bytes 331784 | tf_op jit(solution)/shard_map/ppermute | solution.py:295
  533.4 35.1 %collective-permute-start.75 = (bf16[4,368,896]{2,1,0:T(8,128)(2,1)}, bf16[4,368,896]{2,1,0:T(8,128)(2,1)}, u32[]{:S(2)}, u32[]{:S(2)}) collective-permute-start(bf16[4,368,896]{2,1,0:T(8,128)(2,1)} %pad_maximum_fusion.near_ref), channel_id=1, source_target_pairs={{0,4},{4,0},{8,12},{12,8},{16,20},{20,16},{24,28},{28,24},{1,5},{5... | collective-permute-start | bytes 7913480 | tf_op jit(solution)/shard_map/ppermute | solution.py:290
  546.4 14.6 %collective-permute-start.56 = (bf16[4,48,1152]{2,1,0:T(8,128)(2,1)S(1)}, bf16[4,48,1152]{2,1,0:T(8,128)(2,1)S(1)}, u32[]{:S(2)}, u32[]{:S(2)}) collective-permute-start(bf16[4,48,1152]{2,1,0:T(8,128)(2,1)S(1)} %pad_maximum_fusion.14.near_ref), channel_id=1, source_target_pairs={{0,4},{4,0},{8,12},{12,8},{16,20},{20,16},{24,28},{28,24},{1,5},{5... | collective-permute-start | bytes 1327112 | tf_op jit(solution)/shard_map/ppermute | solution.py:290
  (72 other events, 553.5 us)
Sparse Core Ops, SparseCore 0:
  11.3 60.2 all-gather.2
  73.8 33.8 all-gather.4
  370.9 40.6 reduce-scatter.4
  435.8 51.0 reduce-scatter.2

commit v3 on v2

v3 whole, which is shorter than its diff:
```python
import functools

import jax
import jax.numpy as jnp
import numpy as np
from jax import lax
from jax.experimental import pallas as pl
from jax.experimental.pallas import tpu as pltpu
from jax.sharding import PartitionSpec as P

BUCKETS = 32
GROUP = 8
EPSILON = 1e-06
NEGATIVE = -1e30
PRECISE = lax.Precision.HIGHEST
BUCKET_EDGES = (12, 16, 23, 32, 46, 64, 91)
FLOAT = jnp.float32
BFLOAT = jnp.bfloat16


SCALE = 0.2


def cost(flops, bytes_accessed, transcendentals):
    return pl.CostEstimate(
        flops=int(SCALE * flops), bytes_accessed=int(SCALE * bytes_accessed), transcendentals=int(SCALE * transcendentals)
    )


def bucket_number(offset):
    distance = abs(offset)
    level = distance if distance < 8 else 8 + sum(distance >= edge for edge in BUCKET_EDGES)
    return level + (16 if offset > 0 else 0)


def bucket_of(offsets):
    distance = jnp.abs(offsets)
    coarse = 8 + sum(((distance >= boundary).astype(jnp.int32) for boundary in BUCKET_EDGES))
    level = jnp.where(distance < 8, distance, coarse)
    return level + jnp.where(offsets > 0, 16, 0)


def near_radius(rows):
    return -(-(BUCKET_EDGES[-1] - 1) // rows)


def tile_offsets(block_gap, rows):
    keys = lax.broadcasted_iota(jnp.int32, (rows, rows), 0)
    queries = lax.broadcasted_iota(jnp.int32, (rows, rows), 1)
    return block_gap * rows + keys - queries


def tile_buckets(block_gap, rows):
    low, high = block_gap * rows - (rows - 1), block_gap * rows + (rows - 1)
    return sorted({bucket_number(offset) for offset in range(low, high + 1)})


def nt(left, right):
    return lax.dot_general(left, right, (((1,), (1,)), ((), ())), preferred_element_type=FLOAT)


def tn(left, right):
    return lax.dot_general(left, right, (((0,), (0,)), ((), ())), preferred_element_type=FLOAT)


def block_number(meta, half, position, count):
    low = lax.rem(meta, GROUP)
    part, group = divmod(position, count // 4)
    return group * GROUP + lax.bitwise_xor(low, jnp.int32(2 * part + half))


def tile_index(meta, half, position, count, radius):
    gap = block_number(meta, half, position, count) - meta
    return jnp.clip(gap, -(radius + 1), radius + 1) + radius + 1


def build_bias(bias_ref, table_ref, pair, rows, radius):
    for side, bucket in ((0, 15), (2 * radius + 2, 31)):
        for head in range(2):
            bias_ref[head, side] = jnp.full((rows, rows), table_ref[bucket, 2 * pair + head], FLOAT)
    for gap in range(-radius, radius + 1):
        buckets = bucket_of(tile_offsets(gap, rows))
        present = tile_buckets(gap, rows)
        tiles = [jnp.full((rows, rows), table_ref[present[0], 2 * pair + head], FLOAT) for head in range(2)]
        for bucket in present[1:]:
            hit = buckets == bucket
            tiles = [jnp.where(hit, table_ref[bucket, 2 * pair + head], tiles[head]) for head in range(2)]
        for head in range(2):
            bias_ref[head, gap + radius + 1] = tiles[head]


def build_mask(mask_ref, segs_ref, meta, seq, rows, count):
    own = segs_ref[seq, pl.ds(meta, 1), :]
    for half in range(2):
        for position in range(count):
            row = segs_ref[seq, pl.ds(block_number(meta, half, position, count), 1), :]
            keys = jnp.transpose(jnp.broadcast_to(row, (rows, rows)))
            mask_ref[seq, half * count + position] = jnp.where(keys == own, 0.0, NEGATIVE)


def half_scores(keys, query, meta, head, half, seq, bias_ref, mask_ref, rows, count, radius):
    raw = nt(keys, query)
    parts = []
    for position in range(count):
        extra = bias_ref[head, tile_index(meta, half, position, count, radius)]
        masked = mask_ref[seq, half * count + position]
        parts.append(raw[position * rows : (position + 1) * rows] + (extra + masked))
    return jnp.concatenate(parts, axis=0)


def joined(refs):
    return jnp.concatenate([ref[...].reshape(-1, ref.shape[-1]) for ref in refs], axis=0)


def head_rows(value, head, lane):
    return jnp.where((lane < 64) == (head == 0), value, jnp.zeros_like(value))


def forward_kernel(
    meta_ref, table_ref, segs_ref, q_ref, *refs, rows, count, radius,
):
    key_refs, value_refs, (out_ref, lse_ref, bias_ref, mask_ref) = refs[:8], refs[8:16], refs[16:]
    pair, seq = pl.program_id(0), pl.program_id(1)
    meta = meta_ref[0]

    @pl.when(seq == 0)
    def _():
        build_bias(bias_ref, table_ref, pair, rows, radius)

    @pl.when(pair == 0)
    def _():
        build_mask(mask_ref, segs_ref, meta, seq, rows, count)

    query = q_ref[0]
    lane = lax.broadcasted_iota(jnp.int32, query.shape, 1)
    keys = [joined(key_refs[:4]), joined(key_refs[4:])]
    values = [joined(value_refs[:4]), joined(value_refs[4:])]
    pieces = []
    for head in range(2):
        one = head_rows(query, head, lane)
        scores = [
            half_scores(keys[half], one, meta, head, half, seq, bias_ref, mask_ref, rows, count, radius)
            for half in range(2)
        ]
        top = jnp.maximum(jnp.max(scores[0], axis=0, keepdims=True), jnp.max(scores[1], axis=0, keepdims=True))
        raised = [jnp.exp(part - top) for part in scores]
        total = jnp.sum(raised[0], axis=0, keepdims=True) + jnp.sum(raised[1], axis=0, keepdims=True)
        scale = 1.0 / total
        mixed = sum(tn(values[half], (raised[half] * scale).astype(BFLOAT)) for half in range(2))
        pieces.append(mixed[64 * head : 64 * head + 64])
        lse_ref[0, 0, head : head + 1] = top + jnp.log(total)
    out_ref[0] = jnp.transpose(jnp.concatenate(pieces, axis=0))


def backward_kernel(
    meta_ref, table_ref, segs_ref, q_ref, *refs, rows, count, radius,
):
    key_refs, value_refs, (do_ref, out_ref, lse_ref, dq_ref) = refs[:8], refs[8:16], refs[16:20]
    both_refs, (tab_ref, bias_ref, mask_ref, sum_ref) = refs[20:28], refs[28:]
    pair, seq = pl.program_id(0), pl.program_id(1)
    meta = meta_ref[0]

    @pl.when(seq == 0)
    def _():
        build_bias(bias_ref, table_ref, pair, rows, radius)
        sum_ref[...] = jnp.zeros_like(sum_ref)

    @pl.when(pair == 0)
    def _():
        build_mask(mask_ref, segs_ref, meta, seq, rows, count)

    query, grad = q_ref[0], do_ref[0]
    lane = lax.broadcasted_iota(jnp.int32, query.shape, 1)
    keys = [joined(key_refs[:4]), joined(key_refs[4:])]
    values = [joined(value_refs[:4]), joined(value_refs[4:])]
    picks = (
        lax.broadcasted_iota(jnp.int32, (8, 128), 1) // 64 == lax.broadcasted_iota(jnp.int32, (8, 128), 0)
    ).astype(FLOAT)
    deltas = lax.dot_general(
        picks, grad.astype(FLOAT) * out_ref[0], (((1,), (1,)), ((), ())), precision=PRECISE, preferred_element_type=FLOAT
    )
    query_heads = [head_rows(query, head, lane) for head in range(2)]
    grad_heads = [head_rows(grad, head, lane) for head in range(2)]
    probs, slopes = [[], []], [[], []]
    pieces = []
    for head in range(2):
        logsum = lse_ref[0, 0, head : head + 1]
        delta = deltas[head : head + 1]
        flow = None
        for half in range(2):
            scores = half_scores(
                keys[half], query_heads[head], meta, head, half, seq, bias_ref, mask_ref, rows, count, radius
            )
            prob = jnp.exp(scores - logsum)
            slope = prob * (nt(values[half], grad_heads[head]) - delta)
            for position in range(count):
                index = tile_index(meta, half, position, count, radius)
                sum_ref[head, index] = sum_ref[head, index] + slope[position * rows : (position + 1) * rows]
            slope_low = slope.astype(BFLOAT)
            probs[half].append(prob.astype(BFLOAT))
            slopes[half].append(slope_low)
            term = tn(keys[half], slope_low)
            flow = term if flow is None else flow + term
        pieces.append(flow[64 * head : 64 * head + 64])
    dq_ref[0] = jnp.transpose(jnp.concatenate(pieces, axis=0)).astype(BFLOAT)
    query_stack = jnp.concatenate(query_heads, axis=0)
    grad_stack = jnp.concatenate(grad_heads, axis=0)
    for half in range(2):
        dk = jnp.dot(jnp.concatenate(slopes[half], axis=1), query_stack, preferred_element_type=FLOAT)
        dv = jnp.dot(jnp.concatenate(probs[half], axis=1), grad_stack, preferred_element_type=FLOAT)
        dk = dk.astype(BFLOAT).reshape(count, 1, rows, 128)
        dv = dv.astype(BFLOAT).reshape(count, 1, rows, 128)
        for part, both_ref in enumerate(both_refs[4 * half : 4 * half + 4]):
            side = slice(part * count // 4, (part + 1) * count // 4)
            both_ref[:, :, :, :128] = dk[side]
            both_ref[:, :, :, 128:] = dv[side]

    @pl.when(seq == pl.num_programs(1) - 1)
    def _():
        for head in range(2):
            sums = {}
            for side, bucket in ((0, 15), (2 * radius + 2, 31)):
                sums[bucket] = jnp.sum(sum_ref[head, side], axis=0, keepdims=True)
            for gap in range(-radius, radius + 1):
                buckets = bucket_of(tile_offsets(gap, rows))
                tile = sum_ref[head, gap + radius + 1]
                for bucket in tile_buckets(gap, rows):
                    part = jnp.sum(jnp.where(buckets == bucket, tile, 0.0), axis=0, keepdims=True)
                    sums[bucket] = sums[bucket] + part if bucket in sums else part
            for bucket in range(BUCKETS):
                tab_ref[0, head, bucket : bucket + 1] = sums.get(bucket, jnp.zeros((1, rows), FLOAT))


def attention_specs(seqs, rows, count, blocks, pairs):
    small = [
        pl.BlockSpec(memory_space=pltpu.SMEM),
        pl.BlockSpec(memory_space=pltpu.SMEM),
        pl.BlockSpec((seqs, blocks, rows), lambda p, s: (0, 0, 0)),
    ]
    query = pl.BlockSpec((1, rows, 128), lambda p, s: (s, 0, p))
    key = pl.BlockSpec((count // 4, 1, rows, 128), lambda p, s: (0, s, 0, 2 * p))
    value = pl.BlockSpec((count // 4, 1, rows, 128), lambda p, s: (0, s, 0, 2 * p + 1))
    stat = pl.BlockSpec((1, 1, 8, rows), lambda p, s: (p, s, 0, 0))
    return small, query, key, value, stat


def attention_scratch(seqs, rows, count, radius):
    return [
        pltpu.VMEM((2, 2 * radius + 3, rows, rows), FLOAT),
        pltpu.VMEM((seqs, 2 * count, rows, rows), FLOAT),
    ]


def attention_cost(seqs, rows, keys, width, products):
    return cost(
        flops=2 * products * seqs * rows * keys * width,
        bytes_accessed=4 * seqs * keys * width * products,
        transcendentals=seqs * rows * keys * width // 64,
    )


def attention_forward(meta, table, segs, queries, kv):
    seqs, rows, inner = queries.shape
    count, blocks, pairs = 4 * kv[0].shape[0], segs.shape[1], inner // 128
    radius = near_radius(rows)
    small, query, key, value, stat = attention_specs(seqs, rows, count, blocks, pairs)
    return pl.pallas_call(
        functools.partial(forward_kernel, rows=rows, count=count, radius=radius),
        grid=(pairs, seqs),
        in_specs=[*small, query, *[key] * 8, *[value] * 8],
        out_specs=[query, stat],
        out_shape=[
            jax.ShapeDtypeStruct((seqs, rows, inner), FLOAT),
            jax.ShapeDtypeStruct((pairs, seqs, 8, rows), FLOAT),
        ],
        scratch_shapes=attention_scratch(seqs, rows, count, radius),
        cost_estimate=attention_cost(seqs, rows, blocks * rows, inner, 2),
        name="attention_forward",
    )(meta, table, segs, queries, *kv, *kv)


def attention_backward(meta, table, segs, queries, kv, grad, out, lse, *deps):
    seqs, rows, inner = queries.shape
    count, blocks, pairs = 4 * kv[0].shape[0], segs.shape[1], inner // 128
    radius = near_radius(rows)
    small, query, key, value, stat = attention_specs(seqs, rows, count, blocks, pairs)
    side = jax.ShapeDtypeStruct((count // 4, seqs, rows, 2 * inner), BFLOAT)
    both = pl.BlockSpec((count // 4, 1, rows, 256), lambda p, s: (0, s, 0, p))
    return pl.pallas_call(
        skipping(functools.partial(backward_kernel, rows=rows, count=count, radius=radius), 23, len(deps)),
        grid=(pairs, seqs),
        in_specs=[*small, query, *[key] * 8, *[value] * 8, query, query, stat] + [UNREAD] * len(deps),
        out_specs=[query, *[both] * 8, pl.BlockSpec((1, 2, BUCKETS, rows), lambda p, s: (p, 0, 0, 0))],
        out_shape=[
            jax.ShapeDtypeStruct((seqs, rows, inner), BFLOAT), *[side] * 8,
            jax.ShapeDtypeStruct((pairs, 2, BUCKETS, rows), FLOAT),
        ],
        scratch_shapes=[
            *attention_scratch(seqs, rows, count, radius),
            pltpu.VMEM((2, 2 * radius + 3, rows, rows), FLOAT),
        ],
        cost_estimate=attention_cost(seqs, rows, blocks * rows, inner, 5),
        name="attention_backward",
    )(meta, table, segs, queries, *kv, *kv, grad, out, lse, *deps)


def swap(value, bit):
    count = lax.axis_size("ctx")
    return lax.ppermute(value, "ctx", [(source, source ^ bit) for source in range(count)])


def swap_depth(value, bit):
    count = lax.axis_size("wsh")
    return lax.ppermute(value, "wsh", [(source, source ^ bit) for source in range(count)])


def after(value, *others):
    return lax.optimization_barrier((value, *others))[0]


def gather_halves(own):
    near, far = own
    first_near, second_far = swap(near, 2), swap(far, 4)
    first_far, second_near = swap(far, 2), swap(near, 4)
    return [near, far, first_near, first_far, second_near, second_far, swap(first_near, 4), swap(second_far, 2)]


def gather_direct(own):
    return [own, swap(own, 2), swap(own, 4), swap(own, 6)]


def gather_relay(own, cut):
    first, second = swap(own, 2), swap(own, 4)
    return jnp.stack((own, first, second, jnp.concatenate((swap(first[:cut], 4), swap(second[cut:], 2)), axis=0)))


VMEM_WHOLE = pl.BlockSpec(memory_space=pltpu.VMEM)
UNREAD = pl.BlockSpec(memory_space=pl.ANY)


def skipping(kernel, inputs, count):
    return lambda *refs: kernel(*refs[:inputs], *refs[inputs + count :])


SMEM_WHOLE = pl.BlockSpec(memory_space=pltpu.SMEM)
BIG = pltpu.CompilerParams(vmem_limit_bytes=60 * 1024 * 1024)


def moved(*arrays):
    return cost(
        flops=0, bytes_accessed=sum(int(np.prod(array.shape)) * array.dtype.itemsize for array in arrays), transcendentals=0
    )


def slice_size(total):
    return -(-total // (GROUP * 16)) * 16


def slice_start(index, total, size):
    return jnp.minimum(index * size, total - size)


def column_cut(width):
    return -(-width // 512) * 128


def pack_kernel(place_ref, q_ref, k_ref, v_ref, proj_ref, early_ref, late_ref, table_ref, out_ref, *, size, wide):
    low = place_ref[0]
    chip, core = low // 2, lax.rem(low, 2)
    inner = q_ref.shape[1]
    shard = q_ref.shape[0]
    start = pl.multiple_of(slice_start(low, shard, size), 16)
    out_ref[:size, :inner] = q_ref[pl.ds(start, size), :]
    for index, ref in enumerate((k_ref, v_ref)):
        rows = ref[pl.ds(start, size), :]
        for pair in range(inner // 128):
            base = inner + 256 * pair + 128 * index
            out_ref[:size, base : base + 128] = rows[:, 128 * pair : 128 * pair + 128]
    part = proj_ref.shape[0] // 2
    each = part // 3
    out_ref[size:, :] = jnp.zeros((out_ref.shape[0] - size, out_ref.shape[1]), BFLOAT)
    for column in range(4):
        reach = min(wide, proj_ref.shape[1] - column * wide)

        @pl.when(chip == column)
        def _(column=column, reach=reach):
            for lane in range(3):
                row = pl.multiple_of(core * part + lane * each, 16)
                out_ref[size : size + each, lane * wide : lane * wide + reach] = proj_ref[
                    pl.ds(row, each), column * wide : column * wide + reach
                ]

    base = size + each
    out_ref[base : base + 1, :shard] = early_ref[...]
    out_ref[base + 1 : base + 2, :shard] = late_ref[...]
    out_ref[base + 8 : base + 16, :128] = table_ref[...]


def unpack_kernel(place_ref, misc_ref, near_ref, far_ref, qkv_ref, proj_ref, gains_ref, table_ref, segs_ref, *, depth, size, wide):
    low = place_ref[0]
    shard, part = qkv_ref.shape[0] // depth, proj_ref.shape[0] // depth // 2
    each = part // 3
    span = size + each
    buckets = table_ref.shape[0] // depth
    for level in range(depth):
        rows = misc_ref[level].astype(FLOAT)
        gains_ref[:, level * shard : (level + 1) * shard] = rows[:8, :shard]
        table_ref[level * buckets : (level + 1) * buckets, :] = rows[8 : 8 + buckets, :128]
    seqs, _, rows = segs_ref.shape
    for index in range(GROUP):
        gap = lax.bitwise_xor(low, jnp.int32(index))
        slot, odd = gap // 2, lax.rem(gap, 2)
        block = jnp.where(odd == 0, near_ref[slot], far_ref[slot])
        for level in range(depth):
            base = level * shard + min(index * size, shard - size)
            qkv_ref[base : base + size, :] = block[level * span : level * span + size]
            column = (index // 2) * wide
            reach = min(wide, proj_ref.shape[1] - column)
            for lane in range(3):
                base = (level * 2 + index % 2) * part + lane * each
                proj_ref[base : base + each, column : column + reach] = block[
                    level * span + size : level * span + span, lane * wide : lane * wide + reach
                ]
        own = block[depth * span : depth * span + 16, :128].astype(FLOAT)
        for seq in range(seqs):
            segs_ref[seq, index : index + 1, :] = own[seq : seq + 1, :rows]


def grad_kernel(
    place_ref, normed_ref, *refs, depth, size, wide
):
    owns, gots, (dq_ref, table_ref, proj_ref) = refs[:4], refs[4:8], refs[8:11]
    sums, (keep_ref, send_ref, kv_scr, q_scr, t_scr) = refs[11:15], refs[15:]
    step = pl.program_id(0)
    for index in range(4):

        @pl.when(step == index)
        def _(index=index):
            total = (owns[index][0].astype(FLOAT) + gots[index][0].astype(FLOAT)).astype(BFLOAT)
            t_scr[...] = total
            sums[index][...] = total

    part = tn(normed_ref[0], t_scr[...])

    @pl.when(step == 0)
    def _():
        kv_scr[...] = part
        q_scr[...] = tn(normed_ref[0], dq_ref[...]).astype(BFLOAT)

    @pl.when(step > 0)
    def _():
        kv_scr[...] = kv_scr[...] + part

    @pl.when(step == 3)
    def _():
        low = place_ref[0]
        zed = place_ref[1]
        inner = q_scr.shape[1]
        shard = q_scr.shape[0] // depth
        for index in range(GROUP):
            target = lax.bitwise_xor(low, jnp.int32(index))
            out_ref = keep_ref if index % 2 == 0 else send_ref
            for gap in range(depth):
                level = lax.bitwise_xor(zed, jnp.int32(gap))
                start = pl.multiple_of(level * shard + slice_start(target, shard, size), 16)
                out_ref[index // 2, gap, :size, :inner] = q_scr[pl.ds(start, size), :]
                out_ref[index // 2, gap, :size, inner:] = kv_scr[pl.ds(start, size), :].astype(BFLOAT)
                part = proj_ref.shape[0] // depth // 2
                each = part // 3
                column = pl.multiple_of((target // 2) * wide, 128)
                for lane in range(3):
                    row = pl.multiple_of((level * 2 + lax.rem(target, 2)) * part + lane * each, 16)
                    out_ref[index // 2, gap, size:, lane * wide : (lane + 1) * wide] = proj_ref[
                        pl.ds(row, each), pl.ds(column, wide)
                    ]
                last = target == GROUP - 1
                rows = table_ref[pl.ds(pl.multiple_of(level * 16, 16), 16), :]
                out_ref[index // 2, gap, :16, :128] = jnp.where(last, rows, out_ref[index // 2, gap, :16, :128])


def weight_grads(place, normed, own, got, dq, table, proj, depth, size, wide):
    _, tokens, width = normed.shape
    inner = dq.shape[1]
    block = once((1, tokens, 2 * inner))
    summed = pl.BlockSpec((tokens, 2 * inner), lambda g: (0, 0))
    span = size + proj.shape[0] // depth // 6
    piece = jax.ShapeDtypeStruct((4, depth, span, 3 * inner), BFLOAT)
    kept = pl.BlockSpec((4, depth, span, 3 * inner), lambda g: (0, 0, 0, 0))
    return pl.pallas_call(
        functools.partial(grad_kernel, depth=depth, size=size, wide=wide),
        grid=(4,),
        in_specs=[
            SMEM_WHOLE, pl.BlockSpec((1, tokens, width), lambda g: (g, 0, 0)), *[block] * 8, once(dq.shape), once(table.shape),
            once(proj.shape),
        ],
        out_specs=[*[summed] * 4, kept, kept],
        out_shape=[*[jax.ShapeDtypeStruct((tokens, 2 * inner), BFLOAT)] * 4, piece, piece],
        scratch_shapes=[
            pltpu.VMEM((width, 2 * inner), FLOAT), pltpu.VMEM((width, inner), BFLOAT), pltpu.VMEM((tokens, 2 * inner), BFLOAT),
        ],
        compiler_params=BIG,
        cost_estimate=cost(flops=18 * tokens * width * inner, bytes_accessed=12 * tokens * width, transcendentals=0),
        name="weight_grads",
    )(place, normed, *own, *got, dq, table, proj)


def pick_block(refs, step, scratch_ref):
    cut = refs[0].shape[0]
    for index in range(4):

        @pl.when(step == index)
        def _(index=index):
            scratch_ref[:cut] = refs[2 * index][...]
            scratch_ref[cut:] = refs[2 * index + 1][...]


def pick_whole(refs, step, scratch_ref):
    for index in range(4):

        @pl.when(step == index)
        def _(index=index):
            scratch_ref[...] = refs[index][...]


def once(shape):
    return pl.BlockSpec(shape, lambda g, *_: (0,) * len(shape), pipeline_mode=pl.Buffered(1))


def norm_kernel(*refs, inner):
    pieces, (gain_ref, weight_ref, normed_ref, k0, k1, k2, k3, q_ref, x_scr) = refs[:8], refs[8:]
    step = pl.program_id(0)
    pick_block(pieces, step, x_scr)
    hidden = x_scr[...].astype(FLOAT)
    scale = lax.rsqrt(jnp.mean(hidden * hidden, axis=-1, keepdims=True) + EPSILON)
    normed = (hidden * scale * gain_ref[...]).astype(BFLOAT)
    normed_ref[0] = normed
    both = jnp.dot(normed, weight_ref[:, inner:], preferred_element_type=FLOAT).astype(BFLOAT)

    for index, kv_ref in enumerate((k0, k1, k2, k3)):

        @pl.when(step == index)
        def _(kv_ref=kv_ref):
            kv_ref[0] = both

    @pl.when(step == 0)
    def _():
        q_ref[...] = jnp.dot(normed, weight_ref[:, :inner], preferred_element_type=FLOAT).astype(BFLOAT)


def norm_project(pieces, gain, weight, inner):
    tokens, width = 2 * pieces[0].shape[0], pieces[0].shape[1]
    return pl.pallas_call(
        functools.partial(norm_kernel, inner=inner),
        grid=(4,),
        in_specs=[*[once(piece.shape) for piece in pieces], once(gain.shape), once(weight.shape)],
        out_specs=[
            pl.BlockSpec((1, tokens, width), lambda g: (g, 0, 0)),
            *[pl.BlockSpec((1, tokens, 2 * inner), lambda g: (0, 0, 0))] * 4,
            pl.BlockSpec((tokens, inner), lambda g: (0, 0)),
        ],
        out_shape=[
            jax.ShapeDtypeStruct((4, tokens, width), BFLOAT),
            *[jax.ShapeDtypeStruct((1, tokens, 2 * inner), BFLOAT)] * 4,
            jax.ShapeDtypeStruct((tokens, inner), BFLOAT),
        ],
        scratch_shapes=[pltpu.VMEM((tokens, width), BFLOAT)],
        compiler_params=BIG,
        cost_estimate=cost(
            flops=18 * tokens * width * inner, bytes_accessed=18 * tokens * width, transcendentals=0
        ),
        name="norm_project",
    )(*pieces, gain, weight)


GELU_SCALE = float(np.sqrt(2.0 / np.pi))


def late_kernel(*refs):
    attn, inputs = refs[:4], refs[4:12]
    proj_ref, gain_ref, after_ref, normed_ref, a_scr, x_scr = refs[12:]
    step = pl.program_id(0)
    pick_whole(attn, step, a_scr)
    pick_block(inputs, step, x_scr)
    after_attn = x_scr[...].astype(FLOAT) + jnp.dot(a_scr[...], proj_ref[...], preferred_element_type=FLOAT)

    @pl.when(step == 0)
    def _():
        after_ref[...] = after_attn

    scale = lax.rsqrt(jnp.mean(after_attn * after_attn, axis=-1, keepdims=True) + EPSILON)
    normed_ref[0] = (after_attn * scale * gain_ref[...]).astype(BFLOAT)


def late_norm(attn, inputs, proj, gain):
    tokens, inner = attn[0].shape
    width = proj.shape[1]
    return pl.pallas_call(
        late_kernel,
        grid=(4,),
        in_specs=[once(value.shape) for value in (*attn, *inputs, proj, gain)],
        out_specs=[
            pl.BlockSpec((tokens, width), lambda g: (0, 0)), pl.BlockSpec((1, tokens, width), lambda g: (g, 0, 0)),
        ],
        out_shape=[
            jax.ShapeDtypeStruct((tokens, width), FLOAT), jax.ShapeDtypeStruct((4, tokens, width), BFLOAT),
        ],
        scratch_shapes=[pltpu.VMEM((tokens, inner), BFLOAT), pltpu.VMEM((tokens, width), BFLOAT)],
        compiler_params=BIG,
        cost_estimate=cost(flops=8 * tokens * width * inner, bytes_accessed=24 * tokens * width, transcendentals=0),
        name="late_norm",
    )(*attn, *inputs, proj, gain)


def feed_kernel(
    spot_ref, normed_ref, cots_ref, mine_ref, other_ref, down_ref,
    act_ref, dmine_ref, dother_ref, out_ref, l0, l1, l2, l3, cot_ref,
):
    is_zero = spot_ref[0] == 0
    tokens = normed_ref.shape[1]
    cot = cots_ref[...].reshape(tokens, cots_ref.shape[2])
    cot_ref[0] = cot
    normed = normed_ref[0]
    pre_mine = jnp.dot(normed, mine_ref[...], preferred_element_type=FLOAT)
    pre_other = jnp.dot(normed, other_ref[...], preferred_element_type=FLOAT)
    gate = jnp.where(is_zero, pre_mine, pre_other)
    up = jnp.where(is_zero, pre_other, pre_mine)
    square = gate * gate
    lifted = jnp.tanh(GELU_SCALE * (gate + 0.044715 * gate * square))
    half = 0.5 * (1.0 + lifted)
    smooth = gate * half
    act = (smooth * up).astype(BFLOAT)
    act_ref[0] = act
    out = jnp.dot(act, down_ref[...], preferred_element_type=FLOAT).astype(BFLOAT)
    out_ref[...] = out.reshape(out_ref.shape)
    act_back = nt(cot, down_ref[...])
    slope = half + 0.5 * gate * (1.0 - lifted * lifted) * (GELU_SCALE * (1.0 + 3 * 0.044715 * square))
    gate_back = act_back * up * slope
    up_back = act_back * smooth
    dmine = jnp.where(is_zero, gate_back, up_back).astype(BFLOAT)
    dother = jnp.where(is_zero, up_back, gate_back).astype(BFLOAT)
    dmine_ref[0] = dmine
    dother_ref[0] = dother
    late = (nt(dmine, mine_ref[...]) + nt(dother, other_ref[...])).astype(BFLOAT)
    for index, late_ref in enumerate((l0, l1, l2, l3)):

        @pl.when(pl.program_id(0) == index)
        def _(late_ref=late_ref):
            late_ref[...] = late.reshape(late_ref.shape)


def feed_forward(spot, normed, cots, mine, other, down):
    _, tokens, width = normed.shape
    wide = mine.shape[1]

    def block(size):
        return pl.BlockSpec((1, tokens, size), lambda g, spot: (g, 0, 0))

    def shape(size):
        return jax.ShapeDtypeStruct((4, tokens, size), BFLOAT)

    placed = pl.BlockSpec((2, tokens // 2, width), lambda g, spot: (lax.bitwise_xor(g, spot[1]), 0, 0))
    sent = jax.ShapeDtypeStruct((8, tokens // 2, width), BFLOAT)
    half = jax.ShapeDtypeStruct((2, tokens // 2, width), BFLOAT)
    piece = pl.BlockSpec((2, tokens // 2, width), lambda g, spot: (0, 0, 0))
    return pl.pallas_call(
        feed_kernel,
        grid_spec=pltpu.PrefetchScalarGridSpec(
            num_scalar_prefetch=1,
            grid=(4,),
            in_specs=[block(width), placed, *[once(value.shape) for value in (mine, other, down)]],
            out_specs=[block(wide), block(wide), block(wide), placed, *[piece] * 4, block(width)],
        ),
        out_shape=[shape(wide), shape(wide), shape(wide), sent, *[half] * 4, shape(width)],
        compiler_params=BIG,
        cost_estimate=cost(
            flops=48 * tokens * width * wide, bytes_accessed=30 * tokens * width, transcendentals=4 * tokens * wide
        ),
        name="feed_forward",
    )(spot, normed, cots, mine, other, down)


def outer_kernel(left_ref, *refs):
    rights, outs, scratch = refs[: len(refs) // 3], refs[len(refs) // 3 : 2 * len(refs) // 3], refs[2 * len(refs) // 3 :]
    step = pl.program_id(0)
    for right_ref, out_ref, acc_ref in zip(rights, outs, scratch):
        part = tn(left_ref[0], right_ref[0]).reshape(out_ref.shape)

        @pl.when(step == 0)
        def _(acc_ref=acc_ref, part=part):
            acc_ref[...] = part

        @pl.when((step > 0) & (step < 3))
        def _(acc_ref=acc_ref, part=part):
            acc_ref[...] = acc_ref[...] + part

        @pl.when(step == 3)
        def _(acc_ref=acc_ref, out_ref=out_ref, part=part):
            out_ref[...] = (acc_ref[...] + part).astype(BFLOAT)


def outer_sums(left, rights, *deps):
    _, tokens, width = left.shape
    shapes = [(2, width // 2, right.shape[2]) for right in rights]
    count = len(rights)
    return pl.pallas_call(
        skipping(outer_kernel, 1 + count, len(deps)),
        grid=(4,),
        in_specs=[pl.BlockSpec((1, tokens, value.shape[2]), lambda g: (g, 0, 0)) for value in (left, *rights)]
        + [UNREAD] * len(deps),
        out_specs=[pl.BlockSpec(shape, lambda g: (0, 0, 0)) for shape in shapes],
        out_shape=[jax.ShapeDtypeStruct(shape, BFLOAT) for shape in shapes],
        scratch_shapes=[pltpu.VMEM(shape, FLOAT) for shape in shapes],
        compiler_params=BIG,
        cost_estimate=cost(flops=8 * tokens * width * 2 * sum(shape[2] for shape in shapes), bytes_accessed=0, transcendentals=0),
        name="outer_sums",
    )(left, *rights, *deps)


def norm_back(hidden, gain, back):
    scale = lax.rsqrt(jnp.mean(hidden * hidden, axis=-1, keepdims=True) + EPSILON)
    lifted = back * gain
    return scale * lifted - hidden * (scale * scale * scale) * jnp.mean(lifted * hidden, axis=-1, keepdims=True)


def quarter_specs(tile, width):
    whole = pl.BlockSpec((tile, width), lambda g: (g, 0))
    near = pl.BlockSpec((tile, width), lambda g: (jnp.minimum(g, 1), 0))
    far = pl.BlockSpec((tile, width), lambda g: (jnp.maximum(g - 2, 0), 0))
    return whole, [near, near, far, far]


def summed(own_ref, parts):
    near = pl.program_id(0) < 2
    first = jnp.where(near, parts[0][...], parts[2][...]).astype(FLOAT)
    second = jnp.where(near, parts[1][...], parts[3][...]).astype(FLOAT)
    return own_ref[...].astype(FLOAT) + first + second


def middle_kernel(after_ref, p0, p1, p2, p3, cot_ref, gain_ref, proj_ref, residual_ref, mix_ref, attn_ref):
    back = sum(ref[0].astype(FLOAT) for ref in (p0, p1, p2, p3))
    residual = cot_ref[0].astype(FLOAT) + norm_back(after_ref[...], gain_ref[...], back)
    residual_ref[...] = residual
    mix = residual.astype(BFLOAT)
    mix_ref[...] = mix
    attn_ref[...] = nt(mix, proj_ref[...]).astype(BFLOAT)


def middle(after_attn, parts, cots, gain, proj):
    tokens, width = after_attn.shape
    inner = proj.shape[0]
    tile = tokens // 4
    whole = pl.BlockSpec((tile, width), lambda g: (g, 0))
    half = pl.BlockSpec((1, tile, width), lambda g: (g // 2, g % 2, 0))
    return pl.pallas_call(
        middle_kernel,
        grid=(4,),
        in_specs=[whole, half, half, half, half, half, once(gain.shape), once(proj.shape)],
        out_specs=[whole, whole, pl.BlockSpec((tile, inner), lambda g: (g, 0))],
        out_shape=[
            jax.ShapeDtypeStruct((tokens, width), FLOAT),
            jax.ShapeDtypeStruct((tokens, width), BFLOAT),
            jax.ShapeDtypeStruct((tokens, inner), BFLOAT),
        ],
        compiler_params=BIG,
        cost_estimate=pl.CostEstimate(flops=10**11, bytes_accessed=0, transcendentals=0),
        name="middle",
    )(after_attn, *parts, cots, gain, proj)


def plus_kernel(left_ref, *refs):
    rights, out_ref = refs[:-1], refs[-1]
    for index, right_ref in enumerate(rights):

        @pl.when(pl.program_id(0) * len(rights) // pl.num_programs(0) == index)
        def _(right_ref=right_ref):
            out_ref[0] = (left_ref[0].astype(FLOAT) + right_ref[0].astype(FLOAT)).astype(BFLOAT)


def plus(left, rights, *deps):
    shape = left.shape
    each = shape[0] // len(rights)
    spec = pl.BlockSpec((1, *shape[1:]), lambda g: (g,) + (0,) * (len(shape) - 1))

    def part(index):
        return pl.BlockSpec(
            (1, *shape[1:]), lambda g: (jnp.clip(g - index * each, 0, each - 1),) + (0,) * (len(shape) - 1)
        )

    return pl.pallas_call(
        skipping(plus_kernel, 1 + len(rights), len(deps)),
        grid=(shape[0],),
        in_specs=[spec, *[part(index) for index in range(len(rights))]] + [UNREAD] * len(deps),
        out_specs=spec,
        out_shape=jax.ShapeDtypeStruct(shape, BFLOAT),
        compiler_params=BIG,
        cost_estimate=moved(left, left, left),
        name="plus",
    )(left, *rights, *deps)


def last_kernel(dq_ref, own_ref, p1, p2, p3, x0, x1, residual_ref, gain_ref, weight_ref, out_ref):
    dkv = sum(ref[...].astype(FLOAT) for ref in (own_ref, p1, p2, p3)).astype(BFLOAT)
    inner = dq_ref.shape[1]
    back = nt(dq_ref[...], weight_ref[:, :inner]) + nt(dkv, weight_ref[:, inner:])
    hidden = jnp.where(pl.program_id(0) < 2, x0[...], x1[...]).astype(FLOAT)
    out_ref[...] = (residual_ref[...] + norm_back(hidden, gain_ref[...], back)).astype(BFLOAT)


def last(dq, own, parts, inputs, residual, gain, weight):
    tokens, width = residual.shape
    inner = dq.shape[1]
    tile = tokens // 4
    whole = pl.BlockSpec((tile, width), lambda g: (g, 0))
    near = pl.BlockSpec((tile, width), lambda g: (jnp.minimum(g, 1), 0))
    far = pl.BlockSpec((tile, width), lambda g: (jnp.maximum(g - 2, 0), 0))
    piece = pl.BlockSpec((tile, 2 * inner), lambda g: (g, 0))
    return pl.pallas_call(
        last_kernel,
        grid=(4,),
        in_specs=[
            pl.BlockSpec((tile, inner), lambda g: (g, 0)), piece, piece, piece, piece, near, far, whole,
            once(gain.shape), once(weight.shape),
        ],
        out_specs=whole,
        out_shape=jax.ShapeDtypeStruct((tokens, width), BFLOAT),
        compiler_params=BIG,
        cost_estimate=cost(flops=6 * tokens * width * inner, bytes_accessed=12 * tokens * width, transcendentals=0),
        name="input_gradient",
    )(dq, own, *parts, *inputs, residual, gain, weight)


def choose(refs, slot):
    value = refs[0][...]
    for index in range(1, len(refs)):
        value = jnp.where(slot == index, refs[index][...], value)
    return value


def spread_kernel(place_ref, *refs, depth, part):
    nears, fars, (gate_ref, up_ref, gate_out, up_out, late_ref) = refs[:4], refs[4:8], refs[8:]
    low = place_ref[0]
    chip, core = low // 2, lax.rem(low, 2)
    for index in range(4):
        slot = lax.bitwise_xor(chip, jnp.int32(index))
        near, far = choose(nears, slot), choose(fars, slot)
        gate = jnp.where(core == 0, near, far).astype(FLOAT)
        up = jnp.where(core == 0, far, near).astype(FLOAT)
        for level in range(depth):
            base = (level * 4 + index) * part
            gate_out[:, base : base + part] = gate[:, level * part : (level + 1) * part]
            up_out[:, base : base + part] = up[:, level * part : (level + 1) * part]
    total = gate_out[...] * gate_ref[...].astype(FLOAT) + up_out[...] * up_ref[...].astype(FLOAT)
    late_ref[...] = jnp.broadcast_to(jnp.sum(total, axis=1, keepdims=True), late_ref.shape)


def spread(place, nears, fars, gate, up, depth, part):
    shard, hidden = gate.shape
    tile = 184 if shard % 184 == 0 else shard
    pieces = pl.BlockSpec((tile, nears[0].shape[1]), lambda g: (g, 0))
    rows = pl.BlockSpec((tile, hidden), lambda g: (g, 0))
    return pl.pallas_call(
        functools.partial(spread_kernel, depth=depth, part=part),
        grid=(shard // tile,),
        in_specs=[SMEM_WHOLE, *[pieces] * 8, rows, rows],
        out_specs=[rows, rows, pl.BlockSpec((tile, 128), lambda g: (g, 0))],
        out_shape=[
            jax.ShapeDtypeStruct((shard, hidden), FLOAT),
            jax.ShapeDtypeStruct((shard, hidden), FLOAT),
            jax.ShapeDtypeStruct((shard, 128), FLOAT),
        ],
        compiler_params=BIG,
        cost_estimate=cost(flops=4 * shard * hidden, bytes_accessed=16 * shard * hidden, transcendentals=0),
        name="spread_columns",
    )(place, *nears, *fars, gate, up)


def rows_kernel(place_ref, *refs):
    nears, fars, out_ref = refs[:4], refs[4:8], refs[8]
    low = place_ref[0]
    size = nears[0].shape[0]
    for index in range(GROUP):
        gap = lax.bitwise_xor(low, jnp.int32(index))
        slot, odd = gap // 2, lax.rem(gap, 2)
        rows = jnp.where(odd == 0, choose(nears, slot), choose(fars, slot))
        out_ref[index * size : (index + 1) * size, :] = rows.astype(FLOAT)


def finish_kernel(
    place_ref, near_ref, far_ref, q_ref, k_ref, v_ref, q_out, k_out, v_out, proj_out, early_ref, table_ref, *, size, wide
):
    low = place_ref[0]
    shard, inner = q_ref.shape
    part = proj_out.shape[0] // 2
    each = part // 3
    for index in range(GROUP):
        gap = lax.bitwise_xor(low, jnp.int32(index))
        slot, odd = gap // 2, lax.rem(gap, 2)
        block = jnp.where(odd == 0, near_ref[slot], far_ref[slot]).astype(FLOAT)
        base = min(index * size, shard - size)
        skip = index * size - base
        q_out[base + skip : base + size, :] = block[skip:size, :inner]
        for pair in range(inner // 128):
            for offset, out_ref in enumerate((k_out, v_out)):
                column = inner + 256 * pair + 128 * offset
                out_ref[base + skip : base + size, 128 * pair : 128 * pair + 128] = block[skip:size, column : column + 128]
        if index == GROUP - 1:
            table_ref[...] = block[:16, :128]
        column = (index // 2) * wide
        reach = min(wide, proj_out.shape[1] - column)
        for lane in range(3):
            base = (index % 2) * part + lane * each
            proj_out[base : base + each, column : column + reach] = block[size:, lane * wide : lane * wide + reach]
    total = q_out[...] * q_ref[...].astype(FLOAT) + k_out[...] * k_ref[...].astype(FLOAT)
    total = total + v_out[...] * v_ref[...].astype(FLOAT)
    early_ref[...] = jnp.broadcast_to(jnp.sum(total, axis=1, keepdims=True), early_ref.shape)


def rows_of_kernel(x_ref, cot_ref, near_ref, far_ref, rows_ref):
    rows, cut = x_ref.shape[2], near_ref.shape[0]
    for seq in range(x_ref.shape[0]):
        turned = jnp.transpose(x_ref[seq])
        start = seq * rows
        split = min(max(cut - start, 0), rows)
        if split > 0:
            near_ref[start : start + split, :] = turned[:split]
        if split < rows:
            far_ref[start + split - cut : start + rows - cut, :] = turned[split:]
        turned = jnp.transpose(cot_ref[seq])
        for copy in range(4):
            if split > 0:
                rows_ref[2 * copy, start : start + split, :] = turned[:split]
            if split < rows:
                rows_ref[2 * copy + 1, start + split - cut : start + rows - cut, :] = turned[split:]


def on_device(
    layer_input, segments, cotangent, query_weight, key_weight, value_weight, projection, gate_weight, up_weight,
    down_weight, gain_early, gain_late, bias_table,
):
    ring = lax.axis_size("ctx")
    depth = lax.axis_size("wsh")
    groups = ring // GROUP
    mine = lax.axis_index("ctx")
    low = lax.rem(mine, GROUP)
    chip, core = low // 2, lax.rem(low, 2)
    zed = lax.axis_index("wsh")
    seqs, rows, width = layer_input.shape
    inner = query_weight.shape[1]
    heads = bias_table.shape[1]
    shard = width // depth
    slab = gate_weight.shape[1] // depth
    part = slab // 4
    piece = part // 2
    tokens = seqs * rows
    cut = tokens // 2
    buckets = BUCKETS // depth
    size, wide = slice_size(shard), column_cut(width)
    each = inner // depth // 6
    upper = [[group * GROUP + index for group in range(groups)] for index in range(GROUP)]
    is_zero = core == 0
    place = jnp.stack((low, zed)).astype(jnp.int32)
    meta = mine.astype(jnp.int32).reshape(1)
    spot = jnp.stack((core, chip)).astype(jnp.int32)

    half = jax.ShapeDtypeStruct((cut, width), BFLOAT)
    chips = [[group * GROUP + 2 * index + side for index in range(4)] for group in range(groups) for side in range(2)]

    def exchange(blocks):
        return lax.all_to_all(blocks, "ctx", split_axis=0, concat_axis=0, tiled=True, axis_index_groups=chips)

    x_near, x_far, own_cots = pl.pallas_call(
        rows_of_kernel,
        in_specs=[VMEM_WHOLE] * 2,
        out_specs=[VMEM_WHOLE] * 3,
        out_shape=[half, half, jax.ShapeDtypeStruct((8, cut, width), BFLOAT)],
        compiler_params=BIG,
        cost_estimate=moved(layer_input, layer_input, cotangent, cotangent),
        name="token_rows",
    )(jnp.swapaxes(layer_input, 1, 2), jnp.swapaxes(cotangent, 1, 2))
    inputs = gather_halves((x_near, x_far))

    def columns(weight):
        return jnp.concatenate(
            [lax.dynamic_slice_in_dim(weight, index * slab + chip * part, part, 1) for index in range(depth)], axis=1
        )

    pair_slice = jnp.where(is_zero, columns(gate_weight), columns(up_weight))
    down_slice = lax.dynamic_slice_in_dim(down_weight, chip * part + core * piece, piece, 0)

    packed = pl.pallas_call(
        functools.partial(pack_kernel, size=size, wide=wide),
        in_specs=[SMEM_WHOLE] + [VMEM_WHOLE] * 7,
        out_specs=VMEM_WHOLE,
        out_shape=jax.ShapeDtypeStruct((size + each + 16, 3 * inner), BFLOAT),
        cost_estimate=moved(query_weight, query_weight),
        name="pack",
    )(
        after(place, pair_slice, down_slice), query_weight, key_weight, value_weight, projection, gain_early.reshape(1, shard), gain_late.reshape(1, shard),
        jnp.pad(bias_table, ((0, 8 - buckets), (0, 128 - heads))),
    )
    packed = lax.all_gather(packed, "wsh", axis=0)
    pair_mine = lax.all_gather(after(pair_slice, packed), "wsh", axis=0, tiled=True)
    seg_rows = jnp.pad(segments.astype(BFLOAT), ((0, 16 - seqs), (0, 3 * inner - rows)))
    small = jnp.concatenate((packed[:, : size + each].reshape(-1, 3 * inner), seg_rows), axis=0)
    small = after(small, *inputs[2:6])
    near = gather_relay(small, small.shape[0] // 32 * 16)
    far = swap(near, 1)
    down_mine = lax.all_gather(after(down_slice, near), "wsh", axis=0, tiled=True).reshape(depth, piece, width)
    qkv_full, proj_full, gains, table, segs = pl.pallas_call(
        functools.partial(unpack_kernel, depth=depth, size=size, wide=wide),
        in_specs=[SMEM_WHOLE, VMEM_WHOLE, VMEM_WHOLE, VMEM_WHOLE],
        out_specs=[VMEM_WHOLE] * 5,
        out_shape=[
            jax.ShapeDtypeStruct((width, 3 * inner), BFLOAT),
            jax.ShapeDtypeStruct((inner, width), BFLOAT),
            jax.ShapeDtypeStruct((8, width), FLOAT),
            jax.ShapeDtypeStruct((BUCKETS, 128), FLOAT),
            jax.ShapeDtypeStruct((seqs, GROUP, rows), FLOAT),
        ],
        compiler_params=BIG,
        cost_estimate=moved(near, far, near),
        name="unpack",
    )(place, packed[:, size + each :], near, far)

    def whole(value, axis=0):
        if groups == 1:
            return value
        return lax.all_gather(value, "ctx", axis=axis, tiled=True, axis_index_groups=upper)

    segs = whole(segs, 1)

    normed, *kv, queries = norm_project(inputs, gains[0:1], qkv_full, inner)
    cots = exchange(own_cots)
    kv = [value.reshape(1, seqs, rows, 2 * inner) for value in kv]
    queries = queries.reshape(seqs, rows, inner)
    kv = [whole(value) for value in (*kv, *[swap(value, 1) for value in kv])]
    attention, lse = attention_forward(meta, table, segs, queries, kv)
    attn_low = attention.astype(BFLOAT).reshape(tokens, inner)
    attn = gather_direct(attn_low)

    after_attn, normed_late = late_norm(attn, inputs, proj_full, gains[1:2])
    pair_mine = after(pair_mine, attn_low)
    pair_other = swap(pair_mine, 1)
    down_mine = after(down_mine, attn_low)
    down_other = swap(down_mine, 1)
    down_full = jnp.where(
        is_zero, jnp.stack((down_mine, down_other), axis=1), jnp.stack((down_other, down_mine), axis=1)
    ).reshape(depth * part, width)
    activation, back_mine, back_other, out_part, *late_part, cot_all = feed_forward(
        spot, normed_late, cots, pair_mine, pair_other, down_full
    )

    def flat(value):
        return value.reshape(4 * tokens, value.shape[2])

    def over_groups(value):
        return lax.psum(value, "ctx", axis_index_groups=upper) if groups > 1 else value

    late_parts = [late_part[0]] + [swap(late_part[index], 2 * index) for index in range(1, 4)]
    other_grad, mine_grad = outer_sums(normed_late, (back_other, back_mine))
    other_got = [swap(other_grad[index : index + 1], 1) for index in range(2)]
    down_grad = outer_sums(activation, (cot_all,))[0].reshape(depth, 2, piece, width)
    down_keep = jnp.where(is_zero, down_grad[:, 0], down_grad[:, 1])
    down_send = jnp.where(is_zero, down_grad[:, 1], down_grad[:, 0])
    down_got = swap(down_send, 1)
    residual_grad, mix_low, attn_grad = middle(after_attn, late_parts, own_cots, gains[1:2], proj_full)
    pair_sum = plus(mine_grad, other_got, mix_low).reshape(width, 2 * piece * depth)
    down_sum = plus(down_keep, [down_got], pair_sum).reshape(depth * piece, width)
    pair_own = over_groups(lax.psum_scatter(pair_sum, "wsh", scatter_dimension=0, tiled=True))
    down_own = over_groups(lax.psum_scatter(down_sum, "wsh", scatter_dimension=0, tiled=True))
    attn_grad = attn_grad.reshape(seqs, rows, inner)
    proj_grad = tn(attn_low, jnp.pad(mix_low, ((0, 0), (0, 4 * wide - width)))).astype(BFLOAT)
    dq, *dkv, table_part = attention_backward(
        meta, table, segs, queries, kv, attn_grad, attention, lse, down_sum
    )

    def owned(value):
        if groups > 1:
            value = lax.psum_scatter(value, "ctx", scatter_dimension=0, tiled=True, axis_index_groups=upper)
        return value.reshape(1, tokens, 2 * inner)

    dkv = [owned(value) for value in dkv]
    dkv_got = [swap(value, 1) for value in dkv[4:]]
    dq = dq.reshape(tokens, inner)
    table_sum = jnp.transpose(jnp.sum(table_part, axis=-1).reshape(heads, BUCKETS)).reshape(depth, buckets, heads)
    table_sum = jnp.pad(table_sum, ((0, 0), (0, 16 - buckets), (0, 128 - heads))).reshape(depth * 16, 128).astype(BFLOAT)
    *dkv_four, keep, send = weight_grads(place, normed, dkv[:4], dkv_got, dq, table_sum, proj_grad, depth, size, wide)
    out_parts = exchange(out_part).astype(FLOAT).reshape(4, tokens, width)
    result = (after_attn + jnp.sum(out_parts, axis=0)).astype(BFLOAT)

    blocks = plus(keep, [swap(send, 1)], result)
    dkv_parts = [swap(dkv_four[index], 2 * index) for index in range(1, 4)]
    total = blocks[0].astype(FLOAT)
    for index in range(1, 4):
        total = total + swap(blocks[index], 2 * index).astype(FLOAT)
    levels = total.astype(BFLOAT)
    total = levels[0].astype(FLOAT)
    for gap in range(1, depth):
        total = total + swap_depth(levels[gap], gap).astype(FLOAT)
    input_grad = last(dq, dkv_four[0], dkv_parts, (x_near, x_far), residual_grad, gains[0:1], qkv_full)
    grads_near = jnp.stack(gather_direct(over_groups(total.astype(BFLOAT))))
    grads_far = swap(grads_near, 1)
    column = jax.ShapeDtypeStruct((shard, inner), FLOAT)
    query_out, key_out, value_out, proj_out, early_sum, table_rows = pl.pallas_call(
        functools.partial(finish_kernel, size=size, wide=wide),
        in_specs=[SMEM_WHOLE] + [VMEM_WHOLE] * 5,
        out_specs=[VMEM_WHOLE] * 6,
        out_shape=[
            column, column, column, jax.ShapeDtypeStruct((inner // depth, width), FLOAT),
            jax.ShapeDtypeStruct((shard, 128), FLOAT), jax.ShapeDtypeStruct((16, 128), FLOAT),
        ],
        compiler_params=BIG,
        cost_estimate=moved(grads_near, grads_far, grads_near),
        name="finish_small",
    )(place, grads_near, grads_far, query_weight, key_weight, value_weight)

    pair_own, down_own = after(pair_own, levels), after(down_own, levels)
    pair_near, down_near = gather_direct(pair_own), gather_direct(down_own)
    pair_far, down_far = [[swap(value, 1) for value in values] for values in (pair_near, down_near)]
    gate_out, up_out, late_sum = spread(place, pair_near, pair_far, gate_weight, up_weight, depth, part)
    down_out = pl.pallas_call(
        rows_kernel,
        in_specs=[SMEM_WHOLE] + [VMEM_WHOLE] * 8,
        out_specs=VMEM_WHOLE,
        out_shape=jax.ShapeDtypeStruct((slab, width), FLOAT),
        compiler_params=BIG,
        cost_estimate=moved(down_own, down_own, down_own),
        name="join_down",
    )(place, *down_near, *down_far)
    return (
        result.reshape(seqs, rows, width),
        input_grad.reshape(seqs, rows, width),
        query_out,
        key_out,
        value_out,
        proj_out,
        gate_out,
        up_out,
        down_out,
        early_sum[:, 0] / gain_early.astype(FLOAT),
        late_sum[:, 0] / gain_late.astype(FLOAT),
        table_rows[:buckets, :heads],
    )


def solution(mesh):
    rows = P("wsh", "ctx", None)
    split = P("wsh", None)
    vector = P("wsh")
    return jax.shard_map(
        on_device,
        mesh=mesh,
        in_specs=(rows, P("wsh", "ctx"), rows, split, split, split, split, split, split, split, vector, vector, split),
        out_specs=(rows, rows, split, split, split, split, split, split, split, vector, vector, split),
        check_vma=False,
    )
```

time: 591 us -> 516 us (0.87)
  Pallas kernels: 126 us -> 215 us
  local copies, waits for them, and re-layouts: 88.9 us -> 31.5 us
  other arithmetic: 65.6 us -> 19.4 us
  starting transfers between devices: 103 us -> 57 us
  matrix products: 43 us -> 1.81 us
  blocking collectives: 0 us -> 19.4 us
  waiting for transfers between devices: 144 us -> 152 us
    pallas_call x10 -> x16, Pallas kernels: 91.9 us -> 180 us  [the longest x2 43.7 us: outer_sums(): pl.pallas_call(skipping(outer_kernel, 1 + count, len(deps)), grid=(4,), i...]
    dot_general x6 -> x1, matrix products: 38.4 us -> 1.81 us  [tn(): lax.dot_general(left, right, (((0,), (0,)), ((), ())), preferred_element_...]
    ppermute x14 -> x3, starting transfers between devices: 39 us -> 3.55 us  [swap_depth(): lax.ppermute(value, 'wsh', [(source, source ^ bit) for source in range(co...]
    convert_element_type x16 -> x3, other arithmetic: 24.4 us -> 2.75 us  [the longest x1 1.36 us: on_device(): levels = total.astype(BFLOAT)]
    ppermute x73 -> x55, starting transfers between devices: 63.9 us -> 43.1 us  [swap(): lax.ppermute(value, 'ctx', [(source, source ^ bit) for source in range(co...]
    all_gather x0 -> x1, blocking collectives: none -> 19.4 us  [on_device(): packed = lax.all_gather(packed, 'wsh', axis=0)]
    ppermute x14 -> x3, waiting for transfers between devices: 22.7 us -> 4.95 us  [swap_depth(): lax.ppermute(value, 'wsh', [(source, source ^ bit) for source in range(co...]
    ppermute x8 -> x0, local copies, waits for them, and re-layouts: 16.5 us -> none  [swap(): lax.ppermute(value, 'ctx', [(source, source ^ bit) for source in range(co...]
  transfers between devices with their start and end apart: 91 -> 64, of which waited for: 28 -> 31; matrix products, arithmetic and copies ran while one was open for 32% -> 9% of each run, Pallas kernels for 12% -> 31%
where the time goes in v3:
time: 516 us; the launch traced here: 512 us
  Pallas kernels  215 us (42%)
  waiting for transfers between devices  152 us (29%)
  starting transfers between devices  57 us (11%)
  local copies, waits for them, and re-layouts  31.5 us (6%)
  other arithmetic  19.4 us (4%)
  blocking collectives  19.4 us (4%)
  between operations  14.5 us (3%)
    ppermute x55, waiting for transfers between devices, swap(): lax.ppermute(value, 'ctx', [(source, source ^ bit) for source in range(co...  120 us
    pallas_call x2, Pallas kernels, outer_sums(): pl.pallas_call(skipping(outer_kernel, 1 + count, len(deps)), grid=(4,), i...  43.7 us
    ppermute x55, starting transfers between devices, swap(): lax.ppermute(value, 'ctx', [(source, source ^ bit) for source in range(co...  43.1 us
    pallas_call x1, Pallas kernels, feed_forward(): pl.pallas_call(feed_kernel, grid_spec=pltpu.PrefetchScalarGridSpec(num_sc...  41.9 us
    pallas_call x1, Pallas kernels, attention_backward(): pl.pallas_call(skipping(functools.partial(backward_kernel, rows=rows, cou...  20.7 us
    all_gather x1, blocking collectives, on_device(): packed = lax.all_gather(packed, 'wsh', axis=0)  19.4 us
    pallas_call x1, Pallas kernels, weight_grads(): pl.pallas_call(functools.partial(grad_kernel, depth=depth, size=size, wid...  15.4 us
    pallas_call x1, Pallas kernels, attention_forward(): pl.pallas_call(functools.partial(forward_kernel, rows=rows, count=count,...  14.9 us
  transfers between devices with their start and end apart: 64, of which 31 were waited for; matrix products, arithmetic and copies ran while one was open for 9% of the time, Pallas kernels for 31%

profile of v3, /device:TPU:0, one launch (start us, length us, event | category | flops | bytes accessed | tf_op | source)
XLA Modules:
  0.0 511.6 jit_solution(2542061025412290629)
XLA Ops:
  7.2 4.7 token_rows.1
  11.9 3.0 collective-permute-start.2
  14.9 1.5 collective-permute-start
  17.1 2.3 constant_dynamic-slice_fusion.4
  24.2 2.0 pack.1
  26.2 19.4 %all-gather = bf16[320,1152]{1,0:T(8,128)(2,1)S(1)} all-gather(bf16[80,1152]{1,0:T(8,128)(2,1)} %pack.1), channel_id=2, replica_groups=mesh['ctx'=8,'wsh'=4] {'wsh'}, dimensions={0}, use_global_device_ids=true | all-gather | bytes 921600 | tf_op jit(solution)/shard_map/all_gather | solution.py:1001
  45.8 1.6 collective-permute-start.5
  48.9 9.9 %collective-permute-done.5 = bf16[272,1152]{1,0:T(8,128)(2,1)S(1)} collective-permute-done((bf16[272,1152]{1,0:T(8,128)(2,1)S(1)}, bf16[272,1152]{1,0:T(8,128)(2,1)S(1)}, u32[]{:S(2)}, u32[]{:S(2)}) %collective-permute-start.5) | collective-permute-done | bytes 626720 | tf_op jit(solution)/shard_map/ppermute | solution.py:309
  58.8 2.5 collective-permute-start.7
  62.7 5.8 %collective-permute-done.6 = bf16[128,1152]{1,0:T(8,128)(2,1)S(1)} collective-permute-done((bf16[128,1152]{1,0:T(8,128)(2,1)S(1)}, bf16[128,1152]{1,0:T(8,128)(2,1)S(1)}, u32[]{:S(2)}, u32[]{:S(2)}) %collective-permute-start.6) | collective-permute-done | bytes 294944 | tf_op jit(solution)/shard_map/ppermute | solution.py:309
  68.6 1.8 pad_maximum_fusion.near_ref
  71.5 1.5 collective-permute-start.10
  73.0 5.0 all-to-all-start
  79.1 4.9 unpack.1
  83.9 1.5 fusion.11
  85.4 1.7 collective-permute-done.9.refs_6_.refs_10_
  88.0 12.2 %norm_project.1 = (bf16[4,384,1472]{2,1,0:T(8,128)(2,1)}, bf16[1,384,768]{2,1,0:T(8,128)(2,1)}, bf16[1,384,768]{2,1,0:T(8,128)(2,1)}, bf16[1,384,768]{2,1,0:T(8,...) custom-call(bf16[192,1472]{1,0:T(8,128)(2,1)} %get-tuple-element.78.refs_0_.refs_4_.x0, ...), custom_call_target="tpu_custom_call" | custom-call | flops 781398848 | bytes 2034892 | tf_op jit(solution)/shard_map/norm_project/pallas_call | solution.py:552
  105.8 14.9 %attention_forward.1 = (f32[3,128,384]{2,1,0:T(8,128)}, f32[3,3,8,128]{3,2,1,0:T(8,128)}) custom-call(s32[1]{0:T(128)} %bitcast.meta_ref.refs_0_, f32[32,128]{1,0:T(8,128)} %get-tuple-element.81.table_ref.refs_1_, f32[3,8,128]{2,1,0:T(8,128)} %get-tuple-element.82.segs_ref.refs_2_, bf16[3,128,384]{2,1,0:T(8,128)(2,1)} %bitcast.132, ...), custom_call_target="tpu_custom_call" | custom-call | flops 120795952 | bytes 1887436 | tf_op jit(solution)/shard_map/attention_forward/pallas_call | solution.py:267
  122.0 14.8 %all-gather.6.cloned.1.call-done = bf16[448,1472]{1,0:T(8,128)(2,1)} async-done(((bf16[112,1472]{1,0:T(8,128)(2,1)}), bf16[448,1472]{1,0:T(8,128)(2,1)}) %all-gather.6.cloned.1.call-update) | async-done | bytes 1318928 | tf_op jit(solution)/shard_map/all_gather | solution.py:1008
  136.9 2.4 collective-permute-start.17
  140.9 6.7 %collective-permute-done.17.refs_3_ = bf16[384,384]{1,0:T(8,128)(2,1)S(1)} collective-permute-done((bf16[384,384]{1,0:T(8,128)(2,1)S(1)}, bf16[384,384]{1,0:T(8,128)(2,1)S(1)}, u32[]{:S(2)}, u32[]{:S(2)}) %collective-permute-start.17) | collective-permute-done | bytes 294944 | tf_op jit(solution)/shard_map/ppermute | solution.py:309
  147.6 5.9 %collective-permute-done.16.refs_2_ = bf16[384,384]{1,0:T(8,128)(2,1)S(1)} collective-permute-done((bf16[384,384]{1,0:T(8,128)(2,1)S(1)}, bf16[384,384]{1,0:T(8,128)(2,1)S(1)}, u32[]{:S(2)}, u32[]{:S(2)}) %collective-permute-start.16) | collective-permute-done | bytes 294944 | tf_op jit(solution)/shard_map/ppermute | solution.py:309
  154.3 10.0 %late_norm.1 = (f32[384,1472]{1,0:T(8,128)}, bf16[4,384,1472]{2,1,0:T(8,128)(2,1)}) custom-call(bf16[384,384]{1,0:T(8,128)(2,1)} %bitcast.122, bf16[384,384]{1,0:T(8,128)(2,1)} %copy-done.30, bf16[384,384]{1,0:T(8,128)(2,1)} %copy-done.29, bf16[384,384]{1,0:T(8,128)(2,1)} %copy-done.28, bf16[192,1472]{1,0:T(8,128)(2,1)} %get-tuple-element.78.refs_0_.refs_4_.x0, ...), custom_call_target="tpu_custom_call" | custom-call | flops 347288384 | bytes 2713190 | tf_op jit(solution)/shard_map/late_norm/pallas_call | solution.py:597
  164.3 2.2 maximum_select_fusion
  166.5 1.7 copy.31
  168.3 41.9 %feed_forward.1 = (bf16[4,384,896]{2,1,0:T(8,128)(2,1)}, bf16[4,384,896]{2,1,0:T(8,128)(2,1)}, bf16[4,384,896]{2,1,0:T(8,128)(2,1)}, bf16[8,192,1472]{2,1,0:T(8,...) custom-call(s32[2]{0:T(128)} %pad_add_fusion.1.spot_ref, ...), custom_call_target="tpu_custom_call" | custom-call | flops 4862036992 | bytes 3391488 | tf_op jit(solution)/shard_map/feed_forward/pallas_call | solution.py:665
  210.2 1.5 collective-permute-start.20
  213.7 32.2 %outer_sums.3 = (bf16[2,736,896]{2,1,0:T(8,128)(2,1)}, bf16[2,736,896]{2,1,0:T(8,128)(2,1)}) custom-call(bf16[4,384,1472]{2,1,0:T(8,128)(2,1)} %get-tuple-element.93.normed_ref.refs_0_, bf16[4,384,896]{2,1,0:T(8,128)(2,1)} %get-tuple-element.108.refs_1_, bf16[4,384,896]{2,1,0:T(8,128)(2,1)} %get-tuple-element.109.refs_2_), custom_call_target="tpu_custom_call" | custom-call | flops 3241358080 | tf_op jit(solution)/shard_map/outer_sums/pallas_call | solution.py:705
  245.9 3.5 fusion.10
  249.8 11.5 %outer_sums.2 = bf16[2,448,1472]{2,1,0:T(8,128)(2,1)} custom-call(bf16[4,384,896]{2,1,0:T(8,128)(2,1)} %get-tuple-element.106.refs_0_, bf16[4,384,1472]{2,1,0:T(8,128)(2,1)} %get-tuple-element.107.refs_1_), custom_call_target="tpu_custom_call" | custom-call | flops 1620679040 | tf_op jit(solution)/shard_map/outer_sums/pallas_call | solution.py:705
  261.3 3.0 select_bitcast_fusion
  265.4 6.9 %middle.1 = (f32[384,1472]{1,0:T(8,128)}, bf16[384,1472]{1,0:T(8,128)(2,1)}, bf16[384,384]{1,0:T(8,128)(2,1)}) custom-call(f32[384,1472]{1,0:T(8,128)} %get-tuple-element.92.after_ref, bf16[2,192,1472]{2,1,0:T(8,128)(2,1)} %get-tuple-element.100.p0, bf16[2,192,1472]{2,1,0:T(8,128)(2,1)} %copy-done.38, bf16[2,192,1472]{2,1,0:T(8,128)(2,1)} %collective-permute-done.21.p2, ...), custom_call_target="tpu_custom_call" | custom-call | flops 99999997952 | tf_op jit(solution)/shard_map/middle/pallas_call | solution.py:754
  272.3 3.9 plus.3
  277.4 3.8 plus.4
  281.2 5.0 all-to-all-start.1
  286.3 20.7 %attention_backward.1 = (bf16[3,128,384]{2,1,0:T(8,128)(2,1)}, bf16[1,3,128,768]{3,2,1,0:T(8,128)(2,1)}, bf16[1,3,128,768]{3,2,1,0:T(8,128)(2,1)}, bf16[1,3,128,...) custom-call(s32[1]{0:T(128)} %bitcast.meta_ref.refs_0_, ...), custom_call_target="tpu_custom_call" | custom-call | flops 301989888 | bytes 4718592 | tf_op jit(solution)/shard_map/attention_backward/pallas_call | solution.py:289
  308.1 1.8 convolution_convert_fusion.refs_10_
  311.9 15.4 %weight_grads.1 = (bf16[384,768]{1,0:T(8,128)(2,1)}, bf16[384,768]{1,0:T(8,128)(2,1)}, bf16[384,768]{1,0:T(8,128)(2,1)}, bf16[384,768]{1,0:T(8,128)(2,1)}, bf16[...) custom-call(s32[2]{0:T(128)} %pad_add_fusion.place_ref, ...), custom_call_target="tpu_custom_call" | custom-call | flops 781398848 | bytes 1356595 | tf_op jit(solution)/shard_map/weight_grads/pallas_call | solution.py:489
  327.5 12.1 %all-to-all-done.1 = bf16[8,192,1472]{2,1,0:T(8,128)(2,1)} async-done(((bf16[8,192,1472]{2,1,0:T(8,128)(2,1)}), bf16[8,192,1472]{2,1,0:T(8,128)(2,1)}, u32[]{:S(2)}, u32[]{:S(2)}) %all-to-all-start.1) | async-done | bytes 4522016 | tf_op jit(solution)/shard_map/all_to_all | solution.py:969
  339.7 3.5 convert_reduce_fusion
  344.5 4.7 plus.5
  349.1 1.6 slice_bitcast_fusion.4
  350.7 1.5 collective-permute-start.34
  352.2 1.5 collective-permute-start.36
  354.3 12.8 %collective-permute-done.34 = bf16[4,64,1152]{2,1,0:T(8,128)(2,1)S(1)} collective-permute-done((bf16[4,64,1152]{2,1,0:T(8,128)(2,1)S(1)}, bf16[4,64,1152]{2,1,0:T(8,128)(2,1)S(1)}, u32[]{:S(2)}, u32[]{:S(2)}) %collective-permute-start.34) | collective-permute-done | bytes 589856 | tf_op jit(solution)/shard_map/ppermute | solution.py:309
  367.1 11.8 %collective-permute-done.36 = bf16[4,64,1152]{2,1,0:T(8,128)(2,1)S(1)} collective-permute-done((bf16[4,64,1152]{2,1,0:T(8,128)(2,1)S(1)}, bf16[4,64,1152]{2,1,0:T(8,128)(2,1)S(1)}, u32[]{:S(2)}, u32[]{:S(2)}) %collective-permute-start.36) | collective-permute-done | bytes 589856 | tf_op jit(solution)/shard_map/ppermute | solution.py:309
  382.4 2.1 collective-permute-start.39
  387.2 1.5 collective-permute-start.32
  391.3 3.7 collective-permute-done.38
  396.5 5.2 %collective-permute-done.30.p1 = bf16[384,768]{1,0:T(8,128)(2,1)S(1)} collective-permute-done((bf16[384,768]{1,0:T(8,128)(2,1)}, bf16[384,768]{1,0:T(8,128)(2,1)S(1)}, u32[]{:S(2)}, u32[]{:S(2)}) %collective-permute-start.30) | collective-permute-done | bytes 589856 | tf_op jit(solution)/shard_map/ppermute | solution.py:309
  401.7 18.6 %collective-permute-done.31.p2 = bf16[384,768]{1,0:T(8,128)(2,1)S(1)} collective-permute-done((bf16[384,768]{1,0:T(8,128)(2,1)}, bf16[384,768]{1,0:T(8,128)(2,1)S(1)}, u32[]{:S(2)}, u32[]{:S(2)}) %collective-permute-start.31) | collective-permute-done | bytes 589856 | tf_op jit(solution)/shard_map/ppermute | solution.py:309
  420.3 2.0 collective-permute-start.41
  422.9 7.8 %collective-permute-done.41 = bf16[64,1152]{1,0:T(8,128)(2,1)S(1)} collective-permute-done((bf16[64,1152]{1,0:T(8,128)(2,1)S(1)}, bf16[64,1152]{1,0:T(8,128)(2,1)S(1)}, u32[]{:S(2)}, u32[]{:S(2)}) %collective-permute-start.41) | collective-permute-done | bytes 147488 | tf_op jit(solution)/shard_map/ppermute | solution.py:309
  432.2 3.8 collective-permute-done.40
  436.0 1.5 collective-permute-start.46
  437.5 2.3 collective-permute-start.45
  442.7 12.2 %collective-permute-done.46.refs_3_ = bf16[368,896]{1,0:T(8,128)(2,1)S(1)} collective-permute-done((bf16[368,896]{1,0:T(8,128)(2,1)}, bf16[368,896]{1,0:T(8,128)(2,1)S(1)}, u32[]{:S(2)}, u32[]{:S(2)}) %collective-permute-start.46) | collective-permute-done | bytes 659488 | tf_op jit(solution)/shard_map/ppermute | solution.py:309
  454.9 9.2 %collective-permute-done.45.refs_2_ = bf16[368,896]{1,0:T(8,128)(2,1)S(1)} collective-permute-done((bf16[368,896]{1,0:T(8,128)(2,1)}, bf16[368,896]{1,0:T(8,128)(2,1)S(1)}, u32[]{:S(2)}, u32[]{:S(2)}) %collective-permute-start.45) | collective-permute-done | bytes 659488 | tf_op jit(solution)/shard_map/ppermute | solution.py:309
  464.6 9.0 %input_gradient.1 = bf16[384,1472]{1,0:T(8,128)(2,1)} custom-call(bf16[384,384]{1,0:T(8,128)(2,1)} %bitcast.131, bf16[384,768]{1,0:T(8,128)(2,1)} %get-tuple-element.124.own_ref, bf16[384,768]{1,0:T(8,128)(2,1)} %copy-done.22, bf16[384,768]{1,0:T(8,128)(2,1)} %copy-done.23, bf16[384,768]{1,0:T(8,128)(2,1)} %copy-done.24, ...), custom_call_target="tpu_custom_call" | custom-call | flops 260466272 | bytes 1356595 | tf_op jit(solution)/shard_map/input_gradient/pallas_call | solution.py:817
  473.6 2.5 copy.36
  477.4 5.2 %join_down.1 = f32[896,1472]{1,0:T(8,128)} custom-call(s32[2]{0:T(128)} %pad_add_fusion.place_ref, bf16[112,1472]{1,0:T(8,128)(2,1)} %reduce-scatter.5.cloned.1.call-done.refs_0_, bf16[112,1472]{1,0:T(8,128)(2,1)} %collective-permute-done.51.refs_1_, bf16[112,1472]{1,0:T(8,128)(2,1)} %collective-permute-done.52.refs_2_, ...), custom_call_target="tpu_custom_call" | custom-call | bytes 197836 | tf_op jit(solution)/shard_map/join_down/pallas_call | solution.py:1121
  482.6 6.0 %copy.37 = f32[896,1472]{0,1:T(8,128)} copy(f32[896,1472]{1,0:T(8,128)} %join_down.1) | data formatting | bytes 10551296
  488.6 3.2 finish_small.1
  494.8 8.4 %spread_columns.1 = (f32[368,3584]{1,0:T(8,128)}, f32[368,3584]{1,0:T(8,128)}, f32[368,128]{1,0:T(8,128)}) custom-call(s32[2]{0:T(128)} %pad_add_fusion.place_ref, bf16[368,896]{1,0:T(8,128)(2,1)} %reduce-scatter.3.cloned.1.call-done.refs_0_, bf16[368,896]{1,0:T(8,128)(2,1)} %collective-permute-done.44.refs_1_, bf16[368,896]{1,0:T(8,128)(2,1)} %copy-done.19, ...), custom_call_target="tpu_custom_call" | custom-call | flops 1055129 | bytes 4220518 | tf_op jit(solution)/shard_map/spread_columns/pallas_call | solution.py:861
  (209 shorter events, 52.6 us)
Async XLA Ops:
  7.2 114.6 %all-gather.4.cloned.1.call-start = ((), (), s32[]{:S(2)}) async-start(), calls=%async_computation.4 | async-start | bytes 3297280 | tf_op jit(solution)/shard_map/all_gather | solution.py:1002
  11.9 33.8 %collective-permute-start.2 = (bf16[192,1472]{1,0:T(8,128)(2,1)}, bf16[192,1472]{1,0:T(8,128)(2,1)}, u32[]{:S(2)}, u32[]{:S(2)}) collective-permute-start(bf16[192,1472]{1,0:T(8,128)(2,1)} %get-tuple-element.78.refs_0_.refs_4_.x0), channel_id=1, source_target_pairs={{0,16},{4,20},{8,24},{12,28},{16,0},{20,4},{24,8},{28,12},{1,17},{... | collective-permute-start | bytes 1695752 | tf_op jit(solution)/shard_map/ppermute | solution.py:309
  14.9 30.9 %collective-permute-start = (bf16[192,1472]{1,0:T(8,128)(2,1)}, bf16[192,1472]{1,0:T(8,128)(2,1)}, u32[]{:S(2)}, u32[]{:S(2)}) collective-permute-start(bf16[192,1472]{1,0:T(8,128)(2,1)} %get-tuple-element.78.refs_0_.refs_4_.x0), channel_id=1, source_target_pairs={{0,8},{4,12},{8,0},{12,4},{16,24},{20,28},{24,16},{28,20},{1,9},{5... | collective-permute-start | bytes 1695752 | tf_op jit(solution)/shard_map/ppermute | solution.py:309
  16.4 29.4 %collective-permute-start.3 = (bf16[192,1472]{1,0:T(8,128)(2,1)}, bf16[192,1472]{1,0:T(8,128)(2,1)}, u32[]{:S(2)}, u32[]{:S(2)}) collective-permute-start(bf16[192,1472]{1,0:T(8,128)(2,1)} %get-tuple-element.79.refs_1_.refs_5_.x1), channel_id=1, source_target_pairs={{0,16},{4,20},{8,24},{12,28},{16,0},{20,4},{24,8},{28,12},{1,17},{... | collective-permute-start | bytes 1695752 | tf_op jit(solution)/shard_map/ppermute | solution.py:309
  16.9 28.9 %collective-permute-start.1 = (bf16[192,1472]{1,0:T(8,128)(2,1)}, bf16[192,1472]{1,0:T(8,128)(2,1)}, u32[]{:S(2)}, u32[]{:S(2)}) collective-permute-start(bf16[192,1472]{1,0:T(8,128)(2,1)} %get-tuple-element.79.refs_1_.refs_5_.x1), channel_id=1, source_target_pairs={{0,8},{4,12},{8,0},{12,4},{16,24},{20,28},{24,16},{28,20},{1,9},{5... | collective-permute-start | bytes 1695752 | tf_op jit(solution)/shard_map/ppermute | solution.py:309
  45.8 12.9 %collective-permute-start.5 = (bf16[272,1152]{1,0:T(8,128)(2,1)S(1)}, bf16[272,1152]{1,0:T(8,128)(2,1)S(1)}, u32[]{:S(2)}, u32[]{:S(2)}) collective-permute-start(bf16[272,1152]{1,0:T(8,128)(2,1)S(1)} %fusion.5), channel_id=1, source_target_pairs={{0,16},{4,20},{8,24},{12,28},{16,0},{20,4},{24,8},{28,12},{1,17},{... | collective-permute-start | bytes 1880072 | tf_op jit(solution)/shard_map/ppermute | solution.py:309
  47.4 14.3 %collective-permute-start.4 = (bf16[272,1152]{1,0:T(8,128)(2,1)S(1)}, bf16[272,1152]{1,0:T(8,128)(2,1)S(1)}, u32[]{:S(2)}, u32[]{:S(2)}) collective-permute-start(bf16[272,1152]{1,0:T(8,128)(2,1)S(1)} %fusion.5), channel_id=1, source_target_pairs={{0,8},{4,12},{8,0},{12,4},{16,24},{20,28},{24,16},{28,20},{1,9},{5... | collective-permute-start | bytes 1880072 | tf_op jit(solution)/shard_map/ppermute | solution.py:309
  58.8 9.8 %collective-permute-start.7 = (bf16[144,1152]{1,0:T(8,128)(2,1)S(1)}, bf16[144,1152]{1,0:T(8,128)(2,1)S(1)}, u32[]{:S(2)}, u32[]{:S(2)}) collective-permute-start(bf16[144,1152]{1,0:T(8,128)(2,1)S(1)} %slice.91), channel_id=1, source_target_pairs={{0,8},{4,12},{8,0},{12,4},{16,24},{20,28},{24,16},{28,20},{1,9},{5... | collective-permute-start | bytes 995336 | tf_op jit(solution)/shard_map/ppermute | solution.py:309
  61.8 6.8 %collective-permute-start.6 = (bf16[128,1152]{1,0:T(8,128)(2,1)S(1)}, bf16[128,1152]{1,0:T(8,128)(2,1)S(1)}, u32[]{:S(2)}, u32[]{:S(2)}) collective-permute-start(bf16[128,1152]{1,0:T(8,128)(2,1)S(1)} %slice.90), channel_id=1, source_target_pairs={{0,16},{4,20},{8,24},{12,28},{16,0},{20,4},{24,8},{28,12},{1,17},{... | collective-permute-start | bytes 884744 | tf_op jit(solution)/shard_map/ppermute | solution.py:309
  70.5 8.6 %collective-permute-start.8 = (bf16[4,272,1152]{2,1,0:T(8,128)(2,1)S(1)}, bf16[4,272,1152]{2,1,0:T(8,128)(2,1)}, u32[]{:S(2)}, u32[]{:S(2)}) collective-permute-start(bf16[4,272,1152]{2,1,0:T(8,128)(2,1)S(1)} %pad_maximum_fusion.near_ref), channel_id=1, source_target_pairs={{0,4},{4,0},{8,12},{12,8},{16,20},{20,16},{24,28},{28,24},{1,5},{5... | collective-permute-start | bytes 7520264 | tf_op jit(solution)/shard_map/ppermute | solution.py:309
  70.6 16.5 %collective-permute-start.9 = (bf16[192,1472]{1,0:T(8,128)(2,1)}, bf16[192,1472]{1,0:T(8,128)(2,1)}, u32[]{:S(2)}, u32[]{:S(2)}) collective-permute-start(bf16[192,1472]{1,0:T(8,128)(2,1)} %collective-permute-done.refs_2_.refs_6_), channel_id=1, source_target_pairs={{0,16},{4,20},{8,24},{12,28},{16,0},{20,4},{24,8},{28,12},{1,17},{... | collective-permute-start | bytes 1695752 | tf_op jit(solution)/shard_map/ppermute | solution.py:309
  71.5 16.5 %collective-permute-start.10 = (bf16[192,1472]{1,0:T(8,128)(2,1)}, bf16[192,1472]{1,0:T(8,128)(2,1)}, u32[]{:S(2)}, u32[]{:S(2)}) collective-permute-start(bf16[192,1472]{1,0:T(8,128)(2,1)} %collective-permute-done.3.refs_5_.refs_9_), channel_id=1, source_target_pairs={{0,8},{4,12},{8,0},{12,4},{16,24},{20,28},{24,16},{28,20},{1,9},{5... | collective-permute-start | bytes 1695752 | tf_op jit(solution)/shard_map/ppermute | solution.py:309
  73.0 95.2 %all-to-all-start = ((bf16[8,192,1472]{2,1,0:T(8,128)(2,1)}), bf16[8,192,1472]{2,1,0:T(8,128)(2,1)}, u32[]{:S(2)}, u32[]{:S(2)}) async-start(bf16[8,192,1472]{2,1,0:T(8,128)(2,1)} %get-tuple-element.94.cot_ref), calls=%async_computation | async-start | bytes 9437184 | tf_op jit(solution)/shard_map/all_to_all | solution.py:969
  78.0 58.8 %all-gather.6.cloned.1.call-start = ((), (), s32[]{:S(2)}) async-start(), calls=%async_computation.5 | async-start | bytes 1720320 | tf_op jit(solution)/shard_map/all_gather | solution.py:1008
  78.8 308.4 %reduce-scatter.5.cloned.1.call-start = ((), (), s32[]{:S(2)}) async-start(), calls=%async_computation.7 | async-start | bytes 1720320 | tf_op jit(solution)/shard_map/reduce_scatter | solution.py:1070
  100.2 2.3 collective-permute-start.11
  100.2 3.0 collective-permute-start.12
  100.7 3.4 collective-permute-start.13
  100.8 4.2 collective-permute-start.14
  121.8 46.4 %collective-permute-start.18 = (bf16[1472,896]{1,0:T(8,128)(2,1)}, bf16[1472,896]{1,0:T(8,128)(2,1)}, u32[]{:S(2)}, u32[]{:S(2)}) collective-permute-start(bf16[1472,896]{1,0:T(8,128)(2,1)} %all-gather.4.cloned.1.call-done.mine_ref), channel_id=1, source_target_pairs={{0,4},{4,0},{8,12},{12,8},{16,20},{20,16},{24,28},{28,24},{1,5},{5... | collective-permute-start | bytes 7913480 | tf_op jit(solution)/shard_map/ppermute | solution.py:309
  136.9 27.5 %collective-permute-start.19 = (bf16[4,112,1472]{2,1,0:T(8,128)(2,1)}, bf16[4,112,1472]{2,1,0:T(8,128)(2,1)}, u32[]{:S(2)}, u32[]{:S(2)}) collective-permute-start(bf16[4,112,1472]{2,1,0:T(8,128)(2,1)} %bitcast.127), channel_id=1, source_target_pairs={{0,4},{4,0},{8,12},{12,8},{16,20},{20,16},{24,28},{28,24},{1,5},{5... | collective-permute-start | bytes 3956744 | tf_op jit(solution)/shard_map/ppermute | solution.py:309
  136.9 10.7 %collective-permute-start.17 = (bf16[384,384]{1,0:T(8,128)(2,1)S(1)}, bf16[384,384]{1,0:T(8,128)(2,1)S(1)}, u32[]{:S(2)}, u32[]{:S(2)}) collective-permute-start(bf16[384,384]{1,0:T(8,128)(2,1)S(1)} %bitcast.119), channel_id=1, source_target_pairs={{0,24},{4,28},{8,16},{12,20},{16,8},{20,12},{24,0},{28,4},{1,25},{... | collective-permute-start | bytes 884744 | tf_op jit(solution)/shard_map/ppermute | solution.py:309
  139.2 14.3 %collective-permute-start.16 = (bf16[384,384]{1,0:T(8,128)(2,1)S(1)}, bf16[384,384]{1,0:T(8,128)(2,1)S(1)}, u32[]{:S(2)}, u32[]{:S(2)}) collective-permute-start(bf16[384,384]{1,0:T(8,128)(2,1)S(1)} %bitcast.120), channel_id=1, source_target_pairs={{0,16},{4,20},{8,24},{12,28},{16,0},{20,4},{24,8},{28,12},{1,17},{... | collective-permute-start | bytes 884744 | tf_op jit(solution)/shard_map/ppermute | solution.py:309
  139.8 13.7 %collective-permute-start.15 = (bf16[384,384]{1,0:T(8,128)(2,1)S(1)}, bf16[384,384]{1,0:T(8,128)(2,1)S(1)}, u32[]{:S(2)}, u32[]{:S(2)}) collective-permute-start(bf16[384,384]{1,0:T(8,128)(2,1)S(1)} %bitcast.121), channel_id=1, source_target_pairs={{0,8},{4,12},{8,0},{12,4},{16,24},{20,28},{24,16},{28,20},{1,9},{5... | collective-permute-start | bytes 884744 | tf_op jit(solution)/shard_map/ppermute | solution.py:309
  210.2 54.2 %collective-permute-start.20 = (bf16[2,192,1472]{2,1,0:T(8,128)(2,1)}, bf16[2,192,1472]{2,1,0:T(8,128)(2,1)S(1)}, u32[]{:S(2)}, u32[]{:S(2)}) collective-permute-start(bf16[2,192,1472]{2,1,0:T(8,128)(2,1)} %get-tuple-element.101), channel_id=1, source_target_pairs={{0,8},{4,12},{8,0},{12,4},{16,24},{20,28},{24,16},{28,20},{1,9},{5... | collective-permute-start | bytes 3391496 | tf_op jit(solution)/shard_map/ppermute | solution.py:309
  211.7 53.2 %collective-permute-start.21 = (bf16[2,192,1472]{2,1,0:T(8,128)(2,1)}, bf16[2,192,1472]{2,1,0:T(8,128)(2,1)}, u32[]{:S(2)}, u32[]{:S(2)}) collective-permute-start(bf16[2,192,1472]{2,1,0:T(8,128)(2,1)} %get-tuple-element.102), channel_id=1, source_target_pairs={{0,16},{4,20},{8,24},{12,28},{16,0},{20,4},{24,8},{28,12},{1,17},{... | collective-permute-start | bytes 3391496 | tf_op jit(solution)/shard_map/ppermute | solution.py:309
  212.5 52.4 %collective-permute-start.22 = (bf16[2,192,1472]{2,1,0:T(8,128)(2,1)}, bf16[2,192,1472]{2,1,0:T(8,128)(2,1)}, u32[]{:S(2)}, u32[]{:S(2)}) collective-permute-start(bf16[2,192,1472]{2,1,0:T(8,128)(2,1)} %get-tuple-element.103), channel_id=1, source_target_pairs={{0,24},{4,28},{8,16},{12,20},{16,8},{20,12},{24,0},{28,4},{1,25},{... | collective-permute-start | bytes 3391496 | tf_op jit(solution)/shard_map/ppermute | solution.py:309
  249.3 23.0 %collective-permute-start.25 = (bf16[1,736,896]{2,1,0:T(8,128)(2,1)}, bf16[1,736,896]{2,1,0:T(8,128)(2,1)}, u32[]{:S(2)}, u32[]{:S(2)}) collective-permute-start(bf16[1,736,896]{2,1,0:T(8,128)(2,1)} %get-tuple-element.168), channel_id=1, source_target_pairs={{0,4},{4,0},{8,12},{12,8},{16,20},{20,16},{24,28},{28,24},{1,5},{5... | collective-permute-start | bytes 3956744 | tf_op jit(solution)/shard_map/ppermute | solution.py:309
  249.3 23.0 %collective-permute-start.24 = (bf16[1,736,896]{2,1,0:T(8,128)(2,1)}, bf16[1,736,896]{2,1,0:T(8,128)(2,1)}, u32[]{:S(2)}, u32[]{:S(2)}) collective-permute-start(bf16[1,736,896]{2,1,0:T(8,128)(2,1)} %get-tuple-element.169), channel_id=1, source_target_pairs={{0,4},{4,0},{8,12},{12,8},{16,20},{20,16},{24,28},{28,24},{1,5},{5... | collective-permute-start | bytes 3956744 | tf_op jit(solution)/shard_map/ppermute | solution.py:309
  264.3 11.9 %collective-permute-start.23 = (bf16[4,112,1472]{2,1,0:T(8,128)(2,1)S(1)}, bf16[4,112,1472]{2,1,0:T(8,128)(2,1)S(1)}, u32[]{:S(2)}, u32[]{:S(2)}) collective-permute-start(bf16[4,112,1472]{2,1,0:T(8,128)(2,1)S(1)} %get-tuple-element.166), channel_id=1, source_target_pairs={{0,4},{4,0},{8,12},{12,8},{16,20},{20,16},{24,28},{28,24},{1,5},{5... | collective-permute-start | bytes 3956744 | tf_op jit(solution)/shard_map/ppermute | solution.py:309
  281.2 58.4 %all-to-all-start.1 = ((bf16[8,192,1472]{2,1,0:T(8,128)(2,1)}), bf16[8,192,1472]{2,1,0:T(8,128)(2,1)}, u32[]{:S(2)}, u32[]{:S(2)}) async-start(bf16[8,192,1472]{2,1,0:T(8,128)(2,1)} %get-tuple-element.99), calls=%async_computation.1 | async-start | bytes 9437184 | tf_op jit(solution)/shard_map/all_to_all | solution.py:969
  286.2 146.0 %reduce-scatter.3.cloned.1.call-start = ((), (), s32[]{:S(2)}) async-start(), calls=%async_computation.6 | async-start | bytes 3297280 | tf_op jit(solution)/shard_map/reduce_scatter | solution.py:1069
  307.0 3.8 collective-permute-start.26
  307.1 3.9 collective-permute-start.27
  307.6 3.5 collective-permute-start.28
  307.6 4.3 collective-permute-start.29
  327.4 17.1 %collective-permute-start.33 = (bf16[4,4,64,1152]{3,2,1,0:T(8,128)(2,1)}, bf16[4,4,64,1152]{3,2,1,0:T(8,128)(2,1)}, u32[]{:S(2)}, u32[]{:S(2)}) collective-permute-start(bf16[4,4,64,1152]{3,2,1,0:T(8,128)(2,1)} %get-tuple-element.130), channel_id=1, source_target_pairs={{0,4},{4,0},{8,12},{12,8},{16,20},{20,16},{24,28},{28,24},{1,5},{5... | collective-permute-start | bytes 7077896 | tf_op jit(solution)/shard_map/ppermute | solution.py:309
  350.7 16.3 %collective-permute-start.34 = (bf16[4,64,1152]{2,1,0:T(8,128)(2,1)S(1)}, bf16[4,64,1152]{2,1,0:T(8,128)(2,1)S(1)}, u32[]{:S(2)}, u32[]{:S(2)}) collective-permute-start(bf16[4,64,1152]{2,1,0:T(8,128)(2,1)S(1)} %get-tuple-element.178), channel_id=1, source_target_pairs={{0,8},{4,12},{8,0},{12,4},{16,24},{20,28},{24,16},{28,20},{1,9},{5... | collective-permute-start | bytes 1769480 | tf_op jit(solution)/shard_map/ppermute | solution.py:309
  352.2 26.6 %collective-permute-start.36 = (bf16[4,64,1152]{2,1,0:T(8,128)(2,1)S(1)}, bf16[4,64,1152]{2,1,0:T(8,128)(2,1)S(1)}, u32[]{:S(2)}, u32[]{:S(2)}) collective-permute-start(bf16[4,64,1152]{2,1,0:T(8,128)(2,1)S(1)} %get-tuple-element.179), channel_id=1, source_target_pairs={{0,24},{4,28},{8,16},{12,20},{16,8},{20,12},{24,0},{28,4},{1,25},{... | collective-permute-start | bytes 1769480 | tf_op jit(solution)/shard_map/ppermute | solution.py:309
  353.7 26.5 %collective-permute-start.35 = (bf16[4,64,1152]{2,1,0:T(8,128)(2,1)S(1)}, bf16[4,64,1152]{2,1,0:T(8,128)(2,1)S(1)}, u32[]{:S(2)}, u32[]{:S(2)}) collective-permute-start(bf16[4,64,1152]{2,1,0:T(8,128)(2,1)S(1)} %get-tuple-element.180), channel_id=1, source_target_pairs={{0,16},{4,20},{8,24},{12,28},{16,0},{20,4},{24,8},{28,12},{1,17},{... | collective-permute-start | bytes 1769480 | tf_op jit(solution)/shard_map/ppermute | solution.py:309
  381.6 5.6 %collective-permute-start.37 = (bf16[64,1152]{1,0:T(8,128)(2,1)S(1)}, bf16[64,1152]{1,0:T(8,128)(2,1)S(1)}, u32[]{:S(2)}, u32[]{:S(2)}) collective-permute-start(bf16[64,1152]{1,0:T(8,128)(2,1)S(1)} %get-tuple-element.181), channel_id=1, source_target_pairs={{0,1},{1,0},{2,3},{3,2},{4,5},{5,4},{6,7},{7,6},{8,9},{9,8},{10,11... | collective-permute-start | bytes 442376 | tf_op jit(solution)/shard_map/ppermute | solution.py:314
  382.4 7.5 %collective-permute-start.39 = (bf16[64,1152]{1,0:T(8,128)(2,1)S(1)}, bf16[64,1152]{1,0:T(8,128)(2,1)S(1)}, u32[]{:S(2)}, u32[]{:S(2)}) collective-permute-start(bf16[64,1152]{1,0:T(8,128)(2,1)S(1)} %get-tuple-element.182), channel_id=1, source_target_pairs={{0,3},{1,2},{2,1},{3,0},{4,7},{5,6},{6,5},{7,4},{8,11},{9,10},{10,... | collective-permute-start | bytes 442376 | tf_op jit(solution)/shard_map/ppermute | solution.py:314
  384.5 10.5 %collective-permute-start.38 = (bf16[64,1152]{1,0:T(8,128)(2,1)S(1)}, bf16[64,1152]{1,0:T(8,128)(2,1)S(1)}, u32[]{:S(2)}, u32[]{:S(2)}) collective-permute-start(bf16[64,1152]{1,0:T(8,128)(2,1)S(1)} %get-tuple-element.183), channel_id=1, source_target_pairs={{0,2},{1,3},{2,0},{3,1},{4,6},{5,7},{6,4},{7,5},{8,10},{9,11},{10,... | collective-permute-start | bytes 442376 | tf_op jit(solution)/shard_map/ppermute | solution.py:314
  385.2 16.5 %collective-permute-start.30 = (bf16[384,768]{1,0:T(8,128)(2,1)}, bf16[384,768]{1,0:T(8,128)(2,1)S(1)}, u32[]{:S(2)}, u32[]{:S(2)}) collective-permute-start(bf16[384,768]{1,0:T(8,128)(2,1)} %get-tuple-element.125), channel_id=1, source_target_pairs={{0,8},{4,12},{8,0},{12,4},{16,24},{20,28},{24,16},{28,20},{1,9},{5... | collective-permute-start | bytes 1769480 | tf_op jit(solution)/shard_map/ppermute | solution.py:309
  385.8 34.5 %collective-permute-start.31 = (bf16[384,768]{1,0:T(8,128)(2,1)}, bf16[384,768]{1,0:T(8,128)(2,1)S(1)}, u32[]{:S(2)}, u32[]{:S(2)}) collective-permute-start(bf16[384,768]{1,0:T(8,128)(2,1)} %get-tuple-element.126), channel_id=1, source_target_pairs={{0,16},{4,20},{8,24},{12,28},{16,0},{20,4},{24,8},{28,12},{1,17},{... | collective-permute-start | bytes 1769480 | tf_op jit(solution)/shard_map/ppermute | solution.py:309
  387.2 33.1 %collective-permute-start.32 = (bf16[384,768]{1,0:T(8,128)(2,1)}, bf16[384,768]{1,0:T(8,128)(2,1)S(1)}, u32[]{:S(2)}, u32[]{:S(2)}) collective-permute-start(bf16[384,768]{1,0:T(8,128)(2,1)} %get-tuple-element.127), channel_id=1, source_target_pairs={{0,24},{4,28},{8,16},{12,20},{16,8},{20,12},{24,0},{28,4},{1,25},{... | collective-permute-start | bytes 1769480 | tf_op jit(solution)/shard_map/ppermute | solution.py:309
  389.9 33.0 %collective-permute-start.53 = (bf16[112,1472]{1,0:T(8,128)(2,1)}, bf16[112,1472]{1,0:T(8,128)(2,1)}, u32[]{:S(2)}, u32[]{:S(2)}) collective-permute-start(bf16[112,1472]{1,0:T(8,128)(2,1)} %reduce-scatter.5.cloned.1.call-done.refs_0_), channel_id=1, source_target_pairs={{0,24},{4,28},{8,16},{12,20},{16,8},{20,12},{24,0},{28,4},{1,25},{... | collective-permute-start | bytes 989192 | tf_op jit(solution)/shard_map/ppermute | solution.py:309
  395.1 27.2 %collective-permute-start.42 = (bf16[64,1152]{1,0:T(8,128)(2,1)S(1)}, bf16[64,1152]{1,0:T(8,128)(2,1)S(1)}, u32[]{:S(2)}, u32[]{:S(2)}) collective-permute-start(bf16[64,1152]{1,0:T(8,128)(2,1)S(1)} %fusion.8), channel_id=1, source_target_pairs={{0,24},{4,28},{8,16},{12,20},{16,8},{20,12},{24,0},{28,4},{1,25},{... | collective-permute-start | bytes 442376 | tf_op jit(solution)/shard_map/ppermute | solution.py:309
  401.7 35.8 %collective-permute-start.54 = (bf16[112,1472]{1,0:T(8,128)(2,1)}, bf16[112,1472]{1,0:T(8,128)(2,1)S(1)}, u32[]{:S(2)}, u32[]{:S(2)}) collective-permute-start(bf16[112,1472]{1,0:T(8,128)(2,1)} %reduce-scatter.5.cloned.1.call-done.refs_0_), channel_id=1, source_target_pairs={{0,4},{4,0},{8,12},{12,8},{16,20},{20,16},{24,28},{28,24},{1,5},{5... | collective-permute-start | bytes 989192 | tf_op jit(solution)/shard_map/ppermute | solution.py:309
  420.3 19.5 %collective-permute-start.52 = (bf16[112,1472]{1,0:T(8,128)(2,1)}, bf16[112,1472]{1,0:T(8,128)(2,1)}, u32[]{:S(2)}, u32[]{:S(2)}) collective-permute-start(bf16[112,1472]{1,0:T(8,128)(2,1)} %reduce-scatter.5.cloned.1.call-done.refs_0_), channel_id=1, source_target_pairs={{0,16},{4,20},{8,24},{12,28},{16,0},{20,4},{24,8},{28,12},{1,17},{... | collective-permute-start | bytes 989192 | tf_op jit(solution)/shard_map/ppermute | solution.py:309
  420.3 10.4 %collective-permute-start.41 = (bf16[64,1152]{1,0:T(8,128)(2,1)S(1)}, bf16[64,1152]{1,0:T(8,128)(2,1)S(1)}, u32[]{:S(2)}, u32[]{:S(2)}) collective-permute-start(bf16[64,1152]{1,0:T(8,128)(2,1)S(1)} %fusion.8), channel_id=1, source_target_pairs={{0,16},{4,20},{8,24},{12,28},{16,0},{20,4},{24,8},{28,12},{1,17},{... | collective-permute-start | bytes 442376 | tf_op jit(solution)/shard_map/ppermute | solution.py:309
  422.3 17.9 %collective-permute-start.51 = (bf16[112,1472]{1,0:T(8,128)(2,1)}, bf16[112,1472]{1,0:T(8,128)(2,1)}, u32[]{:S(2)}, u32[]{:S(2)}) collective-permute-start(bf16[112,1472]{1,0:T(8,128)(2,1)} %reduce-scatter.5.cloned.1.call-done.refs_0_), channel_id=1, source_target_pairs={{0,8},{4,12},{8,0},{12,4},{16,24},{20,28},{24,16},{28,20},{1,9},{5... | collective-permute-start | bytes 989192 | tf_op jit(solution)/shard_map/ppermute | solution.py:309
  422.9 17.3 %collective-permute-start.57 = (bf16[112,1472]{1,0:T(8,128)(2,1)}, bf16[112,1472]{1,0:T(8,128)(2,1)}, u32[]{:S(2)}, u32[]{:S(2)}) collective-permute-start(bf16[112,1472]{1,0:T(8,128)(2,1)} %collective-permute-done.53.refs_3_), channel_id=1, source_target_pairs={{0,4},{4,0},{8,12},{12,8},{16,20},{20,16},{24,28},{28,24},{1,5},{5... | collective-permute-start | bytes 989192 | tf_op jit(solution)/shard_map/ppermute | solution.py:309
  430.7 5.2 %collective-permute-start.40 = (bf16[64,1152]{1,0:T(8,128)(2,1)S(1)}, bf16[64,1152]{1,0:T(8,128)(2,1)}, u32[]{:S(2)}, u32[]{:S(2)}) collective-permute-start(bf16[64,1152]{1,0:T(8,128)(2,1)S(1)} %fusion.8), channel_id=1, source_target_pairs={{0,8},{4,12},{8,0},{12,4},{16,24},{20,28},{24,16},{28,20},{1,9},{5... | collective-permute-start | bytes 442376 | tf_op jit(solution)/shard_map/ppermute | solution.py:309
  436.0 18.9 %collective-permute-start.46 = (bf16[368,896]{1,0:T(8,128)(2,1)}, bf16[368,896]{1,0:T(8,128)(2,1)S(1)}, u32[]{:S(2)}, u32[]{:S(2)}) collective-permute-start(bf16[368,896]{1,0:T(8,128)(2,1)} %reduce-scatter.3.cloned.1.call-done.refs_0_), channel_id=1, source_target_pairs={{0,24},{4,28},{8,16},{12,20},{16,8},{20,12},{24,0},{28,4},{1,25},{... | collective-permute-start | bytes 1978376 | tf_op jit(solution)/shard_map/ppermute | solution.py:309
  437.5 26.6 %collective-permute-start.45 = (bf16[368,896]{1,0:T(8,128)(2,1)}, bf16[368,896]{1,0:T(8,128)(2,1)S(1)}, u32[]{:S(2)}, u32[]{:S(2)}) collective-permute-start(bf16[368,896]{1,0:T(8,128)(2,1)} %reduce-scatter.3.cloned.1.call-done.refs_0_), channel_id=1, source_target_pairs={{0,16},{4,20},{8,24},{12,28},{16,0},{20,4},{24,8},{28,12},{1,17},{... | collective-permute-start | bytes 1978376 | tf_op jit(solution)/shard_map/ppermute | solution.py:309
  439.8 24.5 %collective-permute-start.44 = (bf16[368,896]{1,0:T(8,128)(2,1)}, bf16[368,896]{1,0:T(8,128)(2,1)}, u32[]{:S(2)}, u32[]{:S(2)}) collective-permute-start(bf16[368,896]{1,0:T(8,128)(2,1)} %reduce-scatter.3.cloned.1.call-done.refs_0_), channel_id=1, source_target_pairs={{0,8},{4,12},{8,0},{12,4},{16,24},{20,28},{24,16},{28,20},{1,9},{5... | collective-permute-start | bytes 1978376 | tf_op jit(solution)/shard_map/ppermute | solution.py:309
  440.2 1.9 collective-permute-start.56
  440.2 2.3 collective-permute-start.55
  442.1 46.5 %collective-permute-start.43 = (bf16[4,64,1152]{2,1,0:T(8,128)(2,1)S(1)}, bf16[4,64,1152]{2,1,0:T(8,128)(2,1)}, u32[]{:S(2)}, u32[]{:S(2)}) collective-permute-start(bf16[4,64,1152]{2,1,0:T(8,128)(2,1)S(1)} %pad_maximum_fusion.1.near_ref), channel_id=1, source_target_pairs={{0,4},{4,0},{8,12},{12,8},{16,20},{20,16},{24,28},{28,24},{1,5},{5... | collective-permute-start | bytes 1769480 | tf_op jit(solution)/shard_map/ppermute | solution.py:309
  442.6 52.2 %collective-permute-start.47 = (bf16[368,896]{1,0:T(8,128)(2,1)}, bf16[368,896]{1,0:T(8,128)(2,1)}, u32[]{:S(2)}, u32[]{:S(2)}) collective-permute-start(bf16[368,896]{1,0:T(8,128)(2,1)} %reduce-scatter.3.cloned.1.call-done.refs_0_), channel_id=1, source_target_pairs={{0,4},{4,0},{8,12},{12,8},{16,20},{20,16},{24,28},{28,24},{1,5},{5... | collective-permute-start | bytes 1978376 | tf_op jit(solution)/shard_map/ppermute | solution.py:309
  454.9 39.9 %collective-permute-start.50 = (bf16[368,896]{1,0:T(8,128)(2,1)S(1)}, bf16[368,896]{1,0:T(8,128)(2,1)}, u32[]{:S(2)}, u32[]{:S(2)}) collective-permute-start(bf16[368,896]{1,0:T(8,128)(2,1)S(1)} %collective-permute-done.46.refs_3_), channel_id=1, source_target_pairs={{0,4},{4,0},{8,12},{12,8},{16,20},{20,16},{24,28},{28,24},{1,5},{5... | collective-permute-start | bytes 1978376 | tf_op jit(solution)/shard_map/ppermute | solution.py:309
  464.0 30.7 %collective-permute-start.49 = (bf16[368,896]{1,0:T(8,128)(2,1)S(1)}, bf16[368,896]{1,0:T(8,128)(2,1)}, u32[]{:S(2)}, u32[]{:S(2)}) collective-permute-start(bf16[368,896]{1,0:T(8,128)(2,1)S(1)} %collective-permute-done.45.refs_2_), channel_id=1, source_target_pairs={{0,4},{4,0},{8,12},{12,8},{16,20},{20,16},{24,28},{28,24},{1,5},{5... | collective-permute-start | bytes 1978376 | tf_op jit(solution)/shard_map/ppermute | solution.py:309
  464.3 30.5 %collective-permute-start.48 = (bf16[368,896]{1,0:T(8,128)(2,1)}, bf16[368,896]{1,0:T(8,128)(2,1)}, u32[]{:S(2)}, u32[]{:S(2)}) collective-permute-start(bf16[368,896]{1,0:T(8,128)(2,1)} %collective-permute-done.44.refs_1_), channel_id=1, source_target_pairs={{0,4},{4,0},{8,12},{12,8},{16,20},{20,16},{24,28},{28,24},{1,5},{5... | collective-permute-start | bytes 1978376 | tf_op jit(solution)/shard_map/ppermute | solution.py:309
  (39 other events, 431.3 us)
Sparse Core Ops, SparseCore 0:
  49.0 53.0 all-gather.3
  104.2 32.5 all-gather.5
  281.4 30.5 reduce-scatter.4
  327.7 51.9 reduce-scatter.2

commit v4 on v3

--- a/solution.py
+++ b/solution.py
@@ -478,7 +478,7 @@
                 out_ref[index // 2, gap, :16, :128] = jnp.where(last, rows, out_ref[index // 2, gap, :16, :128])
 
 
-def weight_grads(place, normed, own, got, dq, table, proj, depth, size, wide):
+def weight_grads(place, normed, own, got, dq, table, proj, depth, size, wide, *deps):
     _, tokens, width = normed.shape
     inner = dq.shape[1]
     block = once((1, tokens, 2 * inner))
@@ -487,12 +487,13 @@
     piece = jax.ShapeDtypeStruct((4, depth, span, 3 * inner), BFLOAT)
     kept = pl.BlockSpec((4, depth, span, 3 * inner), lambda g: (0, 0, 0, 0))
     return pl.pallas_call(
-        functools.partial(grad_kernel, depth=depth, size=size, wide=wide),
+        skipping(functools.partial(grad_kernel, depth=depth, size=size, wide=wide), 13, len(deps)),
         grid=(4,),
         in_specs=[
             SMEM_WHOLE, pl.BlockSpec((1, tokens, width), lambda g: (g, 0, 0)), *[block] * 8, once(dq.shape), once(table.shape),
             once(proj.shape),
-        ],
+        ]
+        + [UNREAD] * len(deps),
         out_specs=[*[summed] * 4, kept, kept],
         out_shape=[*[jax.ShapeDtypeStruct((tokens, 2 * inner), BFLOAT)] * 4, piece, piece],
         scratch_shapes=[
@@ -501,7 +502,7 @@
         compiler_params=BIG,
         cost_estimate=cost(flops=18 * tokens * width * inner, bytes_accessed=12 * tokens * width, transcendentals=0),
         name="weight_grads",
-    )(place, normed, *own, *got, dq, table, proj)
+    )(place, normed, *own, *got, dq, table, proj, *deps)
 
 
 def pick_block(refs, step, scratch_ref):
@@ -612,11 +613,21 @@
 
 
 def feed_kernel(
-    spot_ref, normed_ref, cots_ref, mine_ref, other_ref, down_ref,
-    act_ref, dmine_ref, dother_ref, out_ref, l0, l1, l2, l3, cot_ref,
+    spot_ref, normed_ref, cots_ref, mine_ref, other_ref, down_mine, down_other,
+    act_ref, dmine_ref, dother_ref, out_ref, l0, l1, l2, l3, cot_ref, down_ref,
 ):
     is_zero = spot_ref[0] == 0
     tokens = normed_ref.shape[1]
+
+    @pl.when(pl.program_id(0) == 0)
+    def _():
+        depth, piece, _ = down_mine.shape
+        for level in range(depth):
+            first = jnp.where(is_zero, down_mine[level], down_other[level])
+            second = jnp.where(is_zero, down_other[level], down_mine[level])
+            down_ref[2 * level * piece : (2 * level + 1) * piece, :] = first
+            down_ref[(2 * level + 1) * piece : (2 * level + 2) * piece, :] = second
+
     cot = cots_ref[...].reshape(tokens, cots_ref.shape[2])
     cot_ref[0] = cot
     normed = normed_ref[0]
@@ -648,7 +659,7 @@
             late_ref[...] = late.reshape(late_ref.shape)
 
 
-def feed_forward(spot, normed, cots, mine, other, down):
+def feed_forward(spot, normed, cots, mine, other, downs):
     _, tokens, width = normed.shape
     wide = mine.shape[1]
 
@@ -667,8 +678,9 @@
         grid_spec=pltpu.PrefetchScalarGridSpec(
             num_scalar_prefetch=1,
             grid=(4,),
-            in_specs=[block(width), placed, *[once(value.shape) for value in (mine, other, down)]],
+            in_specs=[block(width), placed, *[once(value.shape) for value in (mine, other, *downs)]],
             out_specs=[block(wide), block(wide), block(wide), placed, *[piece] * 4, block(width)],
+            scratch_shapes=[pltpu.VMEM((wide, width), BFLOAT)],
         ),
         out_shape=[shape(wide), shape(wide), shape(wide), sent, *[half] * 4, shape(width)],
         compiler_params=BIG,
@@ -676,44 +688,44 @@
             flops=48 * tokens * width * wide, bytes_accessed=30 * tokens * width, transcendentals=4 * tokens * wide
         ),
         name="feed_forward",
-    )(spot, normed, cots, mine, other, down)
+    )(spot, normed, cots, mine, other, *downs)
 
 
 def outer_kernel(left_ref, *refs):
-    rights, outs, scratch = refs[: len(refs) // 3], refs[len(refs) // 3 : 2 * len(refs) // 3], refs[2 * len(refs) // 3 :]
+    count = len(refs) // 3
+    rights, outs, scratch = refs[:count], refs[count : 2 * count], refs[2 * count :]
     step = pl.program_id(0)
+
+    def rows(ref):
+        return ref[...].reshape(-1, ref.shape[2])
+
+    left = jnp.transpose(rows(left_ref))
     for right_ref, out_ref, acc_ref in zip(rights, outs, scratch):
-        part = tn(left_ref[0], right_ref[0]).reshape(out_ref.shape)
+        part = jnp.dot(left, rows(right_ref), preferred_element_type=FLOAT).reshape(out_ref.shape)
 
         @pl.when(step == 0)
         def _(acc_ref=acc_ref, part=part):
             acc_ref[...] = part
 
-        @pl.when((step > 0) & (step < 3))
-        def _(acc_ref=acc_ref, part=part):
-            acc_ref[...] = acc_ref[...] + part
-
-        @pl.when(step == 3)
+        @pl.when(step == 1)
         def _(acc_ref=acc_ref, out_ref=out_ref, part=part):
             out_ref[...] = (acc_ref[...] + part).astype(BFLOAT)
 
 
-def outer_sums(left, rights, *deps):
+def outer_sums(left, rights):
     _, tokens, width = left.shape
     shapes = [(2, width // 2, right.shape[2]) for right in rights]
-    count = len(rights)
     return pl.pallas_call(
-        skipping(outer_kernel, 1 + count, len(deps)),
-        grid=(4,),
-        in_specs=[pl.BlockSpec((1, tokens, value.shape[2]), lambda g: (g, 0, 0)) for value in (left, *rights)]
-        + [UNREAD] * len(deps),
+        outer_kernel,
+        grid=(2,),
+        in_specs=[pl.BlockSpec((2, tokens, value.shape[2]), lambda g: (g, 0, 0)) for value in (left, *rights)],
         out_specs=[pl.BlockSpec(shape, lambda g: (0, 0, 0)) for shape in shapes],
         out_shape=[jax.ShapeDtypeStruct(shape, BFLOAT) for shape in shapes],
         scratch_shapes=[pltpu.VMEM(shape, FLOAT) for shape in shapes],
         compiler_params=BIG,
-        cost_estimate=cost(flops=8 * tokens * width * 2 * sum(shape[2] for shape in shapes), bytes_accessed=0, transcendentals=0),
+        cost_estimate=cost(flops=16 * tokens * width * sum(shape[2] for shape in shapes), bytes_accessed=0, transcendentals=0),
         name="outer_sums",
-    )(left, *rights, *deps)
+    )(left, *rights)
 
 
 def norm_back(hidden, gain, back):
@@ -745,16 +757,16 @@
     attn_ref[...] = nt(mix, proj_ref[...]).astype(BFLOAT)
 
 
-def middle(after_attn, parts, cots, gain, proj):
+def middle(after_attn, parts, cots, gain, proj, *deps):
     tokens, width = after_attn.shape
     inner = proj.shape[0]
     tile = tokens // 4
     whole = pl.BlockSpec((tile, width), lambda g: (g, 0))
     half = pl.BlockSpec((1, tile, width), lambda g: (g // 2, g % 2, 0))
     return pl.pallas_call(
-        middle_kernel,
+        skipping(middle_kernel, 8, len(deps)),
         grid=(4,),
-        in_specs=[whole, half, half, half, half, half, once(gain.shape), once(proj.shape)],
+        in_specs=[whole, half, half, half, half, half, once(gain.shape), once(proj.shape)] + [UNREAD] * len(deps),
         out_specs=[whole, whole, pl.BlockSpec((tile, inner), lambda g: (g, 0))],
         out_shape=[
             jax.ShapeDtypeStruct((tokens, width), FLOAT),
@@ -764,7 +776,7 @@
         compiler_params=BIG,
         cost_estimate=pl.CostEstimate(flops=10**11, bytes_accessed=0, transcendentals=0),
         name="middle",
-    )(after_attn, *parts, cots, gain, proj)
+    )(after_attn, *parts, cots, gain, proj, *deps)
 
 
 def plus_kernel(left_ref, *refs):
@@ -824,7 +836,7 @@
         out_specs=whole,
         out_shape=jax.ShapeDtypeStruct((tokens, width), BFLOAT),
         compiler_params=BIG,
-        cost_estimate=cost(flops=6 * tokens * width * inner, bytes_accessed=12 * tokens * width, transcendentals=0),
+        cost_estimate=pl.CostEstimate(flops=10**11, bytes_accessed=0, transcendentals=0),
         name="input_gradient",
     )(dq, own, *parts, *inputs, residual, gain, weight)
 
@@ -875,14 +887,43 @@
 
 
 def rows_kernel(place_ref, *refs):
-    nears, fars, out_ref = refs[:4], refs[4:8], refs[8]
+    nears, fars, (out_ref, scratch_ref) = refs[:4], refs[4:8], refs[8:]
     low = place_ref[0]
     size = nears[0].shape[0]
-    for index in range(GROUP):
-        gap = lax.bitwise_xor(low, jnp.int32(index))
-        slot, odd = gap // 2, lax.rem(gap, 2)
-        rows = jnp.where(odd == 0, choose(nears, slot), choose(fars, slot))
-        out_ref[index * size : (index + 1) * size, :] = rows.astype(FLOAT)
+
+    @pl.when(pl.program_id(0) == 0)
+    def _():
+        for index in range(GROUP):
+            gap = lax.bitwise_xor(low, jnp.int32(index))
+            slot, odd = gap // 2, lax.rem(gap, 2)
+            rows = jnp.where(odd == 0, choose(nears, slot), choose(fars, slot))
+            scratch_ref[index * size : (index + 1) * size, :] = rows
+
+    base = pl.multiple_of(pl.program_id(0) * 128, 128)
+    out_ref[...] = jnp.transpose(scratch_ref[pl.ds(base, 128), :].astype(FLOAT))
+
+
+def gathered_kernel(own_ref, *refs):
+    total = own_ref[...].astype(FLOAT)
+    for ref in refs[:-1]:
+        total = total + ref[...].astype(FLOAT)
+    refs[-1][...] = total.astype(BFLOAT)
+
+
+def sum_parts(parts, *deps):
+    return pl.pallas_call(
+        skipping(gathered_kernel, len(parts), len(deps)),
+        in_specs=[VMEM_WHOLE] * len(parts) + [UNREAD] * len(deps),
+        out_specs=VMEM_WHOLE,
+        out_shape=jax.ShapeDtypeStruct(parts[0].shape, BFLOAT),
+        cost_estimate=moved(*parts),
+        name="sum_parts",
+    )(*parts, *deps)
+
+
+def stack_kernel(*refs):
+    for index, ref in enumerate(refs[:-1]):
+        refs[-1][index] = ref[...]
 
 
 def finish_kernel(
@@ -1041,13 +1082,10 @@
     after_attn, normed_late = late_norm(attn, inputs, proj_full, gains[1:2])
     pair_mine = after(pair_mine, attn_low)
     pair_other = swap(pair_mine, 1)
-    down_mine = after(down_mine, attn_low)
+    down_mine = after(down_mine, normed_late)
     down_other = swap(down_mine, 1)
-    down_full = jnp.where(
-        is_zero, jnp.stack((down_mine, down_other), axis=1), jnp.stack((down_other, down_mine), axis=1)
-    ).reshape(depth * part, width)
     activation, back_mine, back_other, out_part, *late_part, cot_all = feed_forward(
-        spot, normed_late, cots, pair_mine, pair_other, down_full
+        spot, normed_late, cots, pair_mine, pair_other, (down_mine, down_other)
     )
 
     def flat(value):
@@ -1059,20 +1097,17 @@
     late_parts = [late_part[0]] + [swap(late_part[index], 2 * index) for index in range(1, 4)]
     other_grad, mine_grad = outer_sums(normed_late, (back_other, back_mine))
     other_got = [swap(other_grad[index : index + 1], 1) for index in range(2)]
-    down_grad = outer_sums(activation, (cot_all,))[0].reshape(depth, 2, piece, width)
+    down_whole = outer_sums(activation, (cot_all,))[0]
+    down_grad = down_whole.reshape(depth, 2, piece, width)
     down_keep = jnp.where(is_zero, down_grad[:, 0], down_grad[:, 1])
     down_send = jnp.where(is_zero, down_grad[:, 1], down_grad[:, 0])
     down_got = swap(down_send, 1)
-    residual_grad, mix_low, attn_grad = middle(after_attn, late_parts, own_cots, gains[1:2], proj_full)
-    pair_sum = plus(mine_grad, other_got, mix_low).reshape(width, 2 * piece * depth)
-    down_sum = plus(down_keep, [down_got], pair_sum).reshape(depth * piece, width)
-    pair_own = over_groups(lax.psum_scatter(pair_sum, "wsh", scatter_dimension=0, tiled=True))
-    down_own = over_groups(lax.psum_scatter(down_sum, "wsh", scatter_dimension=0, tiled=True))
+    residual_grad, mix_low, attn_grad = middle(
+        after_attn, late_parts, own_cots, gains[1:2], proj_full, down_whole, mine_grad
+    )
     attn_grad = attn_grad.reshape(seqs, rows, inner)
     proj_grad = tn(attn_low, jnp.pad(mix_low, ((0, 0), (0, 4 * wide - width)))).astype(BFLOAT)
-    dq, *dkv, table_part = attention_backward(
-        meta, table, segs, queries, kv, attn_grad, attention, lse, down_sum
-    )
+    dq, *dkv, table_part = attention_backward(meta, table, segs, queries, kv, attn_grad, attention, lse)
 
     def owned(value):
         if groups > 1:
@@ -1082,23 +1117,47 @@
     dkv = [owned(value) for value in dkv]
     dkv_got = [swap(value, 1) for value in dkv[4:]]
     dq = dq.reshape(tokens, inner)
+    pair_sum = plus(mine_grad, other_got, mix_low).reshape(width, 2 * piece * depth)
     table_sum = jnp.transpose(jnp.sum(table_part, axis=-1).reshape(heads, BUCKETS)).reshape(depth, buckets, heads)
     table_sum = jnp.pad(table_sum, ((0, 0), (0, 16 - buckets), (0, 128 - heads))).reshape(depth * 16, 128).astype(BFLOAT)
-    *dkv_four, keep, send = weight_grads(place, normed, dkv[:4], dkv_got, dq, table_sum, proj_grad, depth, size, wide)
-    out_parts = exchange(out_part).astype(FLOAT).reshape(4, tokens, width)
+    *dkv_four, keep, send = weight_grads(place, normed, dkv[:4], dkv_got, dq, table_sum, proj_grad, depth, size, wide, pair_sum)
+    down_sum = plus(down_keep, [down_got], keep).reshape(depth * piece, width)
+    pair_own = over_groups(lax.psum_scatter(pair_sum, "wsh", scatter_dimension=0, tiled=True))
+    down_own = over_groups(lax.psum_scatter(down_sum, "wsh", scatter_dimension=0, tiled=True))
+    out_parts = exchange(after(out_part, attn_grad)).astype(FLOAT).reshape(4, tokens, width)
     result = (after_attn + jnp.sum(out_parts, axis=0)).astype(BFLOAT)
 
     blocks = plus(keep, [swap(send, 1)], result)
     dkv_parts = [swap(dkv_four[index], 2 * index) for index in range(1, 4)]
-    total = blocks[0].astype(FLOAT)
-    for index in range(1, 4):
-        total = total + swap(blocks[index], 2 * index).astype(FLOAT)
-    levels = total.astype(BFLOAT)
-    total = levels[0].astype(FLOAT)
-    for gap in range(1, depth):
-        total = total + swap_depth(levels[gap], gap).astype(FLOAT)
     input_grad = last(dq, dkv_four[0], dkv_parts, (x_near, x_far), residual_grad, gains[0:1], qkv_full)
-    grads_near = jnp.stack(gather_direct(over_groups(total.astype(BFLOAT))))
+    levels = sum_parts([blocks[0]] + [swap(blocks[index], 2 * index) for index in range(1, 4)], input_grad, pair_own)
+    pair_near = gather_direct(after(pair_own, levels))
+    down_near = gather_direct(after(down_own, levels))
+    total = sum_parts(
+        [levels[0]] + [swap_depth(levels[gap], gap) for gap in range(1, depth)], *pair_near[1:]
+    )
+    grads_near = gather_direct(over_groups(total))
+    pair_far, down_far = [[swap(value, 1) for value in values] for values in (pair_near, down_near)]
+    gate_out, up_out, late_sum = spread(place, pair_near, pair_far, gate_weight, up_weight, depth, part)
+    down_out = pl.pallas_call(
+        rows_kernel,
+        grid=(slab // 128,),
+        in_specs=[SMEM_WHOLE] + [once((piece, width))] * 8,
+        out_specs=pl.BlockSpec((width, 128), lambda g: (0, g)),
+        out_shape=jax.ShapeDtypeStruct((width, slab), FLOAT),
+        scratch_shapes=[pltpu.VMEM((slab, width), BFLOAT)],
+        compiler_params=BIG,
+        cost_estimate=moved(down_own, down_own, down_own),
+        name="join_down",
+    )(place, *down_near, *down_far)
+    grads_near = pl.pallas_call(
+        skipping(stack_kernel, 4, 1),
+        in_specs=[VMEM_WHOLE] * 4 + [UNREAD],
+        out_specs=VMEM_WHOLE,
+        out_shape=jax.ShapeDtypeStruct((4, *total.shape), BFLOAT),
+        cost_estimate=moved(total, total),
+        name="stack_small",
+    )(*grads_near, late_sum)
     grads_far = swap(grads_near, 1)
     column = jax.ShapeDtypeStruct((shard, inner), FLOAT)
     query_out, key_out, value_out, proj_out, early_sum, table_rows = pl.pallas_call(
@@ -1114,19 +1173,6 @@
         name="finish_small",
     )(place, grads_near, grads_far, query_weight, key_weight, value_weight)
 
-    pair_own, down_own = after(pair_own, levels), after(down_own, levels)
-    pair_near, down_near = gather_direct(pair_own), gather_direct(down_own)
-    pair_far, down_far = [[swap(value, 1) for value in values] for values in (pair_near, down_near)]
-    gate_out, up_out, late_sum = spread(place, pair_near, pair_far, gate_weight, up_weight, depth, part)
-    down_out = pl.pallas_call(
-        rows_kernel,
-        in_specs=[SMEM_WHOLE] + [VMEM_WHOLE] * 8,
-        out_specs=VMEM_WHOLE,
-        out_shape=jax.ShapeDtypeStruct((slab, width), FLOAT),
-        compiler_params=BIG,
-        cost_estimate=moved(down_own, down_own, down_own),
-        name="join_down",
-    )(place, *down_near, *down_far)
     return (
         result.reshape(seqs, rows, width),
         input_grad.reshape(seqs, rows, width),
@@ -1136,7 +1182,7 @@
         proj_out,
         gate_out,
         up_out,
-        down_out,
+        jnp.transpose(down_out),
         early_sum[:, 0] / gain_early.astype(FLOAT),
         late_sum[:, 0] / gain_late.astype(FLOAT),
         table_rows[:buckets, :heads],

time: 516 us -> 497 us (0.963)
  waiting for transfers between devices: 152 us -> 135 us
  other arithmetic: 19.4 us -> 14 us
    all_gather x1, waiting for transfers between devices: 14.8 us -> 0.01 us  [on_device(): lax.all_gather(after(down_slice, near), 'wsh', axis=0, tiled=True)]
    all_to_all x2, waiting for transfers between devices: 12.1 us -> 0.5 us  [exchange(): lax.all_to_all(blocks, 'ctx', split_axis=0, concat_axis=0, tiled=True, ax...]
    ppermute x3, waiting for transfers between devices: 4.95 us -> 16.1 us  [swap_depth(): lax.ppermute(value, 'wsh', [(source, source ^ bit) for source in range(co...]
    unnamed x81 -> x104, local copies, waits for them, and re-layouts: 13.2 us -> 11.5 us
    pallas_call x5 -> x8, Pallas kernels: 71.2 us -> 72.6 us  [the longest x2 36.4 us: outer_sums(): pl.pallas_call(outer_kernel, grid=(2,), in_specs=[pl.BlockSpec((2, tokens...]
  transfers between devices with their start and end apart: 64 -> 64, of which waited for: 31 -> 28; matrix products, arithmetic and copies ran while one was open for 9% -> 7% of each run, Pallas kernels for 31% -> 33%
where the time goes in v4:
time: 497 us; the launch traced here: 488 us
  Pallas kernels  217 us (44%)
  waiting for transfers between devices  135 us (27%)
  starting transfers between devices  57.6 us (12%)
  local copies, waits for them, and re-layouts  28.5 us (6%)
  blocking collectives  19.4 us (4%)
  between operations  14.6 us (3%)
  other arithmetic  14 us (3%)
    ppermute x55, waiting for transfers between devices, swap(): lax.ppermute(value, 'ctx', [(source, source ^ bit) for source in range(co...  118 us
    ppermute x55, starting transfers between devices, swap(): lax.ppermute(value, 'ctx', [(source, source ^ bit) for source in range(co...  44.4 us
    pallas_call x1, Pallas kernels, feed_forward(): pl.pallas_call(feed_kernel, grid_spec=pltpu.PrefetchScalarGridSpec(num_sc...  42.1 us
    pallas_call x2, Pallas kernels, outer_sums(): pl.pallas_call(outer_kernel, grid=(2,), in_specs=[pl.BlockSpec((2, tokens...  36.4 us
    pallas_call x1, Pallas kernels, attention_backward(): pl.pallas_call(skipping(functools.partial(backward_kernel, rows=rows, cou...  21 us
    all_gather x1, blocking collectives, on_device(): packed = lax.all_gather(packed, 'wsh', axis=0)  19.4 us
    ppermute x3, waiting for transfers between devices, swap_depth(): lax.ppermute(value, 'wsh', [(source, source ^ bit) for source in range(co...  16.1 us
    pallas_call x1, Pallas kernels, weight_grads(): pl.pallas_call(skipping(functools.partial(grad_kernel, depth=depth, size=...  15.6 us
  transfers between devices with their start and end apart: 64, of which 28 were waited for; matrix products, arithmetic and copies ran while one was open for 7% of the time, Pallas kernels for 33%

profile of v4, /device:TPU:0, one launch (start us, length us, event | category | flops | bytes accessed | tf_op | source)
XLA Modules:
  0.0 487.7 jit_solution(12260905729864146496)
XLA Ops:
  7.2 4.7 token_rows.1
  11.9 3.0 collective-permute-start.2
  14.9 1.5 collective-permute-start
  17.1 2.3 constant_dynamic-slice_fusion.4
  24.2 2.0 pack.1
  26.1 19.4 %all-gather = bf16[320,1152]{1,0:T(8,128)(2,1)S(1)} all-gather(bf16[80,1152]{1,0:T(8,128)(2,1)} %pack.1), channel_id=2, replica_groups=mesh['ctx'=8,'wsh'=4] {'wsh'}, dimensions={0}, use_global_device_ids=true | all-gather | bytes 921600 | tf_op jit(solution)/shard_map/all_gather | solution.py:1042
  45.8 1.6 collective-permute-start.5
  48.8 9.9 %collective-permute-done.5 = bf16[272,1152]{1,0:T(8,128)(2,1)S(1)} collective-permute-done((bf16[272,1152]{1,0:T(8,128)(2,1)S(1)}, bf16[272,1152]{1,0:T(8,128)(2,1)S(1)}, u32[]{:S(2)}, u32[]{:S(2)}) %collective-permute-start.5) | collective-permute-done | bytes 626720 | tf_op jit(solution)/shard_map/ppermute | solution.py:309
  58.7 2.5 collective-permute-start.7
  62.7 5.7 %collective-permute-done.6 = bf16[128,1152]{1,0:T(8,128)(2,1)S(1)} collective-permute-done((bf16[128,1152]{1,0:T(8,128)(2,1)S(1)}, bf16[128,1152]{1,0:T(8,128)(2,1)S(1)}, u32[]{:S(2)}, u32[]{:S(2)}) %collective-permute-start.6) | collective-permute-done | bytes 294944 | tf_op jit(solution)/shard_map/ppermute | solution.py:309
  68.5 1.8 pad_maximum_fusion.near_ref
  71.5 1.5 collective-permute-start.10
  73.0 4.9 %all-to-all-start = ((bf16[8,192,1472]{2,1,0:T(8,128)(2,1)}), bf16[8,192,1472]{2,1,0:T(8,128)(2,1)}, u32[]{:S(2)}, u32[]{:S(2)}) async-start(bf16[8,192,1472]{2,1,0:T(8,128)(2,1)} %get-tuple-element.95.refs_5_), calls=%async_computation | async-start | bytes 9437184 | tf_op jit(solution)/shard_map/all_to_all | solution.py:1010
  78.8 4.8 unpack.1
  83.6 1.5 fusion.5
  85.1 1.9 collective-permute-done.9.refs_6_.refs_10_
  88.0 12.2 %norm_project.1 = (bf16[4,384,1472]{2,1,0:T(8,128)(2,1)}, bf16[1,384,768]{2,1,0:T(8,128)(2,1)}, bf16[1,384,768]{2,1,0:T(8,128)(2,1)}, bf16[1,384,768]{2,1,0:T(8,...) custom-call(bf16[192,1472]{1,0:T(8,128)(2,1)} %get-tuple-element.79.refs_0_.refs_4_.x0, ...), custom_call_target="tpu_custom_call" | custom-call | flops 781398848 | bytes 2034892 | tf_op jit(solution)/shard_map/norm_project/pallas_call | solution.py:553
  105.8 14.9 %attention_forward.1 = (f32[3,128,384]{2,1,0:T(8,128)}, f32[3,3,8,128]{3,2,1,0:T(8,128)}) custom-call(s32[1]{0:T(128)} %bitcast.meta_ref.refs_0_, f32[32,128]{1,0:T(8,128)} %get-tuple-element.82.table_ref.refs_1_, f32[3,8,128]{2,1,0:T(8,128)} %get-tuple-element.83.segs_ref.refs_2_, bf16[3,128,384]{2,1,0:T(8,128)(2,1)} %bitcast.115, ...), custom_call_target="tpu_custom_call" | custom-call | flops 120795952 | bytes 1887436 | tf_op jit(solution)/shard_map/attention_forward/pallas_call | solution.py:267
  122.0 1.8 collective-permute-start.17
  125.5 19.8 %collective-permute-done.17.refs_3_ = bf16[384,384]{1,0:T(8,128)(2,1)S(1)} collective-permute-done((bf16[384,384]{1,0:T(8,128)(2,1)S(1)}, bf16[384,384]{1,0:T(8,128)(2,1)S(1)}, u32[]{:S(2)}, u32[]{:S(2)}) %collective-permute-start.17) | collective-permute-done | bytes 294944 | tf_op jit(solution)/shard_map/ppermute | solution.py:309
  145.3 4.3 collective-permute-done.16.refs_2_
  151.1 9.9 %late_norm.1 = (f32[384,1472]{1,0:T(8,128)}, bf16[4,384,1472]{2,1,0:T(8,128)(2,1)}) custom-call(bf16[384,384]{1,0:T(8,128)(2,1)} %bitcast.109, bf16[384,384]{1,0:T(8,128)(2,1)} %copy-done.35, bf16[384,384]{1,0:T(8,128)(2,1)} %copy-done.34, bf16[384,384]{1,0:T(8,128)(2,1)} %copy-done.33, bf16[192,1472]{1,0:T(8,128)(2,1)} %get-tuple-element.79.refs_0_.refs_4_.x0, ...), custom_call_target="tpu_custom_call" | custom-call | flops 347288384 | bytes 2713190 | tf_op jit(solution)/shard_map/late_norm/pallas_call | solution.py:598
  161.6 2.7 collective-permute-done.19.down_other
  165.5 42.1 %feed_forward.1 = (bf16[4,384,896]{2,1,0:T(8,128)(2,1)}, bf16[4,384,896]{2,1,0:T(8,128)(2,1)}, bf16[4,384,896]{2,1,0:T(8,128)(2,1)}, bf16[8,192,1472]{2,1,0:T(8,...) custom-call(s32[2]{0:T(128)} %pad_add_fusion.1.spot_ref, ...), custom_call_target="tpu_custom_call" | custom-call | flops 4862036992 | bytes 3391488 | tf_op jit(solution)/shard_map/feed_forward/pallas_call | solution.py:676
  207.6 1.9 collective-permute-start.20
  211.1 27.2 %outer_sums.3 = (bf16[2,736,896]{2,1,0:T(8,128)(2,1)}, bf16[2,736,896]{2,1,0:T(8,128)(2,1)}) custom-call(bf16[4,384,1472]{2,1,0:T(8,128)(2,1)} %get-tuple-element.94.normed_ref.left_ref, bf16[4,384,896]{2,1,0:T(8,128)(2,1)} %get-tuple-element.107.refs_0_, bf16[4,384,896]{2,1,0:T(8,128)(2,1)} %get-tuple-element.108.refs_1_), custom_call_target="tpu_custom_call" | custom-call | flops 3241358080 | tf_op jit(solution)/shard_map/outer_sums/pallas_call | solution.py:718
  238.4 1.9 fusion.4
  240.9 9.1 %outer_sums.2.refs_8_ = bf16[2,448,1472]{2,1,0:T(8,128)(2,1)} custom-call(bf16[4,384,896]{2,1,0:T(8,128)(2,1)} %get-tuple-element.105.left_ref, bf16[4,384,1472]{2,1,0:T(8,128)(2,1)} %get-tuple-element.106.refs_0_), custom_call_target="tpu_custom_call" | custom-call | flops 1620679040 | tf_op jit(solution)/shard_map/outer_sums/pallas_call | solution.py:718
  250.0 12.8 %collective-permute-done.21.refs_3_ = bf16[2,192,1472]{2,1,0:T(8,128)(2,1)} collective-permute-done((bf16[2,192,1472]{2,1,0:T(8,128)(2,1)}, bf16[2,192,1472]{2,1,0:T(8,128)(2,1)}, u32[]{:S(2)}, u32[]{:S(2)}) %collective-permute-start.21) | collective-permute-done | bytes 1130528 | tf_op jit(solution)/shard_map/ppermute | solution.py:309
  262.8 6.9 %middle.1 = (f32[384,1472]{1,0:T(8,128)}, bf16[384,1472]{1,0:T(8,128)(2,1)}, bf16[384,384]{1,0:T(8,128)(2,1)}) custom-call(f32[384,1472]{1,0:T(8,128)} %get-tuple-element.93.refs_0_, bf16[2,192,1472]{2,1,0:T(8,128)(2,1)} %get-tuple-element.101.refs_1_, bf16[2,192,1472]{2,1,0:T(8,128)(2,1)} %collective-permute-done.20.refs_2_, ...), custom_call_target="tpu_custom_call" | custom-call | flops 99999997952 | tf_op jit(solution)/shard_map/middle/pallas_call | solution.py:766
  270.8 3.9 plus.3
  274.8 4.9 %all-to-all-start.1 = ((bf16[8,192,1472]{2,1,0:T(8,128)(2,1)}), bf16[8,192,1472]{2,1,0:T(8,128)(2,1)}, u32[]{:S(2)}, u32[]{:S(2)}) async-start(bf16[8,192,1472]{2,1,0:T(8,128)(2,1)} %get-tuple-element.111), calls=%async_computation.1 | async-start | bytes 9437184 | tf_op jit(solution)/shard_map/all_to_all | solution.py:1010
  279.8 21.0 %attention_backward.1 = (bf16[3,128,384]{2,1,0:T(8,128)(2,1)}, bf16[1,3,128,768]{3,2,1,0:T(8,128)(2,1)}, bf16[1,3,128,768]{3,2,1,0:T(8,128)(2,1)}, bf16[1,3,128,...) custom-call(s32[1]{0:T(128)} %bitcast.meta_ref.refs_0_, ...), custom_call_target="tpu_custom_call" | custom-call | flops 301989888 | bytes 4718592 | tf_op jit(solution)/shard_map/attention_backward/pallas_call | solution.py:289
  303.6 1.8 convolution_convert_fusion.refs_12_
  306.6 15.6 %weight_grads.1 = (bf16[384,768]{1,0:T(8,128)(2,1)}, bf16[384,768]{1,0:T(8,128)(2,1)}, bf16[384,768]{1,0:T(8,128)(2,1)}, bf16[384,768]{1,0:T(8,128)(2,1)}, bf16[...) custom-call(s32[2]{0:T(128)} %pad_add_fusion.place_ref.refs_0_, ...), custom_call_target="tpu_custom_call" | custom-call | flops 781398848 | bytes 1356595 | tf_op jit(solution)/shard_map/weight_grads/pallas_call | solution.py:489
  324.0 1.8 collective-permute-start.29
  329.8 3.8 plus.5
  334.1 3.5 convert_reduce_fusion
  339.0 4.5 plus.4
  343.5 2.7 slice_bitcast_fusion.2
  346.1 2.3 collective-permute-start.35
  349.6 10.8 %collective-permute-done.31.p3 = bf16[384,768]{1,0:T(8,128)(2,1)} collective-permute-done((bf16[384,768]{1,0:T(8,128)(2,1)S(1)}, bf16[384,768]{1,0:T(8,128)(2,1)}, u32[]{:S(2)}, u32[]{:S(2)}) %collective-permute-start.31) | collective-permute-done | bytes 589856 | tf_op jit(solution)/shard_map/ppermute | solution.py:309
  360.4 9.2 %input_gradient.1.refs_4_ = bf16[384,1472]{1,0:T(8,128)(2,1)} custom-call(bf16[384,384]{1,0:T(8,128)(2,1)} %bitcast.125, bf16[384,768]{1,0:T(8,128)(2,1)} %get-tuple-element.126.own_ref, bf16[384,768]{1,0:T(8,128)(2,1)} %collective-permute-done.29.p1, bf16[384,768]{1,0:T(8,128)(2,1)} %collective-permute-done.30.p2, ...), custom_call_target="tpu_custom_call" | custom-call | flops 99999997952 | tf_op jit(solution)/shard_map/input_gradient/pallas_call | solution.py:829
  369.7 3.2 collective-permute-done.35.refs_3_
  372.9 10.3 %collective-permute-done.34.refs_2_ = bf16[4,64,1152]{2,1,0:T(8,128)(2,1)S(1)} collective-permute-done((bf16[4,64,1152]{2,1,0:T(8,128)(2,1)S(1)}, bf16[4,64,1152]{2,1,0:T(8,128)(2,1)S(1)}, u32[]{:S(2)}, u32[]{:S(2)}) %collective-permute-start.34) | collective-permute-done | bytes 589856 | tf_op jit(solution)/shard_map/ppermute | solution.py:309
  384.2 2.8 sum_parts.2
  387.5 1.5 collective-permute-start.40
  390.5 1.8 slice_bitcast_fusion.6
  392.3 3.2 collective-permute-start.38
  395.5 5.2 %collective-permute-done.38.refs_3_ = bf16[64,1152]{1,0:T(8,128)(2,1)S(1)} collective-permute-done((bf16[64,1152]{1,0:T(8,128)(2,1)S(1)}, bf16[64,1152]{1,0:T(8,128)(2,1)S(1)}, u32[]{:S(2)}, u32[]{:S(2)}) %collective-permute-start.38) | collective-permute-done | bytes 147488 | tf_op jit(solution)/shard_map/ppermute | solution.py:314
  401.2 5.8 %collective-permute-done.37.refs_2_ = bf16[64,1152]{1,0:T(8,128)(2,1)S(1)} collective-permute-done((bf16[64,1152]{1,0:T(8,128)(2,1)S(1)}, bf16[64,1152]{1,0:T(8,128)(2,1)S(1)}, u32[]{:S(2)}, u32[]{:S(2)}) %collective-permute-start.37) | collective-permute-done | bytes 147488 | tf_op jit(solution)/shard_map/ppermute | solution.py:314
  407.0 5.1 %collective-permute-done.36.refs_1_ = bf16[64,1152]{1,0:T(8,128)(2,1)S(1)} collective-permute-done((bf16[64,1152]{1,0:T(8,128)(2,1)S(1)}, bf16[64,1152]{1,0:T(8,128)(2,1)S(1)}, u32[]{:S(2)}, u32[]{:S(2)}) %collective-permute-start.36) | collective-permute-done | bytes 147488 | tf_op jit(solution)/shard_map/ppermute | solution.py:314
  412.8 13.5 %collective-permute-done.53.refs_3_ = bf16[112,1472]{1,0:T(8,128)(2,1)S(1)} collective-permute-done((bf16[112,1472]{1,0:T(8,128)(2,1)}, bf16[112,1472]{1,0:T(8,128)(2,1)S(1)}, u32[]{:S(2)}, u32[]{:S(2)}) %collective-permute-start.53) | collective-permute-done | bytes 329760 | tf_op jit(solution)/shard_map/ppermute | solution.py:309
  427.4 5.6 %collective-permute-done.52.refs_2_ = bf16[112,1472]{1,0:T(8,128)(2,1)} collective-permute-done((bf16[112,1472]{1,0:T(8,128)(2,1)}, bf16[112,1472]{1,0:T(8,128)(2,1)}, u32[]{:S(2)}, u32[]{:S(2)}) %collective-permute-start.52) | collective-permute-done | bytes 329760 | tf_op jit(solution)/shard_map/ppermute | solution.py:309
  434.2 1.9 sum_parts.3.refs_0_
  436.1 6.7 %collective-permute-done.51.refs_1_ = bf16[112,1472]{1,0:T(8,128)(2,1)} collective-permute-done((bf16[112,1472]{1,0:T(8,128)(2,1)}, bf16[112,1472]{1,0:T(8,128)(2,1)}, u32[]{:S(2)}, u32[]{:S(2)}) %collective-permute-start.51) | collective-permute-done | bytes 329760 | tf_op jit(solution)/shard_map/ppermute | solution.py:309
  442.7 1.7 collective-permute-start.44
  444.4 1.5 collective-permute-start.43
  446.0 3.1 collective-permute-done.44.refs_3_
  449.1 1.7 collective-permute-start.42
  452.4 8.2 %spread_columns.1 = (f32[368,3584]{1,0:T(8,128)}, f32[368,3584]{1,0:T(8,128)}, f32[368,128]{1,0:T(8,128)}) custom-call(s32[2]{0:T(128)} %pad_add_fusion.place_ref.refs_0_, bf16[368,896]{1,0:T(8,128)(2,1)} %reduce-scatter.3.cloned.1.call-done.refs_5_.refs_0_, bf16[368,896]{1,0:T(8,128)(2,1)} %copy-done.16, bf16[368,896]{1,0:T(8,128)(2,1)} %copy-done.15, ...), custom_call_target="tpu_custom_call" | custom-call | flops 1055129 | bytes 4220518 | tf_op jit(solution)/shard_map/spread_columns/pallas_call | solution.py:873
  461.3 2.0 stack_small.1.near_ref
  466.2 7.1 %join_down.1 = f32[1472,896]{1,0:T(8,128)} custom-call(s32[2]{0:T(128)} %pad_add_fusion.place_ref.refs_0_, bf16[112,1472]{1,0:T(8,128)(2,1)} %reduce-scatter.5.cloned.1.call-done.refs_0_, bf16[112,1472]{1,0:T(8,128)(2,1)} %collective-permute-done.51.refs_1_, bf16[112,1472]{1,0:T(8,128)(2,1)} %collective-permute-done.52.refs_2_, ...), custom_call_target="tpu_custom_call" | custom-call | bytes 197836 | tf_op jit(solution)/shard_map/join_down/pallas_call | solution.py:1142
  474.9 3.2 finish_small.1
  (230 shorter events, 55.6 us)
Async XLA Ops:
  7.2 114.6 %all-gather.4.cloned.1.call-start = ((), (), s32[]{:S(2)}) async-start(), calls=%async_computation.4 | async-start | bytes 3297280 | tf_op jit(solution)/shard_map/all_gather | solution.py:1043
  11.9 33.8 %collective-permute-start.2 = (bf16[192,1472]{1,0:T(8,128)(2,1)}, bf16[192,1472]{1,0:T(8,128)(2,1)}, u32[]{:S(2)}, u32[]{:S(2)}) collective-permute-start(bf16[192,1472]{1,0:T(8,128)(2,1)} %get-tuple-element.79.refs_0_.refs_4_.x0), channel_id=1, source_target_pairs={{0,16},{4,20},{8,24},{12,28},{16,0},{20,4},{24,8},{28,12},{1,17},{... | collective-permute-start | bytes 1695752 | tf_op jit(solution)/shard_map/ppermute | solution.py:309
  14.9 30.8 %collective-permute-start = (bf16[192,1472]{1,0:T(8,128)(2,1)}, bf16[192,1472]{1,0:T(8,128)(2,1)}, u32[]{:S(2)}, u32[]{:S(2)}) collective-permute-start(bf16[192,1472]{1,0:T(8,128)(2,1)} %get-tuple-element.79.refs_0_.refs_4_.x0), channel_id=1, source_target_pairs={{0,8},{4,12},{8,0},{12,4},{16,24},{20,28},{24,16},{28,20},{1,9},{5... | collective-permute-start | bytes 1695752 | tf_op jit(solution)/shard_map/ppermute | solution.py:309
  16.4 29.3 %collective-permute-start.3 = (bf16[192,1472]{1,0:T(8,128)(2,1)}, bf16[192,1472]{1,0:T(8,128)(2,1)}, u32[]{:S(2)}, u32[]{:S(2)}) collective-permute-start(bf16[192,1472]{1,0:T(8,128)(2,1)} %get-tuple-element.80.refs_1_.refs_5_.x1), channel_id=1, source_target_pairs={{0,16},{4,20},{8,24},{12,28},{16,0},{20,4},{24,8},{28,12},{1,17},{... | collective-permute-start | bytes 1695752 | tf_op jit(solution)/shard_map/ppermute | solution.py:309
  16.9 28.9 %collective-permute-start.1 = (bf16[192,1472]{1,0:T(8,128)(2,1)}, bf16[192,1472]{1,0:T(8,128)(2,1)}, u32[]{:S(2)}, u32[]{:S(2)}) collective-permute-start(bf16[192,1472]{1,0:T(8,128)(2,1)} %get-tuple-element.80.refs_1_.refs_5_.x1), channel_id=1, source_target_pairs={{0,8},{4,12},{8,0},{12,4},{16,24},{20,28},{24,16},{28,20},{1,9},{5... | collective-permute-start | bytes 1695752 | tf_op jit(solution)/shard_map/ppermute | solution.py:309
  45.8 12.9 %collective-permute-start.5 = (bf16[272,1152]{1,0:T(8,128)(2,1)S(1)}, bf16[272,1152]{1,0:T(8,128)(2,1)S(1)}, u32[]{:S(2)}, u32[]{:S(2)}) collective-permute-start(bf16[272,1152]{1,0:T(8,128)(2,1)S(1)} %fusion.2), channel_id=1, source_target_pairs={{0,16},{4,20},{8,24},{12,28},{16,0},{20,4},{24,8},{28,12},{1,17},{... | collective-permute-start | bytes 1880072 | tf_op jit(solution)/shard_map/ppermute | solution.py:309
  47.3 14.3 %collective-permute-start.4 = (bf16[272,1152]{1,0:T(8,128)(2,1)S(1)}, bf16[272,1152]{1,0:T(8,128)(2,1)S(1)}, u32[]{:S(2)}, u32[]{:S(2)}) collective-permute-start(bf16[272,1152]{1,0:T(8,128)(2,1)S(1)} %fusion.2), channel_id=1, source_target_pairs={{0,8},{4,12},{8,0},{12,4},{16,24},{20,28},{24,16},{28,20},{1,9},{5... | collective-permute-start | bytes 1880072 | tf_op jit(solution)/shard_map/ppermute | solution.py:309
  58.7 9.7 %collective-permute-start.7 = (bf16[144,1152]{1,0:T(8,128)(2,1)S(1)}, bf16[144,1152]{1,0:T(8,128)(2,1)S(1)}, u32[]{:S(2)}, u32[]{:S(2)}) collective-permute-start(bf16[144,1152]{1,0:T(8,128)(2,1)S(1)} %slice.91), channel_id=1, source_target_pairs={{0,8},{4,12},{8,0},{12,4},{16,24},{20,28},{24,16},{28,20},{1,9},{5... | collective-permute-start | bytes 995336 | tf_op jit(solution)/shard_map/ppermute | solution.py:309
  61.6 6.8 %collective-permute-start.6 = (bf16[128,1152]{1,0:T(8,128)(2,1)S(1)}, bf16[128,1152]{1,0:T(8,128)(2,1)S(1)}, u32[]{:S(2)}, u32[]{:S(2)}) collective-permute-start(bf16[128,1152]{1,0:T(8,128)(2,1)S(1)} %slice.90), channel_id=1, source_target_pairs={{0,16},{4,20},{8,24},{12,28},{16,0},{20,4},{24,8},{28,12},{1,17},{... | collective-permute-start | bytes 884744 | tf_op jit(solution)/shard_map/ppermute | solution.py:309
  70.4 8.4 %collective-permute-start.8 = (bf16[4,272,1152]{2,1,0:T(8,128)(2,1)S(1)}, bf16[4,272,1152]{2,1,0:T(8,128)(2,1)}, u32[]{:S(2)}, u32[]{:S(2)}) collective-permute-start(bf16[4,272,1152]{2,1,0:T(8,128)(2,1)S(1)} %pad_maximum_fusion.near_ref), channel_id=1, source_target_pairs={{0,4},{4,0},{8,12},{12,8},{16,20},{20,16},{24,28},{28,24},{1,5},{5... | collective-permute-start | bytes 7520264 | tf_op jit(solution)/shard_map/ppermute | solution.py:309
  70.4 16.5 %collective-permute-start.9 = (bf16[192,1472]{1,0:T(8,128)(2,1)}, bf16[192,1472]{1,0:T(8,128)(2,1)}, u32[]{:S(2)}, u32[]{:S(2)}) collective-permute-start(bf16[192,1472]{1,0:T(8,128)(2,1)} %collective-permute-done.refs_2_.refs_6_), channel_id=1, source_target_pairs={{0,16},{4,20},{8,24},{12,28},{16,0},{20,4},{24,8},{28,12},{1,17},{... | collective-permute-start | bytes 1695752 | tf_op jit(solution)/shard_map/ppermute | solution.py:309
  71.5 16.5 %collective-permute-start.10 = (bf16[192,1472]{1,0:T(8,128)(2,1)}, bf16[192,1472]{1,0:T(8,128)(2,1)}, u32[]{:S(2)}, u32[]{:S(2)}) collective-permute-start(bf16[192,1472]{1,0:T(8,128)(2,1)} %collective-permute-done.3.refs_5_.refs_9_), channel_id=1, source_target_pairs={{0,8},{4,12},{8,0},{12,4},{16,24},{20,28},{24,16},{28,20},{1,9},{5... | collective-permute-start | bytes 1695752 | tf_op jit(solution)/shard_map/ppermute | solution.py:309
  73.0 88.6 %all-to-all-start = ((bf16[8,192,1472]{2,1,0:T(8,128)(2,1)}), bf16[8,192,1472]{2,1,0:T(8,128)(2,1)}, u32[]{:S(2)}, u32[]{:S(2)}) async-start(bf16[8,192,1472]{2,1,0:T(8,128)(2,1)} %get-tuple-element.95.refs_5_), calls=%async_computation | async-start | bytes 9437184 | tf_op jit(solution)/shard_map/all_to_all | solution.py:1010
  78.0 83.1 %all-gather.6.cloned.1.call-start = ((), (), s32[]{:S(2)}) async-start(), calls=%async_computation.5 | async-start | bytes 1720320 | tf_op jit(solution)/shard_map/all_gather | solution.py:1049
  78.7 304.5 %reduce-scatter.3.cloned.1.call-start = ((), (), s32[]{:S(2)}) async-start(), calls=%async_computation.6 | async-start | bytes 3297280 | tf_op jit(solution)/shard_map/reduce_scatter | solution.py:1125
  100.2 2.3 collective-permute-start.11
  100.3 3.0 collective-permute-start.12
  100.7 3.4 collective-permute-start.13
  100.8 4.2 collective-permute-start.14
  121.8 42.5 %collective-permute-start.18 = (bf16[1472,896]{1,0:T(8,128)(2,1)}, bf16[1472,896]{1,0:T(8,128)(2,1)}, u32[]{:S(2)}, u32[]{:S(2)}) collective-permute-start(bf16[1472,896]{1,0:T(8,128)(2,1)} %all-gather.4.cloned.1.call-done.mine_ref), channel_id=1, source_target_pairs={{0,4},{4,0},{8,12},{12,8},{16,20},{20,16},{24,28},{28,24},{1,5},{5... | collective-permute-start | bytes 7913480 | tf_op jit(solution)/shard_map/ppermute | solution.py:309
  122.0 23.3 %collective-permute-start.17 = (bf16[384,384]{1,0:T(8,128)(2,1)S(1)}, bf16[384,384]{1,0:T(8,128)(2,1)S(1)}, u32[]{:S(2)}, u32[]{:S(2)}) collective-permute-start(bf16[384,384]{1,0:T(8,128)(2,1)S(1)} %bitcast.106), channel_id=1, source_target_pairs={{0,24},{4,28},{8,16},{12,20},{16,8},{20,12},{24,0},{28,4},{1,25},{... | collective-permute-start | bytes 884744 | tf_op jit(solution)/shard_map/ppermute | solution.py:309
  123.9 25.7 %collective-permute-start.16 = (bf16[384,384]{1,0:T(8,128)(2,1)S(1)}, bf16[384,384]{1,0:T(8,128)(2,1)S(1)}, u32[]{:S(2)}, u32[]{:S(2)}) collective-permute-start(bf16[384,384]{1,0:T(8,128)(2,1)S(1)} %bitcast.107), channel_id=1, source_target_pairs={{0,16},{4,20},{8,24},{12,28},{16,0},{20,4},{24,8},{28,12},{1,17},{... | collective-permute-start | bytes 884744 | tf_op jit(solution)/shard_map/ppermute | solution.py:309
  125.0 25.4 %collective-permute-start.15 = (bf16[384,384]{1,0:T(8,128)(2,1)S(1)}, bf16[384,384]{1,0:T(8,128)(2,1)S(1)}, u32[]{:S(2)}, u32[]{:S(2)}) collective-permute-start(bf16[384,384]{1,0:T(8,128)(2,1)S(1)} %bitcast.108), channel_id=1, source_target_pairs={{0,8},{4,12},{8,0},{12,4},{16,24},{20,28},{24,16},{28,20},{1,9},{5... | collective-permute-start | bytes 884744 | tf_op jit(solution)/shard_map/ppermute | solution.py:309
  161.0 3.3 collective-permute-start.19
  207.6 42.4 %collective-permute-start.20 = (bf16[2,192,1472]{2,1,0:T(8,128)(2,1)}, bf16[2,192,1472]{2,1,0:T(8,128)(2,1)}, u32[]{:S(2)}, u32[]{:S(2)}) collective-permute-start(bf16[2,192,1472]{2,1,0:T(8,128)(2,1)} %get-tuple-element.102), channel_id=1, source_target_pairs={{0,8},{4,12},{8,0},{12,4},{16,24},{20,28},{24,16},{28,20},{1,9},{5... | collective-permute-start | bytes 3391496 | tf_op jit(solution)/shard_map/ppermute | solution.py:309
  209.4 53.3 %collective-permute-start.21 = (bf16[2,192,1472]{2,1,0:T(8,128)(2,1)}, bf16[2,192,1472]{2,1,0:T(8,128)(2,1)}, u32[]{:S(2)}, u32[]{:S(2)}) collective-permute-start(bf16[2,192,1472]{2,1,0:T(8,128)(2,1)} %get-tuple-element.103), channel_id=1, source_target_pairs={{0,16},{4,20},{8,24},{12,28},{16,0},{20,4},{24,8},{28,12},{1,17},{... | collective-permute-start | bytes 3391496 | tf_op jit(solution)/shard_map/ppermute | solution.py:309
  210.6 52.2 %collective-permute-start.22 = (bf16[2,192,1472]{2,1,0:T(8,128)(2,1)}, bf16[2,192,1472]{2,1,0:T(8,128)(2,1)}, u32[]{:S(2)}, u32[]{:S(2)}) collective-permute-start(bf16[2,192,1472]{2,1,0:T(8,128)(2,1)} %get-tuple-element.104), channel_id=1, source_target_pairs={{0,24},{4,28},{8,16},{12,20},{16,8},{20,12},{24,0},{28,4},{1,25},{... | collective-permute-start | bytes 3391496 | tf_op jit(solution)/shard_map/ppermute | solution.py:309
  240.3 29.4 %collective-permute-start.28 = (bf16[1,736,896]{2,1,0:T(8,128)(2,1)S(1)}, bf16[1,736,896]{2,1,0:T(8,128)(2,1)S(1)}, u32[]{:S(2)}, u32[]{:S(2)}) collective-permute-start(bf16[1,736,896]{2,1,0:T(8,128)(2,1)S(1)} %get-tuple-element.182), channel_id=1, source_target_pairs={{0,4},{4,0},{8,12},{12,8},{16,20},{20,16},{24,28},{28,24},{1,5},{5... | collective-permute-start | bytes 3956744 | tf_op jit(solution)/shard_map/ppermute | solution.py:309
  240.4 29.4 %collective-permute-start.27 = (bf16[1,736,896]{2,1,0:T(8,128)(2,1)S(1)}, bf16[1,736,896]{2,1,0:T(8,128)(2,1)}, u32[]{:S(2)}, u32[]{:S(2)}) collective-permute-start(bf16[1,736,896]{2,1,0:T(8,128)(2,1)S(1)} %get-tuple-element.183), channel_id=1, source_target_pairs={{0,4},{4,0},{8,12},{12,8},{16,20},{20,16},{24,28},{28,24},{1,5},{5... | collective-permute-start | bytes 3956744 | tf_op jit(solution)/shard_map/ppermute | solution.py:309
  274.8 59.4 %all-to-all-start.1 = ((bf16[8,192,1472]{2,1,0:T(8,128)(2,1)}), bf16[8,192,1472]{2,1,0:T(8,128)(2,1)}, u32[]{:S(2)}, u32[]{:S(2)}) async-start(bf16[8,192,1472]{2,1,0:T(8,128)(2,1)} %get-tuple-element.111), calls=%async_computation.1 | async-start | bytes 9437184 | tf_op jit(solution)/shard_map/all_to_all | solution.py:1010
  279.7 115.8 %reduce-scatter.5.cloned.1.call-start = ((), (), s32[]{:S(2)}) async-start(), calls=%async_computation.7 | async-start | bytes 1720320 | tf_op jit(solution)/shard_map/reduce_scatter | solution.py:1126
  300.7 4.7 collective-permute-start.23
  300.8 4.6 collective-permute-start.24
  301.3 4.2 collective-permute-start.25
  301.4 4.2 collective-permute-start.26
  322.2 16.8 %collective-permute-start.32 = (bf16[4,4,64,1152]{3,2,1,0:T(8,128)(2,1)}, bf16[4,4,64,1152]{3,2,1,0:T(8,128)(2,1)}, u32[]{:S(2)}, u32[]{:S(2)}) collective-permute-start(bf16[4,4,64,1152]{3,2,1,0:T(8,128)(2,1)} %get-tuple-element.132), channel_id=1, source_target_pairs={{0,4},{4,0},{8,12},{12,8},{16,20},{20,16},{24,28},{28,24},{1,5},{5... | collective-permute-start | bytes 7077896 | tf_op jit(solution)/shard_map/ppermute | solution.py:309
  323.5 5.2 %collective-permute-start.50 = (bf16[4,112,1472]{2,1,0:T(8,128)(2,1)S(1)}, bf16[4,112,1472]{2,1,0:T(8,128)(2,1)S(1)}, u32[]{:S(2)}, u32[]{:S(2)}) collective-permute-start(bf16[4,112,1472]{2,1,0:T(8,128)(2,1)S(1)} %get-tuple-element.180), channel_id=1, source_target_pairs={{0,4},{4,0},{8,12},{12,8},{16,20},{20,16},{24,28},{28,24},{1,5},{5... | collective-permute-start | bytes 3956744 | tf_op jit(solution)/shard_map/ppermute | solution.py:309
  324.0 25.1 %collective-permute-start.29 = (bf16[384,768]{1,0:T(8,128)(2,1)S(1)}, bf16[384,768]{1,0:T(8,128)(2,1)}, u32[]{:S(2)}, u32[]{:S(2)}) collective-permute-start(bf16[384,768]{1,0:T(8,128)(2,1)S(1)} %copy-done.50), channel_id=1, source_target_pairs={{0,8},{4,12},{8,0},{12,4},{16,24},{20,28},{24,16},{28,20},{1,9},{5... | collective-permute-start | bytes 1769480 | tf_op jit(solution)/shard_map/ppermute | solution.py:309
  325.8 23.8 %collective-permute-start.30 = (bf16[384,768]{1,0:T(8,128)(2,1)}, bf16[384,768]{1,0:T(8,128)(2,1)}, u32[]{:S(2)}, u32[]{:S(2)}) collective-permute-start(bf16[384,768]{1,0:T(8,128)(2,1)} %get-tuple-element.128), channel_id=1, source_target_pairs={{0,16},{4,20},{8,24},{12,28},{16,0},{20,4},{24,8},{28,12},{1,17},{... | collective-permute-start | bytes 1769480 | tf_op jit(solution)/shard_map/ppermute | solution.py:309
  327.3 33.1 %collective-permute-start.31 = (bf16[384,768]{1,0:T(8,128)(2,1)S(1)}, bf16[384,768]{1,0:T(8,128)(2,1)}, u32[]{:S(2)}, u32[]{:S(2)}) collective-permute-start(bf16[384,768]{1,0:T(8,128)(2,1)S(1)} %copy-done.49), channel_id=1, source_target_pairs={{0,24},{4,28},{8,16},{12,20},{16,8},{20,12},{24,0},{28,4},{1,25},{... | collective-permute-start | bytes 1769480 | tf_op jit(solution)/shard_map/ppermute | solution.py:309
  346.1 26.8 %collective-permute-start.35 = (bf16[4,64,1152]{2,1,0:T(8,128)(2,1)S(1)}, bf16[4,64,1152]{2,1,0:T(8,128)(2,1)S(1)}, u32[]{:S(2)}, u32[]{:S(2)}) collective-permute-start(bf16[4,64,1152]{2,1,0:T(8,128)(2,1)S(1)} %get-tuple-element.192), channel_id=1, source_target_pairs={{0,24},{4,28},{8,16},{12,20},{16,8},{20,12},{24,0},{28,4},{1,25},{... | collective-permute-start | bytes 1769480 | tf_op jit(solution)/shard_map/ppermute | solution.py:309
  348.4 34.8 %collective-permute-start.34 = (bf16[4,64,1152]{2,1,0:T(8,128)(2,1)S(1)}, bf16[4,64,1152]{2,1,0:T(8,128)(2,1)S(1)}, u32[]{:S(2)}, u32[]{:S(2)}) collective-permute-start(bf16[4,64,1152]{2,1,0:T(8,128)(2,1)S(1)} %get-tuple-element.193), channel_id=1, source_target_pairs={{0,16},{4,20},{8,24},{12,28},{16,0},{20,4},{24,8},{28,12},{1,17},{... | collective-permute-start | bytes 1769480 | tf_op jit(solution)/shard_map/ppermute | solution.py:309
  349.1 34.1 %collective-permute-start.33 = (bf16[4,64,1152]{2,1,0:T(8,128)(2,1)S(1)}, bf16[4,64,1152]{2,1,0:T(8,128)(2,1)S(1)}, u32[]{:S(2)}, u32[]{:S(2)}) collective-permute-start(bf16[4,64,1152]{2,1,0:T(8,128)(2,1)S(1)} %get-tuple-element.194), channel_id=1, source_target_pairs={{0,8},{4,12},{8,0},{12,4},{16,24},{20,28},{24,16},{28,20},{1,9},{5... | collective-permute-start | bytes 1769480 | tf_op jit(solution)/shard_map/ppermute | solution.py:309
  387.0 39.3 %collective-permute-start.41 = (bf16[368,896]{1,0:T(8,128)(2,1)S(1)}, bf16[368,896]{1,0:T(8,128)(2,1)S(1)}, u32[]{:S(2)}, u32[]{:S(2)}) collective-permute-start(bf16[368,896]{1,0:T(8,128)(2,1)S(1)} %copy-done.13), channel_id=1, source_target_pairs={{0,24},{4,28},{8,16},{12,20},{16,8},{20,12},{24,0},{28,4},{1,25},{... | collective-permute-start | bytes 1978376 | tf_op jit(solution)/shard_map/ppermute | solution.py:309
  387.5 39.3 %collective-permute-start.40 = (bf16[368,896]{1,0:T(8,128)(2,1)S(1)}, bf16[368,896]{1,0:T(8,128)(2,1)S(1)}, u32[]{:S(2)}, u32[]{:S(2)}) collective-permute-start(bf16[368,896]{1,0:T(8,128)(2,1)S(1)} %copy-done.13), channel_id=1, source_target_pairs={{0,16},{4,20},{8,24},{12,28},{16,0},{20,4},{24,8},{28,12},{1,17},{... | collective-permute-start | bytes 1978376 | tf_op jit(solution)/shard_map/ppermute | solution.py:309
  389.0 37.9 %collective-permute-start.39 = (bf16[368,896]{1,0:T(8,128)(2,1)S(1)}, bf16[368,896]{1,0:T(8,128)(2,1)S(1)}, u32[]{:S(2)}, u32[]{:S(2)}) collective-permute-start(bf16[368,896]{1,0:T(8,128)(2,1)S(1)} %copy-done.13), channel_id=1, source_target_pairs={{0,8},{4,12},{8,0},{12,4},{16,24},{20,28},{24,16},{28,20},{1,9},{5... | collective-permute-start | bytes 1978376 | tf_op jit(solution)/shard_map/ppermute | solution.py:309
  392.3 8.4 %collective-permute-start.38 = (bf16[64,1152]{1,0:T(8,128)(2,1)S(1)}, bf16[64,1152]{1,0:T(8,128)(2,1)S(1)}, u32[]{:S(2)}, u32[]{:S(2)}) collective-permute-start(bf16[64,1152]{1,0:T(8,128)(2,1)S(1)} %get-tuple-element.196), channel_id=1, source_target_pairs={{0,3},{1,2},{2,1},{3,0},{4,7},{5,6},{6,5},{7,4},{8,11},{9,10},{10,... | collective-permute-start | bytes 442376 | tf_op jit(solution)/shard_map/ppermute | solution.py:314
  395.5 11.5 %collective-permute-start.37 = (bf16[64,1152]{1,0:T(8,128)(2,1)S(1)}, bf16[64,1152]{1,0:T(8,128)(2,1)S(1)}, u32[]{:S(2)}, u32[]{:S(2)}) collective-permute-start(bf16[64,1152]{1,0:T(8,128)(2,1)S(1)} %get-tuple-element.197), channel_id=1, source_target_pairs={{0,2},{1,3},{2,0},{3,1},{4,6},{5,7},{6,4},{7,5},{8,10},{9,11},{10,... | collective-permute-start | bytes 442376 | tf_op jit(solution)/shard_map/ppermute | solution.py:314
  400.7 25.6 %collective-permute-start.53 = (bf16[112,1472]{1,0:T(8,128)(2,1)}, bf16[112,1472]{1,0:T(8,128)(2,1)S(1)}, u32[]{:S(2)}, u32[]{:S(2)}) collective-permute-start(bf16[112,1472]{1,0:T(8,128)(2,1)} %reduce-scatter.5.cloned.1.call-done.refs_0_), channel_id=1, source_target_pairs={{0,24},{4,28},{8,16},{12,20},{16,8},{20,12},{24,0},{28,4},{1,25},{... | collective-permute-start | bytes 989192 | tf_op jit(solution)/shard_map/ppermute | solution.py:309
  407.0 5.1 %collective-permute-start.36 = (bf16[64,1152]{1,0:T(8,128)(2,1)S(1)}, bf16[64,1152]{1,0:T(8,128)(2,1)S(1)}, u32[]{:S(2)}, u32[]{:S(2)}) collective-permute-start(bf16[64,1152]{1,0:T(8,128)(2,1)S(1)} %get-tuple-element.198), channel_id=1, source_target_pairs={{0,1},{1,0},{2,3},{3,2},{4,5},{5,4},{6,7},{7,6},{8,9},{9,8},{10,11... | collective-permute-start | bytes 442376 | tf_op jit(solution)/shard_map/ppermute | solution.py:314
  412.1 20.8 %collective-permute-start.52 = (bf16[112,1472]{1,0:T(8,128)(2,1)}, bf16[112,1472]{1,0:T(8,128)(2,1)}, u32[]{:S(2)}, u32[]{:S(2)}) collective-permute-start(bf16[112,1472]{1,0:T(8,128)(2,1)} %reduce-scatter.5.cloned.1.call-done.refs_0_), channel_id=1, source_target_pairs={{0,16},{4,20},{8,24},{12,28},{16,0},{20,4},{24,8},{28,12},{1,17},{... | collective-permute-start | bytes 989192 | tf_op jit(solution)/shard_map/ppermute | solution.py:309
  426.3 18.1 %collective-permute-start.45 = (bf16[368,896]{1,0:T(8,128)(2,1)S(1)}, bf16[368,896]{1,0:T(8,128)(2,1)S(1)}, u32[]{:S(2)}, u32[]{:S(2)}) collective-permute-start(bf16[368,896]{1,0:T(8,128)(2,1)S(1)} %copy-done.13), channel_id=1, source_target_pairs={{0,4},{4,0},{8,12},{12,8},{16,20},{20,16},{24,28},{28,24},{1,5},{5... | collective-permute-start | bytes 1978376 | tf_op jit(solution)/shard_map/ppermute | solution.py:309
  426.3 25.0 %collective-permute-start.48 = (bf16[368,896]{1,0:T(8,128)(2,1)S(1)}, bf16[368,896]{1,0:T(8,128)(2,1)}, u32[]{:S(2)}, u32[]{:S(2)}) collective-permute-start(bf16[368,896]{1,0:T(8,128)(2,1)S(1)} %collective-permute-done.41.refs_6_.refs_3_), channel_id=1, source_target_pairs={{0,4},{4,0},{8,12},{12,8},{16,20},{20,16},{24,28},{28,24},{1,5},{5... | collective-permute-start | bytes 1978376 | tf_op jit(solution)/shard_map/ppermute | solution.py:309
  426.8 25.0 %collective-permute-start.47 = (bf16[368,896]{1,0:T(8,128)(2,1)S(1)}, bf16[368,896]{1,0:T(8,128)(2,1)}, u32[]{:S(2)}, u32[]{:S(2)}) collective-permute-start(bf16[368,896]{1,0:T(8,128)(2,1)S(1)} %collective-permute-done.40.refs_5_.refs_2_), channel_id=1, source_target_pairs={{0,4},{4,0},{8,12},{12,8},{16,20},{20,16},{24,28},{28,24},{1,5},{5... | collective-permute-start | bytes 1978376 | tf_op jit(solution)/shard_map/ppermute | solution.py:309
  427.0 24.9 %collective-permute-start.46 = (bf16[368,896]{1,0:T(8,128)(2,1)S(1)}, bf16[368,896]{1,0:T(8,128)(2,1)}, u32[]{:S(2)}, u32[]{:S(2)}) collective-permute-start(bf16[368,896]{1,0:T(8,128)(2,1)S(1)} %collective-permute-done.39.refs_4_.refs_1_), channel_id=1, source_target_pairs={{0,4},{4,0},{8,12},{12,8},{16,20},{20,16},{24,28},{28,24},{1,5},{5... | collective-permute-start | bytes 1978376 | tf_op jit(solution)/shard_map/ppermute | solution.py:309
  433.0 9.8 %collective-permute-start.51 = (bf16[112,1472]{1,0:T(8,128)(2,1)}, bf16[112,1472]{1,0:T(8,128)(2,1)}, u32[]{:S(2)}, u32[]{:S(2)}) collective-permute-start(bf16[112,1472]{1,0:T(8,128)(2,1)} %reduce-scatter.5.cloned.1.call-done.refs_0_), channel_id=1, source_target_pairs={{0,8},{4,12},{8,0},{12,4},{16,24},{20,28},{24,16},{28,20},{1,9},{5... | collective-permute-start | bytes 989192 | tf_op jit(solution)/shard_map/ppermute | solution.py:309
  442.7 6.4 %collective-permute-start.44 = (bf16[64,1152]{1,0:T(8,128)(2,1)}, bf16[64,1152]{1,0:T(8,128)(2,1)S(1)}, u32[]{:S(2)}, u32[]{:S(2)}) collective-permute-start(bf16[64,1152]{1,0:T(8,128)(2,1)} %sum_parts.3.refs_0_), channel_id=1, source_target_pairs={{0,24},{4,28},{8,16},{12,20},{16,8},{20,12},{24,0},{28,4},{1,25},{... | collective-permute-start | bytes 442376 | tf_op jit(solution)/shard_map/ppermute | solution.py:309
  444.4 6.9 %collective-permute-start.43 = (bf16[64,1152]{1,0:T(8,128)(2,1)}, bf16[64,1152]{1,0:T(8,128)(2,1)S(1)}, u32[]{:S(2)}, u32[]{:S(2)}) collective-permute-start(bf16[64,1152]{1,0:T(8,128)(2,1)} %sum_parts.3.refs_0_), channel_id=1, source_target_pairs={{0,16},{4,20},{8,24},{12,28},{16,0},{20,4},{24,8},{28,12},{1,17},{... | collective-permute-start | bytes 442376 | tf_op jit(solution)/shard_map/ppermute | solution.py:309
  449.1 11.5 %collective-permute-start.42 = (bf16[64,1152]{1,0:T(8,128)(2,1)}, bf16[64,1152]{1,0:T(8,128)(2,1)S(1)}, u32[]{:S(2)}, u32[]{:S(2)}) collective-permute-start(bf16[64,1152]{1,0:T(8,128)(2,1)} %sum_parts.3.refs_0_), channel_id=1, source_target_pairs={{0,8},{4,12},{8,0},{12,4},{16,24},{20,28},{24,16},{28,20},{1,9},{5... | collective-permute-start | bytes 442376 | tf_op jit(solution)/shard_map/ppermute | solution.py:309
  451.3 14.8 %collective-permute-start.54 = (bf16[112,1472]{1,0:T(8,128)(2,1)}, bf16[112,1472]{1,0:T(8,128)(2,1)}, u32[]{:S(2)}, u32[]{:S(2)}) collective-permute-start(bf16[112,1472]{1,0:T(8,128)(2,1)} %reduce-scatter.5.cloned.1.call-done.refs_0_), channel_id=1, source_target_pairs={{0,4},{4,0},{8,12},{12,8},{16,20},{20,16},{24,28},{28,24},{1,5},{5... | collective-permute-start | bytes 989192 | tf_op jit(solution)/shard_map/ppermute | solution.py:309
  451.4 14.8 %collective-permute-start.57 = (bf16[112,1472]{1,0:T(8,128)(2,1)}, bf16[112,1472]{1,0:T(8,128)(2,1)}, u32[]{:S(2)}, u32[]{:S(2)}) collective-permute-start(bf16[112,1472]{1,0:T(8,128)(2,1)} %copy-done.32), channel_id=1, source_target_pairs={{0,4},{4,0},{8,12},{12,8},{16,20},{20,16},{24,28},{28,24},{1,5},{5... | collective-permute-start | bytes 989192 | tf_op jit(solution)/shard_map/ppermute | solution.py:309
  451.9 14.3 %collective-permute-start.56 = (bf16[112,1472]{1,0:T(8,128)(2,1)}, bf16[112,1472]{1,0:T(8,128)(2,1)}, u32[]{:S(2)}, u32[]{:S(2)}) collective-permute-start(bf16[112,1472]{1,0:T(8,128)(2,1)} %collective-permute-done.52.refs_2_), channel_id=1, source_target_pairs={{0,4},{4,0},{8,12},{12,8},{16,20},{20,16},{24,28},{28,24},{1,5},{5... | collective-permute-start | bytes 989192 | tf_op jit(solution)/shard_map/ppermute | solution.py:309
  451.9 14.2 %collective-permute-start.55 = (bf16[112,1472]{1,0:T(8,128)(2,1)}, bf16[112,1472]{1,0:T(8,128)(2,1)}, u32[]{:S(2)}, u32[]{:S(2)}) collective-permute-start(bf16[112,1472]{1,0:T(8,128)(2,1)} %collective-permute-done.51.refs_1_), channel_id=1, source_target_pairs={{0,4},{4,0},{8,12},{12,8},{16,20},{20,16},{24,28},{28,24},{1,5},{5... | collective-permute-start | bytes 989192 | tf_op jit(solution)/shard_map/ppermute | solution.py:309
  463.3 10.8 %collective-permute-start.49 = (bf16[4,64,1152]{2,1,0:T(8,128)(2,1)}, bf16[4,64,1152]{2,1,0:T(8,128)(2,1)S(1)}, u32[]{:S(2)}, u32[]{:S(2)}) collective-permute-start(bf16[4,64,1152]{2,1,0:T(8,128)(2,1)} %stack_small.1.near_ref), channel_id=1, source_target_pairs={{0,4},{4,0},{8,12},{12,8},{16,20},{20,16},{24,28},{28,24},{1,5},{5... | collective-permute-start | bytes 1769480 | tf_op jit(solution)/shard_map/ppermute | solution.py:309
  (51 other events, 331.6 us)
Sparse Core Ops, SparseCore 0:
  48.9 53.0 all-gather.3
  104.2 32.5 all-gather.5
  274.9 52.0 reduce-scatter.2
  333.8 32.9 reduce-scatter.4

commit v5 on v4

--- a/solution.py
+++ b/solution.py
@@ -432,27 +432,26 @@
     owns, gots, (dq_ref, table_ref, proj_ref) = refs[:4], refs[4:8], refs[8:11]
     sums, (keep_ref, send_ref, kv_scr, q_scr, t_scr) = refs[11:15], refs[15:]
     step = pl.program_id(0)
+    tokens = dq_ref.shape[0]
     for index in range(4):
 
-        @pl.when(step == index)
+        @pl.when(step == index // 2)
         def _(index=index):
             total = (owns[index][0].astype(FLOAT) + gots[index][0].astype(FLOAT)).astype(BFLOAT)
-            t_scr[...] = total
+            t_scr[index % 2 * tokens : (index % 2 + 1) * tokens, :] = total
             sums[index][...] = total
 
-    part = tn(normed_ref[0], t_scr[...])
+    turned = jnp.transpose(normed_ref[...].reshape(2 * tokens, normed_ref.shape[2]))
+    product = jnp.dot(turned, t_scr[...], preferred_element_type=FLOAT)
 
     @pl.when(step == 0)
     def _():
-        kv_scr[...] = part
-        q_scr[...] = tn(normed_ref[0], dq_ref[...]).astype(BFLOAT)
-
-    @pl.when(step > 0)
+        kv_scr[...] = product
+        q_scr[...] = jnp.dot(turned[:, :tokens], dq_ref[...], preferred_element_type=FLOAT).astype(BFLOAT)
+
+    @pl.when(step == 1)
     def _():
-        kv_scr[...] = kv_scr[...] + part
-
-    @pl.when(step == 3)
-    def _():
+        kv_scr[...] = kv_scr[...] + product
         low = place_ref[0]
         zed = place_ref[1]
         inner = q_scr.shape[1]
@@ -488,16 +487,16 @@
     kept = pl.BlockSpec((4, depth, span, 3 * inner), lambda g: (0, 0, 0, 0))
     return pl.pallas_call(
         skipping(functools.partial(grad_kernel, depth=depth, size=size, wide=wide), 13, len(deps)),
-        grid=(4,),
+        grid=(2,),
         in_specs=[
-            SMEM_WHOLE, pl.BlockSpec((1, tokens, width), lambda g: (g, 0, 0)), *[block] * 8, once(dq.shape), once(table.shape),
+            SMEM_WHOLE, pl.BlockSpec((2, tokens, width), lambda g: (g, 0, 0)), *[block] * 8, once(dq.shape), once(table.shape),
             once(proj.shape),
         ]
         + [UNREAD] * len(deps),
         out_specs=[*[summed] * 4, kept, kept],
         out_shape=[*[jax.ShapeDtypeStruct((tokens, 2 * inner), BFLOAT)] * 4, piece, piece],
         scratch_shapes=[
-            pltpu.VMEM((width, 2 * inner), FLOAT), pltpu.VMEM((width, inner), BFLOAT), pltpu.VMEM((tokens, 2 * inner), BFLOAT),
+            pltpu.VMEM((width, 2 * inner), FLOAT), pltpu.VMEM((width, inner), BFLOAT), pltpu.VMEM((2 * tokens, 2 * inner), BFLOAT),
         ],
         compiler_params=BIG,
         cost_estimate=cost(flops=18 * tokens * width * inner, bytes_accessed=12 * tokens * width, transcendentals=0),
@@ -614,8 +613,9 @@
 
 def feed_kernel(
     spot_ref, normed_ref, cots_ref, mine_ref, other_ref, down_mine, down_other,
-    act_ref, dmine_ref, dother_ref, out_ref, l0, l1, l2, l3, cot_ref, down_ref,
+    act_ref, dmine_ref, dother_ref, out_ref, l0, *refs
 ):
+    late_refs, (cot_ref, down_ref) = refs[:6], refs[6:]
     is_zero = spot_ref[0] == 0
     tokens = normed_ref.shape[1]
 
@@ -637,14 +637,14 @@
     up = jnp.where(is_zero, pre_other, pre_mine)
     square = gate * gate
     lifted = jnp.tanh(GELU_SCALE * (gate + 0.044715 * gate * square))
-    half = 0.5 * (1.0 + lifted)
-    smooth = gate * half
+    gate_half = 0.5 * (1.0 + lifted)
+    smooth = gate * gate_half
     act = (smooth * up).astype(BFLOAT)
     act_ref[0] = act
     out = jnp.dot(act, down_ref[...], preferred_element_type=FLOAT).astype(BFLOAT)
     out_ref[...] = out.reshape(out_ref.shape)
     act_back = nt(cot, down_ref[...])
-    slope = half + 0.5 * gate * (1.0 - lifted * lifted) * (GELU_SCALE * (1.0 + 3 * 0.044715 * square))
+    slope = gate_half + 0.5 * gate * (1.0 - lifted * lifted) * (GELU_SCALE * (1.0 + 3 * 0.044715 * square))
     gate_back = act_back * up * slope
     up_back = act_back * smooth
     dmine = jnp.where(is_zero, gate_back, up_back).astype(BFLOAT)
@@ -652,11 +652,18 @@
     dmine_ref[0] = dmine
     dother_ref[0] = dother
     late = (nt(dmine, mine_ref[...]) + nt(dother, other_ref[...])).astype(BFLOAT)
-    for index, late_ref in enumerate((l0, l1, l2, l3)):
-
-        @pl.when(pl.program_id(0) == index)
-        def _(late_ref=late_ref):
-            late_ref[...] = late.reshape(late_ref.shape)
+    half = late.shape[0] // 2
+
+    @pl.when(pl.program_id(0) == 0)
+    def _():
+        l0[...] = late.reshape(l0.shape)
+
+    for index in range(3):
+
+        @pl.when(pl.program_id(0) == index + 1)
+        def _(index=index):
+            late_refs[2 * index][...] = late[:half]
+            late_refs[2 * index + 1][...] = late[half:]
 
 
 def feed_forward(spot, normed, cots, mine, other, downs):
@@ -673,16 +680,18 @@
     sent = jax.ShapeDtypeStruct((8, tokens // 2, width), BFLOAT)
     half = jax.ShapeDtypeStruct((2, tokens // 2, width), BFLOAT)
     piece = pl.BlockSpec((2, tokens // 2, width), lambda g, spot: (0, 0, 0))
+    rows = jax.ShapeDtypeStruct((tokens // 2, width), BFLOAT)
+    part = pl.BlockSpec((tokens // 2, width), lambda g, spot: (0, 0))
     return pl.pallas_call(
         feed_kernel,
         grid_spec=pltpu.PrefetchScalarGridSpec(
             num_scalar_prefetch=1,
             grid=(4,),
             in_specs=[block(width), placed, *[once(value.shape) for value in (mine, other, *downs)]],
-            out_specs=[block(wide), block(wide), block(wide), placed, *[piece] * 4, block(width)],
+            out_specs=[block(wide), block(wide), block(wide), placed, piece, *[part] * 6, block(width)],
             scratch_shapes=[pltpu.VMEM((wide, width), BFLOAT)],
         ),
-        out_shape=[shape(wide), shape(wide), shape(wide), sent, *[half] * 4, shape(width)],
+        out_shape=[shape(wide), shape(wide), shape(wide), sent, half, *[rows] * 6, shape(width)],
         compiler_params=BIG,
         cost_estimate=cost(
             flops=48 * tokens * width * wide, bytes_accessed=30 * tokens * width, transcendentals=4 * tokens * wide
@@ -748,8 +757,10 @@
     return own_ref[...].astype(FLOAT) + first + second
 
 
-def middle_kernel(after_ref, p0, p1, p2, p3, cot_ref, gain_ref, proj_ref, residual_ref, mix_ref, attn_ref):
-    back = sum(ref[0].astype(FLOAT) for ref in (p0, p1, p2, p3))
+def middle_kernel(after_ref, own_ref, n0, n1, f0, f1, cot_ref, gain_ref, proj_ref, residual_ref, mix_ref, attn_ref):
+    near = pl.program_id(0) < 2
+    back = own_ref[0].astype(FLOAT) + jnp.where(near, n0[...], f0[...]).astype(FLOAT)
+    back = back + jnp.where(near, n1[...], f1[...]).astype(FLOAT)
     residual = cot_ref[0].astype(FLOAT) + norm_back(after_ref[...], gain_ref[...], back)
     residual_ref[...] = residual
     mix = residual.astype(BFLOAT)
@@ -757,16 +768,18 @@
     attn_ref[...] = nt(mix, proj_ref[...]).astype(BFLOAT)
 
 
-def middle(after_attn, parts, cots, gain, proj, *deps):
+def middle(after_attn, own, parts, cots, gain, proj, *deps):
     tokens, width = after_attn.shape
     inner = proj.shape[0]
     tile = tokens // 4
     whole = pl.BlockSpec((tile, width), lambda g: (g, 0))
     half = pl.BlockSpec((1, tile, width), lambda g: (g // 2, g % 2, 0))
-    return pl.pallas_call(
-        skipping(middle_kernel, 8, len(deps)),
+    near = pl.BlockSpec((tile, width), lambda g: (jnp.minimum(g, 1), 0))
+    far = pl.BlockSpec((tile, width), lambda g: (jnp.maximum(g - 2, 0), 0))
+    return pl.pallas_call(
+        skipping(middle_kernel, 9, len(deps)),
         grid=(4,),
-        in_specs=[whole, half, half, half, half, half, once(gain.shape), once(proj.shape)] + [UNREAD] * len(deps),
+        in_specs=[whole, half, near, near, far, far, half, once(gain.shape), once(proj.shape)] + [UNREAD] * len(deps),
         out_specs=[whole, whole, pl.BlockSpec((tile, inner), lambda g: (g, 0))],
         out_shape=[
             jax.ShapeDtypeStruct((tokens, width), FLOAT),
@@ -776,7 +789,47 @@
         compiler_params=BIG,
         cost_estimate=pl.CostEstimate(flops=10**11, bytes_accessed=0, transcendentals=0),
         name="middle",
-    )(after_attn, *parts, cots, gain, proj, *deps)
+    )(after_attn, own, *parts, cots, gain, proj, *deps)
+
+
+def apart_kernel(left_ref, right_ref, *outs):
+    for index, out_ref in enumerate(outs):
+
+        @pl.when(pl.program_id(0) == index)
+        def _(out_ref=out_ref):
+            out_ref[...] = (left_ref[0].astype(FLOAT) + right_ref[0].astype(FLOAT)).astype(BFLOAT)
+
+
+def plus_apart(left, right, *deps):
+    count, *shape = left.shape
+    spec = pl.BlockSpec((1, *shape), lambda g: (g,) + (0,) * len(shape))
+    return pl.pallas_call(
+        skipping(apart_kernel, 2, len(deps)),
+        grid=(count,),
+        in_specs=[spec, spec] + [UNREAD] * len(deps),
+        out_specs=[pl.BlockSpec(tuple(shape), lambda g: (0,) * len(shape))] * count,
+        out_shape=[jax.ShapeDtypeStruct(tuple(shape), BFLOAT)] * count,
+        compiler_params=BIG,
+        cost_estimate=moved(left, left, left),
+        name="plus_apart",
+    )(left, right, *deps)
+
+
+def relay_kernel(a_ref, b_ref, c_ref, d_ref, first_ref, second_ref):
+    first_ref[...] = (a_ref[...].astype(FLOAT) + b_ref[...].astype(FLOAT)).astype(BFLOAT)
+    second_ref[...] = (c_ref[...].astype(FLOAT) + d_ref[...].astype(FLOAT)).astype(BFLOAT)
+
+
+def relay_sums(first, second, *deps):
+    shape = jax.ShapeDtypeStruct(first[0].shape, BFLOAT)
+    return pl.pallas_call(
+        skipping(relay_kernel, 4, len(deps)),
+        in_specs=[VMEM_WHOLE] * 4 + [UNREAD] * len(deps),
+        out_specs=[VMEM_WHOLE] * 2,
+        out_shape=[shape, shape],
+        cost_estimate=moved(*first, *second),
+        name="relay_sums",
+    )(*first, *second, *deps)
 
 
 def plus_kernel(left_ref, *refs):
@@ -818,7 +871,7 @@
     out_ref[...] = (residual_ref[...] + norm_back(hidden, gain_ref[...], back)).astype(BFLOAT)
 
 
-def last(dq, own, parts, inputs, residual, gain, weight):
+def last(dq, own, parts, inputs, residual, gain, weight, *deps):
     tokens, width = residual.shape
     inner = dq.shape[1]
     tile = tokens // 4
@@ -827,18 +880,19 @@
     far = pl.BlockSpec((tile, width), lambda g: (jnp.maximum(g - 2, 0), 0))
     piece = pl.BlockSpec((tile, 2 * inner), lambda g: (g, 0))
     return pl.pallas_call(
-        last_kernel,
+        skipping(last_kernel, 10, len(deps)),
         grid=(4,),
         in_specs=[
             pl.BlockSpec((tile, inner), lambda g: (g, 0)), piece, piece, piece, piece, near, far, whole,
             once(gain.shape), once(weight.shape),
-        ],
+        ]
+        + [UNREAD] * len(deps),
         out_specs=whole,
         out_shape=jax.ShapeDtypeStruct((tokens, width), BFLOAT),
         compiler_params=BIG,
         cost_estimate=pl.CostEstimate(flops=10**11, bytes_accessed=0, transcendentals=0),
         name="input_gradient",
-    )(dq, own, *parts, *inputs, residual, gain, weight)
+    )(dq, own, *parts, *inputs, residual, gain, weight, *deps)
 
 
 def choose(refs, slot):
@@ -1094,8 +1148,12 @@
     def over_groups(value):
         return lax.psum(value, "ctx", axis_index_groups=upper) if groups > 1 else value
 
-    late_parts = [late_part[0]] + [swap(late_part[index], 2 * index) for index in range(1, 4)]
+    late_own, first_near, first_far, second_near, second_far, last_near, last_far = late_part
+    low, high = swap(last_near, 4), swap(last_far, 2)
+    got_far, got_near = swap(first_far, 2), swap(second_near, 4)
     other_grad, mine_grad = outer_sums(normed_late, (back_other, back_mine))
+    first_near, second_far = relay_sums((first_near, low), (second_far, high), mine_grad, got_far, got_near)
+    late_parts = (swap(first_near, 2), got_near, got_far, swap(second_far, 4))
     other_got = [swap(other_grad[index : index + 1], 1) for index in range(2)]
     down_whole = outer_sums(activation, (cot_all,))[0]
     down_grad = down_whole.reshape(depth, 2, piece, width)
@@ -1103,7 +1161,7 @@
     down_send = jnp.where(is_zero, down_grad[:, 1], down_grad[:, 0])
     down_got = swap(down_send, 1)
     residual_grad, mix_low, attn_grad = middle(
-        after_attn, late_parts, own_cots, gains[1:2], proj_full, down_whole, mine_grad
+        after_attn, late_own, late_parts, own_cots, gains[1:2], proj_full, down_whole, mine_grad
     )
     attn_grad = attn_grad.reshape(seqs, rows, inner)
     proj_grad = tn(attn_low, jnp.pad(mix_low, ((0, 0), (0, 4 * wide - width)))).astype(BFLOAT)
@@ -1127,7 +1185,7 @@
     out_parts = exchange(after(out_part, attn_grad)).astype(FLOAT).reshape(4, tokens, width)
     result = (after_attn + jnp.sum(out_parts, axis=0)).astype(BFLOAT)
 
-    blocks = plus(keep, [swap(send, 1)], result)
+    blocks = plus_apart(keep, swap(send, 1), result)
     dkv_parts = [swap(dkv_four[index], 2 * index) for index in range(1, 4)]
     input_grad = last(dq, dkv_four[0], dkv_parts, (x_near, x_far), residual_grad, gains[0:1], qkv_full)
     levels = sum_parts([blocks[0]] + [swap(blocks[index], 2 * index) for index in range(1, 4)], input_grad, pair_own)

time: 497 us -> 489 us (0.984)
  Pallas kernels: 217 us -> 208 us
    pallas_call x2, Pallas kernels: 36.4 us -> 25.8 us  [outer_sums(): pl.pallas_call(outer_kernel, grid=(2,), in_specs=[pl.BlockSpec((2, tokens...]
    pallas_call x2 -> x4, Pallas kernels: 16.2 us -> 23.6 us  [the longest x1 9.28 us: last(): pl.pallas_call(skipping(last_kernel, 10, len(deps)), grid=(4,), in_specs=...]
    pallas_call x3 -> x2, Pallas kernels: 12.2 us -> 7.77 us  [plus(): pl.pallas_call(skipping(plus_kernel, 1 + len(rights), len(deps)), grid=(s...]
    ppermute x55 -> x58, starting transfers between devices: 44.4 us -> 47.4 us  [swap(): lax.ppermute(value, 'ctx', [(source, source ^ bit) for source in range(co...]
    unnamed x104 -> x118, local copies, waits for them, and re-layouts: 11.5 us -> 13.5 us
    ppermute x55 -> x58, waiting for transfers between devices: 118 us -> 118 us  [swap(): lax.ppermute(value, 'ctx', [(source, source ^ bit) for source in range(co...]
  transfers between devices with their start and end apart: 64 -> 67, of which waited for: 28 -> 31; matrix products, arithmetic and copies ran while one was open for 7% -> 6% of each run, Pallas kernels for 33% -> 31%
where the time goes in v5:
time: 489 us; the launch traced here: 480 us
  Pallas kernels  208 us (43%)
  waiting for transfers between devices  134 us (27%)
  starting transfers between devices  60.4 us (12%)
  local copies, waits for them, and re-layouts  27.6 us (6%)
  blocking collectives  19.4 us (4%)
  between operations  14.8 us (3%)
  other arithmetic  13.9 us (3%)
    ppermute x58, waiting for transfers between devices, swap(): lax.ppermute(value, 'ctx', [(source, source ^ bit) for source in range(co...  118 us
    ppermute x58, starting transfers between devices, swap(): lax.ppermute(value, 'ctx', [(source, source ^ bit) for source in range(co...  47.4 us
    pallas_call x1, Pallas kernels, feed_forward(): pl.pallas_call(feed_kernel, grid_spec=pltpu.PrefetchScalarGridSpec(num_sc...  42.4 us
    pallas_call x2, Pallas kernels, outer_sums(): pl.pallas_call(outer_kernel, grid=(2,), in_specs=[pl.BlockSpec((2, tokens...  25.8 us
    pallas_call x1, Pallas kernels, attention_backward(): pl.pallas_call(skipping(functools.partial(backward_kernel, rows=rows, cou...  21.2 us
    all_gather x1, blocking collectives, on_device(): packed = lax.all_gather(packed, 'wsh', axis=0)  19.4 us
    pallas_call x1, Pallas kernels, attention_forward(): pl.pallas_call(functools.partial(forward_kernel, rows=rows, count=count,...  14.9 us
    ppermute x3, waiting for transfers between devices, swap_depth(): lax.ppermute(value, 'wsh', [(source, source ^ bit) for source in range(co...  13.9 us
  transfers between devices with their start and end apart: 67, of which 31 were waited for; matrix products, arithmetic and copies ran while one was open for 6% of the time, Pallas kernels for 31%

profile of v5, /device:TPU:0, one launch (start us, length us, event | category | flops | bytes accessed | tf_op | source)
XLA Modules:
  0.0 479.9 jit_solution(7312890669430055983)
XLA Ops:
  7.2 4.7 token_rows.1
  11.9 3.0 collective-permute-start.2
  14.9 1.5 collective-permute-start
  17.1 2.3 constant_dynamic-slice_fusion.4
  24.1 2.0 pack.1
  26.1 19.4 %all-gather = bf16[320,1152]{1,0:T(8,128)(2,1)S(1)} all-gather(bf16[80,1152]{1,0:T(8,128)(2,1)} %pack.1), channel_id=2, replica_groups=mesh['ctx'=8,'wsh'=4] {'wsh'}, dimensions={0}, use_global_device_ids=true | all-gather | bytes 921600 | tf_op jit(solution)/shard_map/all_gather | solution.py:1096
  45.7 1.6 collective-permute-start.5
  48.8 9.9 %collective-permute-done.5 = bf16[272,1152]{1,0:T(8,128)(2,1)S(1)} collective-permute-done((bf16[272,1152]{1,0:T(8,128)(2,1)S(1)}, bf16[272,1152]{1,0:T(8,128)(2,1)S(1)}, u32[]{:S(2)}, u32[]{:S(2)}) %collective-permute-start.5) | collective-permute-done | bytes 626720 | tf_op jit(solution)/shard_map/ppermute | solution.py:309
  58.7 2.5 collective-permute-start.7
  62.7 5.6 %collective-permute-done.6 = bf16[128,1152]{1,0:T(8,128)(2,1)S(1)} collective-permute-done((bf16[128,1152]{1,0:T(8,128)(2,1)S(1)}, bf16[128,1152]{1,0:T(8,128)(2,1)S(1)}, u32[]{:S(2)}, u32[]{:S(2)}) %collective-permute-start.6) | collective-permute-done | bytes 294944 | tf_op jit(solution)/shard_map/ppermute | solution.py:309
  68.4 1.8 pad_maximum_fusion.near_ref
  71.5 1.5 collective-permute-start.10
  73.0 5.0 %all-to-all-start = ((bf16[8,192,1472]{2,1,0:T(8,128)(2,1)}), bf16[8,192,1472]{2,1,0:T(8,128)(2,1)}, u32[]{:S(2)}, u32[]{:S(2)}) async-start(bf16[8,192,1472]{2,1,0:T(8,128)(2,1)} %get-tuple-element.104.refs_6_), calls=%async_computation | async-start | bytes 9437184 | tf_op jit(solution)/shard_map/all_to_all | solution.py:1064
  78.8 4.8 %unpack.1 = (bf16[1472,1152]{1,0:T(8,128)(2,1)}, bf16[384,1472]{1,0:T(8,128)(2,1)}, f32[8,1472]{1,0:T(8,128)}, f32[32,128]{1,0:T(8,128)}, f32[3,8,128]{2,1,0:T(8,128)}) custom-call(s32[2]{0:T(128)} %pad_add_fusion.place_ref.refs_0_, bf16[4,16,1152]{2,1,0:T(8,128)(2,1)} %slice.72.misc_ref, bf16[4,272,1152]{2,1,0:T(8,128)(2,1)} %copy-done.4, ...), custom_call_target="tpu_custom_call" | custom-call | bytes 1504051 | tf_op jit(solution)/shard_map/unpack/pallas_call | solution.py:1104
  85.1 1.7 collective-permute-done.9.refs_6_.refs_10_
  88.0 12.2 %norm_project.1 = (bf16[4,384,1472]{2,1,0:T(8,128)(2,1)}, bf16[1,384,768]{2,1,0:T(8,128)(2,1)}, bf16[1,384,768]{2,1,0:T(8,128)(2,1)}, bf16[1,384,768]{2,1,0:T(8,...) custom-call(bf16[192,1472]{1,0:T(8,128)(2,1)} %get-tuple-element.88.refs_0_.refs_4_.refs_5_, ...), custom_call_target="tpu_custom_call" | custom-call | flops 781398848 | bytes 2034892 | tf_op jit(solution)/shard_map/norm_project/pallas_call | solution.py:552
  105.8 14.9 %attention_forward.1 = (f32[3,128,384]{2,1,0:T(8,128)}, f32[3,3,8,128]{3,2,1,0:T(8,128)}) custom-call(s32[1]{0:T(128)} %bitcast.meta_ref.refs_0_, f32[32,128]{1,0:T(8,128)} %get-tuple-element.91.table_ref.refs_1_, f32[3,8,128]{2,1,0:T(8,128)} %get-tuple-element.92.segs_ref.refs_2_, bf16[3,128,384]{2,1,0:T(8,128)(2,1)} %bitcast.107, ...), custom_call_target="tpu_custom_call" | custom-call | flops 120795952 | bytes 1887436 | tf_op jit(solution)/shard_map/attention_forward/pallas_call | solution.py:267
  122.0 1.7 collective-permute-start.17
  125.5 19.6 %collective-permute-done.17.refs_3_ = bf16[384,384]{1,0:T(8,128)(2,1)S(1)} collective-permute-done((bf16[384,384]{1,0:T(8,128)(2,1)S(1)}, bf16[384,384]{1,0:T(8,128)(2,1)S(1)}, u32[]{:S(2)}, u32[]{:S(2)}) %collective-permute-start.17) | collective-permute-done | bytes 294944 | tf_op jit(solution)/shard_map/ppermute | solution.py:309
  145.2 4.3 collective-permute-done.16.refs_2_
  151.1 9.9 %late_norm.1 = (f32[384,1472]{1,0:T(8,128)}, bf16[4,384,1472]{2,1,0:T(8,128)(2,1)}) custom-call(bf16[384,384]{1,0:T(8,128)(2,1)} %bitcast.101, bf16[384,384]{1,0:T(8,128)(2,1)} %copy-done.41, bf16[384,384]{1,0:T(8,128)(2,1)} %copy-done.40, bf16[384,384]{1,0:T(8,128)(2,1)} %copy-done.39, bf16[192,1472]{1,0:T(8,128)(2,1)} %get-tuple-element.88.refs_0_.refs_4_.refs_5_, ...), custom_call_target="tpu_custom_call" | custom-call | flops 347288384 | bytes 2713190 | tf_op jit(solution)/shard_map/late_norm/pallas_call | solution.py:597
  161.6 2.7 collective-permute-done.19.down_other
  165.5 42.4 %feed_forward.1 = (bf16[4,384,896]{2,1,0:T(8,128)(2,1)}, bf16[4,384,896]{2,1,0:T(8,128)(2,1)}, bf16[4,384,896]{2,1,0:T(8,128)(2,1)}, bf16[8,192,1472]{2,1,0:T(8,...) custom-call(s32[2]{0:T(128)} %pad_add_fusion.1.spot_ref, ...), custom_call_target="tpu_custom_call" | custom-call | flops 4862036992 | bytes 3391488 | tf_op jit(solution)/shard_map/feed_forward/pallas_call | solution.py:685
  208.8 2.1 collective-permute-start.21
  212.0 16.7 %outer_sums.2 = (bf16[2,736,896]{2,1,0:T(8,128)(2,1)}, bf16[2,736,896]{2,1,0:T(8,128)(2,1)}) custom-call(bf16[4,384,1472]{2,1,0:T(8,128)(2,1)} %get-tuple-element.103.normed_ref.left_ref, bf16[4,384,896]{2,1,0:T(8,128)(2,1)} %get-tuple-element.115.refs_0_, bf16[4,384,896]{2,1,0:T(8,128)(2,1)} %get-tuple-element.116.refs_1_), custom_call_target="tpu_custom_call" | custom-call | flops 3241358080 | tf_op jit(solution)/shard_map/outer_sums/pallas_call | solution.py:727
  228.7 8.4 %collective-permute-done.22.refs_5_.refs_4_ = bf16[192,1472]{1,0:T(8,128)(2,1)S(1)} collective-permute-done((bf16[192,1472]{1,0:T(8,128)(2,1)}, bf16[192,1472]{1,0:T(8,128)(2,1)S(1)}, u32[]{:S(2)}, u32[]{:S(2)}) %collective-permute-start.22) | collective-permute-done | bytes 565280 | tf_op jit(solution)/shard_map/ppermute | solution.py:309
  238.1 2.9 relay_sums.1
  241.0 1.7 collective-permute-start.24
  243.5 1.7 fusion.4
  245.8 9.1 %outer_sums.3.refs_9_ = bf16[2,448,1472]{2,1,0:T(8,128)(2,1)} custom-call(bf16[4,384,896]{2,1,0:T(8,128)(2,1)} %get-tuple-element.122.left_ref, bf16[4,384,1472]{2,1,0:T(8,128)(2,1)} %get-tuple-element.123.refs_0_), custom_call_target="tpu_custom_call" | custom-call | flops 1620679040 | tf_op jit(solution)/shard_map/outer_sums/pallas_call | solution.py:727
  257.0 6.7 %middle.1 = (f32[384,1472]{1,0:T(8,128)}, bf16[384,1472]{1,0:T(8,128)(2,1)}, bf16[384,384]{1,0:T(8,128)(2,1)}) custom-call(f32[384,1472]{1,0:T(8,128)} %get-tuple-element.102.refs_0_, bf16[2,192,1472]{2,1,0:T(8,128)(2,1)} %get-tuple-element.110.refs_1_, bf16[192,1472]{1,0:T(8,128)(2,1)} %copy-done.57, bf16[192,1472]{1,0:T(8,128)(2,1)} %copy-done.28, ...), custom_call_target="tpu_custom_call" | custom-call | flops 99999997952 | tf_op jit(solution)/shard_map/middle/pallas_call | solution.py:779
  265.2 3.9 plus.2
  269.1 5.0 %all-to-all-start.1 = ((bf16[8,192,1472]{2,1,0:T(8,128)(2,1)}), bf16[8,192,1472]{2,1,0:T(8,128)(2,1)}, u32[]{:S(2)}, u32[]{:S(2)}) async-start(bf16[8,192,1472]{2,1,0:T(8,128)(2,1)} %get-tuple-element.125), calls=%async_computation.1 | async-start | bytes 9437184 | tf_op jit(solution)/shard_map/all_to_all | solution.py:1064
  274.1 21.2 %attention_backward.1 = (bf16[3,128,384]{2,1,0:T(8,128)(2,1)}, bf16[1,3,128,768]{3,2,1,0:T(8,128)(2,1)}, bf16[1,3,128,768]{3,2,1,0:T(8,128)(2,1)}, bf16[1,3,128,...) custom-call(s32[1]{0:T(128)} %bitcast.meta_ref.refs_0_, ...), custom_call_target="tpu_custom_call" | custom-call | flops 301989888 | bytes 4718592 | tf_op jit(solution)/shard_map/attention_backward/pallas_call | solution.py:289
  298.1 1.9 convolution_convert_fusion.refs_12_
  301.2 13.4 %weight_grads.1 = (bf16[384,768]{1,0:T(8,128)(2,1)}, bf16[384,768]{1,0:T(8,128)(2,1)}, bf16[384,768]{1,0:T(8,128)(2,1)}, bf16[384,768]{1,0:T(8,128)(2,1)}, bf16[...) custom-call(s32[2]{0:T(128)} %pad_add_fusion.place_ref.refs_0_, ...), custom_call_target="tpu_custom_call" | custom-call | flops 781398848 | bytes 1356595 | tf_op jit(solution)/shard_map/weight_grads/pallas_call | solution.py:488
  316.4 1.9 collective-permute-start.32
  322.2 3.9 plus.3
  326.0 2.5 all-to-all-done.1
  328.5 3.5 convert_reduce_fusion
  333.4 4.7 plus_apart.1
  338.0 1.5 collective-permute-start.36
  341.9 1.5 collective-permute-start.38
  343.4 11.4 %collective-permute-done.34.refs_4_ = bf16[384,768]{1,0:T(8,128)(2,1)} collective-permute-done((bf16[384,768]{1,0:T(8,128)(2,1)S(1)}, bf16[384,768]{1,0:T(8,128)(2,1)}, u32[]{:S(2)}, u32[]{:S(2)}) %collective-permute-start.34) | collective-permute-done | bytes 589856 | tf_op jit(solution)/shard_map/ppermute | solution.py:309
  354.7 9.3 %input_gradient.1.refs_4_ = bf16[384,1472]{1,0:T(8,128)(2,1)} custom-call(bf16[384,384]{1,0:T(8,128)(2,1)} %bitcast.117, bf16[384,768]{1,0:T(8,128)(2,1)} %get-tuple-element.140.refs_1_, bf16[384,768]{1,0:T(8,128)(2,1)} %copy-done.56, bf16[384,768]{1,0:T(8,128)(2,1)} %collective-permute-done.33.refs_3_, bf16[384,768]{1,0:T(8,128)(2,1)} %collective-permute-done.34.refs_4_, ...), custom_call_target="tpu_custom_call" | custom-call | flops 99999997952 | tf_op jit(solution)/shard_map/input_gradient/pallas_call | solution.py:882
  364.0 2.3 collective-permute-done.36.refs_1_
  366.4 11.2 %collective-permute-done.38.refs_3_ = bf16[4,64,1152]{2,1,0:T(8,128)(2,1)S(1)} collective-permute-done((bf16[4,64,1152]{2,1,0:T(8,128)(2,1)}, bf16[4,64,1152]{2,1,0:T(8,128)(2,1)S(1)}, u32[]{:S(2)}, u32[]{:S(2)}) %collective-permute-start.38) | collective-permute-done | bytes 589856 | tf_op jit(solution)/shard_map/ppermute | solution.py:309
  378.4 2.8 sum_parts.2
  384.7 1.8 slice_bitcast_fusion.2
  386.5 3.0 collective-permute-start.41
  389.5 4.1 collective-permute-done.41.refs_3_
  394.2 4.7 collective-permute-done.40.refs_2_
  398.9 5.1 %collective-permute-done.39.refs_1_ = bf16[64,1152]{1,0:T(8,128)(2,1)S(1)} collective-permute-done((bf16[64,1152]{1,0:T(8,128)(2,1)S(1)}, bf16[64,1152]{1,0:T(8,128)(2,1)S(1)}, u32[]{:S(2)}, u32[]{:S(2)}) %collective-permute-start.39) | collective-permute-done | bytes 147488 | tf_op jit(solution)/shard_map/ppermute | solution.py:314
  404.7 13.5 %collective-permute-done.56.refs_3_ = bf16[112,1472]{1,0:T(8,128)(2,1)S(1)} collective-permute-done((bf16[112,1472]{1,0:T(8,128)(2,1)}, bf16[112,1472]{1,0:T(8,128)(2,1)S(1)}, u32[]{:S(2)}, u32[]{:S(2)}) %collective-permute-start.56) | collective-permute-done | bytes 329760 | tf_op jit(solution)/shard_map/ppermute | solution.py:309
  419.3 5.6 %collective-permute-done.55.refs_2_ = bf16[112,1472]{1,0:T(8,128)(2,1)} collective-permute-done((bf16[112,1472]{1,0:T(8,128)(2,1)}, bf16[112,1472]{1,0:T(8,128)(2,1)}, u32[]{:S(2)}, u32[]{:S(2)}) %collective-permute-start.55) | collective-permute-done | bytes 329760 | tf_op jit(solution)/shard_map/ppermute | solution.py:309
  426.1 1.9 sum_parts.3.refs_0_
  428.0 6.7 %collective-permute-done.54.refs_1_ = bf16[112,1472]{1,0:T(8,128)(2,1)} collective-permute-done((bf16[112,1472]{1,0:T(8,128)(2,1)}, bf16[112,1472]{1,0:T(8,128)(2,1)}, u32[]{:S(2)}, u32[]{:S(2)}) %collective-permute-start.54) | collective-permute-done | bytes 329760 | tf_op jit(solution)/shard_map/ppermute | solution.py:309
  434.6 1.8 collective-permute-start.47
  437.9 3.1 collective-permute-done.47.refs_3_
  441.0 1.7 collective-permute-start.45
  444.3 8.2 %spread_columns.1 = (f32[368,3584]{1,0:T(8,128)}, f32[368,3584]{1,0:T(8,128)}, f32[368,128]{1,0:T(8,128)}) custom-call(s32[2]{0:T(128)} %pad_add_fusion.place_ref.refs_0_, bf16[368,896]{1,0:T(8,128)(2,1)} %reduce-scatter.3.cloned.1.call-done.refs_5_.refs_0_, bf16[368,896]{1,0:T(8,128)(2,1)} %copy-done.17, bf16[368,896]{1,0:T(8,128)(2,1)} %copy-done.16, ...), custom_call_target="tpu_custom_call" | custom-call | flops 1055129 | bytes 4220518 | tf_op jit(solution)/shard_map/spread_columns/pallas_call | solution.py:927
  453.2 2.0 stack_small.1.near_ref
  458.1 7.1 %join_down.1 = f32[1472,896]{1,0:T(8,128)} custom-call(s32[2]{0:T(128)} %pad_add_fusion.place_ref.refs_0_, bf16[112,1472]{1,0:T(8,128)(2,1)} %reduce-scatter.5.cloned.1.call-done.refs_0_, bf16[112,1472]{1,0:T(8,128)(2,1)} %collective-permute-done.54.refs_1_, bf16[112,1472]{1,0:T(8,128)(2,1)} %collective-permute-done.55.refs_2_, ...), custom_call_target="tpu_custom_call" | custom-call | bytes 197836 | tf_op jit(solution)/shard_map/join_down/pallas_call | solution.py:1200
  466.8 3.2 finish_small.1
  (250 shorter events, 65.6 us)
Async XLA Ops:
  7.2 114.6 %all-gather.4.cloned.1.call-start = ((), (), s32[]{:S(2)}) async-start(), calls=%async_computation.4 | async-start | bytes 3297280 | tf_op jit(solution)/shard_map/all_gather | solution.py:1097
  11.9 33.7 %collective-permute-start.2 = (bf16[192,1472]{1,0:T(8,128)(2,1)}, bf16[192,1472]{1,0:T(8,128)(2,1)}, u32[]{:S(2)}, u32[]{:S(2)}) collective-permute-start(bf16[192,1472]{1,0:T(8,128)(2,1)} %get-tuple-element.88.refs_0_.refs_4_.refs_5_), channel_id=1, source_target_pairs={{0,16},{4,20},{8,24},{12,28},{16,0},{20,4},{24,8},{28,12},{1,17},{... | collective-permute-start | bytes 1695752 | tf_op jit(solution)/shard_map/ppermute | solution.py:309
  14.9 30.8 %collective-permute-start = (bf16[192,1472]{1,0:T(8,128)(2,1)}, bf16[192,1472]{1,0:T(8,128)(2,1)}, u32[]{:S(2)}, u32[]{:S(2)}) collective-permute-start(bf16[192,1472]{1,0:T(8,128)(2,1)} %get-tuple-element.88.refs_0_.refs_4_.refs_5_), channel_id=1, source_target_pairs={{0,8},{4,12},{8,0},{12,4},{16,24},{20,28},{24,16},{28,20},{1,9},{5... | collective-permute-start | bytes 1695752 | tf_op jit(solution)/shard_map/ppermute | solution.py:309
  16.4 29.3 %collective-permute-start.3 = (bf16[192,1472]{1,0:T(8,128)(2,1)}, bf16[192,1472]{1,0:T(8,128)(2,1)}, u32[]{:S(2)}, u32[]{:S(2)}) collective-permute-start(bf16[192,1472]{1,0:T(8,128)(2,1)} %get-tuple-element.89.refs_1_.refs_5_.refs_6_), channel_id=1, source_target_pairs={{0,16},{4,20},{8,24},{12,28},{16,0},{20,4},{24,8},{28,12},{1,17},{... | collective-permute-start | bytes 1695752 | tf_op jit(solution)/shard_map/ppermute | solution.py:309
  16.9 28.8 %collective-permute-start.1 = (bf16[192,1472]{1,0:T(8,128)(2,1)}, bf16[192,1472]{1,0:T(8,128)(2,1)}, u32[]{:S(2)}, u32[]{:S(2)}) collective-permute-start(bf16[192,1472]{1,0:T(8,128)(2,1)} %get-tuple-element.89.refs_1_.refs_5_.refs_6_), channel_id=1, source_target_pairs={{0,8},{4,12},{8,0},{12,4},{16,24},{20,28},{24,16},{28,20},{1,9},{5... | collective-permute-start | bytes 1695752 | tf_op jit(solution)/shard_map/ppermute | solution.py:309
  45.7 12.9 %collective-permute-start.5 = (bf16[272,1152]{1,0:T(8,128)(2,1)S(1)}, bf16[272,1152]{1,0:T(8,128)(2,1)S(1)}, u32[]{:S(2)}, u32[]{:S(2)}) collective-permute-start(bf16[272,1152]{1,0:T(8,128)(2,1)S(1)} %fusion.2), channel_id=1, source_target_pairs={{0,16},{4,20},{8,24},{12,28},{16,0},{20,4},{24,8},{28,12},{1,17},{... | collective-permute-start | bytes 1880072 | tf_op jit(solution)/shard_map/ppermute | solution.py:309
  47.3 14.2 %collective-permute-start.4 = (bf16[272,1152]{1,0:T(8,128)(2,1)S(1)}, bf16[272,1152]{1,0:T(8,128)(2,1)S(1)}, u32[]{:S(2)}, u32[]{:S(2)}) collective-permute-start(bf16[272,1152]{1,0:T(8,128)(2,1)S(1)} %fusion.2), channel_id=1, source_target_pairs={{0,8},{4,12},{8,0},{12,4},{16,24},{20,28},{24,16},{28,20},{1,9},{5... | collective-permute-start | bytes 1880072 | tf_op jit(solution)/shard_map/ppermute | solution.py:309
  58.7 9.6 %collective-permute-start.7 = (bf16[144,1152]{1,0:T(8,128)(2,1)S(1)}, bf16[144,1152]{1,0:T(8,128)(2,1)S(1)}, u32[]{:S(2)}, u32[]{:S(2)}) collective-permute-start(bf16[144,1152]{1,0:T(8,128)(2,1)S(1)} %slice.75), channel_id=1, source_target_pairs={{0,8},{4,12},{8,0},{12,4},{16,24},{20,28},{24,16},{28,20},{1,9},{5... | collective-permute-start | bytes 995336 | tf_op jit(solution)/shard_map/ppermute | solution.py:309
  61.5 6.8 %collective-permute-start.6 = (bf16[128,1152]{1,0:T(8,128)(2,1)S(1)}, bf16[128,1152]{1,0:T(8,128)(2,1)S(1)}, u32[]{:S(2)}, u32[]{:S(2)}) collective-permute-start(bf16[128,1152]{1,0:T(8,128)(2,1)S(1)} %slice.74), channel_id=1, source_target_pairs={{0,16},{4,20},{8,24},{12,28},{16,0},{20,4},{24,8},{28,12},{1,17},{... | collective-permute-start | bytes 884744 | tf_op jit(solution)/shard_map/ppermute | solution.py:309
  70.2 8.6 %collective-permute-start.8 = (bf16[4,272,1152]{2,1,0:T(8,128)(2,1)S(1)}, bf16[4,272,1152]{2,1,0:T(8,128)(2,1)}, u32[]{:S(2)}, u32[]{:S(2)}) collective-permute-start(bf16[4,272,1152]{2,1,0:T(8,128)(2,1)S(1)} %pad_maximum_fusion.near_ref), channel_id=1, source_target_pairs={{0,4},{4,0},{8,12},{12,8},{16,20},{20,16},{24,28},{28,24},{1,5},{5... | collective-permute-start | bytes 7520264 | tf_op jit(solution)/shard_map/ppermute | solution.py:309
  70.3 16.5 %collective-permute-start.9 = (bf16[192,1472]{1,0:T(8,128)(2,1)}, bf16[192,1472]{1,0:T(8,128)(2,1)}, u32[]{:S(2)}, u32[]{:S(2)}) collective-permute-start(bf16[192,1472]{1,0:T(8,128)(2,1)} %collective-permute-done.refs_2_.refs_6_), channel_id=1, source_target_pairs={{0,16},{4,20},{8,24},{12,28},{16,0},{20,4},{24,8},{28,12},{1,17},{... | collective-permute-start | bytes 1695752 | tf_op jit(solution)/shard_map/ppermute | solution.py:309
  71.5 16.5 %collective-permute-start.10 = (bf16[192,1472]{1,0:T(8,128)(2,1)}, bf16[192,1472]{1,0:T(8,128)(2,1)}, u32[]{:S(2)}, u32[]{:S(2)}) collective-permute-start(bf16[192,1472]{1,0:T(8,128)(2,1)} %collective-permute-done.3.refs_5_.refs_9_), channel_id=1, source_target_pairs={{0,8},{4,12},{8,0},{12,4},{16,24},{20,28},{24,16},{28,20},{1,9},{5... | collective-permute-start | bytes 1695752 | tf_op jit(solution)/shard_map/ppermute | solution.py:309
  73.0 88.6 %all-to-all-start = ((bf16[8,192,1472]{2,1,0:T(8,128)(2,1)}), bf16[8,192,1472]{2,1,0:T(8,128)(2,1)}, u32[]{:S(2)}, u32[]{:S(2)}) async-start(bf16[8,192,1472]{2,1,0:T(8,128)(2,1)} %get-tuple-element.104.refs_6_), calls=%async_computation | async-start | bytes 9437184 | tf_op jit(solution)/shard_map/all_to_all | solution.py:1064
  78.0 83.0 %all-gather.6.cloned.1.call-start = ((), (), s32[]{:S(2)}) async-start(), calls=%async_computation.5 | async-start | bytes 1720320 | tf_op jit(solution)/shard_map/all_gather | solution.py:1103
  78.7 298.9 %reduce-scatter.3.cloned.1.call-start = ((), (), s32[]{:S(2)}) async-start(), calls=%async_computation.6 | async-start | bytes 3297280 | tf_op jit(solution)/shard_map/reduce_scatter | solution.py:1183
  100.7 3.4 collective-permute-start.13
  100.8 4.2 collective-permute-start.14
  121.8 42.5 %collective-permute-start.18 = (bf16[1472,896]{1,0:T(8,128)(2,1)}, bf16[1472,896]{1,0:T(8,128)(2,1)}, u32[]{:S(2)}, u32[]{:S(2)}) collective-permute-start(bf16[1472,896]{1,0:T(8,128)(2,1)} %all-gather.4.cloned.1.call-done.mine_ref), channel_id=1, source_target_pairs={{0,4},{4,0},{8,12},{12,8},{16,20},{20,16},{24,28},{28,24},{1,5},{5... | collective-permute-start | bytes 7913480 | tf_op jit(solution)/shard_map/ppermute | solution.py:309
  122.0 23.2 %collective-permute-start.17 = (bf16[384,384]{1,0:T(8,128)(2,1)S(1)}, bf16[384,384]{1,0:T(8,128)(2,1)S(1)}, u32[]{:S(2)}, u32[]{:S(2)}) collective-permute-start(bf16[384,384]{1,0:T(8,128)(2,1)S(1)} %bitcast.98), channel_id=1, source_target_pairs={{0,24},{4,28},{8,16},{12,20},{16,8},{20,12},{24,0},{28,4},{1,25},{... | collective-permute-start | bytes 884744 | tf_op jit(solution)/shard_map/ppermute | solution.py:309
  123.7 25.7 %collective-permute-start.16 = (bf16[384,384]{1,0:T(8,128)(2,1)S(1)}, bf16[384,384]{1,0:T(8,128)(2,1)S(1)}, u32[]{:S(2)}, u32[]{:S(2)}) collective-permute-start(bf16[384,384]{1,0:T(8,128)(2,1)S(1)} %bitcast.99), channel_id=1, source_target_pairs={{0,16},{4,20},{8,24},{12,28},{16,0},{20,4},{24,8},{28,12},{1,17},{... | collective-permute-start | bytes 884744 | tf_op jit(solution)/shard_map/ppermute | solution.py:309
  125.0 25.4 %collective-permute-start.15 = (bf16[384,384]{1,0:T(8,128)(2,1)S(1)}, bf16[384,384]{1,0:T(8,128)(2,1)S(1)}, u32[]{:S(2)}, u32[]{:S(2)}) collective-permute-start(bf16[384,384]{1,0:T(8,128)(2,1)S(1)} %bitcast.100), channel_id=1, source_target_pairs={{0,8},{4,12},{8,0},{12,4},{16,24},{20,28},{24,16},{28,20},{1,9},{5... | collective-permute-start | bytes 884744 | tf_op jit(solution)/shard_map/ppermute | solution.py:309
  207.8 20.8 %collective-permute-start.20 = (bf16[192,1472]{1,0:T(8,128)(2,1)}, bf16[192,1472]{1,0:T(8,128)(2,1)S(1)}, u32[]{:S(2)}, u32[]{:S(2)}) collective-permute-start(bf16[192,1472]{1,0:T(8,128)(2,1)} %get-tuple-element.112), channel_id=1, source_target_pairs={{0,16},{4,20},{8,24},{12,28},{16,0},{20,4},{24,8},{28,12},{1,17},{... | collective-permute-start | bytes 1695752 | tf_op jit(solution)/shard_map/ppermute | solution.py:309
  208.8 19.9 %collective-permute-start.21 = (bf16[192,1472]{1,0:T(8,128)(2,1)}, bf16[192,1472]{1,0:T(8,128)(2,1)S(1)}, u32[]{:S(2)}, u32[]{:S(2)}) collective-permute-start(bf16[192,1472]{1,0:T(8,128)(2,1)} %get-tuple-element.114), channel_id=1, source_target_pairs={{0,8},{4,12},{8,0},{12,4},{16,24},{20,28},{24,16},{28,20},{1,9},{5... | collective-permute-start | bytes 1695752 | tf_op jit(solution)/shard_map/ppermute | solution.py:309
  210.9 26.2 %collective-permute-start.22 = (bf16[192,1472]{1,0:T(8,128)(2,1)}, bf16[192,1472]{1,0:T(8,128)(2,1)S(1)}, u32[]{:S(2)}, u32[]{:S(2)}) collective-permute-start(bf16[192,1472]{1,0:T(8,128)(2,1)} %get-tuple-element.118), channel_id=1, source_target_pairs={{0,8},{4,12},{8,0},{12,4},{16,24},{20,28},{24,16},{28,20},{1,9},{5... | collective-permute-start | bytes 1695752 | tf_op jit(solution)/shard_map/ppermute | solution.py:309
  210.9 26.2 %collective-permute-start.23 = (bf16[192,1472]{1,0:T(8,128)(2,1)}, bf16[192,1472]{1,0:T(8,128)(2,1)S(1)}, u32[]{:S(2)}, u32[]{:S(2)}) collective-permute-start(bf16[192,1472]{1,0:T(8,128)(2,1)} %get-tuple-element.119), channel_id=1, source_target_pairs={{0,16},{4,20},{8,24},{12,28},{16,0},{20,4},{24,8},{28,12},{1,17},{... | collective-permute-start | bytes 1695752 | tf_op jit(solution)/shard_map/ppermute | solution.py:309
  241.0 14.7 %collective-permute-start.24 = (bf16[192,1472]{1,0:T(8,128)(2,1)}, bf16[192,1472]{1,0:T(8,128)(2,1)S(1)}, u32[]{:S(2)}, u32[]{:S(2)}) collective-permute-start(bf16[192,1472]{1,0:T(8,128)(2,1)} %get-tuple-element.120), channel_id=1, source_target_pairs={{0,8},{4,12},{8,0},{12,4},{16,24},{20,28},{24,16},{28,20},{1,9},{5... | collective-permute-start | bytes 1695752 | tf_op jit(solution)/shard_map/ppermute | solution.py:309
  242.8 14.2 %collective-permute-start.25 = (bf16[192,1472]{1,0:T(8,128)(2,1)}, bf16[192,1472]{1,0:T(8,128)(2,1)}, u32[]{:S(2)}, u32[]{:S(2)}) collective-permute-start(bf16[192,1472]{1,0:T(8,128)(2,1)} %get-tuple-element.121), channel_id=1, source_target_pairs={{0,16},{4,20},{8,24},{12,28},{16,0},{20,4},{24,8},{28,12},{1,17},{... | collective-permute-start | bytes 1695752 | tf_op jit(solution)/shard_map/ppermute | solution.py:309
  245.2 18.4 %collective-permute-start.31 = (bf16[1,736,896]{2,1,0:T(8,128)(2,1)}, bf16[1,736,896]{2,1,0:T(8,128)(2,1)S(1)}, u32[]{:S(2)}, u32[]{:S(2)}) collective-permute-start(bf16[1,736,896]{2,1,0:T(8,128)(2,1)} %get-tuple-element.200), channel_id=1, source_target_pairs={{0,4},{4,0},{8,12},{12,8},{16,20},{20,16},{24,28},{28,24},{1,5},{5... | collective-permute-start | bytes 3956744 | tf_op jit(solution)/shard_map/ppermute | solution.py:309
  245.2 18.5 %collective-permute-start.30 = (bf16[1,736,896]{2,1,0:T(8,128)(2,1)}, bf16[1,736,896]{2,1,0:T(8,128)(2,1)S(1)}, u32[]{:S(2)}, u32[]{:S(2)}) collective-permute-start(bf16[1,736,896]{2,1,0:T(8,128)(2,1)} %get-tuple-element.201), channel_id=1, source_target_pairs={{0,4},{4,0},{8,12},{12,8},{16,20},{20,16},{24,28},{28,24},{1,5},{5... | collective-permute-start | bytes 3956744 | tf_op jit(solution)/shard_map/ppermute | solution.py:309
  269.1 59.4 %all-to-all-start.1 = ((bf16[8,192,1472]{2,1,0:T(8,128)(2,1)}), bf16[8,192,1472]{2,1,0:T(8,128)(2,1)}, u32[]{:S(2)}, u32[]{:S(2)}) async-start(bf16[8,192,1472]{2,1,0:T(8,128)(2,1)} %get-tuple-element.125), calls=%async_computation.1 | async-start | bytes 9437184 | tf_op jit(solution)/shard_map/all_to_all | solution.py:1064
  274.1 115.4 %reduce-scatter.5.cloned.1.call-start = ((), (), s32[]{:S(2)}) async-start(), calls=%async_computation.7 | async-start | bytes 1720320 | tf_op jit(solution)/shard_map/reduce_scatter | solution.py:1184
  295.3 4.7 collective-permute-start.26
  295.4 4.6 collective-permute-start.27
  295.9 4.2 collective-permute-start.28
  296.0 4.2 collective-permute-start.29
  314.6 18.8 %collective-permute-start.35 = (bf16[4,4,64,1152]{3,2,1,0:T(8,128)(2,1)}, bf16[4,4,64,1152]{3,2,1,0:T(8,128)(2,1)}, u32[]{:S(2)}, u32[]{:S(2)}) collective-permute-start(bf16[4,4,64,1152]{3,2,1,0:T(8,128)(2,1)} %get-tuple-element.146), channel_id=1, source_target_pairs={{0,4},{4,0},{8,12},{12,8},{16,20},{20,16},{24,28},{28,24},{1,5},{5... | collective-permute-start | bytes 7077896 | tf_op jit(solution)/shard_map/ppermute | solution.py:309
  315.9 5.2 %collective-permute-start.53 = (bf16[4,112,1472]{2,1,0:T(8,128)(2,1)S(1)}, bf16[4,112,1472]{2,1,0:T(8,128)(2,1)S(1)}, u32[]{:S(2)}, u32[]{:S(2)}) collective-permute-start(bf16[4,112,1472]{2,1,0:T(8,128)(2,1)S(1)} %get-tuple-element.198), channel_id=1, source_target_pairs={{0,4},{4,0},{8,12},{12,8},{16,20},{20,16},{24,28},{28,24},{1,5},{5... | collective-permute-start | bytes 3956744 | tf_op jit(solution)/shard_map/ppermute | solution.py:309
  316.4 24.7 %collective-permute-start.32 = (bf16[384,768]{1,0:T(8,128)(2,1)}, bf16[384,768]{1,0:T(8,128)(2,1)S(1)}, u32[]{:S(2)}, u32[]{:S(2)}) collective-permute-start(bf16[384,768]{1,0:T(8,128)(2,1)} %get-tuple-element.141), channel_id=1, source_target_pairs={{0,8},{4,12},{8,0},{12,4},{16,24},{20,28},{24,16},{28,20},{1,9},{5... | collective-permute-start | bytes 1769480 | tf_op jit(solution)/shard_map/ppermute | solution.py:309
  318.2 25.1 %collective-permute-start.33 = (bf16[384,768]{1,0:T(8,128)(2,1)}, bf16[384,768]{1,0:T(8,128)(2,1)}, u32[]{:S(2)}, u32[]{:S(2)}) collective-permute-start(bf16[384,768]{1,0:T(8,128)(2,1)} %get-tuple-element.142), channel_id=1, source_target_pairs={{0,16},{4,20},{8,24},{12,28},{16,0},{20,4},{24,8},{28,12},{1,17},{... | collective-permute-start | bytes 1769480 | tf_op jit(solution)/shard_map/ppermute | solution.py:309
  319.7 35.0 %collective-permute-start.34 = (bf16[384,768]{1,0:T(8,128)(2,1)S(1)}, bf16[384,768]{1,0:T(8,128)(2,1)}, u32[]{:S(2)}, u32[]{:S(2)}) collective-permute-start(bf16[384,768]{1,0:T(8,128)(2,1)S(1)} %copy-done.55), channel_id=1, source_target_pairs={{0,24},{4,28},{8,16},{12,20},{16,8},{20,12},{24,0},{28,4},{1,25},{... | collective-permute-start | bytes 1769480 | tf_op jit(solution)/shard_map/ppermute | solution.py:309
  338.0 28.3 %collective-permute-start.36 = (bf16[4,64,1152]{2,1,0:T(8,128)(2,1)}, bf16[4,64,1152]{2,1,0:T(8,128)(2,1)S(1)}, u32[]{:S(2)}, u32[]{:S(2)}) collective-permute-start(bf16[4,64,1152]{2,1,0:T(8,128)(2,1)} %get-tuple-element.148), channel_id=1, source_target_pairs={{0,8},{4,12},{8,0},{12,4},{16,24},{20,28},{24,16},{28,20},{1,9},{5... | collective-permute-start | bytes 1769480 | tf_op jit(solution)/shard_map/ppermute | solution.py:309
  339.6 26.8 %collective-permute-start.37 = (bf16[4,64,1152]{2,1,0:T(8,128)(2,1)}, bf16[4,64,1152]{2,1,0:T(8,128)(2,1)S(1)}, u32[]{:S(2)}, u32[]{:S(2)}) collective-permute-start(bf16[4,64,1152]{2,1,0:T(8,128)(2,1)} %get-tuple-element.149), channel_id=1, source_target_pairs={{0,16},{4,20},{8,24},{12,28},{16,0},{20,4},{24,8},{28,12},{1,17},{... | collective-permute-start | bytes 1769480 | tf_op jit(solution)/shard_map/ppermute | solution.py:309
  341.9 35.7 %collective-permute-start.38 = (bf16[4,64,1152]{2,1,0:T(8,128)(2,1)}, bf16[4,64,1152]{2,1,0:T(8,128)(2,1)S(1)}, u32[]{:S(2)}, u32[]{:S(2)}) collective-permute-start(bf16[4,64,1152]{2,1,0:T(8,128)(2,1)} %get-tuple-element.150), channel_id=1, source_target_pairs={{0,24},{4,28},{8,16},{12,20},{16,8},{20,12},{24,0},{28,4},{1,25},{... | collective-permute-start | bytes 1769480 | tf_op jit(solution)/shard_map/ppermute | solution.py:309
  381.2 37.1 %collective-permute-start.44 = (bf16[368,896]{1,0:T(8,128)(2,1)S(1)}, bf16[368,896]{1,0:T(8,128)(2,1)S(1)}, u32[]{:S(2)}, u32[]{:S(2)}) collective-permute-start(bf16[368,896]{1,0:T(8,128)(2,1)S(1)} %copy-done.14), channel_id=1, source_target_pairs={{0,24},{4,28},{8,16},{12,20},{16,8},{20,12},{24,0},{28,4},{1,25},{... | collective-permute-start | bytes 1978376 | tf_op jit(solution)/shard_map/ppermute | solution.py:309
  381.8 36.9 %collective-permute-start.43 = (bf16[368,896]{1,0:T(8,128)(2,1)S(1)}, bf16[368,896]{1,0:T(8,128)(2,1)S(1)}, u32[]{:S(2)}, u32[]{:S(2)}) collective-permute-start(bf16[368,896]{1,0:T(8,128)(2,1)S(1)} %copy-done.14), channel_id=1, source_target_pairs={{0,16},{4,20},{8,24},{12,28},{16,0},{20,4},{24,8},{28,12},{1,17},{... | collective-permute-start | bytes 1978376 | tf_op jit(solution)/shard_map/ppermute | solution.py:309
  383.2 35.7 %collective-permute-start.42 = (bf16[368,896]{1,0:T(8,128)(2,1)S(1)}, bf16[368,896]{1,0:T(8,128)(2,1)S(1)}, u32[]{:S(2)}, u32[]{:S(2)}) collective-permute-start(bf16[368,896]{1,0:T(8,128)(2,1)S(1)} %copy-done.14), channel_id=1, source_target_pairs={{0,8},{4,12},{8,0},{12,4},{16,24},{20,28},{24,16},{28,20},{1,9},{5... | collective-permute-start | bytes 1978376 | tf_op jit(solution)/shard_map/ppermute | solution.py:309
  386.5 7.0 %collective-permute-start.41 = (bf16[64,1152]{1,0:T(8,128)(2,1)S(1)}, bf16[64,1152]{1,0:T(8,128)(2,1)S(1)}, u32[]{:S(2)}, u32[]{:S(2)}) collective-permute-start(bf16[64,1152]{1,0:T(8,128)(2,1)S(1)} %get-tuple-element.210), channel_id=1, source_target_pairs={{0,3},{1,2},{2,1},{3,0},{4,7},{5,6},{6,5},{7,4},{8,11},{9,10},{10,... | collective-permute-start | bytes 442376 | tf_op jit(solution)/shard_map/ppermute | solution.py:314
  389.5 9.4 %collective-permute-start.40 = (bf16[64,1152]{1,0:T(8,128)(2,1)S(1)}, bf16[64,1152]{1,0:T(8,128)(2,1)S(1)}, u32[]{:S(2)}, u32[]{:S(2)}) collective-permute-start(bf16[64,1152]{1,0:T(8,128)(2,1)S(1)} %get-tuple-element.211), channel_id=1, source_target_pairs={{0,2},{1,3},{2,0},{3,1},{4,6},{5,7},{6,4},{7,5},{8,10},{9,11},{10,... | collective-permute-start | bytes 442376 | tf_op jit(solution)/shard_map/ppermute | solution.py:314
  393.5 24.7 %collective-permute-start.56 = (bf16[112,1472]{1,0:T(8,128)(2,1)}, bf16[112,1472]{1,0:T(8,128)(2,1)S(1)}, u32[]{:S(2)}, u32[]{:S(2)}) collective-permute-start(bf16[112,1472]{1,0:T(8,128)(2,1)} %reduce-scatter.5.cloned.1.call-done.refs_0_), channel_id=1, source_target_pairs={{0,24},{4,28},{8,16},{12,20},{16,8},{20,12},{24,0},{28,4},{1,25},{... | collective-permute-start | bytes 989192 | tf_op jit(solution)/shard_map/ppermute | solution.py:309
  398.9 5.1 %collective-permute-start.39 = (bf16[64,1152]{1,0:T(8,128)(2,1)S(1)}, bf16[64,1152]{1,0:T(8,128)(2,1)S(1)}, u32[]{:S(2)}, u32[]{:S(2)}) collective-permute-start(bf16[64,1152]{1,0:T(8,128)(2,1)S(1)} %get-tuple-element.212), channel_id=1, source_target_pairs={{0,1},{1,0},{2,3},{3,2},{4,5},{5,4},{6,7},{7,6},{8,9},{9,8},{10,11... | collective-permute-start | bytes 442376 | tf_op jit(solution)/shard_map/ppermute | solution.py:314
  404.0 20.9 %collective-permute-start.55 = (bf16[112,1472]{1,0:T(8,128)(2,1)}, bf16[112,1472]{1,0:T(8,128)(2,1)}, u32[]{:S(2)}, u32[]{:S(2)}) collective-permute-start(bf16[112,1472]{1,0:T(8,128)(2,1)} %reduce-scatter.5.cloned.1.call-done.refs_0_), channel_id=1, source_target_pairs={{0,16},{4,20},{8,24},{12,28},{16,0},{20,4},{24,8},{28,12},{1,17},{... | collective-permute-start | bytes 989192 | tf_op jit(solution)/shard_map/ppermute | solution.py:309
  418.2 18.2 %collective-permute-start.48 = (bf16[368,896]{1,0:T(8,128)(2,1)S(1)}, bf16[368,896]{1,0:T(8,128)(2,1)S(1)}, u32[]{:S(2)}, u32[]{:S(2)}) collective-permute-start(bf16[368,896]{1,0:T(8,128)(2,1)S(1)} %copy-done.14), channel_id=1, source_target_pairs={{0,4},{4,0},{8,12},{12,8},{16,20},{20,16},{24,28},{28,24},{1,5},{5... | collective-permute-start | bytes 1978376 | tf_op jit(solution)/shard_map/ppermute | solution.py:309
  418.3 25.0 %collective-permute-start.51 = (bf16[368,896]{1,0:T(8,128)(2,1)S(1)}, bf16[368,896]{1,0:T(8,128)(2,1)}, u32[]{:S(2)}, u32[]{:S(2)}) collective-permute-start(bf16[368,896]{1,0:T(8,128)(2,1)S(1)} %collective-permute-done.44.refs_6_.refs_3_), channel_id=1, source_target_pairs={{0,4},{4,0},{8,12},{12,8},{16,20},{20,16},{24,28},{28,24},{1,5},{5... | collective-permute-start | bytes 1978376 | tf_op jit(solution)/shard_map/ppermute | solution.py:309
  418.8 25.0 %collective-permute-start.50 = (bf16[368,896]{1,0:T(8,128)(2,1)S(1)}, bf16[368,896]{1,0:T(8,128)(2,1)}, u32[]{:S(2)}, u32[]{:S(2)}) collective-permute-start(bf16[368,896]{1,0:T(8,128)(2,1)S(1)} %collective-permute-done.43.refs_5_.refs_2_), channel_id=1, source_target_pairs={{0,4},{4,0},{8,12},{12,8},{16,20},{20,16},{24,28},{28,24},{1,5},{5... | collective-permute-start | bytes 1978376 | tf_op jit(solution)/shard_map/ppermute | solution.py:309
  419.0 24.9 %collective-permute-start.49 = (bf16[368,896]{1,0:T(8,128)(2,1)S(1)}, bf16[368,896]{1,0:T(8,128)(2,1)}, u32[]{:S(2)}, u32[]{:S(2)}) collective-permute-start(bf16[368,896]{1,0:T(8,128)(2,1)S(1)} %collective-permute-done.42.refs_4_.refs_1_), channel_id=1, source_target_pairs={{0,4},{4,0},{8,12},{12,8},{16,20},{20,16},{24,28},{28,24},{1,5},{5... | collective-permute-start | bytes 1978376 | tf_op jit(solution)/shard_map/ppermute | solution.py:309
  425.0 9.7 %collective-permute-start.54 = (bf16[112,1472]{1,0:T(8,128)(2,1)}, bf16[112,1472]{1,0:T(8,128)(2,1)}, u32[]{:S(2)}, u32[]{:S(2)}) collective-permute-start(bf16[112,1472]{1,0:T(8,128)(2,1)} %reduce-scatter.5.cloned.1.call-done.refs_0_), channel_id=1, source_target_pairs={{0,8},{4,12},{8,0},{12,4},{16,24},{20,28},{24,16},{28,20},{1,9},{5... | collective-permute-start | bytes 989192 | tf_op jit(solution)/shard_map/ppermute | solution.py:309
  434.6 6.4 %collective-permute-start.47 = (bf16[64,1152]{1,0:T(8,128)(2,1)}, bf16[64,1152]{1,0:T(8,128)(2,1)S(1)}, u32[]{:S(2)}, u32[]{:S(2)}) collective-permute-start(bf16[64,1152]{1,0:T(8,128)(2,1)} %sum_parts.3.refs_0_), channel_id=1, source_target_pairs={{0,24},{4,28},{8,16},{12,20},{16,8},{20,12},{24,0},{28,4},{1,25},{... | collective-permute-start | bytes 442376 | tf_op jit(solution)/shard_map/ppermute | solution.py:309
  436.4 6.8 %collective-permute-start.46 = (bf16[64,1152]{1,0:T(8,128)(2,1)}, bf16[64,1152]{1,0:T(8,128)(2,1)S(1)}, u32[]{:S(2)}, u32[]{:S(2)}) collective-permute-start(bf16[64,1152]{1,0:T(8,128)(2,1)} %sum_parts.3.refs_0_), channel_id=1, source_target_pairs={{0,16},{4,20},{8,24},{12,28},{16,0},{20,4},{24,8},{28,12},{1,17},{... | collective-permute-start | bytes 442376 | tf_op jit(solution)/shard_map/ppermute | solution.py:309
  441.0 11.5 %collective-permute-start.45 = (bf16[64,1152]{1,0:T(8,128)(2,1)}, bf16[64,1152]{1,0:T(8,128)(2,1)S(1)}, u32[]{:S(2)}, u32[]{:S(2)}) collective-permute-start(bf16[64,1152]{1,0:T(8,128)(2,1)} %sum_parts.3.refs_0_), channel_id=1, source_target_pairs={{0,8},{4,12},{8,0},{12,4},{16,24},{20,28},{24,16},{28,20},{1,9},{5... | collective-permute-start | bytes 442376 | tf_op jit(solution)/shard_map/ppermute | solution.py:309
  443.3 14.8 %collective-permute-start.57 = (bf16[112,1472]{1,0:T(8,128)(2,1)}, bf16[112,1472]{1,0:T(8,128)(2,1)}, u32[]{:S(2)}, u32[]{:S(2)}) collective-permute-start(bf16[112,1472]{1,0:T(8,128)(2,1)} %reduce-scatter.5.cloned.1.call-done.refs_0_), channel_id=1, source_target_pairs={{0,4},{4,0},{8,12},{12,8},{16,20},{20,16},{24,28},{28,24},{1,5},{5... | collective-permute-start | bytes 989192 | tf_op jit(solution)/shard_map/ppermute | solution.py:309
  443.3 14.8 %collective-permute-start.60 = (bf16[112,1472]{1,0:T(8,128)(2,1)}, bf16[112,1472]{1,0:T(8,128)(2,1)}, u32[]{:S(2)}, u32[]{:S(2)}) collective-permute-start(bf16[112,1472]{1,0:T(8,128)(2,1)} %copy-done.38), channel_id=1, source_target_pairs={{0,4},{4,0},{8,12},{12,8},{16,20},{20,16},{24,28},{28,24},{1,5},{5... | collective-permute-start | bytes 989192 | tf_op jit(solution)/shard_map/ppermute | solution.py:309
  443.8 14.3 %collective-permute-start.59 = (bf16[112,1472]{1,0:T(8,128)(2,1)}, bf16[112,1472]{1,0:T(8,128)(2,1)}, u32[]{:S(2)}, u32[]{:S(2)}) collective-permute-start(bf16[112,1472]{1,0:T(8,128)(2,1)} %collective-permute-done.55.refs_2_), channel_id=1, source_target_pairs={{0,4},{4,0},{8,12},{12,8},{16,20},{20,16},{24,28},{28,24},{1,5},{5... | collective-permute-start | bytes 989192 | tf_op jit(solution)/shard_map/ppermute | solution.py:309
  443.8 14.2 %collective-permute-start.58 = (bf16[112,1472]{1,0:T(8,128)(2,1)}, bf16[112,1472]{1,0:T(8,128)(2,1)}, u32[]{:S(2)}, u32[]{:S(2)}) collective-permute-start(bf16[112,1472]{1,0:T(8,128)(2,1)} %collective-permute-done.54.refs_1_), channel_id=1, source_target_pairs={{0,4},{4,0},{8,12},{12,8},{16,20},{20,16},{24,28},{28,24},{1,5},{5... | collective-permute-start | bytes 989192 | tf_op jit(solution)/shard_map/ppermute | solution.py:309
  455.2 10.8 %collective-permute-start.52 = (bf16[4,64,1152]{2,1,0:T(8,128)(2,1)}, bf16[4,64,1152]{2,1,0:T(8,128)(2,1)S(1)}, u32[]{:S(2)}, u32[]{:S(2)}) collective-permute-start(bf16[4,64,1152]{2,1,0:T(8,128)(2,1)} %stack_small.1.near_ref), channel_id=1, source_target_pairs={{0,4},{4,0},{8,12},{12,8},{16,20},{20,16},{24,28},{28,24},{1,5},{5... | collective-permute-start | bytes 1769480 | tf_op jit(solution)/shard_map/ppermute | solution.py:309
  (61 other events, 374.5 us)
Sparse Core Ops, SparseCore 0:
  48.9 53.0 all-gather.3
  104.1 32.5 all-gather.5
  269.2 51.8 reduce-scatter.2
  326.2 33.4 reduce-scatter.4

commit v6 on v5

--- a/solution.py
+++ b/solution.py
@@ -77,7 +77,7 @@
 def build_bias(bias_ref, table_ref, pair, rows, radius):
     for side, bucket in ((0, 15), (2 * radius + 2, 31)):
         for head in range(2):
-            bias_ref[head, side] = jnp.full((rows, rows), table_ref[bucket, 2 * pair + head], FLOAT)
+            bias_ref[pair, head, side] = jnp.full((rows, rows), table_ref[bucket, 2 * pair + head], FLOAT)
     for gap in range(-radius, radius + 1):
         buckets = bucket_of(tile_offsets(gap, rows))
         present = tile_buckets(gap, rows)
@@ -86,7 +86,7 @@
             hit = buckets == bucket
             tiles = [jnp.where(hit, table_ref[bucket, 2 * pair + head], tiles[head]) for head in range(2)]
         for head in range(2):
-            bias_ref[head, gap + radius + 1] = tiles[head]
+            bias_ref[pair, head, gap + radius + 1] = tiles[head]
 
 
 def build_mask(mask_ref, segs_ref, meta, seq, rows, count):
@@ -102,8 +102,8 @@
     raw = nt(keys, query)
     parts = []
     for position in range(count):
-        extra = bias_ref[head, tile_index(meta, half, position, count, radius)]
-        masked = mask_ref[seq, half * count + position]
+        extra = bias_ref[0, head, tile_index(meta, half, position, count, radius)]
+        masked = mask_ref[0, half * count + position]
         parts.append(raw[position * rows : (position + 1) * rows] + (extra + masked))
     return jnp.concatenate(parts, axis=0)
 
@@ -117,19 +117,11 @@
 
 
 def forward_kernel(
-    meta_ref, table_ref, segs_ref, q_ref, *refs, rows, count, radius,
+    meta_ref, bias_ref, mask_ref, q_ref, *refs, rows, count, radius,
 ):
-    key_refs, value_refs, (out_ref, lse_ref, bias_ref, mask_ref) = refs[:8], refs[8:16], refs[16:]
+    key_refs, value_refs, (out_ref, lse_ref) = refs[:8], refs[8:16], refs[16:]
     pair, seq = pl.program_id(0), pl.program_id(1)
     meta = meta_ref[0]
-
-    @pl.when(seq == 0)
-    def _():
-        build_bias(bias_ref, table_ref, pair, rows, radius)
-
-    @pl.when(pair == 0)
-    def _():
-        build_mask(mask_ref, segs_ref, meta, seq, rows, count)
 
     query = q_ref[0]
     lane = lax.broadcasted_iota(jnp.int32, query.shape, 1)
@@ -153,21 +145,16 @@
 
 
 def backward_kernel(
-    meta_ref, table_ref, segs_ref, q_ref, *refs, rows, count, radius,
+    meta_ref, bias_ref, mask_ref, q_ref, *refs, rows, count, radius,
 ):
     key_refs, value_refs, (do_ref, out_ref, lse_ref, dq_ref) = refs[:8], refs[8:16], refs[16:20]
-    both_refs, (tab_ref, bias_ref, mask_ref, sum_ref) = refs[20:28], refs[28:]
+    both_refs, (tab_ref, sum_ref) = refs[20:28], refs[28:]
     pair, seq = pl.program_id(0), pl.program_id(1)
     meta = meta_ref[0]
 
     @pl.when(seq == 0)
     def _():
-        build_bias(bias_ref, table_ref, pair, rows, radius)
         sum_ref[...] = jnp.zeros_like(sum_ref)
-
-    @pl.when(pair == 0)
-    def _():
-        build_mask(mask_ref, segs_ref, meta, seq, rows, count)
 
     query, grad = q_ref[0], do_ref[0]
     lane = lax.broadcasted_iota(jnp.int32, query.shape, 1)
@@ -231,11 +218,34 @@
                 tab_ref[0, head, bucket : bucket + 1] = sums.get(bucket, jnp.zeros((1, rows), FLOAT))
 
 
-def attention_specs(seqs, rows, count, blocks, pairs):
+def prepare_kernel(meta_ref, table_ref, segs_ref, bias_ref, mask_ref, *, rows, count, radius):
+    for pair in range(bias_ref.shape[0]):
+        build_bias(bias_ref, table_ref, pair, rows, radius)
+    for seq in range(mask_ref.shape[0]):
+        build_mask(mask_ref, segs_ref, meta_ref[0], seq, rows, count)
+
+
+def attention_terms(meta, table, segs, pairs, count):
+    seqs, _, rows = segs.shape
+    radius = near_radius(rows)
+    return pl.pallas_call(
+        functools.partial(prepare_kernel, rows=rows, count=count, radius=radius),
+        in_specs=[pl.BlockSpec(memory_space=pltpu.SMEM)] * 2 + [pl.BlockSpec(memory_space=pltpu.VMEM)],
+        out_specs=[pl.BlockSpec(memory_space=pltpu.VMEM)] * 2,
+        out_shape=[
+            jax.ShapeDtypeStruct((pairs, 2, 2 * radius + 3, rows, rows), FLOAT),
+            jax.ShapeDtypeStruct((seqs, 2 * count, rows, rows), FLOAT),
+        ],
+        cost_estimate=cost(flops=0, bytes_accessed=10**6, transcendentals=0),
+        name="attention_terms",
+    )(meta, table, segs)
+
+
+def attention_specs(bias, mask, rows, count):
     small = [
         pl.BlockSpec(memory_space=pltpu.SMEM),
-        pl.BlockSpec(memory_space=pltpu.SMEM),
-        pl.BlockSpec((seqs, blocks, rows), lambda p, s: (0, 0, 0)),
+        pl.BlockSpec((1, *bias.shape[1:]), lambda p, s: (p, 0, 0, 0, 0)),
+        pl.BlockSpec((1, *mask.shape[1:]), lambda p, s: (s, 0, 0, 0)),
     ]
     query = pl.BlockSpec((1, rows, 128), lambda p, s: (s, 0, p))
     key = pl.BlockSpec((count // 4, 1, rows, 128), lambda p, s: (0, s, 0, 2 * p))
@@ -244,13 +254,6 @@
     return small, query, key, value, stat
 
 
-def attention_scratch(seqs, rows, count, radius):
-    return [
-        pltpu.VMEM((2, 2 * radius + 3, rows, rows), FLOAT),
-        pltpu.VMEM((seqs, 2 * count, rows, rows), FLOAT),
-    ]
-
-
 def attention_cost(seqs, rows, keys, width, products):
     return cost(
         flops=2 * products * seqs * rows * keys * width,
@@ -259,11 +262,11 @@
     )
 
 
-def attention_forward(meta, table, segs, queries, kv):
+def attention_forward(meta, bias, mask, queries, kv):
     seqs, rows, inner = queries.shape
-    count, blocks, pairs = 4 * kv[0].shape[0], segs.shape[1], inner // 128
+    count, blocks, pairs = 4 * kv[0].shape[0], mask.shape[1], inner // 128
     radius = near_radius(rows)
-    small, query, key, value, stat = attention_specs(seqs, rows, count, blocks, pairs)
+    small, query, key, value, stat = attention_specs(bias, mask, rows, count)
     return pl.pallas_call(
         functools.partial(forward_kernel, rows=rows, count=count, radius=radius),
         grid=(pairs, seqs),
@@ -273,17 +276,16 @@
             jax.ShapeDtypeStruct((seqs, rows, inner), FLOAT),
             jax.ShapeDtypeStruct((pairs, seqs, 8, rows), FLOAT),
         ],
-        scratch_shapes=attention_scratch(seqs, rows, count, radius),
         cost_estimate=attention_cost(seqs, rows, blocks * rows, inner, 2),
         name="attention_forward",
-    )(meta, table, segs, queries, *kv, *kv)
-
-
-def attention_backward(meta, table, segs, queries, kv, grad, out, lse, *deps):
+    )(meta, bias, mask, queries, *kv, *kv)
+
+
+def attention_backward(meta, bias, mask, queries, kv, grad, out, lse, *deps):
     seqs, rows, inner = queries.shape
-    count, blocks, pairs = 4 * kv[0].shape[0], segs.shape[1], inner // 128
+    count, blocks, pairs = 4 * kv[0].shape[0], mask.shape[1], inner // 128
     radius = near_radius(rows)
-    small, query, key, value, stat = attention_specs(seqs, rows, count, blocks, pairs)
+    small, query, key, value, stat = attention_specs(bias, mask, rows, count)
     side = jax.ShapeDtypeStruct((count // 4, seqs, rows, 2 * inner), BFLOAT)
     both = pl.BlockSpec((count // 4, 1, rows, 256), lambda p, s: (0, s, 0, p))
     return pl.pallas_call(
@@ -296,12 +298,11 @@
             jax.ShapeDtypeStruct((pairs, 2, BUCKETS, rows), FLOAT),
         ],
         scratch_shapes=[
-            *attention_scratch(seqs, rows, count, radius),
             pltpu.VMEM((2, 2 * radius + 3, rows, rows), FLOAT),
         ],
         cost_estimate=attention_cost(seqs, rows, blocks * rows, inner, 5),
         name="attention_backward",
-    )(meta, table, segs, queries, *kv, *kv, grad, out, lse, *deps)
+    )(meta, bias, mask, queries, *kv, *kv, grad, out, lse, *deps)
 
 
 def swap(value, bit):
@@ -863,36 +864,58 @@
     )(left, *rights, *deps)
 
 
-def last_kernel(dq_ref, own_ref, p1, p2, p3, x0, x1, residual_ref, gain_ref, weight_ref, out_ref):
+def last_kernel(dq_ref, own_ref, p1, p2, p3, x_ref, residual_ref, gain_ref, weight_ref, out_ref):
     dkv = sum(ref[...].astype(FLOAT) for ref in (own_ref, p1, p2, p3)).astype(BFLOAT)
     inner = dq_ref.shape[1]
     back = nt(dq_ref[...], weight_ref[:, :inner]) + nt(dkv, weight_ref[:, inner:])
-    hidden = jnp.where(pl.program_id(0) < 2, x0[...], x1[...]).astype(FLOAT)
-    out_ref[...] = (residual_ref[...] + norm_back(hidden, gain_ref[...], back)).astype(BFLOAT)
-
-
-def last(dq, own, parts, inputs, residual, gain, weight, *deps):
-    tokens, width = residual.shape
+    hidden = jnp.transpose(x_ref[0]).astype(FLOAT)
+    grad = (residual_ref[...] + norm_back(hidden, gain_ref[...], back)).astype(BFLOAT)
+    out_ref[0] = jnp.transpose(grad)
+
+
+def last(dq, own, parts, turned, residual, gain, weight):
+    seqs, width, rows = turned.shape
     inner = dq.shape[1]
-    tile = tokens // 4
-    whole = pl.BlockSpec((tile, width), lambda g: (g, 0))
-    near = pl.BlockSpec((tile, width), lambda g: (jnp.minimum(g, 1), 0))
-    far = pl.BlockSpec((tile, width), lambda g: (jnp.maximum(g - 2, 0), 0))
-    piece = pl.BlockSpec((tile, 2 * inner), lambda g: (g, 0))
-    return pl.pallas_call(
-        skipping(last_kernel, 10, len(deps)),
-        grid=(4,),
+    whole = pl.BlockSpec((rows, width), lambda g: (g, 0))
+    piece = pl.BlockSpec((rows, 2 * inner), lambda g: (g, 0))
+    block = pl.BlockSpec((1, width, rows), lambda g: (g, 0, 0))
+    return pl.pallas_call(
+        last_kernel,
+        grid=(seqs,),
         in_specs=[
-            pl.BlockSpec((tile, inner), lambda g: (g, 0)), piece, piece, piece, piece, near, far, whole,
+            pl.BlockSpec((rows, inner), lambda g: (g, 0)), piece, piece, piece, piece, block, whole,
             once(gain.shape), once(weight.shape),
-        ]
-        + [UNREAD] * len(deps),
-        out_specs=whole,
-        out_shape=jax.ShapeDtypeStruct((tokens, width), BFLOAT),
+        ],
+        out_specs=block,
+        out_shape=jax.ShapeDtypeStruct((seqs, width, rows), BFLOAT),
         compiler_params=BIG,
         cost_estimate=pl.CostEstimate(flops=10**11, bytes_accessed=0, transcendentals=0),
         name="input_gradient",
-    )(dq, own, *parts, *inputs, residual, gain, weight, *deps)
+    )(dq, own, *parts, turned, residual, gain, weight)
+
+
+def output_kernel(after_ref, parts_ref, out_ref):
+    total = after_ref[...]
+    for index in range(4):
+        total = total + parts_ref[index].astype(FLOAT)
+    out_ref[0] = jnp.transpose(total.astype(BFLOAT))
+
+
+def output_sum(after_attn, parts, seqs):
+    tokens, width = after_attn.shape
+    rows = tokens // seqs
+    return pl.pallas_call(
+        output_kernel,
+        grid=(seqs,),
+        in_specs=[
+            pl.BlockSpec((rows, width), lambda g: (g, 0)), pl.BlockSpec((4, rows, width), lambda g: (0, g, 0)),
+        ],
+        out_specs=pl.BlockSpec((1, width, rows), lambda g: (g, 0, 0)),
+        out_shape=jax.ShapeDtypeStruct((seqs, width, rows), BFLOAT),
+        compiler_params=BIG,
+        cost_estimate=moved(after_attn, parts),
+        name="output_sum",
+    )(after_attn, parts)
 
 
 def choose(refs, slot):
@@ -1123,13 +1146,14 @@
         return lax.all_gather(value, "ctx", axis=axis, tiled=True, axis_index_groups=upper)
 
     segs = whole(segs, 1)
+    bias, mask = attention_terms(meta, table, segs, inner // 128, ring // 2)
 
     normed, *kv, queries = norm_project(inputs, gains[0:1], qkv_full, inner)
     cots = exchange(own_cots)
     kv = [value.reshape(1, seqs, rows, 2 * inner) for value in kv]
     queries = queries.reshape(seqs, rows, inner)
     kv = [whole(value) for value in (*kv, *[swap(value, 1) for value in kv])]
-    attention, lse = attention_forward(meta, table, segs, queries, kv)
+    attention, lse = attention_forward(meta, bias, mask, queries, kv)
     attn_low = attention.astype(BFLOAT).reshape(tokens, inner)
     attn = gather_direct(attn_low)
 
@@ -1165,7 +1189,7 @@
     )
     attn_grad = attn_grad.reshape(seqs, rows, inner)
     proj_grad = tn(attn_low, jnp.pad(mix_low, ((0, 0), (0, 4 * wide - width)))).astype(BFLOAT)
-    dq, *dkv, table_part = attention_backward(meta, table, segs, queries, kv, attn_grad, attention, lse)
+    dq, *dkv, table_part = attention_backward(meta, bias, mask, queries, kv, attn_grad, attention, lse)
 
     def owned(value):
         if groups > 1:
@@ -1182,12 +1206,12 @@
     down_sum = plus(down_keep, [down_got], keep).reshape(depth * piece, width)
     pair_own = over_groups(lax.psum_scatter(pair_sum, "wsh", scatter_dimension=0, tiled=True))
     down_own = over_groups(lax.psum_scatter(down_sum, "wsh", scatter_dimension=0, tiled=True))
-    out_parts = exchange(after(out_part, attn_grad)).astype(FLOAT).reshape(4, tokens, width)
-    result = (after_attn + jnp.sum(out_parts, axis=0)).astype(BFLOAT)
+    out_parts = exchange(after(out_part, attn_grad)).reshape(4, tokens, width)
+    result = output_sum(after_attn, out_parts, seqs)
 
     blocks = plus_apart(keep, swap(send, 1), result)
     dkv_parts = [swap(dkv_four[index], 2 * index) for index in range(1, 4)]
-    input_grad = last(dq, dkv_four[0], dkv_parts, (x_near, x_far), residual_grad, gains[0:1], qkv_full)
+    input_grad = last(dq, dkv_four[0], dkv_parts, jnp.swapaxes(layer_input, 1, 2), residual_grad, gains[0:1], qkv_full)
     levels = sum_parts([blocks[0]] + [swap(blocks[index], 2 * index) for index in range(1, 4)], input_grad, pair_own)
     pair_near = gather_direct(after(pair_own, levels))
     down_near = gather_direct(after(down_own, levels))
@@ -1232,8 +1256,8 @@
     )(place, grads_near, grads_far, query_weight, key_weight, value_weight)
 
     return (
-        result.reshape(seqs, rows, width),
-        input_grad.reshape(seqs, rows, width),
+        jnp.swapaxes(result, 1, 2),
+        jnp.swapaxes(input_grad, 1, 2),
         query_out,
         key_out,
         value_out,

time: 489 us -> 482 us (0.986)
    pallas_call x1 -> x3, Pallas kernels: 9.28 us -> 18.1 us  [the longest x1 8.67 us: last(): pl.pallas_call(last_kernel, grid=(seqs,), in_specs=[pl.BlockSpec((rows, i...]
    unnamed x118 -> x110, local copies, waits for them, and re-layouts: 13.5 us -> 11.3 us
  transfers between devices with their start and end apart: 67 -> 67, of which waited for: 31 -> 27; matrix products, arithmetic and copies ran while one was open for 6% -> 5% of each run, Pallas kernels for 31% -> 33%
where the time goes in v6:
time: 482 us; the launch traced here: 477 us
  Pallas kernels  212 us (44%)
  waiting for transfers between devices  134 us (28%)
  starting transfers between devices  60.3 us (13%)
  local copies, waits for them, and re-layouts  25.4 us (5%)
  blocking collectives  19.4 us (4%)
  between operations  14.6 us (3%)
  other arithmetic  9.1 us (2%)
    ppermute x58, waiting for transfers between devices, swap(): lax.ppermute(value, 'ctx', [(source, source ^ bit) for source in range(co...  115 us
    ppermute x58, starting transfers between devices, swap(): lax.ppermute(value, 'ctx', [(source, source ^ bit) for source in range(co...  47.3 us
    pallas_call x1, Pallas kernels, feed_forward(): pl.pallas_call(feed_kernel, grid_spec=pltpu.PrefetchScalarGridSpec(num_sc...  42.2 us
    pallas_call x2, Pallas kernels, outer_sums(): pl.pallas_call(outer_kernel, grid=(2,), in_specs=[pl.BlockSpec((2, tokens...  26.1 us
    all_gather x1, blocking collectives, on_device(): packed = lax.all_gather(packed, 'wsh', axis=0)  19.4 us
    pallas_call x1, Pallas kernels, attention_backward(): pl.pallas_call(skipping(functools.partial(backward_kernel, rows=rows, cou...  18.8 us
    ppermute x3, waiting for transfers between devices, swap_depth(): lax.ppermute(value, 'wsh', [(source, source ^ bit) for source in range(co...  14.3 us
    pallas_call x1, Pallas kernels, weight_grads(): pl.pallas_call(skipping(functools.partial(grad_kernel, depth=depth, size=...  13.4 us
  transfers between devices with their start and end apart: 67, of which 27 were waited for; matrix products, arithmetic and copies ran while one was open for 5% of the time, Pallas kernels for 33%

profile of v6, /device:TPU:0, one launch (start us, length us, event | category | flops | bytes accessed | tf_op | source)
XLA Modules:
  0.0 476.9 jit_solution(9271051931216212337)
XLA Ops:
  7.2 4.7 token_rows.1
  11.9 3.0 collective-permute-start.2
  14.9 1.5 collective-permute-start
  17.1 2.3 constant_dynamic-slice_fusion.4
  24.2 2.0 pack.1
  26.1 19.4 %all-gather = bf16[320,1152]{1,0:T(8,128)(2,1)S(1)} all-gather(bf16[80,1152]{1,0:T(8,128)(2,1)} %pack.1), channel_id=2, replica_groups=mesh['ctx'=8,'wsh'=4] {'wsh'}, dimensions={0}, use_global_device_ids=true | all-gather | bytes 921600 | tf_op jit(solution)/shard_map/all_gather | solution.py:1119
  45.8 1.6 collective-permute-start.5
  48.8 9.9 %collective-permute-done.5 = bf16[272,1152]{1,0:T(8,128)(2,1)S(1)} collective-permute-done((bf16[272,1152]{1,0:T(8,128)(2,1)S(1)}, bf16[272,1152]{1,0:T(8,128)(2,1)S(1)}, u32[]{:S(2)}, u32[]{:S(2)}) %collective-permute-start.5) | collective-permute-done | bytes 626720 | tf_op jit(solution)/shard_map/ppermute | solution.py:310
  58.7 2.5 collective-permute-start.7
  62.7 5.7 %collective-permute-done.6 = bf16[128,1152]{1,0:T(8,128)(2,1)S(1)} collective-permute-done((bf16[128,1152]{1,0:T(8,128)(2,1)S(1)}, bf16[128,1152]{1,0:T(8,128)(2,1)S(1)}, u32[]{:S(2)}, u32[]{:S(2)}) %collective-permute-start.6) | collective-permute-done | bytes 294944 | tf_op jit(solution)/shard_map/ppermute | solution.py:310
  68.5 1.8 pad_maximum_fusion.near_ref
  73.0 5.0 %all-to-all-start = ((bf16[8,192,1472]{2,1,0:T(8,128)(2,1)}), bf16[8,192,1472]{2,1,0:T(8,128)(2,1)}, u32[]{:S(2)}, u32[]{:S(2)}) async-start(bf16[8,192,1472]{2,1,0:T(8,128)(2,1)} %get-tuple-element.108.refs_6_), calls=%async_computation | async-start | bytes 9437184 | tf_op jit(solution)/shard_map/all_to_all | solution.py:1087
  79.0 4.8 %unpack.1 = (bf16[1472,1152]{1,0:T(8,128)(2,1)}, bf16[384,1472]{1,0:T(8,128)(2,1)}, f32[8,1472]{1,0:T(8,128)}, f32[32,128]{1,0:T(8,128)}, f32[3,8,128]{2,1,0:T(8,128)}) custom-call(s32[2]{0:T(128)} %pad_add_fusion.place_ref.refs_0_, bf16[4,16,1152]{2,1,0:T(8,128)(2,1)} %slice.72.misc_ref, bf16[4,272,1152]{2,1,0:T(8,128)(2,1)} %copy-done.3, ...), custom_call_target="tpu_custom_call" | custom-call | bytes 1504051 | tf_op jit(solution)/shard_map/unpack/pallas_call | solution.py:1127
  85.3 1.7 collective-permute-done.9.refs_6_.refs_10_
  88.0 12.2 %norm_project.1 = (bf16[4,384,1472]{2,1,0:T(8,128)(2,1)}, bf16[1,384,768]{2,1,0:T(8,128)(2,1)}, bf16[1,384,768]{2,1,0:T(8,128)(2,1)}, bf16[1,384,768]{2,1,0:T(8,...) custom-call(bf16[192,1472]{1,0:T(8,128)(2,1)} %get-tuple-element.90.refs_0_.refs_4_, ...), custom_call_target="tpu_custom_call" | custom-call | flops 781398848 | bytes 2034892 | tf_op jit(solution)/shard_map/norm_project/pallas_call | solution.py:553
  101.3 4.4 attention_terms.1
  107.1 12.8 %attention_forward.1 = (f32[3,128,384]{2,1,0:T(8,128)}, f32[3,3,8,128]{3,2,1,0:T(8,128)}) custom-call(s32[1]{0:T(128)} %bitcast.meta_ref.refs_0_, f32[3,2,5,128,128]{4,3,2,1,0:T(8,128)} %get-tuple-element.95.bias_ref.refs_1_, f32[3,8,128,128]{3,2,1,0:T(8,128)} %get-tuple-element.96.mask_ref.refs_2_, bf16[3,128,384]{2,1,0:T(8,128)(2,1)} %bitcast.103, ...), custom_call_target="tpu_custom_call" | custom-call | flops 120795952 | bytes 1887436 | tf_op jit(solution)/shard_map/attention_forward/pallas_call | solution.py:270
  121.3 1.8 collective-permute-start.17
  124.8 20.5 %collective-permute-done.17.refs_3_ = bf16[384,384]{1,0:T(8,128)(2,1)S(1)} collective-permute-done((bf16[384,384]{1,0:T(8,128)(2,1)S(1)}, bf16[384,384]{1,0:T(8,128)(2,1)S(1)}, u32[]{:S(2)}, u32[]{:S(2)}) %collective-permute-start.17) | collective-permute-done | bytes 294944 | tf_op jit(solution)/shard_map/ppermute | solution.py:310
  145.3 4.3 collective-permute-done.16.refs_2_
  151.1 9.9 %late_norm.1 = (f32[384,1472]{1,0:T(8,128)}, bf16[4,384,1472]{2,1,0:T(8,128)(2,1)}) custom-call(bf16[384,384]{1,0:T(8,128)(2,1)} %bitcast.97, bf16[384,384]{1,0:T(8,128)(2,1)} %copy-done.38, bf16[384,384]{1,0:T(8,128)(2,1)} %copy-done.37, bf16[384,384]{1,0:T(8,128)(2,1)} %copy-done.36, bf16[192,1472]{1,0:T(8,128)(2,1)} %get-tuple-element.90.refs_0_.refs_4_, ...), custom_call_target="tpu_custom_call" | custom-call | flops 347288384 | bytes 2713190 | tf_op jit(solution)/shard_map/late_norm/pallas_call | solution.py:598
  161.6 2.7 collective-permute-done.19.down_other
  165.4 42.2 %feed_forward.1 = (bf16[4,384,896]{2,1,0:T(8,128)(2,1)}, bf16[4,384,896]{2,1,0:T(8,128)(2,1)}, bf16[4,384,896]{2,1,0:T(8,128)(2,1)}, bf16[8,192,1472]{2,1,0:T(8,...) custom-call(s32[2]{0:T(128)} %pad_add_fusion.1.spot_ref, ...), custom_call_target="tpu_custom_call" | custom-call | flops 4862036992 | bytes 3391488 | tf_op jit(solution)/shard_map/feed_forward/pallas_call | solution.py:686
  208.7 2.0 collective-permute-start.21
  211.7 17.0 %outer_sums.2 = (bf16[2,736,896]{2,1,0:T(8,128)(2,1)}, bf16[2,736,896]{2,1,0:T(8,128)(2,1)}) custom-call(bf16[4,384,1472]{2,1,0:T(8,128)(2,1)} %get-tuple-element.107.normed_ref.left_ref, bf16[4,384,896]{2,1,0:T(8,128)(2,1)} %get-tuple-element.119.refs_0_, bf16[4,384,896]{2,1,0:T(8,128)(2,1)} %get-tuple-element.120.refs_1_), custom_call_target="tpu_custom_call" | custom-call | flops 3241358080 | tf_op jit(solution)/shard_map/outer_sums/pallas_call | solution.py:728
  228.7 8.1 %collective-permute-done.22.refs_5_.refs_4_ = bf16[192,1472]{1,0:T(8,128)(2,1)S(1)} collective-permute-done((bf16[192,1472]{1,0:T(8,128)(2,1)}, bf16[192,1472]{1,0:T(8,128)(2,1)S(1)}, u32[]{:S(2)}, u32[]{:S(2)}) %collective-permute-start.22) | collective-permute-done | bytes 565280 | tf_op jit(solution)/shard_map/ppermute | solution.py:310
  237.8 2.9 relay_sums.1
  240.7 1.7 collective-permute-start.24
  243.4 1.7 fusion.4
  245.6 9.1 %outer_sums.3.refs_9_ = bf16[2,448,1472]{2,1,0:T(8,128)(2,1)} custom-call(bf16[4,384,896]{2,1,0:T(8,128)(2,1)} %get-tuple-element.126.left_ref, bf16[4,384,1472]{2,1,0:T(8,128)(2,1)} %get-tuple-element.127.refs_0_), custom_call_target="tpu_custom_call" | custom-call | flops 1620679040 | tf_op jit(solution)/shard_map/outer_sums/pallas_call | solution.py:728
  256.7 6.7 %middle.1 = (f32[384,1472]{1,0:T(8,128)}, bf16[384,1472]{1,0:T(8,128)(2,1)}, bf16[384,384]{1,0:T(8,128)(2,1)}) custom-call(f32[384,1472]{1,0:T(8,128)} %get-tuple-element.106.refs_0_.after_ref, bf16[2,192,1472]{2,1,0:T(8,128)(2,1)} %get-tuple-element.114.refs_1_, bf16[192,1472]{1,0:T(8,128)(2,1)} %copy-done.54, bf16[192,1472]{1,0:T(8,128)(2,1)} %copy-done.25, ...), custom_call_target="tpu_custom_call" | custom-call | flops 99999997952 | tf_op jit(solution)/shard_map/middle/pallas_call | solution.py:780
  264.9 3.9 plus.2
  268.8 5.0 %all-to-all-start.1 = ((bf16[8,192,1472]{2,1,0:T(8,128)(2,1)}), bf16[8,192,1472]{2,1,0:T(8,128)(2,1)}, u32[]{:S(2)}, u32[]{:S(2)}) async-start(bf16[8,192,1472]{2,1,0:T(8,128)(2,1)} %get-tuple-element.129), calls=%async_computation.1 | async-start | bytes 9437184 | tf_op jit(solution)/shard_map/all_to_all | solution.py:1087
  273.9 18.8 %attention_backward.1 = (bf16[3,128,384]{2,1,0:T(8,128)(2,1)}, bf16[1,3,128,768]{3,2,1,0:T(8,128)(2,1)}, bf16[1,3,128,768]{3,2,1,0:T(8,128)(2,1)}, bf16[1,3,128,...) custom-call(s32[1]{0:T(128)} %bitcast.meta_ref.refs_0_, ...), custom_call_target="tpu_custom_call" | custom-call | flops 301989888 | bytes 4718592 | tf_op jit(solution)/shard_map/attention_backward/pallas_call | solution.py:291
  295.5 1.9 convolution_convert_fusion.refs_12_
  298.6 13.4 %weight_grads.1 = (bf16[384,768]{1,0:T(8,128)(2,1)}, bf16[384,768]{1,0:T(8,128)(2,1)}, bf16[384,768]{1,0:T(8,128)(2,1)}, bf16[384,768]{1,0:T(8,128)(2,1)}, bf16[...) custom-call(s32[2]{0:T(128)} %pad_add_fusion.place_ref.refs_0_, ...), custom_call_target="tpu_custom_call" | custom-call | flops 781398848 | bytes 1356595 | tf_op jit(solution)/shard_map/weight_grads/pallas_call | solution.py:489
  313.7 1.9 collective-permute-start.32
  319.6 3.9 plus.3
  323.4 4.8 %all-to-all-done.1 = bf16[8,192,1472]{2,1,0:T(8,128)(2,1)} async-done(((bf16[8,192,1472]{2,1,0:T(8,128)(2,1)}), bf16[8,192,1472]{2,1,0:T(8,128)(2,1)}, u32[]{:S(2)}, u32[]{:S(2)}) %all-to-all-start.1) | async-done | bytes 4522016 | tf_op jit(solution)/shard_map/all_to_all | solution.py:1087
  328.2 5.0 %output_sum.1.refs_2_ = bf16[3,1472,128]{2,1,0:T(8,128)(2,1)} custom-call(f32[384,1472]{1,0:T(8,128)} %get-tuple-element.106.refs_0_.after_ref, bf16[4,384,1472]{2,1,0:T(8,128)(2,1)} %bitcast.21.parts_ref), custom_call_target="tpu_custom_call" | custom-call | bytes 1356595 | tf_op jit(solution)/shard_map/output_sum/pallas_call | solution.py:907
  333.3 4.6 plus_apart.1
  337.9 1.6 collective-permute-start.36
  341.6 1.5 collective-permute-start.38
  343.1 11.4 %collective-permute-done.34.p3 = bf16[384,768]{1,0:T(8,128)(2,1)} collective-permute-done((bf16[384,768]{1,0:T(8,128)(2,1)S(1)}, bf16[384,768]{1,0:T(8,128)(2,1)}, u32[]{:S(2)}, u32[]{:S(2)}) %collective-permute-start.34) | collective-permute-done | bytes 589856 | tf_op jit(solution)/shard_map/ppermute | solution.py:310
  354.5 8.7 %input_gradient.1.refs_4_ = bf16[3,1472,128]{2,1,0:T(8,128)(2,1)} custom-call(bf16[384,384]{1,0:T(8,128)(2,1)} %bitcast.115, bf16[384,768]{1,0:T(8,128)(2,1)} %get-tuple-element.144.own_ref, bf16[384,768]{1,0:T(8,128)(2,1)} %copy-done.53, bf16[384,768]{1,0:T(8,128)(2,1)} %collective-permute-done.33.p2, bf16[384,768]{1,0:T(8,128)(2,1)} %collective-permute-done.34.p3, ...), custom_call_target="tpu_custom_call" | custom-call | flops 99999997952 | tf_op jit(solution)/shard_map/input_gradient/pallas_call | solution.py:882
  363.1 3.0 collective-permute-done.36.refs_1_
  366.1 11.4 %collective-permute-done.38.refs_3_ = bf16[4,64,1152]{2,1,0:T(8,128)(2,1)S(1)} collective-permute-done((bf16[4,64,1152]{2,1,0:T(8,128)(2,1)}, bf16[4,64,1152]{2,1,0:T(8,128)(2,1)S(1)}, u32[]{:S(2)}, u32[]{:S(2)}) %collective-permute-start.38) | collective-permute-done | bytes 589856 | tf_op jit(solution)/shard_map/ppermute | solution.py:310
  378.3 2.8 sum_parts.2
  384.5 1.8 slice_bitcast_fusion.2
  386.4 2.8 collective-permute-start.41
  389.1 4.3 collective-permute-done.41.refs_3_
  394.1 4.8 %collective-permute-done.40.refs_2_ = bf16[64,1152]{1,0:T(8,128)(2,1)S(1)} collective-permute-done((bf16[64,1152]{1,0:T(8,128)(2,1)S(1)}, bf16[64,1152]{1,0:T(8,128)(2,1)S(1)}, u32[]{:S(2)}, u32[]{:S(2)}) %collective-permute-start.40) | collective-permute-done | bytes 147488 | tf_op jit(solution)/shard_map/ppermute | solution.py:315
  398.9 5.1 %collective-permute-done.39.refs_1_ = bf16[64,1152]{1,0:T(8,128)(2,1)S(1)} collective-permute-done((bf16[64,1152]{1,0:T(8,128)(2,1)S(1)}, bf16[64,1152]{1,0:T(8,128)(2,1)S(1)}, u32[]{:S(2)}, u32[]{:S(2)}) %collective-permute-start.39) | collective-permute-done | bytes 147488 | tf_op jit(solution)/shard_map/ppermute | solution.py:315
  404.7 13.5 %collective-permute-done.56.refs_3_ = bf16[112,1472]{1,0:T(8,128)(2,1)S(1)} collective-permute-done((bf16[112,1472]{1,0:T(8,128)(2,1)}, bf16[112,1472]{1,0:T(8,128)(2,1)S(1)}, u32[]{:S(2)}, u32[]{:S(2)}) %collective-permute-start.56) | collective-permute-done | bytes 329760 | tf_op jit(solution)/shard_map/ppermute | solution.py:310
  419.4 5.6 %collective-permute-done.55.refs_2_ = bf16[112,1472]{1,0:T(8,128)(2,1)} collective-permute-done((bf16[112,1472]{1,0:T(8,128)(2,1)}, bf16[112,1472]{1,0:T(8,128)(2,1)}, u32[]{:S(2)}, u32[]{:S(2)}) %collective-permute-start.55) | collective-permute-done | bytes 329760 | tf_op jit(solution)/shard_map/ppermute | solution.py:310
  426.1 1.9 sum_parts.3.refs_0_
  428.0 6.7 %collective-permute-done.54.refs_1_ = bf16[112,1472]{1,0:T(8,128)(2,1)} collective-permute-done((bf16[112,1472]{1,0:T(8,128)(2,1)}, bf16[112,1472]{1,0:T(8,128)(2,1)}, u32[]{:S(2)}, u32[]{:S(2)}) %collective-permute-start.54) | collective-permute-done | bytes 329760 | tf_op jit(solution)/shard_map/ppermute | solution.py:310
  434.7 1.8 collective-permute-start.47
  437.9 3.1 collective-permute-done.47.refs_3_
  441.0 1.7 collective-permute-start.45
  444.3 8.2 %spread_columns.1 = (f32[368,3584]{1,0:T(8,128)}, f32[368,3584]{1,0:T(8,128)}, f32[368,128]{1,0:T(8,128)}) custom-call(s32[2]{0:T(128)} %pad_add_fusion.place_ref.refs_0_, bf16[368,896]{1,0:T(8,128)(2,1)} %reduce-scatter.3.cloned.1.call-done.refs_5_.refs_0_, bf16[368,896]{1,0:T(8,128)(2,1)} %copy-done.15, bf16[368,896]{1,0:T(8,128)(2,1)} %copy-done.14, ...), custom_call_target="tpu_custom_call" | custom-call | flops 1055129 | bytes 4220518 | tf_op jit(solution)/shard_map/spread_columns/pallas_call | solution.py:950
  453.2 2.0 stack_small.1.near_ref
  455.3 7.1 %join_down.1 = f32[1472,896]{1,0:T(8,128)} custom-call(s32[2]{0:T(128)} %pad_add_fusion.place_ref.refs_0_, bf16[112,1472]{1,0:T(8,128)(2,1)} %reduce-scatter.5.cloned.1.call-done.refs_0_, bf16[112,1472]{1,0:T(8,128)(2,1)} %collective-permute-done.54.refs_1_, bf16[112,1472]{1,0:T(8,128)(2,1)} %collective-permute-done.55.refs_2_, ...), custom_call_target="tpu_custom_call" | custom-call | bytes 197836 | tf_op jit(solution)/shard_map/join_down/pallas_call | solution.py:1224
  464.0 3.2 finish_small.1
  (242 shorter events, 59.4 us)
Async XLA Ops:
  7.2 113.9 %all-gather.4.cloned.1.call-start = ((), (), s32[]{:S(2)}) async-start(), calls=%async_computation.4 | async-start | bytes 3297280 | tf_op jit(solution)/shard_map/all_gather | solution.py:1120
  11.9 33.8 %collective-permute-start.2 = (bf16[192,1472]{1,0:T(8,128)(2,1)}, bf16[192,1472]{1,0:T(8,128)(2,1)}, u32[]{:S(2)}, u32[]{:S(2)}) collective-permute-start(bf16[192,1472]{1,0:T(8,128)(2,1)} %get-tuple-element.90.refs_0_.refs_4_), channel_id=1, source_target_pairs={{0,16},{4,20},{8,24},{12,28},{16,0},{20,4},{24,8},{28,12},{1,17},{... | collective-permute-start | bytes 1695752 | tf_op jit(solution)/shard_map/ppermute | solution.py:310
  14.9 30.8 %collective-permute-start = (bf16[192,1472]{1,0:T(8,128)(2,1)}, bf16[192,1472]{1,0:T(8,128)(2,1)}, u32[]{:S(2)}, u32[]{:S(2)}) collective-permute-start(bf16[192,1472]{1,0:T(8,128)(2,1)} %get-tuple-element.90.refs_0_.refs_4_), channel_id=1, source_target_pairs={{0,8},{4,12},{8,0},{12,4},{16,24},{20,28},{24,16},{28,20},{1,9},{5... | collective-permute-start | bytes 1695752 | tf_op jit(solution)/shard_map/ppermute | solution.py:310
  16.4 29.3 %collective-permute-start.3 = (bf16[192,1472]{1,0:T(8,128)(2,1)}, bf16[192,1472]{1,0:T(8,128)(2,1)}, u32[]{:S(2)}, u32[]{:S(2)}) collective-permute-start(bf16[192,1472]{1,0:T(8,128)(2,1)} %get-tuple-element.91.refs_1_.refs_5_), channel_id=1, source_target_pairs={{0,16},{4,20},{8,24},{12,28},{16,0},{20,4},{24,8},{28,12},{1,17},{... | collective-permute-start | bytes 1695752 | tf_op jit(solution)/shard_map/ppermute | solution.py:310
  16.9 28.8 %collective-permute-start.1 = (bf16[192,1472]{1,0:T(8,128)(2,1)}, bf16[192,1472]{1,0:T(8,128)(2,1)}, u32[]{:S(2)}, u32[]{:S(2)}) collective-permute-start(bf16[192,1472]{1,0:T(8,128)(2,1)} %get-tuple-element.91.refs_1_.refs_5_), channel_id=1, source_target_pairs={{0,8},{4,12},{8,0},{12,4},{16,24},{20,28},{24,16},{28,20},{1,9},{5... | collective-permute-start | bytes 1695752 | tf_op jit(solution)/shard_map/ppermute | solution.py:310
  45.8 12.9 %collective-permute-start.5 = (bf16[272,1152]{1,0:T(8,128)(2,1)S(1)}, bf16[272,1152]{1,0:T(8,128)(2,1)S(1)}, u32[]{:S(2)}, u32[]{:S(2)}) collective-permute-start(bf16[272,1152]{1,0:T(8,128)(2,1)S(1)} %fusion.2), channel_id=1, source_target_pairs={{0,16},{4,20},{8,24},{12,28},{16,0},{20,4},{24,8},{28,12},{1,17},{... | collective-permute-start | bytes 1880072 | tf_op jit(solution)/shard_map/ppermute | solution.py:310
  47.3 14.3 %collective-permute-start.4 = (bf16[272,1152]{1,0:T(8,128)(2,1)S(1)}, bf16[272,1152]{1,0:T(8,128)(2,1)S(1)}, u32[]{:S(2)}, u32[]{:S(2)}) collective-permute-start(bf16[272,1152]{1,0:T(8,128)(2,1)S(1)} %fusion.2), channel_id=1, source_target_pairs={{0,8},{4,12},{8,0},{12,4},{16,24},{20,28},{24,16},{28,20},{1,9},{5... | collective-permute-start | bytes 1880072 | tf_op jit(solution)/shard_map/ppermute | solution.py:310
  58.7 9.7 %collective-permute-start.7 = (bf16[144,1152]{1,0:T(8,128)(2,1)S(1)}, bf16[144,1152]{1,0:T(8,128)(2,1)S(1)}, u32[]{:S(2)}, u32[]{:S(2)}) collective-permute-start(bf16[144,1152]{1,0:T(8,128)(2,1)S(1)} %slice.75), channel_id=1, source_target_pairs={{0,8},{4,12},{8,0},{12,4},{16,24},{20,28},{24,16},{28,20},{1,9},{5... | collective-permute-start | bytes 995336 | tf_op jit(solution)/shard_map/ppermute | solution.py:310
  61.6 6.8 %collective-permute-start.6 = (bf16[128,1152]{1,0:T(8,128)(2,1)S(1)}, bf16[128,1152]{1,0:T(8,128)(2,1)S(1)}, u32[]{:S(2)}, u32[]{:S(2)}) collective-permute-start(bf16[128,1152]{1,0:T(8,128)(2,1)S(1)} %slice.74), channel_id=1, source_target_pairs={{0,16},{4,20},{8,24},{12,28},{16,0},{20,4},{24,8},{28,12},{1,17},{... | collective-permute-start | bytes 884744 | tf_op jit(solution)/shard_map/ppermute | solution.py:310
  70.3 8.7 %collective-permute-start.8 = (bf16[4,272,1152]{2,1,0:T(8,128)(2,1)S(1)}, bf16[4,272,1152]{2,1,0:T(8,128)(2,1)}, u32[]{:S(2)}, u32[]{:S(2)}) collective-permute-start(bf16[4,272,1152]{2,1,0:T(8,128)(2,1)S(1)} %pad_maximum_fusion.near_ref), channel_id=1, source_target_pairs={{0,4},{4,0},{8,12},{12,8},{16,20},{20,16},{24,28},{28,24},{1,5},{5... | collective-permute-start | bytes 7520264 | tf_op jit(solution)/shard_map/ppermute | solution.py:310
  70.4 16.5 %collective-permute-start.9 = (bf16[192,1472]{1,0:T(8,128)(2,1)}, bf16[192,1472]{1,0:T(8,128)(2,1)}, u32[]{:S(2)}, u32[]{:S(2)}) collective-permute-start(bf16[192,1472]{1,0:T(8,128)(2,1)} %collective-permute-done.refs_2_.refs_6_), channel_id=1, source_target_pairs={{0,16},{4,20},{8,24},{12,28},{16,0},{20,4},{24,8},{28,12},{1,17},{... | collective-permute-start | bytes 1695752 | tf_op jit(solution)/shard_map/ppermute | solution.py:310
  71.5 16.5 %collective-permute-start.10 = (bf16[192,1472]{1,0:T(8,128)(2,1)}, bf16[192,1472]{1,0:T(8,128)(2,1)}, u32[]{:S(2)}, u32[]{:S(2)}) collective-permute-start(bf16[192,1472]{1,0:T(8,128)(2,1)} %collective-permute-done.3.refs_5_.refs_9_), channel_id=1, source_target_pairs={{0,8},{4,12},{8,0},{12,4},{16,24},{20,28},{24,16},{28,20},{1,9},{5... | collective-permute-start | bytes 1695752 | tf_op jit(solution)/shard_map/ppermute | solution.py:310
  73.0 88.6 %all-to-all-start = ((bf16[8,192,1472]{2,1,0:T(8,128)(2,1)}), bf16[8,192,1472]{2,1,0:T(8,128)(2,1)}, u32[]{:S(2)}, u32[]{:S(2)}) async-start(bf16[8,192,1472]{2,1,0:T(8,128)(2,1)} %get-tuple-element.108.refs_6_), calls=%async_computation | async-start | bytes 9437184 | tf_op jit(solution)/shard_map/all_to_all | solution.py:1087
  78.0 83.0 %all-gather.6.cloned.1.call-start = ((), (), s32[]{:S(2)}) async-start(), calls=%async_computation.5 | async-start | bytes 1720320 | tf_op jit(solution)/shard_map/all_gather | solution.py:1126
  78.7 298.7 %reduce-scatter.3.cloned.1.call-start = ((), (), s32[]{:S(2)}) async-start(), calls=%async_computation.6 | async-start | bytes 3297280 | tf_op jit(solution)/shard_map/reduce_scatter | solution.py:1207
  100.2 5.5 %collective-permute-start.11 = (bf16[1,3,128,768]{3,2,1,0:T(8,128)(2,1)}, bf16[1,3,128,768]{3,2,1,0:T(8,128)(2,1)S(1)}, u32[]{:S(2)}, u32[]{:S(2)}) collective-permute-start(bf16[1,3,128,768]{3,2,1,0:T(8,128)(2,1)} %bitcast.69), channel_id=1, source_target_pairs={{0,4},{4,0},{8,12},{12,8},{16,20},{20,16},{24,28},{28,24},{1,5},{5... | collective-permute-start | bytes 1769480 | tf_op jit(solution)/shard_map/ppermute | solution.py:310
  100.2 5.4 %collective-permute-start.12 = (bf16[1,3,128,768]{3,2,1,0:T(8,128)(2,1)}, bf16[1,3,128,768]{3,2,1,0:T(8,128)(2,1)S(1)}, u32[]{:S(2)}, u32[]{:S(2)}) collective-permute-start(bf16[1,3,128,768]{3,2,1,0:T(8,128)(2,1)} %bitcast.74), channel_id=1, source_target_pairs={{0,4},{4,0},{8,12},{12,8},{16,20},{20,16},{24,28},{28,24},{1,5},{5... | collective-permute-start | bytes 1769480 | tf_op jit(solution)/shard_map/ppermute | solution.py:310
  100.7 4.9 %collective-permute-start.13 = (bf16[1,3,128,768]{3,2,1,0:T(8,128)(2,1)}, bf16[1,3,128,768]{3,2,1,0:T(8,128)(2,1)S(1)}, u32[]{:S(2)}, u32[]{:S(2)}) collective-permute-start(bf16[1,3,128,768]{3,2,1,0:T(8,128)(2,1)} %bitcast.79), channel_id=1, source_target_pairs={{0,4},{4,0},{8,12},{12,8},{16,20},{20,16},{24,28},{28,24},{1,5},{5... | collective-permute-start | bytes 1769480 | tf_op jit(solution)/shard_map/ppermute | solution.py:310
  100.8 4.9 %collective-permute-start.14 = (bf16[1,3,128,768]{3,2,1,0:T(8,128)(2,1)}, bf16[1,3,128,768]{3,2,1,0:T(8,128)(2,1)S(1)}, u32[]{:S(2)}, u32[]{:S(2)}) collective-permute-start(bf16[1,3,128,768]{3,2,1,0:T(8,128)(2,1)} %bitcast.84), channel_id=1, source_target_pairs={{0,4},{4,0},{8,12},{12,8},{16,20},{20,16},{24,28},{28,24},{1,5},{5... | collective-permute-start | bytes 1769480 | tf_op jit(solution)/shard_map/ppermute | solution.py:310
  121.1 43.3 %collective-permute-start.18 = (bf16[1472,896]{1,0:T(8,128)(2,1)}, bf16[1472,896]{1,0:T(8,128)(2,1)}, u32[]{:S(2)}, u32[]{:S(2)}) collective-permute-start(bf16[1472,896]{1,0:T(8,128)(2,1)} %all-gather.4.cloned.1.call-done.mine_ref), channel_id=1, source_target_pairs={{0,4},{4,0},{8,12},{12,8},{16,20},{20,16},{24,28},{28,24},{1,5},{5... | collective-permute-start | bytes 7913480 | tf_op jit(solution)/shard_map/ppermute | solution.py:310
  121.3 24.0 %collective-permute-start.17 = (bf16[384,384]{1,0:T(8,128)(2,1)S(1)}, bf16[384,384]{1,0:T(8,128)(2,1)S(1)}, u32[]{:S(2)}, u32[]{:S(2)}) collective-permute-start(bf16[384,384]{1,0:T(8,128)(2,1)S(1)} %bitcast.94), channel_id=1, source_target_pairs={{0,24},{4,28},{8,16},{12,20},{16,8},{20,12},{24,0},{28,4},{1,25},{... | collective-permute-start | bytes 884744 | tf_op jit(solution)/shard_map/ppermute | solution.py:310
  123.1 26.5 %collective-permute-start.16 = (bf16[384,384]{1,0:T(8,128)(2,1)S(1)}, bf16[384,384]{1,0:T(8,128)(2,1)S(1)}, u32[]{:S(2)}, u32[]{:S(2)}) collective-permute-start(bf16[384,384]{1,0:T(8,128)(2,1)S(1)} %bitcast.95), channel_id=1, source_target_pairs={{0,16},{4,20},{8,24},{12,28},{16,0},{20,4},{24,8},{28,12},{1,17},{... | collective-permute-start | bytes 884744 | tf_op jit(solution)/shard_map/ppermute | solution.py:310
  124.2 26.2 %collective-permute-start.15 = (bf16[384,384]{1,0:T(8,128)(2,1)S(1)}, bf16[384,384]{1,0:T(8,128)(2,1)S(1)}, u32[]{:S(2)}, u32[]{:S(2)}) collective-permute-start(bf16[384,384]{1,0:T(8,128)(2,1)S(1)} %bitcast.96), channel_id=1, source_target_pairs={{0,8},{4,12},{8,0},{12,4},{16,24},{20,28},{24,16},{28,20},{1,9},{5... | collective-permute-start | bytes 884744 | tf_op jit(solution)/shard_map/ppermute | solution.py:310
  207.6 21.1 %collective-permute-start.20 = (bf16[192,1472]{1,0:T(8,128)(2,1)}, bf16[192,1472]{1,0:T(8,128)(2,1)S(1)}, u32[]{:S(2)}, u32[]{:S(2)}) collective-permute-start(bf16[192,1472]{1,0:T(8,128)(2,1)} %get-tuple-element.116), channel_id=1, source_target_pairs={{0,16},{4,20},{8,24},{12,28},{16,0},{20,4},{24,8},{28,12},{1,17},{... | collective-permute-start | bytes 1695752 | tf_op jit(solution)/shard_map/ppermute | solution.py:310
  208.7 20.0 %collective-permute-start.21 = (bf16[192,1472]{1,0:T(8,128)(2,1)}, bf16[192,1472]{1,0:T(8,128)(2,1)S(1)}, u32[]{:S(2)}, u32[]{:S(2)}) collective-permute-start(bf16[192,1472]{1,0:T(8,128)(2,1)} %get-tuple-element.118), channel_id=1, source_target_pairs={{0,8},{4,12},{8,0},{12,4},{16,24},{20,28},{24,16},{28,20},{1,9},{5... | collective-permute-start | bytes 1695752 | tf_op jit(solution)/shard_map/ppermute | solution.py:310
  210.6 26.2 %collective-permute-start.22 = (bf16[192,1472]{1,0:T(8,128)(2,1)}, bf16[192,1472]{1,0:T(8,128)(2,1)S(1)}, u32[]{:S(2)}, u32[]{:S(2)}) collective-permute-start(bf16[192,1472]{1,0:T(8,128)(2,1)} %get-tuple-element.122), channel_id=1, source_target_pairs={{0,8},{4,12},{8,0},{12,4},{16,24},{20,28},{24,16},{28,20},{1,9},{5... | collective-permute-start | bytes 1695752 | tf_op jit(solution)/shard_map/ppermute | solution.py:310
  210.7 26.1 %collective-permute-start.23 = (bf16[192,1472]{1,0:T(8,128)(2,1)}, bf16[192,1472]{1,0:T(8,128)(2,1)S(1)}, u32[]{:S(2)}, u32[]{:S(2)}) collective-permute-start(bf16[192,1472]{1,0:T(8,128)(2,1)} %get-tuple-element.123), channel_id=1, source_target_pairs={{0,16},{4,20},{8,24},{12,28},{16,0},{20,4},{24,8},{28,12},{1,17},{... | collective-permute-start | bytes 1695752 | tf_op jit(solution)/shard_map/ppermute | solution.py:310
  240.7 14.7 %collective-permute-start.24 = (bf16[192,1472]{1,0:T(8,128)(2,1)}, bf16[192,1472]{1,0:T(8,128)(2,1)S(1)}, u32[]{:S(2)}, u32[]{:S(2)}) collective-permute-start(bf16[192,1472]{1,0:T(8,128)(2,1)} %get-tuple-element.124), channel_id=1, source_target_pairs={{0,8},{4,12},{8,0},{12,4},{16,24},{20,28},{24,16},{28,20},{1,9},{5... | collective-permute-start | bytes 1695752 | tf_op jit(solution)/shard_map/ppermute | solution.py:310
  242.5 14.3 %collective-permute-start.25 = (bf16[192,1472]{1,0:T(8,128)(2,1)}, bf16[192,1472]{1,0:T(8,128)(2,1)}, u32[]{:S(2)}, u32[]{:S(2)}) collective-permute-start(bf16[192,1472]{1,0:T(8,128)(2,1)} %get-tuple-element.125), channel_id=1, source_target_pairs={{0,16},{4,20},{8,24},{12,28},{16,0},{20,4},{24,8},{28,12},{1,17},{... | collective-permute-start | bytes 1695752 | tf_op jit(solution)/shard_map/ppermute | solution.py:310
  245.1 18.3 %collective-permute-start.31 = (bf16[1,736,896]{2,1,0:T(8,128)(2,1)}, bf16[1,736,896]{2,1,0:T(8,128)(2,1)S(1)}, u32[]{:S(2)}, u32[]{:S(2)}) collective-permute-start(bf16[1,736,896]{2,1,0:T(8,128)(2,1)} %get-tuple-element.168), channel_id=1, source_target_pairs={{0,4},{4,0},{8,12},{12,8},{16,20},{20,16},{24,28},{28,24},{1,5},{5... | collective-permute-start | bytes 3956744 | tf_op jit(solution)/shard_map/ppermute | solution.py:310
  245.1 18.3 %collective-permute-start.30 = (bf16[1,736,896]{2,1,0:T(8,128)(2,1)}, bf16[1,736,896]{2,1,0:T(8,128)(2,1)S(1)}, u32[]{:S(2)}, u32[]{:S(2)}) collective-permute-start(bf16[1,736,896]{2,1,0:T(8,128)(2,1)} %get-tuple-element.169), channel_id=1, source_target_pairs={{0,4},{4,0},{8,12},{12,8},{16,20},{20,16},{24,28},{28,24},{1,5},{5... | collective-permute-start | bytes 3956744 | tf_op jit(solution)/shard_map/ppermute | solution.py:310
  268.8 59.4 %all-to-all-start.1 = ((bf16[8,192,1472]{2,1,0:T(8,128)(2,1)}), bf16[8,192,1472]{2,1,0:T(8,128)(2,1)}, u32[]{:S(2)}, u32[]{:S(2)}) async-start(bf16[8,192,1472]{2,1,0:T(8,128)(2,1)} %get-tuple-element.129), calls=%async_computation.1 | async-start | bytes 9437184 | tf_op jit(solution)/shard_map/all_to_all | solution.py:1087
  273.8 115.3 %reduce-scatter.5.cloned.1.call-start = ((), (), s32[]{:S(2)}) async-start(), calls=%async_computation.7 | async-start | bytes 1720320 | tf_op jit(solution)/shard_map/reduce_scatter | solution.py:1208
  292.7 4.7 collective-permute-start.26
  292.8 4.6 collective-permute-start.27
  312.0 21.3 %collective-permute-start.35 = (bf16[4,4,64,1152]{3,2,1,0:T(8,128)(2,1)}, bf16[4,4,64,1152]{3,2,1,0:T(8,128)(2,1)}, u32[]{:S(2)}, u32[]{:S(2)}) collective-permute-start(bf16[4,4,64,1152]{3,2,1,0:T(8,128)(2,1)} %get-tuple-element.150), channel_id=1, source_target_pairs={{0,4},{4,0},{8,12},{12,8},{16,20},{20,16},{24,28},{28,24},{1,5},{5... | collective-permute-start | bytes 7077896 | tf_op jit(solution)/shard_map/ppermute | solution.py:310
  313.3 5.2 %collective-permute-start.53 = (bf16[4,112,1472]{2,1,0:T(8,128)(2,1)S(1)}, bf16[4,112,1472]{2,1,0:T(8,128)(2,1)S(1)}, u32[]{:S(2)}, u32[]{:S(2)}) collective-permute-start(bf16[4,112,1472]{2,1,0:T(8,128)(2,1)S(1)} %get-tuple-element.166), channel_id=1, source_target_pairs={{0,4},{4,0},{8,12},{12,8},{16,20},{20,16},{24,28},{28,24},{1,5},{5... | collective-permute-start | bytes 3956744 | tf_op jit(solution)/shard_map/ppermute | solution.py:310
  313.7 27.0 %collective-permute-start.32 = (bf16[384,768]{1,0:T(8,128)(2,1)}, bf16[384,768]{1,0:T(8,128)(2,1)S(1)}, u32[]{:S(2)}, u32[]{:S(2)}) collective-permute-start(bf16[384,768]{1,0:T(8,128)(2,1)} %get-tuple-element.145), channel_id=1, source_target_pairs={{0,8},{4,12},{8,0},{12,4},{16,24},{20,28},{24,16},{28,20},{1,9},{5... | collective-permute-start | bytes 1769480 | tf_op jit(solution)/shard_map/ppermute | solution.py:310
  315.6 27.5 %collective-permute-start.33 = (bf16[384,768]{1,0:T(8,128)(2,1)}, bf16[384,768]{1,0:T(8,128)(2,1)}, u32[]{:S(2)}, u32[]{:S(2)}) collective-permute-start(bf16[384,768]{1,0:T(8,128)(2,1)} %get-tuple-element.146), channel_id=1, source_target_pairs={{0,16},{4,20},{8,24},{12,28},{16,0},{20,4},{24,8},{28,12},{1,17},{... | collective-permute-start | bytes 1769480 | tf_op jit(solution)/shard_map/ppermute | solution.py:310
  317.1 37.4 %collective-permute-start.34 = (bf16[384,768]{1,0:T(8,128)(2,1)S(1)}, bf16[384,768]{1,0:T(8,128)(2,1)}, u32[]{:S(2)}, u32[]{:S(2)}) collective-permute-start(bf16[384,768]{1,0:T(8,128)(2,1)S(1)} %copy-done.52), channel_id=1, source_target_pairs={{0,24},{4,28},{8,16},{12,20},{16,8},{20,12},{24,0},{28,4},{1,25},{... | collective-permute-start | bytes 1769480 | tf_op jit(solution)/shard_map/ppermute | solution.py:310
  337.9 28.2 %collective-permute-start.36 = (bf16[4,64,1152]{2,1,0:T(8,128)(2,1)}, bf16[4,64,1152]{2,1,0:T(8,128)(2,1)S(1)}, u32[]{:S(2)}, u32[]{:S(2)}) collective-permute-start(bf16[4,64,1152]{2,1,0:T(8,128)(2,1)} %get-tuple-element.152), channel_id=1, source_target_pairs={{0,8},{4,12},{8,0},{12,4},{16,24},{20,28},{24,16},{28,20},{1,9},{5... | collective-permute-start | bytes 1769480 | tf_op jit(solution)/shard_map/ppermute | solution.py:310
  339.5 26.6 %collective-permute-start.37 = (bf16[4,64,1152]{2,1,0:T(8,128)(2,1)}, bf16[4,64,1152]{2,1,0:T(8,128)(2,1)S(1)}, u32[]{:S(2)}, u32[]{:S(2)}) collective-permute-start(bf16[4,64,1152]{2,1,0:T(8,128)(2,1)} %get-tuple-element.153), channel_id=1, source_target_pairs={{0,16},{4,20},{8,24},{12,28},{16,0},{20,4},{24,8},{28,12},{1,17},{... | collective-permute-start | bytes 1769480 | tf_op jit(solution)/shard_map/ppermute | solution.py:310
  341.6 35.9 %collective-permute-start.38 = (bf16[4,64,1152]{2,1,0:T(8,128)(2,1)}, bf16[4,64,1152]{2,1,0:T(8,128)(2,1)S(1)}, u32[]{:S(2)}, u32[]{:S(2)}) collective-permute-start(bf16[4,64,1152]{2,1,0:T(8,128)(2,1)} %get-tuple-element.154), channel_id=1, source_target_pairs={{0,24},{4,28},{8,16},{12,20},{16,8},{20,12},{24,0},{28,4},{1,25},{... | collective-permute-start | bytes 1769480 | tf_op jit(solution)/shard_map/ppermute | solution.py:310
  381.1 37.2 %collective-permute-start.44 = (bf16[368,896]{1,0:T(8,128)(2,1)S(1)}, bf16[368,896]{1,0:T(8,128)(2,1)S(1)}, u32[]{:S(2)}, u32[]{:S(2)}) collective-permute-start(bf16[368,896]{1,0:T(8,128)(2,1)S(1)} %copy-done.12), channel_id=1, source_target_pairs={{0,24},{4,28},{8,16},{12,20},{16,8},{20,12},{24,0},{28,4},{1,25},{... | collective-permute-start | bytes 1978376 | tf_op jit(solution)/shard_map/ppermute | solution.py:310
  381.7 37.1 %collective-permute-start.43 = (bf16[368,896]{1,0:T(8,128)(2,1)S(1)}, bf16[368,896]{1,0:T(8,128)(2,1)S(1)}, u32[]{:S(2)}, u32[]{:S(2)}) collective-permute-start(bf16[368,896]{1,0:T(8,128)(2,1)S(1)} %copy-done.12), channel_id=1, source_target_pairs={{0,16},{4,20},{8,24},{12,28},{16,0},{20,4},{24,8},{28,12},{1,17},{... | collective-permute-start | bytes 1978376 | tf_op jit(solution)/shard_map/ppermute | solution.py:310
  383.1 35.8 %collective-permute-start.42 = (bf16[368,896]{1,0:T(8,128)(2,1)S(1)}, bf16[368,896]{1,0:T(8,128)(2,1)S(1)}, u32[]{:S(2)}, u32[]{:S(2)}) collective-permute-start(bf16[368,896]{1,0:T(8,128)(2,1)S(1)} %copy-done.12), channel_id=1, source_target_pairs={{0,8},{4,12},{8,0},{12,4},{16,24},{20,28},{24,16},{28,20},{1,9},{5... | collective-permute-start | bytes 1978376 | tf_op jit(solution)/shard_map/ppermute | solution.py:310
  386.4 7.0 %collective-permute-start.41 = (bf16[64,1152]{1,0:T(8,128)(2,1)S(1)}, bf16[64,1152]{1,0:T(8,128)(2,1)S(1)}, u32[]{:S(2)}, u32[]{:S(2)}) collective-permute-start(bf16[64,1152]{1,0:T(8,128)(2,1)S(1)} %get-tuple-element.178), channel_id=1, source_target_pairs={{0,3},{1,2},{2,1},{3,0},{4,7},{5,6},{6,5},{7,4},{8,11},{9,10},{10,... | collective-permute-start | bytes 442376 | tf_op jit(solution)/shard_map/ppermute | solution.py:315
  389.1 9.8 %collective-permute-start.40 = (bf16[64,1152]{1,0:T(8,128)(2,1)S(1)}, bf16[64,1152]{1,0:T(8,128)(2,1)S(1)}, u32[]{:S(2)}, u32[]{:S(2)}) collective-permute-start(bf16[64,1152]{1,0:T(8,128)(2,1)S(1)} %get-tuple-element.179), channel_id=1, source_target_pairs={{0,2},{1,3},{2,0},{3,1},{4,6},{5,7},{6,4},{7,5},{8,10},{9,11},{10,... | collective-permute-start | bytes 442376 | tf_op jit(solution)/shard_map/ppermute | solution.py:315
  393.4 24.8 %collective-permute-start.56 = (bf16[112,1472]{1,0:T(8,128)(2,1)}, bf16[112,1472]{1,0:T(8,128)(2,1)S(1)}, u32[]{:S(2)}, u32[]{:S(2)}) collective-permute-start(bf16[112,1472]{1,0:T(8,128)(2,1)} %reduce-scatter.5.cloned.1.call-done.refs_0_), channel_id=1, source_target_pairs={{0,24},{4,28},{8,16},{12,20},{16,8},{20,12},{24,0},{28,4},{1,25},{... | collective-permute-start | bytes 989192 | tf_op jit(solution)/shard_map/ppermute | solution.py:310
  398.9 5.1 %collective-permute-start.39 = (bf16[64,1152]{1,0:T(8,128)(2,1)S(1)}, bf16[64,1152]{1,0:T(8,128)(2,1)S(1)}, u32[]{:S(2)}, u32[]{:S(2)}) collective-permute-start(bf16[64,1152]{1,0:T(8,128)(2,1)S(1)} %get-tuple-element.180), channel_id=1, source_target_pairs={{0,1},{1,0},{2,3},{3,2},{4,5},{5,4},{6,7},{7,6},{8,9},{9,8},{10,11... | collective-permute-start | bytes 442376 | tf_op jit(solution)/shard_map/ppermute | solution.py:315
  404.1 20.9 %collective-permute-start.55 = (bf16[112,1472]{1,0:T(8,128)(2,1)}, bf16[112,1472]{1,0:T(8,128)(2,1)}, u32[]{:S(2)}, u32[]{:S(2)}) collective-permute-start(bf16[112,1472]{1,0:T(8,128)(2,1)} %reduce-scatter.5.cloned.1.call-done.refs_0_), channel_id=1, source_target_pairs={{0,16},{4,20},{8,24},{12,28},{16,0},{20,4},{24,8},{28,12},{1,17},{... | collective-permute-start | bytes 989192 | tf_op jit(solution)/shard_map/ppermute | solution.py:310
  418.3 18.2 %collective-permute-start.48 = (bf16[368,896]{1,0:T(8,128)(2,1)S(1)}, bf16[368,896]{1,0:T(8,128)(2,1)S(1)}, u32[]{:S(2)}, u32[]{:S(2)}) collective-permute-start(bf16[368,896]{1,0:T(8,128)(2,1)S(1)} %copy-done.12), channel_id=1, source_target_pairs={{0,4},{4,0},{8,12},{12,8},{16,20},{20,16},{24,28},{28,24},{1,5},{5... | collective-permute-start | bytes 1978376 | tf_op jit(solution)/shard_map/ppermute | solution.py:310
  418.3 25.0 %collective-permute-start.51 = (bf16[368,896]{1,0:T(8,128)(2,1)S(1)}, bf16[368,896]{1,0:T(8,128)(2,1)}, u32[]{:S(2)}, u32[]{:S(2)}) collective-permute-start(bf16[368,896]{1,0:T(8,128)(2,1)S(1)} %collective-permute-done.44.refs_6_.refs_3_), channel_id=1, source_target_pairs={{0,4},{4,0},{8,12},{12,8},{16,20},{20,16},{24,28},{28,24},{1,5},{5... | collective-permute-start | bytes 1978376 | tf_op jit(solution)/shard_map/ppermute | solution.py:310
  418.8 25.0 %collective-permute-start.50 = (bf16[368,896]{1,0:T(8,128)(2,1)S(1)}, bf16[368,896]{1,0:T(8,128)(2,1)}, u32[]{:S(2)}, u32[]{:S(2)}) collective-permute-start(bf16[368,896]{1,0:T(8,128)(2,1)S(1)} %collective-permute-done.43.refs_5_.refs_2_), channel_id=1, source_target_pairs={{0,4},{4,0},{8,12},{12,8},{16,20},{20,16},{24,28},{28,24},{1,5},{5... | collective-permute-start | bytes 1978376 | tf_op jit(solution)/shard_map/ppermute | solution.py:310
  419.0 24.9 %collective-permute-start.49 = (bf16[368,896]{1,0:T(8,128)(2,1)S(1)}, bf16[368,896]{1,0:T(8,128)(2,1)}, u32[]{:S(2)}, u32[]{:S(2)}) collective-permute-start(bf16[368,896]{1,0:T(8,128)(2,1)S(1)} %collective-permute-done.42.refs_4_.refs_1_), channel_id=1, source_target_pairs={{0,4},{4,0},{8,12},{12,8},{16,20},{20,16},{24,28},{28,24},{1,5},{5... | collective-permute-start | bytes 1978376 | tf_op jit(solution)/shard_map/ppermute | solution.py:310
  425.0 9.7 %collective-permute-start.54 = (bf16[112,1472]{1,0:T(8,128)(2,1)}, bf16[112,1472]{1,0:T(8,128)(2,1)}, u32[]{:S(2)}, u32[]{:S(2)}) collective-permute-start(bf16[112,1472]{1,0:T(8,128)(2,1)} %reduce-scatter.5.cloned.1.call-done.refs_0_), channel_id=1, source_target_pairs={{0,8},{4,12},{8,0},{12,4},{16,24},{20,28},{24,16},{28,20},{1,9},{5... | collective-permute-start | bytes 989192 | tf_op jit(solution)/shard_map/ppermute | solution.py:310
  434.7 6.4 %collective-permute-start.47 = (bf16[64,1152]{1,0:T(8,128)(2,1)}, bf16[64,1152]{1,0:T(8,128)(2,1)S(1)}, u32[]{:S(2)}, u32[]{:S(2)}) collective-permute-start(bf16[64,1152]{1,0:T(8,128)(2,1)} %sum_parts.3.refs_0_), channel_id=1, source_target_pairs={{0,24},{4,28},{8,16},{12,20},{16,8},{20,12},{24,0},{28,4},{1,25},{... | collective-permute-start | bytes 442376 | tf_op jit(solution)/shard_map/ppermute | solution.py:310
  436.5 6.8 %collective-permute-start.46 = (bf16[64,1152]{1,0:T(8,128)(2,1)}, bf16[64,1152]{1,0:T(8,128)(2,1)S(1)}, u32[]{:S(2)}, u32[]{:S(2)}) collective-permute-start(bf16[64,1152]{1,0:T(8,128)(2,1)} %sum_parts.3.refs_0_), channel_id=1, source_target_pairs={{0,16},{4,20},{8,24},{12,28},{16,0},{20,4},{24,8},{28,12},{1,17},{... | collective-permute-start | bytes 442376 | tf_op jit(solution)/shard_map/ppermute | solution.py:310
  441.0 11.5 %collective-permute-start.45 = (bf16[64,1152]{1,0:T(8,128)(2,1)}, bf16[64,1152]{1,0:T(8,128)(2,1)S(1)}, u32[]{:S(2)}, u32[]{:S(2)}) collective-permute-start(bf16[64,1152]{1,0:T(8,128)(2,1)} %sum_parts.3.refs_0_), channel_id=1, source_target_pairs={{0,8},{4,12},{8,0},{12,4},{16,24},{20,28},{24,16},{28,20},{1,9},{5... | collective-permute-start | bytes 442376 | tf_op jit(solution)/shard_map/ppermute | solution.py:310
  443.3 12.0 %collective-permute-start.57 = (bf16[112,1472]{1,0:T(8,128)(2,1)}, bf16[112,1472]{1,0:T(8,128)(2,1)}, u32[]{:S(2)}, u32[]{:S(2)}) collective-permute-start(bf16[112,1472]{1,0:T(8,128)(2,1)} %reduce-scatter.5.cloned.1.call-done.refs_0_), channel_id=1, source_target_pairs={{0,4},{4,0},{8,12},{12,8},{16,20},{20,16},{24,28},{28,24},{1,5},{5... | collective-permute-start | bytes 989192 | tf_op jit(solution)/shard_map/ppermute | solution.py:310
  443.3 12.0 %collective-permute-start.60 = (bf16[112,1472]{1,0:T(8,128)(2,1)}, bf16[112,1472]{1,0:T(8,128)(2,1)}, u32[]{:S(2)}, u32[]{:S(2)}) collective-permute-start(bf16[112,1472]{1,0:T(8,128)(2,1)} %copy-done.35), channel_id=1, source_target_pairs={{0,4},{4,0},{8,12},{12,8},{16,20},{20,16},{24,28},{28,24},{1,5},{5... | collective-permute-start | bytes 989192 | tf_op jit(solution)/shard_map/ppermute | solution.py:310
  443.8 11.5 %collective-permute-start.59 = (bf16[112,1472]{1,0:T(8,128)(2,1)}, bf16[112,1472]{1,0:T(8,128)(2,1)}, u32[]{:S(2)}, u32[]{:S(2)}) collective-permute-start(bf16[112,1472]{1,0:T(8,128)(2,1)} %collective-permute-done.55.refs_2_), channel_id=1, source_target_pairs={{0,4},{4,0},{8,12},{12,8},{16,20},{20,16},{24,28},{28,24},{1,5},{5... | collective-permute-start | bytes 989192 | tf_op jit(solution)/shard_map/ppermute | solution.py:310
  443.9 11.4 %collective-permute-start.58 = (bf16[112,1472]{1,0:T(8,128)(2,1)}, bf16[112,1472]{1,0:T(8,128)(2,1)}, u32[]{:S(2)}, u32[]{:S(2)}) collective-permute-start(bf16[112,1472]{1,0:T(8,128)(2,1)} %collective-permute-done.54.refs_1_), channel_id=1, source_target_pairs={{0,4},{4,0},{8,12},{12,8},{16,20},{20,16},{24,28},{28,24},{1,5},{5... | collective-permute-start | bytes 989192 | tf_op jit(solution)/shard_map/ppermute | solution.py:310
  455.2 8.0 %collective-permute-start.52 = (bf16[4,64,1152]{2,1,0:T(8,128)(2,1)}, bf16[4,64,1152]{2,1,0:T(8,128)(2,1)S(1)}, u32[]{:S(2)}, u32[]{:S(2)}) collective-permute-start(bf16[4,64,1152]{2,1,0:T(8,128)(2,1)} %stack_small.1.near_ref), channel_id=1, source_target_pairs={{0,4},{4,0},{8,12},{12,8},{16,20},{20,16},{24,28},{28,24},{1,5},{5... | collective-permute-start | bytes 1769480 | tf_op jit(solution)/shard_map/ppermute | solution.py:310
  (58 other events, 364.4 us)
Sparse Core Ops, SparseCore 0:
  48.9 53.0 all-gather.3
  104.2 32.5 all-gather.5
  268.9 51.8 reduce-scatter.2
  323.6 33.3 reduce-scatter.4

commit v7 on v6

--- a/solution.py
+++ b/solution.py
@@ -1022,7 +1022,7 @@
                 column = inner + 256 * pair + 128 * offset
                 out_ref[base + skip : base + size, 128 * pair : 128 * pair + 128] = block[skip:size, column : column + 128]
         if index == GROUP - 1:
-            table_ref[...] = block[:16, :128]
+            table_ref[...] = block[: table_ref.shape[0], : table_ref.shape[1]]
         column = (index // 2) * wide
         reach = min(wide, proj_out.shape[1] - column)
         for lane in range(3):
@@ -1248,7 +1248,7 @@
         out_specs=[VMEM_WHOLE] * 6,
         out_shape=[
             column, column, column, jax.ShapeDtypeStruct((inner // depth, width), FLOAT),
-            jax.ShapeDtypeStruct((shard, 128), FLOAT), jax.ShapeDtypeStruct((16, 128), FLOAT),
+            jax.ShapeDtypeStruct((shard, 128), FLOAT), jax.ShapeDtypeStruct((buckets, heads), FLOAT),
         ],
         compiler_params=BIG,
         cost_estimate=moved(grads_near, grads_far, grads_near),
@@ -1267,7 +1267,7 @@
         jnp.transpose(down_out),
         early_sum[:, 0] / gain_early.astype(FLOAT),
         late_sum[:, 0] / gain_late.astype(FLOAT),
-        table_rows[:buckets, :heads],
+        table_rows,
     )
 
 

time: 482 us -> 481 us (level)
  no operation moved by 1% of the time
where the time goes in v7:
time: 481 us; the launch traced here: 476 us
  Pallas kernels  212 us (44%)
  waiting for transfers between devices  134 us (28%)
  starting transfers between devices  60.3 us (13%)
  local copies, waits for them, and re-layouts  24.1 us (5%)
  blocking collectives  19.4 us (4%)
  between operations  14.6 us (3%)
  other arithmetic  9.1 us (2%)
    ppermute x58, waiting for transfers between devices, swap(): lax.ppermute(value, 'ctx', [(source, source ^ bit) for source in range(co...  115 us
    ppermute x58, starting transfers between devices, swap(): lax.ppermute(value, 'ctx', [(source, source ^ bit) for source in range(co...  47.3 us
    pallas_call x1, Pallas kernels, feed_forward(): pl.pallas_call(feed_kernel, grid_spec=pltpu.PrefetchScalarGridSpec(num_sc...  42.2 us
    pallas_call x2, Pallas kernels, outer_sums(): pl.pallas_call(outer_kernel, grid=(2,), in_specs=[pl.BlockSpec((2, tokens...  26.1 us
    all_gather x1, blocking collectives, on_device(): packed = lax.all_gather(packed, 'wsh', axis=0)  19.4 us
    pallas_call x1, Pallas kernels, attention_backward(): pl.pallas_call(skipping(functools.partial(backward_kernel, rows=rows, cou...  18.8 us
    ppermute x3, waiting for transfers between devices, swap_depth(): lax.ppermute(value, 'wsh', [(source, source ^ bit) for source in range(co...  14.3 us
    pallas_call x1, Pallas kernels, weight_grads(): pl.pallas_call(skipping(functools.partial(grad_kernel, depth=depth, size=...  13.4 us
  transfers between devices with their start and end apart: 67, of which 27 were waited for; matrix products, arithmetic and copies ran while one was open for 5% of the time, Pallas kernels for 33%

profile of v7, /device:TPU:0, one launch (start us, length us, event | category | flops | bytes accessed | tf_op | source)
XLA Modules:
  0.0 475.6 jit_solution(1658025233478240333)
XLA Ops:
  7.2 4.7 token_rows.1
  11.9 3.0 collective-permute-start.2
  14.9 1.5 collective-permute-start
  17.1 2.3 constant_dynamic-slice_fusion.4
  24.2 2.0 pack.1
  26.1 19.4 %all-gather = bf16[320,1152]{1,0:T(8,128)(2,1)S(1)} all-gather(bf16[80,1152]{1,0:T(8,128)(2,1)} %pack.1), channel_id=2, replica_groups=mesh['ctx'=8,'wsh'=4] {'wsh'}, dimensions={0}, use_global_device_ids=true | all-gather | bytes 921600 | tf_op jit(solution)/shard_map/all_gather | solution.py:1119
  45.8 1.6 collective-permute-start.5
  48.8 9.9 %collective-permute-done.5 = bf16[272,1152]{1,0:T(8,128)(2,1)S(1)} collective-permute-done((bf16[272,1152]{1,0:T(8,128)(2,1)S(1)}, bf16[272,1152]{1,0:T(8,128)(2,1)S(1)}, u32[]{:S(2)}, u32[]{:S(2)}) %collective-permute-start.5) | collective-permute-done | bytes 626720 | tf_op jit(solution)/shard_map/ppermute | solution.py:310
  58.7 2.5 collective-permute-start.7
  62.7 5.7 %collective-permute-done.6 = bf16[128,1152]{1,0:T(8,128)(2,1)S(1)} collective-permute-done((bf16[128,1152]{1,0:T(8,128)(2,1)S(1)}, bf16[128,1152]{1,0:T(8,128)(2,1)S(1)}, u32[]{:S(2)}, u32[]{:S(2)}) %collective-permute-start.6) | collective-permute-done | bytes 294944 | tf_op jit(solution)/shard_map/ppermute | solution.py:310
  68.5 1.8 pad_maximum_fusion.near_ref
  73.0 5.0 %all-to-all-start = ((bf16[8,192,1472]{2,1,0:T(8,128)(2,1)}), bf16[8,192,1472]{2,1,0:T(8,128)(2,1)}, u32[]{:S(2)}, u32[]{:S(2)}) async-start(bf16[8,192,1472]{2,1,0:T(8,128)(2,1)} %get-tuple-element.108.refs_6_), calls=%async_computation | async-start | bytes 9437184 | tf_op jit(solution)/shard_map/all_to_all | solution.py:1087
  79.0 4.8 %unpack.1 = (bf16[1472,1152]{1,0:T(8,128)(2,1)}, bf16[384,1472]{1,0:T(8,128)(2,1)}, f32[8,1472]{1,0:T(8,128)}, f32[32,128]{1,0:T(8,128)}, f32[3,8,128]{2,1,0:T(8,128)}) custom-call(s32[2]{0:T(128)} %pad_add_fusion.place_ref.refs_0_, bf16[4,16,1152]{2,1,0:T(8,128)(2,1)} %slice.68.misc_ref, bf16[4,272,1152]{2,1,0:T(8,128)(2,1)} %copy-done.3, ...), custom_call_target="tpu_custom_call" | custom-call | bytes 1504051 | tf_op jit(solution)/shard_map/unpack/pallas_call | solution.py:1127
  85.3 1.7 collective-permute-done.9.refs_6_.refs_10_
  88.0 12.2 %norm_project.1 = (bf16[4,384,1472]{2,1,0:T(8,128)(2,1)}, bf16[1,384,768]{2,1,0:T(8,128)(2,1)}, bf16[1,384,768]{2,1,0:T(8,128)(2,1)}, bf16[1,384,768]{2,1,0:T(8,...) custom-call(bf16[192,1472]{1,0:T(8,128)(2,1)} %get-tuple-element.90.refs_0_.refs_4_, ...), custom_call_target="tpu_custom_call" | custom-call | flops 781398848 | bytes 2034892 | tf_op jit(solution)/shard_map/norm_project/pallas_call | solution.py:553
  101.3 4.4 attention_terms.1
  107.1 12.8 %attention_forward.1 = (f32[3,128,384]{2,1,0:T(8,128)}, f32[3,3,8,128]{3,2,1,0:T(8,128)}) custom-call(s32[1]{0:T(128)} %bitcast.meta_ref.refs_0_, f32[3,2,5,128,128]{4,3,2,1,0:T(8,128)} %get-tuple-element.95.bias_ref.refs_1_, f32[3,8,128,128]{3,2,1,0:T(8,128)} %get-tuple-element.96.mask_ref.refs_2_, bf16[3,128,384]{2,1,0:T(8,128)(2,1)} %bitcast.103, ...), custom_call_target="tpu_custom_call" | custom-call | flops 120795952 | bytes 1887436 | tf_op jit(solution)/shard_map/attention_forward/pallas_call | solution.py:270
  121.3 1.8 collective-permute-start.17
  124.8 20.5 %collective-permute-done.17.refs_3_ = bf16[384,384]{1,0:T(8,128)(2,1)S(1)} collective-permute-done((bf16[384,384]{1,0:T(8,128)(2,1)S(1)}, bf16[384,384]{1,0:T(8,128)(2,1)S(1)}, u32[]{:S(2)}, u32[]{:S(2)}) %collective-permute-start.17) | collective-permute-done | bytes 294944 | tf_op jit(solution)/shard_map/ppermute | solution.py:310
  145.3 4.3 collective-permute-done.16.refs_2_
  151.1 9.9 %late_norm.1 = (f32[384,1472]{1,0:T(8,128)}, bf16[4,384,1472]{2,1,0:T(8,128)(2,1)}) custom-call(bf16[384,384]{1,0:T(8,128)(2,1)} %bitcast.97, bf16[384,384]{1,0:T(8,128)(2,1)} %copy-done.38, bf16[384,384]{1,0:T(8,128)(2,1)} %copy-done.37, bf16[384,384]{1,0:T(8,128)(2,1)} %copy-done.36, bf16[192,1472]{1,0:T(8,128)(2,1)} %get-tuple-element.90.refs_0_.refs_4_, ...), custom_call_target="tpu_custom_call" | custom-call | flops 347288384 | bytes 2713190 | tf_op jit(solution)/shard_map/late_norm/pallas_call | solution.py:598
  161.6 2.7 collective-permute-done.19.down_other
  165.4 42.2 %feed_forward.1 = (bf16[4,384,896]{2,1,0:T(8,128)(2,1)}, bf16[4,384,896]{2,1,0:T(8,128)(2,1)}, bf16[4,384,896]{2,1,0:T(8,128)(2,1)}, bf16[8,192,1472]{2,1,0:T(8,...) custom-call(s32[2]{0:T(128)} %pad_add_fusion.1.spot_ref, ...), custom_call_target="tpu_custom_call" | custom-call | flops 4862036992 | bytes 3391488 | tf_op jit(solution)/shard_map/feed_forward/pallas_call | solution.py:686
  208.7 2.0 collective-permute-start.21
  211.7 17.0 %outer_sums.2 = (bf16[2,736,896]{2,1,0:T(8,128)(2,1)}, bf16[2,736,896]{2,1,0:T(8,128)(2,1)}) custom-call(bf16[4,384,1472]{2,1,0:T(8,128)(2,1)} %get-tuple-element.107.normed_ref.left_ref, bf16[4,384,896]{2,1,0:T(8,128)(2,1)} %get-tuple-element.119.refs_0_, bf16[4,384,896]{2,1,0:T(8,128)(2,1)} %get-tuple-element.120.refs_1_), custom_call_target="tpu_custom_call" | custom-call | flops 3241358080 | tf_op jit(solution)/shard_map/outer_sums/pallas_call | solution.py:728
  228.7 8.1 %collective-permute-done.22.refs_5_.refs_4_ = bf16[192,1472]{1,0:T(8,128)(2,1)S(1)} collective-permute-done((bf16[192,1472]{1,0:T(8,128)(2,1)}, bf16[192,1472]{1,0:T(8,128)(2,1)S(1)}, u32[]{:S(2)}, u32[]{:S(2)}) %collective-permute-start.22) | collective-permute-done | bytes 565280 | tf_op jit(solution)/shard_map/ppermute | solution.py:310
  237.8 2.9 relay_sums.1
  240.7 1.7 collective-permute-start.24
  243.4 1.7 fusion.4
  245.6 9.1 %outer_sums.3.refs_9_ = bf16[2,448,1472]{2,1,0:T(8,128)(2,1)} custom-call(bf16[4,384,896]{2,1,0:T(8,128)(2,1)} %get-tuple-element.126.left_ref, bf16[4,384,1472]{2,1,0:T(8,128)(2,1)} %get-tuple-element.127.refs_0_), custom_call_target="tpu_custom_call" | custom-call | flops 1620679040 | tf_op jit(solution)/shard_map/outer_sums/pallas_call | solution.py:728
  256.7 6.7 %middle.1 = (f32[384,1472]{1,0:T(8,128)}, bf16[384,1472]{1,0:T(8,128)(2,1)}, bf16[384,384]{1,0:T(8,128)(2,1)}) custom-call(f32[384,1472]{1,0:T(8,128)} %get-tuple-element.106.refs_0_.after_ref, bf16[2,192,1472]{2,1,0:T(8,128)(2,1)} %get-tuple-element.114.refs_1_, bf16[192,1472]{1,0:T(8,128)(2,1)} %copy-done.54, bf16[192,1472]{1,0:T(8,128)(2,1)} %copy-done.25, ...), custom_call_target="tpu_custom_call" | custom-call | flops 99999997952 | tf_op jit(solution)/shard_map/middle/pallas_call | solution.py:780
  264.9 3.9 plus.2
  268.8 5.0 %all-to-all-start.1 = ((bf16[8,192,1472]{2,1,0:T(8,128)(2,1)}), bf16[8,192,1472]{2,1,0:T(8,128)(2,1)}, u32[]{:S(2)}, u32[]{:S(2)}) async-start(bf16[8,192,1472]{2,1,0:T(8,128)(2,1)} %get-tuple-element.129), calls=%async_computation.1 | async-start | bytes 9437184 | tf_op jit(solution)/shard_map/all_to_all | solution.py:1087
  273.9 18.8 %attention_backward.1 = (bf16[3,128,384]{2,1,0:T(8,128)(2,1)}, bf16[1,3,128,768]{3,2,1,0:T(8,128)(2,1)}, bf16[1,3,128,768]{3,2,1,0:T(8,128)(2,1)}, bf16[1,3,128,...) custom-call(s32[1]{0:T(128)} %bitcast.meta_ref.refs_0_, ...), custom_call_target="tpu_custom_call" | custom-call | flops 301989888 | bytes 4718592 | tf_op jit(solution)/shard_map/attention_backward/pallas_call | solution.py:291
  295.5 1.9 convolution_convert_fusion.refs_12_
  298.6 13.4 %weight_grads.1 = (bf16[384,768]{1,0:T(8,128)(2,1)}, bf16[384,768]{1,0:T(8,128)(2,1)}, bf16[384,768]{1,0:T(8,128)(2,1)}, bf16[384,768]{1,0:T(8,128)(2,1)}, bf16[...) custom-call(s32[2]{0:T(128)} %pad_add_fusion.place_ref.refs_0_, ...), custom_call_target="tpu_custom_call" | custom-call | flops 781398848 | bytes 1356595 | tf_op jit(solution)/shard_map/weight_grads/pallas_call | solution.py:489
  313.7 1.9 collective-permute-start.32
  319.6 3.9 plus.3
  323.4 4.8 %all-to-all-done.1 = bf16[8,192,1472]{2,1,0:T(8,128)(2,1)} async-done(((bf16[8,192,1472]{2,1,0:T(8,128)(2,1)}), bf16[8,192,1472]{2,1,0:T(8,128)(2,1)}, u32[]{:S(2)}, u32[]{:S(2)}) %all-to-all-start.1) | async-done | bytes 4522016 | tf_op jit(solution)/shard_map/all_to_all | solution.py:1087
  328.2 5.0 %output_sum.1.refs_2_ = bf16[3,1472,128]{2,1,0:T(8,128)(2,1)} custom-call(f32[384,1472]{1,0:T(8,128)} %get-tuple-element.106.refs_0_.after_ref, bf16[4,384,1472]{2,1,0:T(8,128)(2,1)} %bitcast.21.parts_ref), custom_call_target="tpu_custom_call" | custom-call | bytes 1356595 | tf_op jit(solution)/shard_map/output_sum/pallas_call | solution.py:907
  333.3 4.6 plus_apart.1
  337.9 1.6 collective-permute-start.36
  341.6 1.5 collective-permute-start.38
  343.1 11.4 %collective-permute-done.34.p3 = bf16[384,768]{1,0:T(8,128)(2,1)} collective-permute-done((bf16[384,768]{1,0:T(8,128)(2,1)S(1)}, bf16[384,768]{1,0:T(8,128)(2,1)}, u32[]{:S(2)}, u32[]{:S(2)}) %collective-permute-start.34) | collective-permute-done | bytes 589856 | tf_op jit(solution)/shard_map/ppermute | solution.py:310
  354.5 8.7 %input_gradient.1.refs_4_ = bf16[3,1472,128]{2,1,0:T(8,128)(2,1)} custom-call(bf16[384,384]{1,0:T(8,128)(2,1)} %bitcast.115, bf16[384,768]{1,0:T(8,128)(2,1)} %get-tuple-element.144.own_ref, bf16[384,768]{1,0:T(8,128)(2,1)} %copy-done.53, bf16[384,768]{1,0:T(8,128)(2,1)} %collective-permute-done.33.p2, bf16[384,768]{1,0:T(8,128)(2,1)} %collective-permute-done.34.p3, ...), custom_call_target="tpu_custom_call" | custom-call | flops 99999997952 | tf_op jit(solution)/shard_map/input_gradient/pallas_call | solution.py:882
  363.1 3.0 collective-permute-done.36.refs_1_
  366.1 11.4 %collective-permute-done.38.refs_3_ = bf16[4,64,1152]{2,1,0:T(8,128)(2,1)S(1)} collective-permute-done((bf16[4,64,1152]{2,1,0:T(8,128)(2,1)}, bf16[4,64,1152]{2,1,0:T(8,128)(2,1)S(1)}, u32[]{:S(2)}, u32[]{:S(2)}) %collective-permute-start.38) | collective-permute-done | bytes 589856 | tf_op jit(solution)/shard_map/ppermute | solution.py:310
  378.3 2.8 sum_parts.2
  384.5 1.8 slice_bitcast_fusion.2
  386.4 2.8 collective-permute-start.41
  389.1 4.3 collective-permute-done.41.refs_3_
  394.1 4.8 %collective-permute-done.40.refs_2_ = bf16[64,1152]{1,0:T(8,128)(2,1)S(1)} collective-permute-done((bf16[64,1152]{1,0:T(8,128)(2,1)S(1)}, bf16[64,1152]{1,0:T(8,128)(2,1)S(1)}, u32[]{:S(2)}, u32[]{:S(2)}) %collective-permute-start.40) | collective-permute-done | bytes 147488 | tf_op jit(solution)/shard_map/ppermute | solution.py:315
  398.9 5.1 %collective-permute-done.39.refs_1_ = bf16[64,1152]{1,0:T(8,128)(2,1)S(1)} collective-permute-done((bf16[64,1152]{1,0:T(8,128)(2,1)S(1)}, bf16[64,1152]{1,0:T(8,128)(2,1)S(1)}, u32[]{:S(2)}, u32[]{:S(2)}) %collective-permute-start.39) | collective-permute-done | bytes 147488 | tf_op jit(solution)/shard_map/ppermute | solution.py:315
  404.7 13.5 %collective-permute-done.56.refs_3_ = bf16[112,1472]{1,0:T(8,128)(2,1)S(1)} collective-permute-done((bf16[112,1472]{1,0:T(8,128)(2,1)}, bf16[112,1472]{1,0:T(8,128)(2,1)S(1)}, u32[]{:S(2)}, u32[]{:S(2)}) %collective-permute-start.56) | collective-permute-done | bytes 329760 | tf_op jit(solution)/shard_map/ppermute | solution.py:310
  419.4 5.6 %collective-permute-done.55.refs_2_ = bf16[112,1472]{1,0:T(8,128)(2,1)} collective-permute-done((bf16[112,1472]{1,0:T(8,128)(2,1)}, bf16[112,1472]{1,0:T(8,128)(2,1)}, u32[]{:S(2)}, u32[]{:S(2)}) %collective-permute-start.55) | collective-permute-done | bytes 329760 | tf_op jit(solution)/shard_map/ppermute | solution.py:310
  426.1 1.9 sum_parts.3.refs_0_
  428.0 6.7 %collective-permute-done.54.refs_1_ = bf16[112,1472]{1,0:T(8,128)(2,1)} collective-permute-done((bf16[112,1472]{1,0:T(8,128)(2,1)}, bf16[112,1472]{1,0:T(8,128)(2,1)}, u32[]{:S(2)}, u32[]{:S(2)}) %collective-permute-start.54) | collective-permute-done | bytes 329760 | tf_op jit(solution)/shard_map/ppermute | solution.py:310
  434.7 1.8 collective-permute-start.47
  437.9 3.1 collective-permute-done.47.refs_3_
  441.0 1.7 collective-permute-start.45
  444.3 8.2 %spread_columns.1 = (f32[368,3584]{1,0:T(8,128)}, f32[368,3584]{1,0:T(8,128)}, f32[368,128]{1,0:T(8,128)}) custom-call(s32[2]{0:T(128)} %pad_add_fusion.place_ref.refs_0_, bf16[368,896]{1,0:T(8,128)(2,1)} %reduce-scatter.3.cloned.1.call-done.refs_5_.refs_0_, bf16[368,896]{1,0:T(8,128)(2,1)} %copy-done.15, bf16[368,896]{1,0:T(8,128)(2,1)} %copy-done.14, ...), custom_call_target="tpu_custom_call" | custom-call | flops 1055129 | bytes 4220518 | tf_op jit(solution)/shard_map/spread_columns/pallas_call | solution.py:950
  453.2 2.0 stack_small.1.near_ref
  455.3 7.1 %join_down.1 = f32[1472,896]{1,0:T(8,128)} custom-call(s32[2]{0:T(128)} %pad_add_fusion.place_ref.refs_0_, bf16[112,1472]{1,0:T(8,128)(2,1)} %reduce-scatter.5.cloned.1.call-done.refs_0_, bf16[112,1472]{1,0:T(8,128)(2,1)} %collective-permute-done.54.refs_1_, bf16[112,1472]{1,0:T(8,128)(2,1)} %collective-permute-done.55.refs_2_, ...), custom_call_target="tpu_custom_call" | custom-call | bytes 197836 | tf_op jit(solution)/shard_map/join_down/pallas_call | solution.py:1224
  464.0 3.2 finish_small.1
  (241 shorter events, 58.1 us)
Async XLA Ops:
  7.2 113.9 %all-gather.4.cloned.1.call-start = ((), (), s32[]{:S(2)}) async-start(), calls=%async_computation.4 | async-start | bytes 3297280 | tf_op jit(solution)/shard_map/all_gather | solution.py:1120
  11.9 33.8 %collective-permute-start.2 = (bf16[192,1472]{1,0:T(8,128)(2,1)}, bf16[192,1472]{1,0:T(8,128)(2,1)}, u32[]{:S(2)}, u32[]{:S(2)}) collective-permute-start(bf16[192,1472]{1,0:T(8,128)(2,1)} %get-tuple-element.90.refs_0_.refs_4_), channel_id=1, source_target_pairs={{0,16},{4,20},{8,24},{12,28},{16,0},{20,4},{24,8},{28,12},{1,17},{... | collective-permute-start | bytes 1695752 | tf_op jit(solution)/shard_map/ppermute | solution.py:310
  14.9 30.8 %collective-permute-start = (bf16[192,1472]{1,0:T(8,128)(2,1)}, bf16[192,1472]{1,0:T(8,128)(2,1)}, u32[]{:S(2)}, u32[]{:S(2)}) collective-permute-start(bf16[192,1472]{1,0:T(8,128)(2,1)} %get-tuple-element.90.refs_0_.refs_4_), channel_id=1, source_target_pairs={{0,8},{4,12},{8,0},{12,4},{16,24},{20,28},{24,16},{28,20},{1,9},{5... | collective-permute-start | bytes 1695752 | tf_op jit(solution)/shard_map/ppermute | solution.py:310
  16.4 29.3 %collective-permute-start.3 = (bf16[192,1472]{1,0:T(8,128)(2,1)}, bf16[192,1472]{1,0:T(8,128)(2,1)}, u32[]{:S(2)}, u32[]{:S(2)}) collective-permute-start(bf16[192,1472]{1,0:T(8,128)(2,1)} %get-tuple-element.91.refs_1_.refs_5_), channel_id=1, source_target_pairs={{0,16},{4,20},{8,24},{12,28},{16,0},{20,4},{24,8},{28,12},{1,17},{... | collective-permute-start | bytes 1695752 | tf_op jit(solution)/shard_map/ppermute | solution.py:310
  16.9 28.8 %collective-permute-start.1 = (bf16[192,1472]{1,0:T(8,128)(2,1)}, bf16[192,1472]{1,0:T(8,128)(2,1)}, u32[]{:S(2)}, u32[]{:S(2)}) collective-permute-start(bf16[192,1472]{1,0:T(8,128)(2,1)} %get-tuple-element.91.refs_1_.refs_5_), channel_id=1, source_target_pairs={{0,8},{4,12},{8,0},{12,4},{16,24},{20,28},{24,16},{28,20},{1,9},{5... | collective-permute-start | bytes 1695752 | tf_op jit(solution)/shard_map/ppermute | solution.py:310
  45.8 12.9 %collective-permute-start.5 = (bf16[272,1152]{1,0:T(8,128)(2,1)S(1)}, bf16[272,1152]{1,0:T(8,128)(2,1)S(1)}, u32[]{:S(2)}, u32[]{:S(2)}) collective-permute-start(bf16[272,1152]{1,0:T(8,128)(2,1)S(1)} %fusion.2), channel_id=1, source_target_pairs={{0,16},{4,20},{8,24},{12,28},{16,0},{20,4},{24,8},{28,12},{1,17},{... | collective-permute-start | bytes 1880072 | tf_op jit(solution)/shard_map/ppermute | solution.py:310
  47.3 14.3 %collective-permute-start.4 = (bf16[272,1152]{1,0:T(8,128)(2,1)S(1)}, bf16[272,1152]{1,0:T(8,128)(2,1)S(1)}, u32[]{:S(2)}, u32[]{:S(2)}) collective-permute-start(bf16[272,1152]{1,0:T(8,128)(2,1)S(1)} %fusion.2), channel_id=1, source_target_pairs={{0,8},{4,12},{8,0},{12,4},{16,24},{20,28},{24,16},{28,20},{1,9},{5... | collective-permute-start | bytes 1880072 | tf_op jit(solution)/shard_map/ppermute | solution.py:310
  58.7 9.7 %collective-permute-start.7 = (bf16[144,1152]{1,0:T(8,128)(2,1)S(1)}, bf16[144,1152]{1,0:T(8,128)(2,1)S(1)}, u32[]{:S(2)}, u32[]{:S(2)}) collective-permute-start(bf16[144,1152]{1,0:T(8,128)(2,1)S(1)} %slice.71), channel_id=1, source_target_pairs={{0,8},{4,12},{8,0},{12,4},{16,24},{20,28},{24,16},{28,20},{1,9},{5... | collective-permute-start | bytes 995336 | tf_op jit(solution)/shard_map/ppermute | solution.py:310
  61.6 6.8 %collective-permute-start.6 = (bf16[128,1152]{1,0:T(8,128)(2,1)S(1)}, bf16[128,1152]{1,0:T(8,128)(2,1)S(1)}, u32[]{:S(2)}, u32[]{:S(2)}) collective-permute-start(bf16[128,1152]{1,0:T(8,128)(2,1)S(1)} %slice.70), channel_id=1, source_target_pairs={{0,16},{4,20},{8,24},{12,28},{16,0},{20,4},{24,8},{28,12},{1,17},{... | collective-permute-start | bytes 884744 | tf_op jit(solution)/shard_map/ppermute | solution.py:310
  70.3 8.7 %collective-permute-start.8 = (bf16[4,272,1152]{2,1,0:T(8,128)(2,1)S(1)}, bf16[4,272,1152]{2,1,0:T(8,128)(2,1)}, u32[]{:S(2)}, u32[]{:S(2)}) collective-permute-start(bf16[4,272,1152]{2,1,0:T(8,128)(2,1)S(1)} %pad_maximum_fusion.near_ref), channel_id=1, source_target_pairs={{0,4},{4,0},{8,12},{12,8},{16,20},{20,16},{24,28},{28,24},{1,5},{5... | collective-permute-start | bytes 7520264 | tf_op jit(solution)/shard_map/ppermute | solution.py:310
  70.4 16.5 %collective-permute-start.9 = (bf16[192,1472]{1,0:T(8,128)(2,1)}, bf16[192,1472]{1,0:T(8,128)(2,1)}, u32[]{:S(2)}, u32[]{:S(2)}) collective-permute-start(bf16[192,1472]{1,0:T(8,128)(2,1)} %collective-permute-done.refs_2_.refs_6_), channel_id=1, source_target_pairs={{0,16},{4,20},{8,24},{12,28},{16,0},{20,4},{24,8},{28,12},{1,17},{... | collective-permute-start | bytes 1695752 | tf_op jit(solution)/shard_map/ppermute | solution.py:310
  71.5 16.5 %collective-permute-start.10 = (bf16[192,1472]{1,0:T(8,128)(2,1)}, bf16[192,1472]{1,0:T(8,128)(2,1)}, u32[]{:S(2)}, u32[]{:S(2)}) collective-permute-start(bf16[192,1472]{1,0:T(8,128)(2,1)} %collective-permute-done.3.refs_5_.refs_9_), channel_id=1, source_target_pairs={{0,8},{4,12},{8,0},{12,4},{16,24},{20,28},{24,16},{28,20},{1,9},{5... | collective-permute-start | bytes 1695752 | tf_op jit(solution)/shard_map/ppermute | solution.py:310
  73.0 88.6 %all-to-all-start = ((bf16[8,192,1472]{2,1,0:T(8,128)(2,1)}), bf16[8,192,1472]{2,1,0:T(8,128)(2,1)}, u32[]{:S(2)}, u32[]{:S(2)}) async-start(bf16[8,192,1472]{2,1,0:T(8,128)(2,1)} %get-tuple-element.108.refs_6_), calls=%async_computation | async-start | bytes 9437184 | tf_op jit(solution)/shard_map/all_to_all | solution.py:1087
  78.0 83.0 %all-gather.6.cloned.1.call-start = ((), (), s32[]{:S(2)}) async-start(), calls=%async_computation.5 | async-start | bytes 1720320 | tf_op jit(solution)/shard_map/all_gather | solution.py:1126
  78.7 298.7 %reduce-scatter.3.cloned.1.call-start = ((), (), s32[]{:S(2)}) async-start(), calls=%async_computation.6 | async-start | bytes 3297280 | tf_op jit(solution)/shard_map/reduce_scatter | solution.py:1207
  100.2 5.5 %collective-permute-start.11 = (bf16[1,3,128,768]{3,2,1,0:T(8,128)(2,1)}, bf16[1,3,128,768]{3,2,1,0:T(8,128)(2,1)S(1)}, u32[]{:S(2)}, u32[]{:S(2)}) collective-permute-start(bf16[1,3,128,768]{3,2,1,0:T(8,128)(2,1)} %bitcast.69), channel_id=1, source_target_pairs={{0,4},{4,0},{8,12},{12,8},{16,20},{20,16},{24,28},{28,24},{1,5},{5... | collective-permute-start | bytes 1769480 | tf_op jit(solution)/shard_map/ppermute | solution.py:310
  100.2 5.4 %collective-permute-start.12 = (bf16[1,3,128,768]{3,2,1,0:T(8,128)(2,1)}, bf16[1,3,128,768]{3,2,1,0:T(8,128)(2,1)S(1)}, u32[]{:S(2)}, u32[]{:S(2)}) collective-permute-start(bf16[1,3,128,768]{3,2,1,0:T(8,128)(2,1)} %bitcast.74), channel_id=1, source_target_pairs={{0,4},{4,0},{8,12},{12,8},{16,20},{20,16},{24,28},{28,24},{1,5},{5... | collective-permute-start | bytes 1769480 | tf_op jit(solution)/shard_map/ppermute | solution.py:310
  100.7 4.9 %collective-permute-start.13 = (bf16[1,3,128,768]{3,2,1,0:T(8,128)(2,1)}, bf16[1,3,128,768]{3,2,1,0:T(8,128)(2,1)S(1)}, u32[]{:S(2)}, u32[]{:S(2)}) collective-permute-start(bf16[1,3,128,768]{3,2,1,0:T(8,128)(2,1)} %bitcast.79), channel_id=1, source_target_pairs={{0,4},{4,0},{8,12},{12,8},{16,20},{20,16},{24,28},{28,24},{1,5},{5... | collective-permute-start | bytes 1769480 | tf_op jit(solution)/shard_map/ppermute | solution.py:310
  100.8 4.9 %collective-permute-start.14 = (bf16[1,3,128,768]{3,2,1,0:T(8,128)(2,1)}, bf16[1,3,128,768]{3,2,1,0:T(8,128)(2,1)S(1)}, u32[]{:S(2)}, u32[]{:S(2)}) collective-permute-start(bf16[1,3,128,768]{3,2,1,0:T(8,128)(2,1)} %bitcast.84), channel_id=1, source_target_pairs={{0,4},{4,0},{8,12},{12,8},{16,20},{20,16},{24,28},{28,24},{1,5},{5... | collective-permute-start | bytes 1769480 | tf_op jit(solution)/shard_map/ppermute | solution.py:310
  121.1 43.3 %collective-permute-start.18 = (bf16[1472,896]{1,0:T(8,128)(2,1)}, bf16[1472,896]{1,0:T(8,128)(2,1)}, u32[]{:S(2)}, u32[]{:S(2)}) collective-permute-start(bf16[1472,896]{1,0:T(8,128)(2,1)} %all-gather.4.cloned.1.call-done.mine_ref), channel_id=1, source_target_pairs={{0,4},{4,0},{8,12},{12,8},{16,20},{20,16},{24,28},{28,24},{1,5},{5... | collective-permute-start | bytes 7913480 | tf_op jit(solution)/shard_map/ppermute | solution.py:310
  121.3 24.0 %collective-permute-start.17 = (bf16[384,384]{1,0:T(8,128)(2,1)S(1)}, bf16[384,384]{1,0:T(8,128)(2,1)S(1)}, u32[]{:S(2)}, u32[]{:S(2)}) collective-permute-start(bf16[384,384]{1,0:T(8,128)(2,1)S(1)} %bitcast.94), channel_id=1, source_target_pairs={{0,24},{4,28},{8,16},{12,20},{16,8},{20,12},{24,0},{28,4},{1,25},{... | collective-permute-start | bytes 884744 | tf_op jit(solution)/shard_map/ppermute | solution.py:310
  123.1 26.5 %collective-permute-start.16 = (bf16[384,384]{1,0:T(8,128)(2,1)S(1)}, bf16[384,384]{1,0:T(8,128)(2,1)S(1)}, u32[]{:S(2)}, u32[]{:S(2)}) collective-permute-start(bf16[384,384]{1,0:T(8,128)(2,1)S(1)} %bitcast.95), channel_id=1, source_target_pairs={{0,16},{4,20},{8,24},{12,28},{16,0},{20,4},{24,8},{28,12},{1,17},{... | collective-permute-start | bytes 884744 | tf_op jit(solution)/shard_map/ppermute | solution.py:310
  124.2 26.2 %collective-permute-start.15 = (bf16[384,384]{1,0:T(8,128)(2,1)S(1)}, bf16[384,384]{1,0:T(8,128)(2,1)S(1)}, u32[]{:S(2)}, u32[]{:S(2)}) collective-permute-start(bf16[384,384]{1,0:T(8,128)(2,1)S(1)} %bitcast.96), channel_id=1, source_target_pairs={{0,8},{4,12},{8,0},{12,4},{16,24},{20,28},{24,16},{28,20},{1,9},{5... | collective-permute-start | bytes 884744 | tf_op jit(solution)/shard_map/ppermute | solution.py:310
  207.6 21.1 %collective-permute-start.20 = (bf16[192,1472]{1,0:T(8,128)(2,1)}, bf16[192,1472]{1,0:T(8,128)(2,1)S(1)}, u32[]{:S(2)}, u32[]{:S(2)}) collective-permute-start(bf16[192,1472]{1,0:T(8,128)(2,1)} %get-tuple-element.116), channel_id=1, source_target_pairs={{0,16},{4,20},{8,24},{12,28},{16,0},{20,4},{24,8},{28,12},{1,17},{... | collective-permute-start | bytes 1695752 | tf_op jit(solution)/shard_map/ppermute | solution.py:310
  208.7 20.0 %collective-permute-start.21 = (bf16[192,1472]{1,0:T(8,128)(2,1)}, bf16[192,1472]{1,0:T(8,128)(2,1)S(1)}, u32[]{:S(2)}, u32[]{:S(2)}) collective-permute-start(bf16[192,1472]{1,0:T(8,128)(2,1)} %get-tuple-element.118), channel_id=1, source_target_pairs={{0,8},{4,12},{8,0},{12,4},{16,24},{20,28},{24,16},{28,20},{1,9},{5... | collective-permute-start | bytes 1695752 | tf_op jit(solution)/shard_map/ppermute | solution.py:310
  210.6 26.2 %collective-permute-start.22 = (bf16[192,1472]{1,0:T(8,128)(2,1)}, bf16[192,1472]{1,0:T(8,128)(2,1)S(1)}, u32[]{:S(2)}, u32[]{:S(2)}) collective-permute-start(bf16[192,1472]{1,0:T(8,128)(2,1)} %get-tuple-element.122), channel_id=1, source_target_pairs={{0,8},{4,12},{8,0},{12,4},{16,24},{20,28},{24,16},{28,20},{1,9},{5... | collective-permute-start | bytes 1695752 | tf_op jit(solution)/shard_map/ppermute | solution.py:310
  210.7 26.1 %collective-permute-start.23 = (bf16[192,1472]{1,0:T(8,128)(2,1)}, bf16[192,1472]{1,0:T(8,128)(2,1)S(1)}, u32[]{:S(2)}, u32[]{:S(2)}) collective-permute-start(bf16[192,1472]{1,0:T(8,128)(2,1)} %get-tuple-element.123), channel_id=1, source_target_pairs={{0,16},{4,20},{8,24},{12,28},{16,0},{20,4},{24,8},{28,12},{1,17},{... | collective-permute-start | bytes 1695752 | tf_op jit(solution)/shard_map/ppermute | solution.py:310
  240.7 14.7 %collective-permute-start.24 = (bf16[192,1472]{1,0:T(8,128)(2,1)}, bf16[192,1472]{1,0:T(8,128)(2,1)S(1)}, u32[]{:S(2)}, u32[]{:S(2)}) collective-permute-start(bf16[192,1472]{1,0:T(8,128)(2,1)} %get-tuple-element.124), channel_id=1, source_target_pairs={{0,8},{4,12},{8,0},{12,4},{16,24},{20,28},{24,16},{28,20},{1,9},{5... | collective-permute-start | bytes 1695752 | tf_op jit(solution)/shard_map/ppermute | solution.py:310
  242.5 14.3 %collective-permute-start.25 = (bf16[192,1472]{1,0:T(8,128)(2,1)}, bf16[192,1472]{1,0:T(8,128)(2,1)}, u32[]{:S(2)}, u32[]{:S(2)}) collective-permute-start(bf16[192,1472]{1,0:T(8,128)(2,1)} %get-tuple-element.125), channel_id=1, source_target_pairs={{0,16},{4,20},{8,24},{12,28},{16,0},{20,4},{24,8},{28,12},{1,17},{... | collective-permute-start | bytes 1695752 | tf_op jit(solution)/shard_map/ppermute | solution.py:310
  245.1 18.3 %collective-permute-start.31 = (bf16[1,736,896]{2,1,0:T(8,128)(2,1)}, bf16[1,736,896]{2,1,0:T(8,128)(2,1)S(1)}, u32[]{:S(2)}, u32[]{:S(2)}) collective-permute-start(bf16[1,736,896]{2,1,0:T(8,128)(2,1)} %get-tuple-element.168), channel_id=1, source_target_pairs={{0,4},{4,0},{8,12},{12,8},{16,20},{20,16},{24,28},{28,24},{1,5},{5... | collective-permute-start | bytes 3956744 | tf_op jit(solution)/shard_map/ppermute | solution.py:310
  245.1 18.3 %collective-permute-start.30 = (bf16[1,736,896]{2,1,0:T(8,128)(2,1)}, bf16[1,736,896]{2,1,0:T(8,128)(2,1)S(1)}, u32[]{:S(2)}, u32[]{:S(2)}) collective-permute-start(bf16[1,736,896]{2,1,0:T(8,128)(2,1)} %get-tuple-element.169), channel_id=1, source_target_pairs={{0,4},{4,0},{8,12},{12,8},{16,20},{20,16},{24,28},{28,24},{1,5},{5... | collective-permute-start | bytes 3956744 | tf_op jit(solution)/shard_map/ppermute | solution.py:310
  268.8 59.4 %all-to-all-start.1 = ((bf16[8,192,1472]{2,1,0:T(8,128)(2,1)}), bf16[8,192,1472]{2,1,0:T(8,128)(2,1)}, u32[]{:S(2)}, u32[]{:S(2)}) async-start(bf16[8,192,1472]{2,1,0:T(8,128)(2,1)} %get-tuple-element.129), calls=%async_computation.1 | async-start | bytes 9437184 | tf_op jit(solution)/shard_map/all_to_all | solution.py:1087
  273.8 115.3 %reduce-scatter.5.cloned.1.call-start = ((), (), s32[]{:S(2)}) async-start(), calls=%async_computation.7 | async-start | bytes 1720320 | tf_op jit(solution)/shard_map/reduce_scatter | solution.py:1208
  292.7 4.7 collective-permute-start.26
  292.8 4.6 collective-permute-start.27
  312.0 21.3 %collective-permute-start.35 = (bf16[4,4,64,1152]{3,2,1,0:T(8,128)(2,1)}, bf16[4,4,64,1152]{3,2,1,0:T(8,128)(2,1)}, u32[]{:S(2)}, u32[]{:S(2)}) collective-permute-start(bf16[4,4,64,1152]{3,2,1,0:T(8,128)(2,1)} %get-tuple-element.150), channel_id=1, source_target_pairs={{0,4},{4,0},{8,12},{12,8},{16,20},{20,16},{24,28},{28,24},{1,5},{5... | collective-permute-start | bytes 7077896 | tf_op jit(solution)/shard_map/ppermute | solution.py:310
  313.3 5.2 %collective-permute-start.53 = (bf16[4,112,1472]{2,1,0:T(8,128)(2,1)S(1)}, bf16[4,112,1472]{2,1,0:T(8,128)(2,1)S(1)}, u32[]{:S(2)}, u32[]{:S(2)}) collective-permute-start(bf16[4,112,1472]{2,1,0:T(8,128)(2,1)S(1)} %get-tuple-element.166), channel_id=1, source_target_pairs={{0,4},{4,0},{8,12},{12,8},{16,20},{20,16},{24,28},{28,24},{1,5},{5... | collective-permute-start | bytes 3956744 | tf_op jit(solution)/shard_map/ppermute | solution.py:310
  313.7 27.0 %collective-permute-start.32 = (bf16[384,768]{1,0:T(8,128)(2,1)}, bf16[384,768]{1,0:T(8,128)(2,1)S(1)}, u32[]{:S(2)}, u32[]{:S(2)}) collective-permute-start(bf16[384,768]{1,0:T(8,128)(2,1)} %get-tuple-element.145), channel_id=1, source_target_pairs={{0,8},{4,12},{8,0},{12,4},{16,24},{20,28},{24,16},{28,20},{1,9},{5... | collective-permute-start | bytes 1769480 | tf_op jit(solution)/shard_map/ppermute | solution.py:310
  315.6 27.5 %collective-permute-start.33 = (bf16[384,768]{1,0:T(8,128)(2,1)}, bf16[384,768]{1,0:T(8,128)(2,1)}, u32[]{:S(2)}, u32[]{:S(2)}) collective-permute-start(bf16[384,768]{1,0:T(8,128)(2,1)} %get-tuple-element.146), channel_id=1, source_target_pairs={{0,16},{4,20},{8,24},{12,28},{16,0},{20,4},{24,8},{28,12},{1,17},{... | collective-permute-start | bytes 1769480 | tf_op jit(solution)/shard_map/ppermute | solution.py:310
  317.1 37.4 %collective-permute-start.34 = (bf16[384,768]{1,0:T(8,128)(2,1)S(1)}, bf16[384,768]{1,0:T(8,128)(2,1)}, u32[]{:S(2)}, u32[]{:S(2)}) collective-permute-start(bf16[384,768]{1,0:T(8,128)(2,1)S(1)} %copy-done.52), channel_id=1, source_target_pairs={{0,24},{4,28},{8,16},{12,20},{16,8},{20,12},{24,0},{28,4},{1,25},{... | collective-permute-start | bytes 1769480 | tf_op jit(solution)/shard_map/ppermute | solution.py:310
  337.9 28.2 %collective-permute-start.36 = (bf16[4,64,1152]{2,1,0:T(8,128)(2,1)}, bf16[4,64,1152]{2,1,0:T(8,128)(2,1)S(1)}, u32[]{:S(2)}, u32[]{:S(2)}) collective-permute-start(bf16[4,64,1152]{2,1,0:T(8,128)(2,1)} %get-tuple-element.152), channel_id=1, source_target_pairs={{0,8},{4,12},{8,0},{12,4},{16,24},{20,28},{24,16},{28,20},{1,9},{5... | collective-permute-start | bytes 1769480 | tf_op jit(solution)/shard_map/ppermute | solution.py:310
  339.5 26.6 %collective-permute-start.37 = (bf16[4,64,1152]{2,1,0:T(8,128)(2,1)}, bf16[4,64,1152]{2,1,0:T(8,128)(2,1)S(1)}, u32[]{:S(2)}, u32[]{:S(2)}) collective-permute-start(bf16[4,64,1152]{2,1,0:T(8,128)(2,1)} %get-tuple-element.153), channel_id=1, source_target_pairs={{0,16},{4,20},{8,24},{12,28},{16,0},{20,4},{24,8},{28,12},{1,17},{... | collective-permute-start | bytes 1769480 | tf_op jit(solution)/shard_map/ppermute | solution.py:310
  341.6 35.9 %collective-permute-start.38 = (bf16[4,64,1152]{2,1,0:T(8,128)(2,1)}, bf16[4,64,1152]{2,1,0:T(8,128)(2,1)S(1)}, u32[]{:S(2)}, u32[]{:S(2)}) collective-permute-start(bf16[4,64,1152]{2,1,0:T(8,128)(2,1)} %get-tuple-element.154), channel_id=1, source_target_pairs={{0,24},{4,28},{8,16},{12,20},{16,8},{20,12},{24,0},{28,4},{1,25},{... | collective-permute-start | bytes 1769480 | tf_op jit(solution)/shard_map/ppermute | solution.py:310
  381.1 37.2 %collective-permute-start.44 = (bf16[368,896]{1,0:T(8,128)(2,1)S(1)}, bf16[368,896]{1,0:T(8,128)(2,1)S(1)}, u32[]{:S(2)}, u32[]{:S(2)}) collective-permute-start(bf16[368,896]{1,0:T(8,128)(2,1)S(1)} %copy-done.12), channel_id=1, source_target_pairs={{0,24},{4,28},{8,16},{12,20},{16,8},{20,12},{24,0},{28,4},{1,25},{... | collective-permute-start | bytes 1978376 | tf_op jit(solution)/shard_map/ppermute | solution.py:310
  381.7 37.1 %collective-permute-start.43 = (bf16[368,896]{1,0:T(8,128)(2,1)S(1)}, bf16[368,896]{1,0:T(8,128)(2,1)S(1)}, u32[]{:S(2)}, u32[]{:S(2)}) collective-permute-start(bf16[368,896]{1,0:T(8,128)(2,1)S(1)} %copy-done.12), channel_id=1, source_target_pairs={{0,16},{4,20},{8,24},{12,28},{16,0},{20,4},{24,8},{28,12},{1,17},{... | collective-permute-start | bytes 1978376 | tf_op jit(solution)/shard_map/ppermute | solution.py:310
  383.1 35.8 %collective-permute-start.42 = (bf16[368,896]{1,0:T(8,128)(2,1)S(1)}, bf16[368,896]{1,0:T(8,128)(2,1)S(1)}, u32[]{:S(2)}, u32[]{:S(2)}) collective-permute-start(bf16[368,896]{1,0:T(8,128)(2,1)S(1)} %copy-done.12), channel_id=1, source_target_pairs={{0,8},{4,12},{8,0},{12,4},{16,24},{20,28},{24,16},{28,20},{1,9},{5... | collective-permute-start | bytes 1978376 | tf_op jit(solution)/shard_map/ppermute | solution.py:310
  386.4 7.0 %collective-permute-start.41 = (bf16[64,1152]{1,0:T(8,128)(2,1)S(1)}, bf16[64,1152]{1,0:T(8,128)(2,1)S(1)}, u32[]{:S(2)}, u32[]{:S(2)}) collective-permute-start(bf16[64,1152]{1,0:T(8,128)(2,1)S(1)} %get-tuple-element.178), channel_id=1, source_target_pairs={{0,3},{1,2},{2,1},{3,0},{4,7},{5,6},{6,5},{7,4},{8,11},{9,10},{10,... | collective-permute-start | bytes 442376 | tf_op jit(solution)/shard_map/ppermute | solution.py:315
  389.1 9.8 %collective-permute-start.40 = (bf16[64,1152]{1,0:T(8,128)(2,1)S(1)}, bf16[64,1152]{1,0:T(8,128)(2,1)S(1)}, u32[]{:S(2)}, u32[]{:S(2)}) collective-permute-start(bf16[64,1152]{1,0:T(8,128)(2,1)S(1)} %get-tuple-element.179), channel_id=1, source_target_pairs={{0,2},{1,3},{2,0},{3,1},{4,6},{5,7},{6,4},{7,5},{8,10},{9,11},{10,... | collective-permute-start | bytes 442376 | tf_op jit(solution)/shard_map/ppermute | solution.py:315
  393.4 24.8 %collective-permute-start.56 = (bf16[112,1472]{1,0:T(8,128)(2,1)}, bf16[112,1472]{1,0:T(8,128)(2,1)S(1)}, u32[]{:S(2)}, u32[]{:S(2)}) collective-permute-start(bf16[112,1472]{1,0:T(8,128)(2,1)} %reduce-scatter.5.cloned.1.call-done.refs_0_), channel_id=1, source_target_pairs={{0,24},{4,28},{8,16},{12,20},{16,8},{20,12},{24,0},{28,4},{1,25},{... | collective-permute-start | bytes 989192 | tf_op jit(solution)/shard_map/ppermute | solution.py:310
  398.9 5.1 %collective-permute-start.39 = (bf16[64,1152]{1,0:T(8,128)(2,1)S(1)}, bf16[64,1152]{1,0:T(8,128)(2,1)S(1)}, u32[]{:S(2)}, u32[]{:S(2)}) collective-permute-start(bf16[64,1152]{1,0:T(8,128)(2,1)S(1)} %get-tuple-element.180), channel_id=1, source_target_pairs={{0,1},{1,0},{2,3},{3,2},{4,5},{5,4},{6,7},{7,6},{8,9},{9,8},{10,11... | collective-permute-start | bytes 442376 | tf_op jit(solution)/shard_map/ppermute | solution.py:315
  404.1 20.9 %collective-permute-start.55 = (bf16[112,1472]{1,0:T(8,128)(2,1)}, bf16[112,1472]{1,0:T(8,128)(2,1)}, u32[]{:S(2)}, u32[]{:S(2)}) collective-permute-start(bf16[112,1472]{1,0:T(8,128)(2,1)} %reduce-scatter.5.cloned.1.call-done.refs_0_), channel_id=1, source_target_pairs={{0,16},{4,20},{8,24},{12,28},{16,0},{20,4},{24,8},{28,12},{1,17},{... | collective-permute-start | bytes 989192 | tf_op jit(solution)/shard_map/ppermute | solution.py:310
  418.3 18.2 %collective-permute-start.48 = (bf16[368,896]{1,0:T(8,128)(2,1)S(1)}, bf16[368,896]{1,0:T(8,128)(2,1)S(1)}, u32[]{:S(2)}, u32[]{:S(2)}) collective-permute-start(bf16[368,896]{1,0:T(8,128)(2,1)S(1)} %copy-done.12), channel_id=1, source_target_pairs={{0,4},{4,0},{8,12},{12,8},{16,20},{20,16},{24,28},{28,24},{1,5},{5... | collective-permute-start | bytes 1978376 | tf_op jit(solution)/shard_map/ppermute | solution.py:310
  418.3 25.0 %collective-permute-start.51 = (bf16[368,896]{1,0:T(8,128)(2,1)S(1)}, bf16[368,896]{1,0:T(8,128)(2,1)}, u32[]{:S(2)}, u32[]{:S(2)}) collective-permute-start(bf16[368,896]{1,0:T(8,128)(2,1)S(1)} %collective-permute-done.44.refs_6_.refs_3_), channel_id=1, source_target_pairs={{0,4},{4,0},{8,12},{12,8},{16,20},{20,16},{24,28},{28,24},{1,5},{5... | collective-permute-start | bytes 1978376 | tf_op jit(solution)/shard_map/ppermute | solution.py:310
  418.8 25.0 %collective-permute-start.50 = (bf16[368,896]{1,0:T(8,128)(2,1)S(1)}, bf16[368,896]{1,0:T(8,128)(2,1)}, u32[]{:S(2)}, u32[]{:S(2)}) collective-permute-start(bf16[368,896]{1,0:T(8,128)(2,1)S(1)} %collective-permute-done.43.refs_5_.refs_2_), channel_id=1, source_target_pairs={{0,4},{4,0},{8,12},{12,8},{16,20},{20,16},{24,28},{28,24},{1,5},{5... | collective-permute-start | bytes 1978376 | tf_op jit(solution)/shard_map/ppermute | solution.py:310
  419.0 24.9 %collective-permute-start.49 = (bf16[368,896]{1,0:T(8,128)(2,1)S(1)}, bf16[368,896]{1,0:T(8,128)(2,1)}, u32[]{:S(2)}, u32[]{:S(2)}) collective-permute-start(bf16[368,896]{1,0:T(8,128)(2,1)S(1)} %collective-permute-done.42.refs_4_.refs_1_), channel_id=1, source_target_pairs={{0,4},{4,0},{8,12},{12,8},{16,20},{20,16},{24,28},{28,24},{1,5},{5... | collective-permute-start | bytes 1978376 | tf_op jit(solution)/shard_map/ppermute | solution.py:310
  425.0 9.7 %collective-permute-start.54 = (bf16[112,1472]{1,0:T(8,128)(2,1)}, bf16[112,1472]{1,0:T(8,128)(2,1)}, u32[]{:S(2)}, u32[]{:S(2)}) collective-permute-start(bf16[112,1472]{1,0:T(8,128)(2,1)} %reduce-scatter.5.cloned.1.call-done.refs_0_), channel_id=1, source_target_pairs={{0,8},{4,12},{8,0},{12,4},{16,24},{20,28},{24,16},{28,20},{1,9},{5... | collective-permute-start | bytes 989192 | tf_op jit(solution)/shard_map/ppermute | solution.py:310
  434.7 6.4 %collective-permute-start.47 = (bf16[64,1152]{1,0:T(8,128)(2,1)}, bf16[64,1152]{1,0:T(8,128)(2,1)S(1)}, u32[]{:S(2)}, u32[]{:S(2)}) collective-permute-start(bf16[64,1152]{1,0:T(8,128)(2,1)} %sum_parts.3.refs_0_), channel_id=1, source_target_pairs={{0,24},{4,28},{8,16},{12,20},{16,8},{20,12},{24,0},{28,4},{1,25},{... | collective-permute-start | bytes 442376 | tf_op jit(solution)/shard_map/ppermute | solution.py:310
  436.5 6.8 %collective-permute-start.46 = (bf16[64,1152]{1,0:T(8,128)(2,1)}, bf16[64,1152]{1,0:T(8,128)(2,1)S(1)}, u32[]{:S(2)}, u32[]{:S(2)}) collective-permute-start(bf16[64,1152]{1,0:T(8,128)(2,1)} %sum_parts.3.refs_0_), channel_id=1, source_target_pairs={{0,16},{4,20},{8,24},{12,28},{16,0},{20,4},{24,8},{28,12},{1,17},{... | collective-permute-start | bytes 442376 | tf_op jit(solution)/shard_map/ppermute | solution.py:310
  441.0 11.5 %collective-permute-start.45 = (bf16[64,1152]{1,0:T(8,128)(2,1)}, bf16[64,1152]{1,0:T(8,128)(2,1)S(1)}, u32[]{:S(2)}, u32[]{:S(2)}) collective-permute-start(bf16[64,1152]{1,0:T(8,128)(2,1)} %sum_parts.3.refs_0_), channel_id=1, source_target_pairs={{0,8},{4,12},{8,0},{12,4},{16,24},{20,28},{24,16},{28,20},{1,9},{5... | collective-permute-start | bytes 442376 | tf_op jit(solution)/shard_map/ppermute | solution.py:310
  443.3 12.0 %collective-permute-start.57 = (bf16[112,1472]{1,0:T(8,128)(2,1)}, bf16[112,1472]{1,0:T(8,128)(2,1)}, u32[]{:S(2)}, u32[]{:S(2)}) collective-permute-start(bf16[112,1472]{1,0:T(8,128)(2,1)} %reduce-scatter.5.cloned.1.call-done.refs_0_), channel_id=1, source_target_pairs={{0,4},{4,0},{8,12},{12,8},{16,20},{20,16},{24,28},{28,24},{1,5},{5... | collective-permute-start | bytes 989192 | tf_op jit(solution)/shard_map/ppermute | solution.py:310
  443.3 12.0 %collective-permute-start.60 = (bf16[112,1472]{1,0:T(8,128)(2,1)}, bf16[112,1472]{1,0:T(8,128)(2,1)}, u32[]{:S(2)}, u32[]{:S(2)}) collective-permute-start(bf16[112,1472]{1,0:T(8,128)(2,1)} %copy-done.35), channel_id=1, source_target_pairs={{0,4},{4,0},{8,12},{12,8},{16,20},{20,16},{24,28},{28,24},{1,5},{5... | collective-permute-start | bytes 989192 | tf_op jit(solution)/shard_map/ppermute | solution.py:310
  443.8 11.5 %collective-permute-start.59 = (bf16[112,1472]{1,0:T(8,128)(2,1)}, bf16[112,1472]{1,0:T(8,128)(2,1)}, u32[]{:S(2)}, u32[]{:S(2)}) collective-permute-start(bf16[112,1472]{1,0:T(8,128)(2,1)} %collective-permute-done.55.refs_2_), channel_id=1, source_target_pairs={{0,4},{4,0},{8,12},{12,8},{16,20},{20,16},{24,28},{28,24},{1,5},{5... | collective-permute-start | bytes 989192 | tf_op jit(solution)/shard_map/ppermute | solution.py:310
  443.9 11.4 %collective-permute-start.58 = (bf16[112,1472]{1,0:T(8,128)(2,1)}, bf16[112,1472]{1,0:T(8,128)(2,1)}, u32[]{:S(2)}, u32[]{:S(2)}) collective-permute-start(bf16[112,1472]{1,0:T(8,128)(2,1)} %collective-permute-done.54.refs_1_), channel_id=1, source_target_pairs={{0,4},{4,0},{8,12},{12,8},{16,20},{20,16},{24,28},{28,24},{1,5},{5... | collective-permute-start | bytes 989192 | tf_op jit(solution)/shard_map/ppermute | solution.py:310
  455.2 8.0 %collective-permute-start.52 = (bf16[4,64,1152]{2,1,0:T(8,128)(2,1)}, bf16[4,64,1152]{2,1,0:T(8,128)(2,1)S(1)}, u32[]{:S(2)}, u32[]{:S(2)}) collective-permute-start(bf16[4,64,1152]{2,1,0:T(8,128)(2,1)} %stack_small.1.near_ref), channel_id=1, source_target_pairs={{0,4},{4,0},{8,12},{12,8},{16,20},{20,16},{24,28},{28,24},{1,5},{5... | collective-permute-start | bytes 1769480 | tf_op jit(solution)/shard_map/ppermute | solution.py:310
  (58 other events, 363.1 us)
Sparse Core Ops, SparseCore 0:
  48.9 53.0 all-gather.3
  104.2 32.5 all-gather.5
  268.9 51.8 reduce-scatter.2
  323.6 33.3 reduce-scatter.4
